TPU v7x, 32 devices: a whole 2x2x4 slice. The times are simulated.
32 devices in a mesh: samp: 4 (over y, x), var: 8 (over z, core).
Axes of the slice: x: 2, y: 2, z: 4, core: 2. Of those that a mesh axis runs over, the one named last changes fastest.
Arguments:
- dosage: bfloat16 [8192, 16384], P('samp', 'var'), may hold values from -6 to 6
- traits: float32 [8192, 128], P(('samp', 'var')), may hold values from -6 to 6
- coef_now: float32 [128, 256, 128], P('var', 'samp'), may hold values from -6 to 6
- coef_prev: float32 [128, 256, 128], P('var', 'samp'), may hold values from -6 to 6
- block_inverse: bfloat16 [128, 256, 4, 256], P('var', 'samp'), may hold values from -0.1875 to 0.1875
- penalty: float32 [128], replicated, may hold values from 0.05 to 0.5
- block_start: int32 [64], replicated, may hold values from 0 to 1, as said below
- unit_owner: int32 [64], replicated, may hold values from 0 to 7, as said below
Outputs:
- coef_next: float32 [128, 256, 128], P('var', 'samp')
- residual: float32 [8192, 128], P(('samp', 'var'))
Inputs may be any that keep to these rules, and one draw needn't show every extreme that they name: `block_start`: 1 where a linkage block begins, else 0. The first unit of every device's 8 units begins a block, and a block holds 1 to 4 units of 256 variants. `unit_owner`: the index along var of the device that owns each unit's block, equal for all units of a block. For a unit of the device with index d along var it is (d + j) modulo the size of var, with 1 <= j <= 4. An owner holds at most 16 units and some owner holds exactly 16; the units of one device that belong to one owner are at most 4, and some device has exactly 4 for one owner.
All inputs are finite; a program needn't handle non-finite values.
Results may differ from a plain program's by a relative error of at most 0.0072.
Values may be sent and summed in bfloat16 or wider, within the bound.
No kernel may reach another device: no remote copies, remote signals or barrier semaphores. Data moves between devices by JAX's collectives and lax.ppermute only.
A program may use at most 64 MiB of HBM per device.

v0:
```python
import functools
import math

import jax
import jax.numpy as jnp
from jax import lax
from jax.experimental import pallas as pl
from jax.experimental.pallas import tpu as pltpu
from jax.sharding import PartitionSpec as P


MOMENTA = (0.4, 0.55)
CORES = 2
MIB = 1 << 20
LARGE = 42


SMEM = pl.BlockSpec(memory_space=pltpu.SMEM)
VMEM = pl.BlockSpec(memory_space=pltpu.VMEM)
FAR = pl.BlockSpec(memory_space=pl.ANY)
F32, HALF = jnp.float32, jnp.bfloat16


def like(shape, dtype):
    return jax.ShapeDtypeStruct(shape, dtype)


def local(body, scalars, arrays, outs, scratch=(), limit=8, flops=0, far=0):
    single = not isinstance(outs, list)
    moved = sum(math.prod(a.shape) * a.dtype.itemsize for a in [*arrays, *([outs] if single else outs)])
    return pl.pallas_call(
        body,
        in_specs=[SMEM] * len(scalars) + [FAR] * far + [VMEM] * (len(arrays) - far),
        out_specs=VMEM if single else [VMEM] * len(outs),
        out_shape=outs,
        scratch_shapes=list(scratch),
        compiler_params=pltpu.CompilerParams(vmem_limit_bytes=limit * MIB),
        cost_estimate=pl.CostEstimate(flops=flops, bytes_accessed=moved, transcendentals=0),
    )(*scalars, *arrays)


def shifted(block, axis, distance):
    count = lax.axis_size(axis)
    return lax.ppermute(block, axis, [((i - distance) % count, i) for i in range(count)])


def crossed(block, axis, mask):
    count = lax.axis_size(axis)
    return lax.ppermute(block, axis, [(i, i ^ mask) for i in range(count)])


def held_by(group, owner):
    return group ^ (2 * (owner & 1))


def held_by_seen(rank, variant):
    return rank ^ (2 * ((variant + rank + 1) & 1))


def to_owners(block, mask):
    quarters, owners = lax.axis_size("samp"), lax.axis_size("var")
    route = [
        (s * owners + v, (s ^ mask) * owners + (v + held_by_seen(s ^ mask, v) + 1) % owners)
        for s in range(quarters)
        for v in range(owners)
    ]
    return lax.ppermute(block, ("samp", "var"), route)


def to_variants(block, mask):
    quarters, owners = lax.axis_size("samp"), lax.axis_size("var")
    route = [
        (s * owners + o, (s ^ mask) * owners + (o - held_by(s, o) - 1) % owners)
        for s in range(quarters)
        for o in range(owners)
    ]
    return lax.ppermute(block, ("samp", "var"), route)


class Layout:
    def __init__(self, codes, capacity, per_device):
        self.slot = 0
        self.live = self.slot + codes
        self.first = self.live + codes
        self.code_of_slot = self.first + codes
        self.local = self.code_of_slot + capacity
        self.unit = self.local + per_device
        self.size = self.unit + codes


def begin_body(spot, owners, reach, pair, per_device, momentum, where, start, owner, now, before, out, *refs):
    sent, (now_here, before_here, arrived) = refs[:reach], refs[reach:]
    copies = [
        pltpu.make_async_copy(now, now_here, arrived.at[0]),
        pltpu.make_async_copy(before, before_here, arrived.at[1]),
    ]
    for copy in copies:
        copy.start()
    tables_body(spot, owners, reach, pair, per_device, where, start, owner, out)
    for copy in copies:
        copy.wait()
    for g in range(reach):
        for p in range(pair):
            slot = out[spot.slot + g * pair + p]
            live = out[spot.live + g * pair + p]
            point = now_here[slot] + momentum * (now_here[slot] - before_here[slot])
            sent[g][p] = jnp.where(live == 1, point, 0.0).astype(HALF)


def tables_body(spot, owners, reach, pair, per_device, where, start, owner, out):
    var = where[0]
    for i in range(spot.size):
        empty = spot.code_of_slot <= i < spot.local or i >= spot.unit
        out[i] = jnp.int32(-1 if empty else 0)
    devices = [lax.rem(var - gap + owners, owners) for gap in range(1, reach + 1)]
    owned = [
        [(owner[d * per_device + j] == var).astype(jnp.int32) for j in range(per_device)]
        for d in devices
    ]
    counts = [functools.reduce(lambda a, b: a + b, flags) for flags in owned]
    for g in range(reach):
        place = jnp.int32(0)
        first = jnp.int32(0)
        base = jnp.int32(0)
        for h in range(reach):
            if h != g:
                base = base + jnp.where(devices[h] < devices[g], counts[h], 0)
        for j in range(per_device):
            first = jnp.where(start[devices[g] * per_device + j] == 1, place, first)

            @pl.when(owned[g][j] == 1)
            def _():
                code = g * pair + place
                out[spot.slot + code] = base + place
                out[spot.live + code] = jnp.int32(1)
                out[spot.first + code] = first
                out[spot.code_of_slot + base + place] = code

            place = place + owned[g][j]
    mine = [owner[var * per_device + j] for j in range(per_device)]
    for j in range(per_device):
        gap = lax.rem(mine[j] - var + owners, owners)
        place = jnp.int32(0)
        for i in range(j):
            place = place + (mine[i] == mine[j]).astype(jnp.int32)
        code = (gap - 1) * pair + place
        out[spot.local + j] = code
        out[spot.unit + code] = jnp.int32(j)


def states_body(spot, quarters, pair, where, table, now, before, *outs):
    for k in range(quarters):
        for p in range(pair):
            code = held_by(where[1] ^ k, where[0]) * pair + p
            slot = table[spot.slot + code]
            live = table[spot.live + code] == 1
            outs[k][0, p] = jnp.where(live, now[slot], 0.0)
            outs[k][1, p] = jnp.where(live, before[slot], 0.0)


def panels_body(spot, quarters, pair, most, where, table, panels, *outs):
    width = panels.shape[2] // most
    for k in range(quarters):
        for p in range(pair):
            row = held_by(where[1] ^ k, where[0]) * pair
            slot = table[spot.slot + row + p]
            first = table[spot.first + row + p]
            live = table[spot.live + row + p]
            for q in range(pair):
                same = (table[spot.first + row + q] == first) & (table[spot.live + row + q] == 1)
                part = jnp.clip(q - first, 0, most - 1)
                block = panels[slot, :, pl.ds(pl.multiple_of(part * width, width), width)]
                use = same & (live == 1)
                outs[k][p, :, q * width : (q + 1) * width] = jnp.where(use, block, jnp.zeros_like(block))


def local_values_body(spot, pair, turned, where, table, *refs):
    pieces, out, held = refs[:-2], refs[-2], refs[-1]
    for k, piece in enumerate(pieces):
        held[k] = piece[...]
    for u in range(out.shape[0]):
        code = table[spot.local + u]
        group = lax.div(code, pair)
        at = (held_by_seen(group, where[0]) ^ where[1]) if turned else group
        out[u] = held[at, lax.rem(code, pair)]


def place_values(quarters, where, pieces, values):
    units, quarter_rows = pieces[0].shape[:2]
    for k in range(quarters):
        for u in range(units):
            at = u * quarters * quarter_rows + (where[1] ^ k) * quarter_rows
            values[pl.ds(pl.multiple_of(at, quarter_rows), quarter_rows), :] = pieces[k][u]


def predict_blocks(scale, blocks, values, out, ready=None):
    chips, rows = out.shape[:2]
    for i in range(chips):
        if ready is not None:
            ready[i].wait()
        block = blocks[i * rows : (i + 1) * rows, :]
        out[i] = jnp.dot(block, values[...], preferred_element_type=F32) * scale


def first_predict_body(quarters, scale, other, where, dosage, *refs):
    pieces, (out, blocks, values, arrived) = refs[:quarters], refs[quarters:]
    chips, rows = out.shape[:2]
    core, chip = lax.rem(where[0], CORES), lax.div(where[0], CORES)
    side = (1 - core) if other else core
    copies = []
    for i in range(chips):
        at = pl.multiple_of(((chip ^ i) * CORES + side) * rows, rows)
        here = blocks.at[pl.ds(i * rows, rows), :]
        copies.append(pltpu.make_async_copy(dosage.at[pl.ds(at, rows), :], here, arrived.at[i]))
        copies[-1].start()
    place_values(quarters, where, pieces, values)
    predict_blocks(scale, blocks, values, out, copies)


def predict_body(quarters, scale, where, blocks, *refs):
    pieces, (out, values) = refs[:quarters], refs[quarters:]
    place_values(quarters, where, pieces, values)
    predict_blocks(scale, blocks, values, out)


def gradient_body(quarters, units, scale, where, *refs):
    sides, pieces, outs = refs[:CORES], refs[CORES : -quarters - 2], refs[-quarters - 2 : -2]
    residual, total = refs[-2:]
    chips, rows = len(pieces) // CORES, pieces[0].shape[0]
    for i, piece in enumerate(pieces):
        residual[i * rows : (i + 1) * rows, :] = piece[...]
    turned = [residual[c * chips * rows : (c + 1) * chips * rows, :].T for c in range(CORES)]
    width = sides[0].shape[1] // units
    quarter_rows = width // quarters
    for u in range(units):
        product = jnp.dot(turned[0], sides[0][:, u * width : (u + 1) * width], preferred_element_type=F32)
        product += jnp.dot(turned[1], sides[1][:, u * width : (u + 1) * width], preferred_element_type=F32)
        total[u] = product.T * scale
        for k in range(quarters):
            at = pl.multiple_of((where[1] ^ k) * quarter_rows, quarter_rows)
            outs[k][u] = total[u, pl.ds(at, quarter_rows), :].astype(outs[k].dtype)


def leave_body(spot, quarters, pair, where, table, *refs):
    sums, outs = refs[:quarters], refs[quarters:]
    for k in range(quarters):
        for p in range(pair):
            unit = table[spot.unit + held_by_seen(where[1] ^ k, where[0]) * pair + p]
            at = jnp.maximum(unit, 0)
            total = sums[0][at]
            for j in range(1, quarters):
                total = total + sums[j][at].astype(F32)
            outs[k][p] = jnp.where(unit >= 0, total, 0.0).astype(HALF)


def update_body(quarters, momenta, where, penalty, *refs):
    last = len(momenta) == 1
    panels, pieces, states = refs[:quarters], refs[quarters : 2 * quarters], refs[2 * quarters : 3 * quarters]
    outs, gradient = refs[3 * quarters : -1], refs[-1]
    pair, quarter_rows = pieces[0].shape[:2]
    for k in range(quarters):
        for p in range(pair):
            at = p * quarters * quarter_rows + (where[1] ^ k) * quarter_rows
            gradient[pl.ds(pl.multiple_of(at, quarter_rows), quarter_rows), :] = pieces[k][p]
    for k in range(quarters):
        panel = panels[k][...].reshape(pair * quarter_rows, -1)
        direction = jnp.dot(panel, gradient[...], preferred_element_type=F32)
        direction = direction.reshape(pair, quarter_rows, -1)
        if last:
            point = states[k][...]
        else:
            now = states[k][0]
            point = now + momenta[0] * (now - states[k][1])
        stepped = point - direction
        size = jnp.maximum(jnp.abs(stepped) - penalty[...], 0.0)
        updated = jnp.where(stepped > 0, size, jnp.where(stepped < 0, -size, 0.0))
        if last:
            outs[k][...] = updated
        else:
            following = updated + momenta[1] * (updated - now)
            outs[k][...] = following
            outs[quarters + k][...] = following.astype(HALF)


def finish_body(spot, pair, where, table, *refs):
    pieces, out, held = refs[:-2], refs[-2], refs[-1]
    for k, piece in enumerate(pieces):
        held[k] = piece[...]
    for slot in range(out.shape[0]):
        code = table[spot.code_of_slot + slot]
        known = jnp.maximum(code, 0)
        block = held[held_by(lax.div(known, pair), where[0]) ^ where[1], lax.rem(known, pair)]
        out[slot] = jnp.where(code >= 0, block, 0.0)


def steps(dosage, traits, coef_now, coef_prev, block_inverse, penalty, block_start, unit_owner):
    owners = lax.axis_size("var")
    quarters = lax.axis_size("samp")
    var_index = lax.axis_index("var").astype(jnp.int32)
    samp_index = lax.axis_index("samp").astype(jnp.int32)
    capacity, quarter_rows, right_cols = coef_now.shape
    block_most, unit_rows = block_inverse.shape[2:]
    per_device = dosage.shape[1] // unit_rows
    pair = min(block_most, per_device)
    reach = capacity // pair
    assert reach == quarters and owners % CORES == 0 and owners & (owners - 1) == 0
    chips = owners // CORES
    rows = dosage.shape[0] // owners
    codes = reach * pair
    inv_scale = 1.0 / math.sqrt(dosage.shape[1] * owners)
    grad_scale = 0.5 / math.sqrt(dosage.shape[0] * quarters)
    spot = Layout(codes, capacity, per_device)
    where = jnp.stack([var_index, samp_index])
    ranks = range(quarters)
    piece = (pair, quarter_rows, right_cols)
    share = (per_device, quarter_rows, right_cols)

    table, *sent = pl.pallas_call(
        functools.partial(begin_body, spot, owners, reach, pair, per_device, MOMENTA[0]),
        name="begin",
        in_specs=[SMEM] * 3 + [FAR] * 2,
        out_specs=[SMEM] + [VMEM] * reach,
        out_shape=[like((spot.size,), jnp.int32)] + [like(piece, HALF)] * reach,
        scratch_shapes=[pltpu.VMEM(coef_now.shape, F32)] * 2 + [pltpu.SemaphoreType.DMA((2,))],
        compiler_params=pltpu.CompilerParams(vmem_limit_bytes=60 * MIB),
    )(where, block_start, unit_owner, coef_now, coef_prev)
    arrived = [shifted(sent[g], "var", -g - 1) for g in range(reach)]
    states = local(
        functools.partial(states_body, spot, quarters, pair),
        [where, table], [coef_now, coef_prev], [like((2, *piece), F32)] * quarters,
    )
    states = [states[0]] + [crossed(states[k], "samp", k) for k in ranks[1:]]
    penalty = penalty.reshape(1, 1, right_cols)

    for step in range(len(MOMENTA)):
        own = local(
            functools.partial(local_values_body, spot, pair, step > 0),
            [where, table], arrived, like(share, HALF),
            [pltpu.VMEM((reach, *piece), HALF)],
        )
        pieces = [own] + [crossed(own, "samp", k) for k in ranks[1:]]
        if step == 0:
            block_inverse = lax.optimization_barrier((own, block_inverse))[1]
            panels = local(
                functools.partial(panels_body, spot, quarters, pair, block_most),
                [where, table],
                [block_inverse.reshape(capacity, quarter_rows, block_most * unit_rows)],
                [like((pair, quarter_rows, block_most * unit_rows), HALF)] * quarters, limit=10,
            )
            pieces, panels = lax.optimization_barrier((pieces, panels))
            panels = [panels[0]] + [crossed(panels[k], "samp", k) for k in ranks[1:]]
        buffers = [pltpu.VMEM((dosage.shape[1], right_cols), HALF)]
        half = like((chips, rows, right_cols), F32)
        flops = dosage.shape[0] * dosage.shape[1] * right_cols
        if step == 0:
            block = like((chips * rows, dosage.shape[1]), HALF)
            (given, given_rows), (kept, kept_rows) = (
                local(
                    functools.partial(first_predict_body, quarters, inv_scale, other),
                    [where], [dosage, *pieces], [half, block],
                    [*buffers, pltpu.SemaphoreType.DMA((chips,))], limit=LARGE, flops=flops, far=1,
                )
                for other in (True, False)
            )
        else:
            given, kept = (
                local(
                    functools.partial(predict_body, quarters, inv_scale),
                    [where], [side, *pieces], half, buffers, limit=8, flops=flops,
                )
                for side in (given_rows, kept_rows)
            )
        both = kept + crossed(given, "var", 1)
        total = both[0]
        for i in range(1, chips):
            total = total + crossed(both[i].astype(HALF), "var", CORES * i).astype(F32)
        residual = total - traits
        residual_b = residual.astype(HALF)
        mine = [residual_b] + [crossed(residual_b, "var", CORES * i) for i in range(1, chips)]
        others = [crossed(block, "var", 1) for block in mine]
        sums = local(
            functools.partial(gradient_body, quarters, per_device, grad_scale),
            [where], [kept_rows, given_rows, *mine, *others],
            [like(share, F32 if k == 0 else HALF) for k in ranks],
            [
                pltpu.VMEM((dosage.shape[0], right_cols), HALF),
                pltpu.VMEM((per_device, unit_rows, right_cols), F32),
            ], limit=15, flops=2 * dosage.shape[0] * dosage.shape[1] * right_cols,
        )
        sums = [sums[0]] + [crossed(sums[k], "samp", k) for k in ranks[1:]]
        leaving = local(
            functools.partial(leave_body, spot, quarters, pair),
            [where, table], sums, [like(piece, HALF)] * quarters,
        )
        landed = [to_owners(leaving[k], k) for k in ranks]
        last = step == len(MOMENTA) - 1
        outs = [like(piece, F32)] * quarters + ([] if last else [like(piece, HALF)] * quarters)
        result = local(
            functools.partial(update_body, quarters, MOMENTA[step : step + 2]),
            [where], [penalty, *panels, *landed, *states], outs,
            [pltpu.VMEM((pair * unit_rows, right_cols), HALF)], limit=12,
            flops=2 * (pair * unit_rows) ** 2 * right_cols,
        )
        states = list(result[:quarters])
        if not last:
            arrived = [to_variants(result[quarters + k], k) for k in ranks]
    states = [states[0]] + [crossed(states[k], "samp", k) for k in ranks[1:]]
    current = local(
        functools.partial(finish_body, spot, pair),
        [where, table], states, like((capacity, quarter_rows, right_cols), F32),
        [pltpu.VMEM((quarters, *piece), F32)],
    )
    return (current, residual)


def solution(mesh):
    placed = (
        P("samp", "var"),
        P(("samp", "var"), None),
        P("var", "samp", None),
        P("var", "samp", None),
        P("var", "samp", None, None),
        P(),
        P(),
        P(),
    )
    return jax.shard_map(
        steps,
        mesh=mesh,
        in_specs=placed,
        out_specs=(P("var", "samp", None), P(("samp", "var"), None)),
        check_vma=False,
    )
```

profile of v0, /device:TPU:0, one launch (start us, length us, event | category | flops | bytes accessed | tf_op | source)
XLA Modules:
  0.0 199.3 jit_solution(12597940260212780877)
XLA Ops:
  1.3 2.7 %begin.1 = (s32[88]{0:T(128)}, bf16[4,64,128]{2,1,0:T(8,128)(2,1)}, bf16[4,64,128]{2,1,0:T(8,128)(2,1)}, bf16[4,64,128]{2,1,0:T(8,128)(2,1)}, bf16[4,64,128]{2,1,0:T(8,128)(2,1)}) custom-call(s32[2]{0:T(128)} %pad_add_fusion.where, s32[64]{0:T(128)} %start.1, s32[64]{0:T(128)} %owner.1, f32[16,64,128]{2,1,0:T(8,128)} %now.3, f32[16,64,128]{2,1,0:T(8,128)} %before.3), custom_call_target="tpu_custom_call" | custom-call | tf_op jit(solution)/shard_map/begin/pallas_call | solution.py:318
  4.0 4.6 %collective-permute-start = (bf16[4,64,128]{2,1,0:T(8,128)(2,1)}, bf16[4,64,128]{2,1,0:T(8,128)(2,1)S(1)}, u32[]{:S(2)}, u32[]{:S(2)}) collective-permute-start(bf16[4,64,128]{2,1,0:T(8,128)(2,1)} %get-tuple-element.57), channel_id=1, source_target_pairs={{1,0},{2,1},{3,2},{4,3},{5,4},{6,5},{7,6},{0,7},{9,8},{10,9},{11,1... | collective-permute-start | bytes 196616 | tf_op jit(solution)/shard_map/ppermute | solution.py:44
  9.2 2.7 %collective-permute-start.3 = (bf16[4,64,128]{2,1,0:T(8,128)(2,1)}, bf16[4,64,128]{2,1,0:T(8,128)(2,1)S(1)}, u32[]{:S(2)}, u32[]{:S(2)}) collective-permute-start(bf16[4,64,128]{2,1,0:T(8,128)(2,1)} %get-tuple-element.60), channel_id=1, source_target_pairs={{4,0},{5,1},{6,2},{7,3},{0,4},{1,5},{2,6},{3,7},{12,8},{13,9},{14,... | collective-permute-start | bytes 196616 | tf_op jit(solution)/shard_map/ppermute | solution.py:44
  14.1 4.0 %collective-permute-done.3.refs_3_ = bf16[4,64,128]{2,1,0:T(8,128)(2,1)S(1)} collective-permute-done((bf16[4,64,128]{2,1,0:T(8,128)(2,1)}, bf16[4,64,128]{2,1,0:T(8,128)(2,1)S(1)}, u32[]{:S(2)}, u32[]{:S(2)}) %collective-permute-start.3) | collective-permute-done | bytes 65568 | tf_op jit(solution)/shard_map/ppermute | solution.py:44
  23.6 3.2 %reshape.17.panels = bf16[16,64,1024]{2,1,0:T(8,128)(2,1)S(1)} reshape(bf16[16,64,4,256]{3,2,1,0:T(4,128)(2,1)} %param.12) | data formatting | bytes 4194304 | tf_op jit(solution)/shard_map/reshape | solution.py:347
  29.4 3.6 %shard_map.98 = (f32[4,256,128]{2,1,0:T(8,128)S(1)}, bf16[1024,2048]{1,0:T(8,128)(2,1)S(1)}) custom-call(s32[2]{0:T(128)S(1)} %copy-done.3, bf16[2048,2048]{1,0:T(8,128)(2,1)} %dosage.3, bf16[8,64,128]{2,1,0:T(8,128)(2,1)S(1)} %shard_map.95.refs_0_, bf16[8,64,128]{2,1,0:T(8,128)(2,1)S(1)} %collective-permute-done.4.refs_1_, ...), custom_call_target="tpu_custom_call" | custom-call | flops 536870912 | bytes 13631488 | tf_op jit(solution)/shard_map/pallas_call | solution.py:31
  33.1 3.6 %shard_map.97 = (f32[4,256,128]{2,1,0:T(8,128)S(1)}, bf16[1024,2048]{1,0:T(8,128)(2,1)S(1)}) custom-call(s32[2]{0:T(128)S(1)} %copy-done.3, bf16[2048,2048]{1,0:T(8,128)(2,1)} %dosage.3, bf16[8,64,128]{2,1,0:T(8,128)(2,1)S(1)} %shard_map.95.refs_0_, bf16[8,64,128]{2,1,0:T(8,128)(2,1)S(1)} %collective-permute-done.4.refs_1_, ...), custom_call_target="tpu_custom_call" | custom-call | flops 536870912 | bytes 13631488 | tf_op jit(solution)/shard_map/pallas_call | solution.py:31
  37.1 3.3 %collective-permute-start.12 = (bf16[256,128]{1,0:T(8,128)(2,1)S(1)}, bf16[256,128]{1,0:T(8,128)(2,1)S(1)}, u32[]{:S(2)}, u32[]{:S(2)}) collective-permute-start(bf16[256,128]{1,0:T(8,128)(2,1)S(1)} %get-tuple-element.121), channel_id=1, source_target_pairs={{0,4},{1,5},{2,6},{3,7},{4,0},{5,1},{6,2},{7,3},{8,12},{9,13},{10,... | collective-permute-start | bytes 196616 | tf_op jit(solution)/shard_map/ppermute | solution.py:49
  41.3 3.3 %collective-permute-done.12 = bf16[256,128]{1,0:T(8,128)(2,1)S(1)} collective-permute-done((bf16[256,128]{1,0:T(8,128)(2,1)S(1)}, bf16[256,128]{1,0:T(8,128)(2,1)S(1)}, u32[]{:S(2)}, u32[]{:S(2)}) %collective-permute-start.12) | collective-permute-done | bytes 65568 | tf_op jit(solution)/shard_map/ppermute | solution.py:49
  51.5 4.2 %collective-permute-done.15.refs_4_ = bf16[256,128]{1,0:T(8,128)(2,1)S(1)} collective-permute-done((bf16[256,128]{1,0:T(8,128)(2,1)S(1)}, bf16[256,128]{1,0:T(8,128)(2,1)S(1)}, u32[]{:S(2)}, u32[]{:S(2)}) %collective-permute-start.15) | collective-permute-done | bytes 65568 | tf_op jit(solution)/shard_map/ppermute | solution.py:49
  57.7 2.0 %shard_map.99 = (f32[8,64,128]{2,1,0:T(8,128)S(1)}, bf16[8,64,128]{2,1,0:T(8,128)(2,1)S(1)}, bf16[8,64,128]{2,1,0:T(8,128)(2,1)S(1)}, bf16[8,64,128]{2,1,0:T(8,128)(2,1)S(1)}) custom-call(s32[2]{0:T(128)S(1)} %copy-done.3, bf16[1024,2048]{1,0:T(8,128)(2,1)S(1)} %get-tuple-element.74.refs_0_.blocks, bf16[1024,2048]{1,0:T(8,128)(2,1)S(1)} %get-tuple-element.75.refs_1_.blocks, ...), custom_call_target="tpu_custom_call" | custom-call | flops 1073741824 | bytes 9568256 | tf_op jit(solution)/shard_map/pallas_call | solution.py:31
  70.0 7.7 %collective-permute-done.22.refs_2_ = bf16[8,64,128]{2,1,0:T(8,128)(2,1)S(1)} collective-permute-done((bf16[8,64,128]{2,1,0:T(8,128)(2,1)S(1)}, bf16[8,64,128]{2,1,0:T(8,128)(2,1)S(1)}, u32[]{:S(2)}, u32[]{:S(2)}) %collective-permute-start.22) | collective-permute-done | bytes 131104 | tf_op jit(solution)/shard_map/ppermute | solution.py:49
  78.7 15.2 %collective-permute-done.23.refs_3_ = bf16[8,64,128]{2,1,0:T(8,128)(2,1)S(1)} collective-permute-done((bf16[8,64,128]{2,1,0:T(8,128)(2,1)S(1)}, bf16[8,64,128]{2,1,0:T(8,128)(2,1)S(1)}, u32[]{:S(2)}, u32[]{:S(2)}) %collective-permute-start.23) | collective-permute-done | bytes 131104 | tf_op jit(solution)/shard_map/ppermute | solution.py:49
  95.6 8.3 %collective-permute-done.29.refs_10_ = f32[2,4,64,128]{3,2,1,0:T(8,128)S(1)} collective-permute-done((f32[2,4,64,128]{3,2,1,0:T(8,128)S(1)}, f32[2,4,64,128]{3,2,1,0:T(8,128)S(1)}, u32[]{:S(2)}, u32[]{:S(2)}) %collective-permute-start.29) | collective-permute-done | bytes 262176 | tf_op jit(solution)/shard_map/ppermute | solution.py:49
  104.5 2.8 %collective-permute-start.25 = (bf16[4,64,128]{2,1,0:T(8,128)(2,1)S(1)}, bf16[4,64,128]{2,1,0:T(8,128)(2,1)S(1)}, u32[]{:S(2)}, u32[]{:S(2)}) collective-permute-start(bf16[4,64,128]{2,1,0:T(8,128)(2,1)S(1)} %get-tuple-element.83), channel_id=1, source_target_pairs={{0,10},{1,13},{2,12},{3,15},{4,14},{5,9},{6,8},{7,11},{8,3},{9,2},... | collective-permute-start | bytes 196616 | tf_op jit(solution)/shard_map/ppermute | solution.py:67
  107.2 4.2 %collective-permute-start.27 = (bf16[4,64,128]{2,1,0:T(8,128)(2,1)S(1)}, bf16[4,64,128]{2,1,0:T(8,128)(2,1)S(1)}, u32[]{:S(2)}, u32[]{:S(2)}) collective-permute-start(bf16[4,64,128]{2,1,0:T(8,128)(2,1)S(1)} %get-tuple-element.85), channel_id=1, source_target_pairs={{0,28},{1,27},{2,30},{3,29},{4,24},{5,31},{6,26},{7,25},{8,17},{9,... | collective-permute-start | bytes 196616 | tf_op jit(solution)/shard_map/ppermute | solution.py:67
  111.5 2.2 %collective-permute-done.26.refs_6_ = bf16[4,64,128]{2,1,0:T(8,128)(2,1)S(1)} collective-permute-done((bf16[4,64,128]{2,1,0:T(8,128)(2,1)S(1)}, bf16[4,64,128]{2,1,0:T(8,128)(2,1)S(1)}, u32[]{:S(2)}, u32[]{:S(2)}) %collective-permute-start.26) | collective-permute-done | bytes 65568 | tf_op jit(solution)/shard_map/ppermute | solution.py:67
  116.2 2.2 %collective-permute-start.31 = (bf16[4,64,128]{2,1,0:T(8,128)(2,1)S(1)}, bf16[4,64,128]{2,1,0:T(8,128)(2,1)S(1)}, u32[]{:S(2)}, u32[]{:S(2)}) collective-permute-start(bf16[4,64,128]{2,1,0:T(8,128)(2,1)S(1)} %get-tuple-element.90), channel_id=1, source_target_pairs={{0,7},{1,6},{2,1},{3,0},{4,3},{5,2},{6,5},{7,4},{8,14},{9,13},{10,... | collective-permute-start | bytes 196616 | tf_op jit(solution)/shard_map/ppermute | solution.py:77
  119.2 2.2 %collective-permute-start.33 = (bf16[4,64,128]{2,1,0:T(8,128)(2,1)S(1)}, bf16[4,64,128]{2,1,0:T(8,128)(2,1)S(1)}, u32[]{:S(2)}, u32[]{:S(2)}) collective-permute-start(bf16[4,64,128]{2,1,0:T(8,128)(2,1)S(1)} %get-tuple-element.92), channel_id=1, source_target_pairs={{0,23},{1,22},{2,17},{3,16},{4,19},{5,18},{6,21},{7,20},{8,30},{9,... | collective-permute-start | bytes 196616 | tf_op jit(solution)/shard_map/ppermute | solution.py:77
  121.4 2.7 %collective-permute-start.34 = (bf16[4,64,128]{2,1,0:T(8,128)(2,1)S(1)}, bf16[4,64,128]{2,1,0:T(8,128)(2,1)S(1)}, u32[]{:S(2)}, u32[]{:S(2)}) collective-permute-start(bf16[4,64,128]{2,1,0:T(8,128)(2,1)S(1)} %get-tuple-element.93), channel_id=1, source_target_pairs={{0,31},{1,30},{2,25},{3,24},{4,27},{5,26},{6,29},{7,28},{8,22},{9,... | collective-permute-start | bytes 196616 | tf_op jit(solution)/shard_map/ppermute | solution.py:77
  124.6 5.1 %collective-permute-done.34.refs_3_ = bf16[4,64,128]{2,1,0:T(8,128)(2,1)S(1)} collective-permute-done((bf16[4,64,128]{2,1,0:T(8,128)(2,1)S(1)}, bf16[4,64,128]{2,1,0:T(8,128)(2,1)S(1)}, u32[]{:S(2)}, u32[]{:S(2)}) %collective-permute-start.34) | collective-permute-done | bytes 65568 | tf_op jit(solution)/shard_map/ppermute | solution.py:77
  131.0 2.9 %collective-permute-start.37 = (bf16[8,64,128]{2,1,0:T(8,128)(2,1)S(1)}, bf16[8,64,128]{2,1,0:T(8,128)(2,1)S(1)}, u32[]{:S(2)}, u32[]{:S(2)}) collective-permute-start(bf16[8,64,128]{2,1,0:T(8,128)(2,1)S(1)} %shard_map.103.refs_0_), channel_id=1, source_target_pairs={{0,24},{8,16},{16,8},{24,0},{1,25},{9,17},{17,9},{25,1},{2,26},{10... | collective-permute-start | bytes 393224 | tf_op jit(solution)/shard_map/ppermute | solution.py:49
  133.9 2.4 %collective-permute-done.35.refs_1_ = bf16[8,64,128]{2,1,0:T(8,128)(2,1)S(1)} collective-permute-done((bf16[8,64,128]{2,1,0:T(8,128)(2,1)S(1)}, bf16[8,64,128]{2,1,0:T(8,128)(2,1)S(1)}, u32[]{:S(2)}, u32[]{:S(2)}) %collective-permute-start.35) | collective-permute-done | bytes 131104 | tf_op jit(solution)/shard_map/ppermute | solution.py:49
  142.4 3.6 %collective-permute-start.40 = (bf16[256,128]{1,0:T(8,128)(2,1)S(1)}, bf16[256,128]{1,0:T(8,128)(2,1)S(1)}, u32[]{:S(2)}, u32[]{:S(2)}) collective-permute-start(bf16[256,128]{1,0:T(8,128)(2,1)S(1)} %get-tuple-element.118), channel_id=1, source_target_pairs={{0,4},{1,5},{2,6},{3,7},{4,0},{5,1},{6,2},{7,3},{8,12},{9,13},{10,... | collective-permute-start | bytes 196616 | tf_op jit(solution)/shard_map/ppermute | solution.py:49
  146.7 3.5 %collective-permute-done.40 = bf16[256,128]{1,0:T(8,128)(2,1)S(1)} collective-permute-done((bf16[256,128]{1,0:T(8,128)(2,1)S(1)}, bf16[256,128]{1,0:T(8,128)(2,1)S(1)}, u32[]{:S(2)}, u32[]{:S(2)}) %collective-permute-start.40) | collective-permute-done | bytes 65568 | tf_op jit(solution)/shard_map/ppermute | solution.py:49
  157.7 4.1 %collective-permute-done.43.refs_4_ = bf16[256,128]{1,0:T(8,128)(2,1)S(1)} collective-permute-done((bf16[256,128]{1,0:T(8,128)(2,1)S(1)}, bf16[256,128]{1,0:T(8,128)(2,1)S(1)}, u32[]{:S(2)}, u32[]{:S(2)}) %collective-permute-start.43) | collective-permute-done | bytes 65568 | tf_op jit(solution)/shard_map/ppermute | solution.py:49
  168.8 2.7 %collective-permute-done.49.refs_1_ = bf16[8,64,128]{2,1,0:T(8,128)(2,1)S(1)} collective-permute-done((bf16[8,64,128]{2,1,0:T(8,128)(2,1)S(1)}, bf16[8,64,128]{2,1,0:T(8,128)(2,1)S(1)}, u32[]{:S(2)}, u32[]{:S(2)}) %collective-permute-start.49) | collective-permute-done | bytes 131104 | tf_op jit(solution)/shard_map/ppermute | solution.py:49
  171.5 3.6 %collective-permute-done.50.refs_2_ = bf16[8,64,128]{2,1,0:T(8,128)(2,1)S(1)} collective-permute-done((bf16[8,64,128]{2,1,0:T(8,128)(2,1)S(1)}, bf16[8,64,128]{2,1,0:T(8,128)(2,1)S(1)}, u32[]{:S(2)}, u32[]{:S(2)}) %collective-permute-start.50) | collective-permute-done | bytes 131104 | tf_op jit(solution)/shard_map/ppermute | solution.py:49
  177.8 4.9 %collective-permute-start.55 = (bf16[4,64,128]{2,1,0:T(8,128)(2,1)S(1)}, bf16[4,64,128]{2,1,0:T(8,128)(2,1)S(1)}, u32[]{:S(2)}, u32[]{:S(2)}) collective-permute-start(bf16[4,64,128]{2,1,0:T(8,128)(2,1)S(1)} %get-tuple-element.101), channel_id=1, source_target_pairs={{0,28},{1,27},{2,30},{3,29},{4,24},{5,31},{6,26},{7,25},{8,17},{9,... | collective-permute-start | bytes 196616 | tf_op jit(solution)/shard_map/ppermute | solution.py:67
  182.7 2.7 %collective-permute-done.54.refs_6_ = bf16[4,64,128]{2,1,0:T(8,128)(2,1)S(1)} collective-permute-done((bf16[4,64,128]{2,1,0:T(8,128)(2,1)S(1)}, bf16[4,64,128]{2,1,0:T(8,128)(2,1)S(1)}, u32[]{:S(2)}, u32[]{:S(2)}) %collective-permute-start.54) | collective-permute-done | bytes 65568 | tf_op jit(solution)/shard_map/ppermute | solution.py:67
  187.1 2.6 %collective-permute-start.56 = (f32[4,64,128]{2,1,0:T(8,128)S(1)}, f32[4,64,128]{2,1,0:T(8,128)S(1)}, u32[]{:S(2)}, u32[]{:S(2)}) collective-permute-start(f32[4,64,128]{2,1,0:T(8,128)S(1)} %get-tuple-element.107), channel_id=1, source_target_pairs={{0,8},{8,0},{16,24},{24,16},{1,9},{9,1},{17,25},{25,17},{2,10},{10... | collective-permute-start | bytes 393224 | tf_op jit(solution)/shard_map/ppermute | solution.py:49
  193.3 4.6 %collective-permute-done.57.refs_2_ = f32[4,64,128]{2,1,0:T(8,128)S(1)} collective-permute-done((f32[4,64,128]{2,1,0:T(8,128)S(1)}, f32[4,64,128]{2,1,0:T(8,128)S(1)}, u32[]{:S(2)}, u32[]{:S(2)}) %collective-permute-start.57) | collective-permute-done | bytes 131104 | tf_op jit(solution)/shard_map/ppermute | solution.py:49
  (126 shorter events, 70.9 us)
Async XLA Ops:
  4.0 7.9 %collective-permute-start = (bf16[4,64,128]{2,1,0:T(8,128)(2,1)}, bf16[4,64,128]{2,1,0:T(8,128)(2,1)S(1)}, u32[]{:S(2)}, u32[]{:S(2)}) collective-permute-start(bf16[4,64,128]{2,1,0:T(8,128)(2,1)} %get-tuple-element.57), channel_id=1, source_target_pairs={{1,0},{2,1},{3,2},{4,3},{5,4},{6,5},{7,6},{0,7},{9,8},{10,9},{11,1... | collective-permute-start | bytes 196616 | tf_op jit(solution)/shard_map/ppermute | solution.py:44
  9.2 8.9 %collective-permute-start.3 = (bf16[4,64,128]{2,1,0:T(8,128)(2,1)}, bf16[4,64,128]{2,1,0:T(8,128)(2,1)S(1)}, u32[]{:S(2)}, u32[]{:S(2)}) collective-permute-start(bf16[4,64,128]{2,1,0:T(8,128)(2,1)} %get-tuple-element.60), channel_id=1, source_target_pairs={{4,0},{5,1},{6,2},{7,3},{0,4},{1,5},{2,6},{3,7},{12,8},{13,9},{14,... | collective-permute-start | bytes 196616 | tf_op jit(solution)/shard_map/ppermute | solution.py:44
  20.1 7.8 %collective-permute-start.4 = (bf16[8,64,128]{2,1,0:T(8,128)(2,1)S(1)}, bf16[8,64,128]{2,1,0:T(8,128)(2,1)S(1)}, u32[]{:S(2)}, u32[]{:S(2)}) collective-permute-start(bf16[8,64,128]{2,1,0:T(8,128)(2,1)S(1)} %shard_map.95.refs_0_), channel_id=1, source_target_pairs={{0,8},{8,0},{16,24},{24,16},{1,9},{9,1},{17,25},{25,17},{2,10},{10... | collective-permute-start | bytes 393224 | tf_op jit(solution)/shard_map/ppermute | solution.py:49
  21.6 7.8 %collective-permute-start.5 = (bf16[8,64,128]{2,1,0:T(8,128)(2,1)S(1)}, bf16[8,64,128]{2,1,0:T(8,128)(2,1)S(1)}, u32[]{:S(2)}, u32[]{:S(2)}) collective-permute-start(bf16[8,64,128]{2,1,0:T(8,128)(2,1)S(1)} %shard_map.95.refs_0_), channel_id=1, source_target_pairs={{0,16},{8,24},{16,0},{24,8},{1,17},{9,25},{17,1},{25,9},{2,18},{10... | collective-permute-start | bytes 393224 | tf_op jit(solution)/shard_map/ppermute | solution.py:49
  37.1 7.5 %collective-permute-start.12 = (bf16[256,128]{1,0:T(8,128)(2,1)S(1)}, bf16[256,128]{1,0:T(8,128)(2,1)S(1)}, u32[]{:S(2)}, u32[]{:S(2)}) collective-permute-start(bf16[256,128]{1,0:T(8,128)(2,1)S(1)} %get-tuple-element.121), channel_id=1, source_target_pairs={{0,4},{1,5},{2,6},{3,7},{4,0},{5,1},{6,2},{7,3},{8,12},{9,13},{10,... | collective-permute-start | bytes 196616 | tf_op jit(solution)/shard_map/ppermute | solution.py:49
  47.8 7.9 %collective-permute-start.15 = (bf16[256,128]{1,0:T(8,128)(2,1)S(1)}, bf16[256,128]{1,0:T(8,128)(2,1)S(1)}, u32[]{:S(2)}, u32[]{:S(2)}) collective-permute-start(bf16[256,128]{1,0:T(8,128)(2,1)S(1)} %fusion.8.refs_2_), channel_id=1, source_target_pairs={{0,4},{1,5},{2,6},{3,7},{4,0},{5,1},{6,2},{7,3},{8,12},{9,13},{10,... | collective-permute-start | bytes 196616 | tf_op jit(solution)/shard_map/ppermute | solution.py:49
  56.9 9.2 %collective-permute-start.28 = (f32[2,4,64,128]{3,2,1,0:T(8,128)S(1)}, f32[2,4,64,128]{3,2,1,0:T(8,128)S(1)}, u32[]{:S(2)}, u32[]{:S(2)}) collective-permute-start(f32[2,4,64,128]{3,2,1,0:T(8,128)S(1)} %get-tuple-element.87), channel_id=1, source_target_pairs={{0,8},{8,0},{16,24},{24,16},{1,9},{9,1},{17,25},{25,17},{2,10},{10... | collective-permute-start | bytes 786440 | tf_op jit(solution)/shard_map/ppermute | solution.py:49
  59.7 9.3 %collective-permute-start.21 = (bf16[8,64,128]{2,1,0:T(8,128)(2,1)S(1)}, bf16[8,64,128]{2,1,0:T(8,128)(2,1)S(1)}, u32[]{:S(2)}, u32[]{:S(2)}) collective-permute-start(bf16[8,64,128]{2,1,0:T(8,128)(2,1)S(1)} %get-tuple-element.79), channel_id=1, source_target_pairs={{0,8},{8,0},{16,24},{24,16},{1,9},{9,1},{17,25},{25,17},{2,10},{10... | collective-permute-start | bytes 393224 | tf_op jit(solution)/shard_map/ppermute | solution.py:49
  61.2 46.1 %collective-permute-start.7 = (bf16[4,64,1024]{2,1,0:T(8,128)(2,1)S(1)}, bf16[4,64,1024]{2,1,0:T(8,128)(2,1)S(1)}, u32[]{:S(2)}, u32[]{:S(2)}) collective-permute-start(bf16[4,64,1024]{2,1,0:T(8,128)(2,1)S(1)} %get-tuple-element.67), channel_id=1, source_target_pairs={{0,8},{8,0},{16,24},{24,16},{1,9},{9,1},{17,25},{25,17},{2,10},{10... | collective-permute-start | bytes 1572872 | tf_op jit(solution)/shard_map/ppermute | solution.py:49
  61.8 45.5 %collective-permute-start.8 = (bf16[4,64,1024]{2,1,0:T(8,128)(2,1)S(1)}, bf16[4,64,1024]{2,1,0:T(8,128)(2,1)S(1)}, u32[]{:S(2)}, u32[]{:S(2)}) collective-permute-start(bf16[4,64,1024]{2,1,0:T(8,128)(2,1)S(1)} %get-tuple-element.68), channel_id=1, source_target_pairs={{0,16},{8,24},{16,0},{24,8},{1,17},{9,25},{17,1},{25,9},{2,18},{10... | collective-permute-start | bytes 1572872 | tf_op jit(solution)/shard_map/ppermute | solution.py:49
  62.7 48.8 %collective-permute-start.9 = (bf16[4,64,1024]{2,1,0:T(8,128)(2,1)S(1)}, bf16[4,64,1024]{2,1,0:T(8,128)(2,1)S(1)}, u32[]{:S(2)}, u32[]{:S(2)}) collective-permute-start(bf16[4,64,1024]{2,1,0:T(8,128)(2,1)S(1)} %get-tuple-element.69), channel_id=1, source_target_pairs={{0,24},{8,16},{16,8},{24,0},{1,25},{9,17},{17,9},{25,1},{2,26},{10... | collective-permute-start | bytes 1572872 | tf_op jit(solution)/shard_map/ppermute | solution.py:49
  66.2 11.5 %collective-permute-start.22 = (bf16[8,64,128]{2,1,0:T(8,128)(2,1)S(1)}, bf16[8,64,128]{2,1,0:T(8,128)(2,1)S(1)}, u32[]{:S(2)}, u32[]{:S(2)}) collective-permute-start(bf16[8,64,128]{2,1,0:T(8,128)(2,1)S(1)} %get-tuple-element.80), channel_id=1, source_target_pairs={{0,16},{8,24},{16,0},{24,8},{1,17},{9,25},{17,1},{25,9},{2,18},{10... | collective-permute-start | bytes 393224 | tf_op jit(solution)/shard_map/ppermute | solution.py:49
  69.0 24.9 %collective-permute-start.23 = (bf16[8,64,128]{2,1,0:T(8,128)(2,1)S(1)}, bf16[8,64,128]{2,1,0:T(8,128)(2,1)S(1)}, u32[]{:S(2)}, u32[]{:S(2)}) collective-permute-start(bf16[8,64,128]{2,1,0:T(8,128)(2,1)S(1)} %get-tuple-element.81), channel_id=1, source_target_pairs={{0,24},{8,16},{16,8},{24,0},{1,25},{9,17},{17,9},{25,1},{2,26},{10... | collective-permute-start | bytes 393224 | tf_op jit(solution)/shard_map/ppermute | solution.py:49
  77.7 26.3 %collective-permute-start.29 = (f32[2,4,64,128]{3,2,1,0:T(8,128)S(1)}, f32[2,4,64,128]{3,2,1,0:T(8,128)S(1)}, u32[]{:S(2)}, u32[]{:S(2)}) collective-permute-start(f32[2,4,64,128]{3,2,1,0:T(8,128)S(1)} %get-tuple-element.88), channel_id=1, source_target_pairs={{0,16},{8,24},{16,0},{24,8},{1,17},{9,25},{17,1},{25,9},{2,18},{10... | collective-permute-start | bytes 786440 | tf_op jit(solution)/shard_map/ppermute | solution.py:49
  93.9 10.6 %collective-permute-start.30 = (f32[2,4,64,128]{3,2,1,0:T(8,128)S(1)}, f32[2,4,64,128]{3,2,1,0:T(8,128)S(1)}, u32[]{:S(2)}, u32[]{:S(2)}) collective-permute-start(f32[2,4,64,128]{3,2,1,0:T(8,128)S(1)} %get-tuple-element.89), channel_id=1, source_target_pairs={{0,24},{8,16},{16,8},{24,0},{1,25},{9,17},{17,9},{25,1},{2,26},{10... | collective-permute-start | bytes 786440 | tf_op jit(solution)/shard_map/ppermute | solution.py:49
  104.0 7.5 %collective-permute-start.24 = (bf16[4,64,128]{2,1,0:T(8,128)(2,1)S(1)}, bf16[4,64,128]{2,1,0:T(8,128)(2,1)S(1)}, u32[]{:S(2)}, u32[]{:S(2)}) collective-permute-start(bf16[4,64,128]{2,1,0:T(8,128)(2,1)S(1)} %get-tuple-element.82), channel_id=1, source_target_pairs={{0,3},{1,2},{2,5},{3,4},{4,7},{5,6},{6,1},{7,0},{8,10},{9,13},{10,... | collective-permute-start | bytes 196616 | tf_op jit(solution)/shard_map/ppermute | solution.py:67
  104.5 7.0 %collective-permute-start.25 = (bf16[4,64,128]{2,1,0:T(8,128)(2,1)S(1)}, bf16[4,64,128]{2,1,0:T(8,128)(2,1)S(1)}, u32[]{:S(2)}, u32[]{:S(2)}) collective-permute-start(bf16[4,64,128]{2,1,0:T(8,128)(2,1)S(1)} %get-tuple-element.83), channel_id=1, source_target_pairs={{0,10},{1,13},{2,12},{3,15},{4,14},{5,9},{6,8},{7,11},{8,3},{9,2},... | collective-permute-start | bytes 196616 | tf_op jit(solution)/shard_map/ppermute | solution.py:67
  107.2 7.7 %collective-permute-start.27 = (bf16[4,64,128]{2,1,0:T(8,128)(2,1)S(1)}, bf16[4,64,128]{2,1,0:T(8,128)(2,1)S(1)}, u32[]{:S(2)}, u32[]{:S(2)}) collective-permute-start(bf16[4,64,128]{2,1,0:T(8,128)(2,1)S(1)} %get-tuple-element.85), channel_id=1, source_target_pairs={{0,28},{1,27},{2,30},{3,29},{4,24},{5,31},{6,26},{7,25},{8,17},{9,... | collective-permute-start | bytes 196616 | tf_op jit(solution)/shard_map/ppermute | solution.py:67
  116.2 7.9 %collective-permute-start.31 = (bf16[4,64,128]{2,1,0:T(8,128)(2,1)S(1)}, bf16[4,64,128]{2,1,0:T(8,128)(2,1)S(1)}, u32[]{:S(2)}, u32[]{:S(2)}) collective-permute-start(bf16[4,64,128]{2,1,0:T(8,128)(2,1)S(1)} %get-tuple-element.90), channel_id=1, source_target_pairs={{0,7},{1,6},{2,1},{3,0},{4,3},{5,2},{6,5},{7,4},{8,14},{9,13},{10,... | collective-permute-start | bytes 196616 | tf_op jit(solution)/shard_map/ppermute | solution.py:77
  121.4 8.3 %collective-permute-start.34 = (bf16[4,64,128]{2,1,0:T(8,128)(2,1)S(1)}, bf16[4,64,128]{2,1,0:T(8,128)(2,1)S(1)}, u32[]{:S(2)}, u32[]{:S(2)}) collective-permute-start(bf16[4,64,128]{2,1,0:T(8,128)(2,1)S(1)} %get-tuple-element.93), channel_id=1, source_target_pairs={{0,31},{1,30},{2,25},{3,24},{4,27},{5,26},{6,29},{7,28},{8,22},{9,... | collective-permute-start | bytes 196616 | tf_op jit(solution)/shard_map/ppermute | solution.py:77
  130.4 7.8 %collective-permute-start.36 = (bf16[8,64,128]{2,1,0:T(8,128)(2,1)S(1)}, bf16[8,64,128]{2,1,0:T(8,128)(2,1)S(1)}, u32[]{:S(2)}, u32[]{:S(2)}) collective-permute-start(bf16[8,64,128]{2,1,0:T(8,128)(2,1)S(1)} %shard_map.103.refs_0_), channel_id=1, source_target_pairs={{0,16},{8,24},{16,0},{24,8},{1,17},{9,25},{17,1},{25,9},{2,18},{10... | collective-permute-start | bytes 393224 | tf_op jit(solution)/shard_map/ppermute | solution.py:49
  131.0 7.2 %collective-permute-start.37 = (bf16[8,64,128]{2,1,0:T(8,128)(2,1)S(1)}, bf16[8,64,128]{2,1,0:T(8,128)(2,1)S(1)}, u32[]{:S(2)}, u32[]{:S(2)}) collective-permute-start(bf16[8,64,128]{2,1,0:T(8,128)(2,1)S(1)} %shard_map.103.refs_0_), channel_id=1, source_target_pairs={{0,24},{8,16},{16,8},{24,0},{1,25},{9,17},{17,9},{25,1},{2,26},{10... | collective-permute-start | bytes 393224 | tf_op jit(solution)/shard_map/ppermute | solution.py:49
  142.4 7.8 %collective-permute-start.40 = (bf16[256,128]{1,0:T(8,128)(2,1)S(1)}, bf16[256,128]{1,0:T(8,128)(2,1)S(1)}, u32[]{:S(2)}, u32[]{:S(2)}) collective-permute-start(bf16[256,128]{1,0:T(8,128)(2,1)S(1)} %get-tuple-element.118), channel_id=1, source_target_pairs={{0,4},{1,5},{2,6},{3,7},{4,0},{5,1},{6,2},{7,3},{8,12},{9,13},{10,... | collective-permute-start | bytes 196616 | tf_op jit(solution)/shard_map/ppermute | solution.py:49
  153.9 7.9 %collective-permute-start.43 = (bf16[256,128]{1,0:T(8,128)(2,1)S(1)}, bf16[256,128]{1,0:T(8,128)(2,1)S(1)}, u32[]{:S(2)}, u32[]{:S(2)}) collective-permute-start(bf16[256,128]{1,0:T(8,128)(2,1)S(1)} %get-tuple-element.110.refs_2_), channel_id=1, source_target_pairs={{0,4},{1,5},{2,6},{3,7},{4,0},{5,1},{6,2},{7,3},{8,12},{9,13},{10,... | collective-permute-start | bytes 196616 | tf_op jit(solution)/shard_map/ppermute | solution.py:49
  166.9 8.3 %collective-permute-start.50 = (bf16[8,64,128]{2,1,0:T(8,128)(2,1)S(1)}, bf16[8,64,128]{2,1,0:T(8,128)(2,1)S(1)}, u32[]{:S(2)}, u32[]{:S(2)}) collective-permute-start(bf16[8,64,128]{2,1,0:T(8,128)(2,1)S(1)} %get-tuple-element.96), channel_id=1, source_target_pairs={{0,16},{8,24},{16,0},{24,8},{1,17},{9,25},{17,1},{25,9},{2,18},{10... | collective-permute-start | bytes 393224 | tf_op jit(solution)/shard_map/ppermute | solution.py:49
  167.4 7.7 %collective-permute-start.51 = (bf16[8,64,128]{2,1,0:T(8,128)(2,1)S(1)}, bf16[8,64,128]{2,1,0:T(8,128)(2,1)S(1)}, u32[]{:S(2)}, u32[]{:S(2)}) collective-permute-start(bf16[8,64,128]{2,1,0:T(8,128)(2,1)S(1)} %get-tuple-element.97), channel_id=1, source_target_pairs={{0,24},{8,16},{16,8},{24,0},{1,25},{9,17},{17,9},{25,1},{2,26},{10... | collective-permute-start | bytes 393224 | tf_op jit(solution)/shard_map/ppermute | solution.py:49
  175.9 6.9 %collective-permute-start.52 = (bf16[4,64,128]{2,1,0:T(8,128)(2,1)S(1)}, bf16[4,64,128]{2,1,0:T(8,128)(2,1)S(1)}, u32[]{:S(2)}, u32[]{:S(2)}) collective-permute-start(bf16[4,64,128]{2,1,0:T(8,128)(2,1)S(1)} %get-tuple-element.98), channel_id=1, source_target_pairs={{0,3},{1,2},{2,5},{3,4},{4,7},{5,6},{6,1},{7,0},{8,10},{9,13},{10,... | collective-permute-start | bytes 196616 | tf_op jit(solution)/shard_map/ppermute | solution.py:67
  175.9 6.8 %collective-permute-start.53 = (bf16[4,64,128]{2,1,0:T(8,128)(2,1)S(1)}, bf16[4,64,128]{2,1,0:T(8,128)(2,1)S(1)}, u32[]{:S(2)}, u32[]{:S(2)}) collective-permute-start(bf16[4,64,128]{2,1,0:T(8,128)(2,1)S(1)} %get-tuple-element.99), channel_id=1, source_target_pairs={{0,10},{1,13},{2,12},{3,15},{4,14},{5,9},{6,8},{7,11},{8,3},{9,2},... | collective-permute-start | bytes 196616 | tf_op jit(solution)/shard_map/ppermute | solution.py:67
  177.8 7.6 %collective-permute-start.54 = (bf16[4,64,128]{2,1,0:T(8,128)(2,1)S(1)}, bf16[4,64,128]{2,1,0:T(8,128)(2,1)S(1)}, u32[]{:S(2)}, u32[]{:S(2)}) collective-permute-start(bf16[4,64,128]{2,1,0:T(8,128)(2,1)S(1)} %get-tuple-element.100), channel_id=1, source_target_pairs={{0,17},{1,20},{2,19},{3,22},{4,21},{5,16},{6,23},{7,18},{8,28},{9,... | collective-permute-start | bytes 196616 | tf_op jit(solution)/shard_map/ppermute | solution.py:67
  177.8 8.0 %collective-permute-start.55 = (bf16[4,64,128]{2,1,0:T(8,128)(2,1)S(1)}, bf16[4,64,128]{2,1,0:T(8,128)(2,1)S(1)}, u32[]{:S(2)}, u32[]{:S(2)}) collective-permute-start(bf16[4,64,128]{2,1,0:T(8,128)(2,1)S(1)} %get-tuple-element.101), channel_id=1, source_target_pairs={{0,28},{1,27},{2,30},{3,29},{4,24},{5,31},{6,26},{7,25},{8,17},{9,... | collective-permute-start | bytes 196616 | tf_op jit(solution)/shard_map/ppermute | solution.py:67
  189.8 8.1 %collective-permute-start.57 = (f32[4,64,128]{2,1,0:T(8,128)S(1)}, f32[4,64,128]{2,1,0:T(8,128)S(1)}, u32[]{:S(2)}, u32[]{:S(2)}) collective-permute-start(f32[4,64,128]{2,1,0:T(8,128)S(1)} %get-tuple-element.108), channel_id=1, source_target_pairs={{0,16},{8,24},{16,0},{24,8},{1,17},{9,25},{17,1},{25,9},{2,18},{10... | collective-permute-start | bytes 393224 | tf_op jit(solution)/shard_map/ppermute | solution.py:49
  190.8 7.1 %collective-permute-start.58 = (f32[4,64,128]{2,1,0:T(8,128)S(1)}, f32[4,64,128]{2,1,0:T(8,128)S(1)}, u32[]{:S(2)}, u32[]{:S(2)}) collective-permute-start(f32[4,64,128]{2,1,0:T(8,128)S(1)} %get-tuple-element.109), channel_id=1, source_target_pairs={{0,24},{8,16},{16,8},{24,0},{1,25},{9,17},{17,9},{25,1},{2,26},{10... | collective-permute-start | bytes 393224 | tf_op jit(solution)/shard_map/ppermute | solution.py:49
  (35 other events, 298.2 us)
where the time goes:
time: 200 us; the launch traced here: 199 us
  waiting for transfers between devices  92 us (46%)
  starting transfers between devices  74.4 us (37%)
  Pallas kernels  25.9 us (13%)
  local copies, waits for them, and re-layouts  4.62 us (2%)
    ppermute x43, waiting for transfers between devices, crossed(): return lax.ppermute(block, axis, [(i, i ^ mask) for i in range(count)])  73.6 us
    ppermute x43, starting transfers between devices, crossed(): return lax.ppermute(block, axis, [(i, i ^ mask) for i in range(count)])  44.2 us
    pallas_call x15, Pallas kernels, local(): pl.pallas_call(body, in_specs=[SMEM] * len(scalars) + [FAR] * far + [VMEM...  23.1 us
    ppermute x8, starting transfers between devices, to_owners(): return lax.ppermute(block, ('samp', 'var'), route)  14.3 us
    ppermute x4, starting transfers between devices, to_variants(): return lax.ppermute(block, ('samp', 'var'), route)  7.91 us
    ppermute x4, starting transfers between devices, shifted(): lax.ppermute(block, axis, [((i - distance) % count, i) for i in range(cou...  7.89 us
    ppermute x8, waiting for transfers between devices, to_owners(): return lax.ppermute(block, ('samp', 'var'), route)  6.57 us
    ppermute x4, waiting for transfers between devices, shifted(): lax.ppermute(block, axis, [((i - distance) % count, i) for i in range(cou...  6.25 us
  transfers between devices with their start and end apart: 59, of which 32 were waited for; matrix products, arithmetic and copies ran while one was open for 2% of the time, Pallas kernels for 5%

commit v1 on v0

--- a/solution.py
+++ b/solution.py
@@ -12,7 +12,7 @@
 MOMENTA = (0.4, 0.55)
 CORES = 2
 MIB = 1 << 20
-LARGE = 42
+LARGE = 45
 
 
 SMEM = pl.BlockSpec(memory_space=pltpu.SMEM)
@@ -158,20 +158,34 @@
             outs[k][1, p] = jnp.where(live, before[slot], 0.0)
 
 
-def panels_body(spot, quarters, pair, most, where, table, panels, *outs):
-    width = panels.shape[2] // most
+def choose_body(spot, quarters, pair, where, table, inverses, *refs):
+    outs, arrived = refs[:quarters], refs[quarters]
+    copies = []
     for k in range(quarters):
         for p in range(pair):
-            row = held_by(where[1] ^ k, where[0]) * pair
-            slot = table[spot.slot + row + p]
-            first = table[spot.first + row + p]
-            live = table[spot.live + row + p]
-            for q in range(pair):
-                same = (table[spot.first + row + q] == first) & (table[spot.live + row + q] == 1)
-                part = jnp.clip(q - first, 0, most - 1)
-                block = panels[slot, :, pl.ds(pl.multiple_of(part * width, width), width)]
-                use = same & (live == 1)
-                outs[k][p, :, q * width : (q + 1) * width] = jnp.where(use, block, jnp.zeros_like(block))
+            slot = table[spot.slot + held_by(where[1] ^ k, where[0]) * pair + p]
+            copies.append(
+                pltpu.make_async_copy(inverses.at[slot], outs[k].at[p], arrived.at[k * pair + p])
+            )
+            copies[-1].start()
+    for copy in copies:
+        copy.wait()
+
+
+def panels_body(spot, quarters, pair, most, where, table, *refs):
+    panels, outs = refs[:quarters], refs[quarters:]
+    width = panels[0].shape[2] // most
+    row = held_by(where[1], where[0]) * pair
+    for p in range(pair):
+        first = table[spot.first + row + p]
+        live = table[spot.live + row + p] == 1
+        for q in range(pair):
+            same = (table[spot.first + row + q] == first) & (table[spot.live + row + q] == 1)
+            part = jnp.clip(q - first, 0, most - 1)
+            columns = pl.ds(pl.multiple_of(part * width, width), width)
+            for k in range(quarters):
+                block = panels[k][p, :, columns]
+                outs[k][p, :, q * width : (q + 1) * width] = jnp.where(same & live, block, jnp.zeros_like(block))
 
 
 def local_values_body(spot, pair, turned, where, table, *refs):
@@ -193,34 +207,30 @@
             values[pl.ds(pl.multiple_of(at, quarter_rows), quarter_rows), :] = pieces[k][u]
 
 
-def predict_blocks(scale, blocks, values, out, ready=None):
-    chips, rows = out.shape[:2]
-    for i in range(chips):
-        if ready is not None:
-            ready[i].wait()
-        block = blocks[i * rows : (i + 1) * rows, :]
-        out[i] = jnp.dot(block, values[...], preferred_element_type=F32) * scale
-
-
-def first_predict_body(quarters, scale, other, where, dosage, *refs):
-    pieces, (out, blocks, values, arrived) = refs[:quarters], refs[quarters:]
-    chips, rows = out.shape[:2]
+def load_body(where, dosage, *refs):
+    outs, arrived = refs[:CORES], refs[CORES]
     core, chip = lax.rem(where[0], CORES), lax.div(where[0], CORES)
-    side = (1 - core) if other else core
+    chips = arrived.shape[0] // CORES
+    rows = outs[0].shape[0] // chips
     copies = []
-    for i in range(chips):
-        at = pl.multiple_of(((chip ^ i) * CORES + side) * rows, rows)
-        here = blocks.at[pl.ds(i * rows, rows), :]
-        copies.append(pltpu.make_async_copy(dosage.at[pl.ds(at, rows), :], here, arrived.at[i]))
-        copies[-1].start()
-    place_values(quarters, where, pieces, values)
-    predict_blocks(scale, blocks, values, out, copies)
+    for c in reversed(range(CORES)):
+        for i in range(chips):
+            at = pl.multiple_of(((chip ^ i) * CORES + (core ^ c)) * rows, rows)
+            here = outs[c].at[pl.ds(i * rows, rows), :]
+            ready = arrived.at[c * chips + i]
+            copies.append(pltpu.make_async_copy(dosage.at[pl.ds(at, rows), :], here, ready))
+            copies[-1].start()
+    for copy in copies:
+        copy.wait()
 
 
 def predict_body(quarters, scale, where, blocks, *refs):
     pieces, (out, values) = refs[:quarters], refs[quarters:]
     place_values(quarters, where, pieces, values)
-    predict_blocks(scale, blocks, values, out)
+    chips, rows = out.shape[:2]
+    for i in range(chips):
+        block = blocks[i * rows : (i + 1) * rows, :]
+        out[i] = jnp.dot(block, values[...], preferred_element_type=F32) * scale
 
 
 def gradient_body(quarters, units, scale, where, *refs):
@@ -329,6 +339,12 @@
         functools.partial(states_body, spot, quarters, pair),
         [where, table], [coef_now, coef_prev], [like((2, *piece), F32)] * quarters,
     )
+    chosen = local(
+        functools.partial(choose_body, spot, quarters, pair),
+        [where, table], [block_inverse], [like((pair, *block_inverse.shape[1:]), HALF)] * quarters,
+        [pltpu.SemaphoreType.DMA((codes,))], limit=LARGE, far=1,
+    )
+    arrived, states, chosen = lax.optimization_barrier((arrived, states, chosen))
     states = [states[0]] + [crossed(states[k], "samp", k) for k in ranks[1:]]
     penalty = penalty.reshape(1, 1, right_cols)
 
@@ -340,37 +356,28 @@
         )
         pieces = [own] + [crossed(own, "samp", k) for k in ranks[1:]]
         if step == 0:
-            block_inverse = lax.optimization_barrier((own, block_inverse))[1]
-            panels = local(
-                functools.partial(panels_body, spot, quarters, pair, block_most),
-                [where, table],
-                [block_inverse.reshape(capacity, quarter_rows, block_most * unit_rows)],
-                [like((pair, quarter_rows, block_most * unit_rows), HALF)] * quarters, limit=10,
+            block = like((chips * rows, dosage.shape[1]), HALF)
+            dosage = lax.optimization_barrier((own, dosage))[1]
+            kept_rows, given_rows = local(
+                load_body, [where], [dosage], [block, block],
+                [pltpu.SemaphoreType.DMA((owners,))], limit=LARGE, far=1,
             )
-            pieces, panels = lax.optimization_barrier((pieces, panels))
-            panels = [panels[0]] + [crossed(panels[k], "samp", k) for k in ranks[1:]]
+            pieces, kept_rows, given_rows, chosen = lax.optimization_barrier(
+                (pieces, kept_rows, given_rows, chosen)
+            )
+            chosen = [chosen[0]] + [crossed(chosen[k], "samp", k) for k in ranks[1:]]
         buffers = [pltpu.VMEM((dosage.shape[1], right_cols), HALF)]
         half = like((chips, rows, right_cols), F32)
         flops = dosage.shape[0] * dosage.shape[1] * right_cols
-        if step == 0:
-            block = like((chips * rows, dosage.shape[1]), HALF)
-            (given, given_rows), (kept, kept_rows) = (
-                local(
-                    functools.partial(first_predict_body, quarters, inv_scale, other),
-                    [where], [dosage, *pieces], [half, block],
-                    [*buffers, pltpu.SemaphoreType.DMA((chips,))], limit=LARGE, flops=flops, far=1,
-                )
-                for other in (True, False)
+        given, kept = (
+            local(
+                functools.partial(predict_body, quarters, inv_scale),
+                [where], [side, *pieces], half, buffers, limit=8, flops=flops,
             )
-        else:
-            given, kept = (
-                local(
-                    functools.partial(predict_body, quarters, inv_scale),
-                    [where], [side, *pieces], half, buffers, limit=8, flops=flops,
-                )
-                for side in (given_rows, kept_rows)
-            )
-        both = kept + crossed(given, "var", 1)
+            for side in (given_rows, kept_rows)
+        )
+        given = crossed(given, "var", 1)
+        both = kept + given
         total = both[0]
         for i in range(1, chips):
             total = total + crossed(both[i].astype(HALF), "var", CORES * i).astype(F32)
@@ -387,7 +394,17 @@
                 pltpu.VMEM((per_device, unit_rows, right_cols), F32),
             ], limit=15, flops=2 * dosage.shape[0] * dosage.shape[1] * right_cols,
         )
-        sums = [sums[0]] + [crossed(sums[k], "samp", k) for k in ranks[1:]]
+        owned = sums[0]
+        sums = [owned] + [crossed(sums[k], "samp", k) for k in ranks[1:]]
+        if step == 0:
+            chosen = lax.optimization_barrier((owned, chosen))[1]
+            panels = local(
+                functools.partial(panels_body, spot, quarters, pair, block_most),
+                [where, table],
+                [part.reshape(pair, quarter_rows, block_most * unit_rows) for part in chosen],
+                [like((pair, quarter_rows, block_most * unit_rows), HALF)] * quarters, limit=10,
+            )
+            sums, panels = lax.optimization_barrier((sums, panels))
         leaving = local(
             functools.partial(leave_body, spot, quarters, pair),
             [where, table], sums, [like(piece, HALF)] * quarters,

time: 200 us -> 180 us (0.900)
  waiting for transfers between devices: 92 us -> 67.6 us
  starting transfers between devices: 74.4 us -> 68.6 us
  Pallas kernels: 25.9 us -> 31.7 us
  local copies, waits for them, and re-layouts: 4.62 us -> 8.73 us
    ppermute x43, waiting for transfers between devices: 73.6 us -> 53.7 us  [crossed(): return lax.ppermute(block, axis, [(i, i ^ mask) for i in range(count)])]
    ppermute x4, waiting for transfers between devices: 6.25 us -> 0.01 us  [shifted(): lax.ppermute(block, axis, [((i - distance) % count, i) for i in range(cou...]
    pallas_call x15 -> x17, Pallas kernels: 23.1 us -> 29.1 us  [local(): pl.pallas_call(body, in_specs=[SMEM] * len(scalars) + [FAR] * far + [VMEM...]
    unnamed x16 -> x34, local copies, waits for them, and re-layouts: 1.36 us -> 6.2 us
    ppermute x43, starting transfers between devices: 44.2 us -> 40.1 us  [crossed(): return lax.ppermute(block, axis, [(i, i ^ mask) for i in range(count)])]
  transfers between devices with their start and end apart: 59 -> 59, of which waited for: 32 -> 34; matrix products, arithmetic and copies ran while one was open for 2% -> 1% of each run, Pallas kernels for 5% -> 10%
where the time goes in v1:
time: 180 us; the launch traced here: 179 us
  starting transfers between devices  68.6 us (38%)
  waiting for transfers between devices  67.6 us (38%)
  Pallas kernels  31.7 us (18%)
  local copies, waits for them, and re-layouts  8.73 us (5%)
    ppermute x43, waiting for transfers between devices, crossed(): return lax.ppermute(block, axis, [(i, i ^ mask) for i in range(count)])  53.7 us
    ppermute x43, starting transfers between devices, crossed(): return lax.ppermute(block, axis, [(i, i ^ mask) for i in range(count)])  40.1 us
    pallas_call x17, Pallas kernels, local(): pl.pallas_call(body, in_specs=[SMEM] * len(scalars) + [FAR] * far + [VMEM...  29.1 us
    ppermute x8, starting transfers between devices, to_owners(): return lax.ppermute(block, ('samp', 'var'), route)  12.7 us
    ppermute x4, starting transfers between devices, to_variants(): return lax.ppermute(block, ('samp', 'var'), route)  7.99 us
    ppermute x4, starting transfers between devices, shifted(): lax.ppermute(block, axis, [((i - distance) % count, i) for i in range(cou...  7.89 us
    ppermute x8, waiting for transfers between devices, to_owners(): return lax.ppermute(block, ('samp', 'var'), route)  7.49 us
    ppermute x4, waiting for transfers between devices, to_variants(): return lax.ppermute(block, ('samp', 'var'), route)  6.42 us
  transfers between devices with their start and end apart: 59, of which 34 were waited for; matrix products, arithmetic and copies ran while one was open for 1% of the time, Pallas kernels for 10%

profile of v1, /device:TPU:0, one launch (start us, length us, event | category | flops | bytes accessed | tf_op | source)
XLA Modules:
  0.0 179.2 jit_solution(17451687303773106658)
XLA Ops:
  1.2 2.6 %begin.1 = (s32[88]{0:T(128)}, bf16[4,64,128]{2,1,0:T(8,128)(2,1)}, bf16[4,64,128]{2,1,0:T(8,128)(2,1)}, bf16[4,64,128]{2,1,0:T(8,128)(2,1)}, bf16[4,64,128]{2,1,0:T(8,128)(2,1)}) custom-call(s32[2]{0:T(128)} %pad_add_fusion.where, s32[64]{0:T(128)} %start.1, s32[64]{0:T(128)} %owner.1, f32[16,64,128]{2,1,0:T(8,128)} %now.3, f32[16,64,128]{2,1,0:T(8,128)} %before.3), custom_call_target="tpu_custom_call" | custom-call | tf_op jit(solution)/shard_map/begin/pallas_call | solution.py:328
  3.9 4.6 %collective-permute-start = (bf16[4,64,128]{2,1,0:T(8,128)(2,1)}, bf16[4,64,128]{2,1,0:T(8,128)(2,1)S(1)}, u32[]{:S(2)}, u32[]{:S(2)}) collective-permute-start(bf16[4,64,128]{2,1,0:T(8,128)(2,1)} %get-tuple-element.85), channel_id=1, source_target_pairs={{1,0},{2,1},{3,2},{4,3},{5,4},{6,5},{7,6},{0,7},{9,8},{10,9},{11,1... | collective-permute-start | bytes 196616 | tf_op jit(solution)/shard_map/ppermute | solution.py:44
  9.1 2.7 %collective-permute-start.3 = (bf16[4,64,128]{2,1,0:T(8,128)(2,1)}, bf16[4,64,128]{2,1,0:T(8,128)(2,1)S(1)}, u32[]{:S(2)}, u32[]{:S(2)}) collective-permute-start(bf16[4,64,128]{2,1,0:T(8,128)(2,1)} %get-tuple-element.88), channel_id=1, source_target_pairs={{4,0},{5,1},{6,2},{7,3},{0,4},{1,5},{2,6},{3,7},{12,8},{13,9},{14,... | collective-permute-start | bytes 196616 | tf_op jit(solution)/shard_map/ppermute | solution.py:44
  19.4 3.6 %shard_map.96 = (bf16[4,64,4,256]{3,2,1,0:T(4,128)(2,1)S(1)}, bf16[4,64,4,256]{3,2,1,0:T(4,128)(2,1)S(1)}, bf16[4,64,4,256]{3,2,1,0:T(4,128)(2,1)S(1)}, bf16[4,64,4,256]{3,2,1,0:T(4,128)(2,1)S(1)}) custom-call(s32[2]{0:T(128)S(1)} %copy-done.8, s32[88]{0:T(128)S(1)} %copy-done.11, bf16[16,64,4,256]{3,2,1,0:T(4,128)(2,1)S(1)} %copy-done.6), custom_call_target="tpu_custom_call" | custom-call | bytes 4194304 | tf_op jit(solution)/shard_map/pallas_call | solution.py:31
  23.6 2.5 %collective-permute-start.6 = (bf16[8,64,128]{2,1,0:T(8,128)(2,1)S(1)}, bf16[8,64,128]{2,1,0:T(8,128)(2,1)S(1)}, u32[]{:S(2)}, u32[]{:S(2)}) collective-permute-start(bf16[8,64,128]{2,1,0:T(8,128)(2,1)S(1)} %shard_map.97.refs_0_), channel_id=1, source_target_pairs={{0,24},{8,16},{16,8},{24,0},{1,25},{9,17},{17,9},{25,1},{2,26},{10... | collective-permute-start | bytes 393224 | tf_op jit(solution)/shard_map/ppermute | solution.py:49
  27.2 4.0 %shard_map.98 = (bf16[1024,2048]{1,0:T(8,128)(2,1)S(1)}, bf16[1024,2048]{1,0:T(8,128)(2,1)S(1)}) custom-call(s32[2]{0:T(128)S(1)} %copy-done.8, bf16[2048,2048]{1,0:T(8,128)(2,1)} %dosage), custom_call_target="tpu_custom_call" | custom-call | bytes 16777216 | tf_op jit(solution)/shard_map/pallas_call | solution.py:31
  36.9 2.0 %collective-permute-start.10 = (bf16[256,128]{1,0:T(8,128)(2,1)S(1)}, bf16[256,128]{1,0:T(8,128)(2,1)S(1)}, u32[]{:S(2)}, u32[]{:S(2)}) collective-permute-start(bf16[256,128]{1,0:T(8,128)(2,1)S(1)} %get-tuple-element.176), channel_id=1, source_target_pairs={{0,6},{1,7},{2,4},{3,5},{4,2},{5,3},{6,0},{7,1},{8,14},{9,15},{10,... | collective-permute-start | bytes 196616 | tf_op jit(solution)/shard_map/ppermute | solution.py:49
  43.8 2.9 %collective-permute-done.9 = bf16[256,128]{1,0:T(8,128)(2,1)S(1)} collective-permute-done((bf16[256,128]{1,0:T(8,128)(2,1)S(1)}, bf16[256,128]{1,0:T(8,128)(2,1)S(1)}, u32[]{:S(2)}, u32[]{:S(2)}) %collective-permute-start.9) | collective-permute-done | bytes 65568 | tf_op jit(solution)/shard_map/ppermute | solution.py:49
  48.6 5.2 %collective-permute-done.13.refs_5_ = bf16[256,128]{1,0:T(8,128)(2,1)S(1)} collective-permute-done((bf16[256,128]{1,0:T(8,128)(2,1)S(1)}, bf16[256,128]{1,0:T(8,128)(2,1)S(1)}, u32[]{:S(2)}, u32[]{:S(2)}) %collective-permute-start.13) | collective-permute-done | bytes 65568 | tf_op jit(solution)/shard_map/ppermute | solution.py:49
  53.8 2.2 %collective-permute-done.12.refs_4_ = bf16[256,128]{1,0:T(8,128)(2,1)S(1)} collective-permute-done((bf16[256,128]{1,0:T(8,128)(2,1)S(1)}, bf16[256,128]{1,0:T(8,128)(2,1)S(1)}, u32[]{:S(2)}, u32[]{:S(2)}) %collective-permute-start.12) | collective-permute-done | bytes 65568 | tf_op jit(solution)/shard_map/ppermute | solution.py:49
  56.0 2.0 %collective-permute-done.11.refs_3_ = bf16[256,128]{1,0:T(8,128)(2,1)S(1)} collective-permute-done((bf16[256,128]{1,0:T(8,128)(2,1)S(1)}, bf16[256,128]{1,0:T(8,128)(2,1)S(1)}, u32[]{:S(2)}, u32[]{:S(2)}) %collective-permute-start.11) | collective-permute-done | bytes 65568 | tf_op jit(solution)/shard_map/ppermute | solution.py:49
  59.5 2.8 %shard_map.101 = (f32[8,64,128]{2,1,0:T(8,128)S(1)}, bf16[8,64,128]{2,1,0:T(8,128)(2,1)S(1)}, bf16[8,64,128]{2,1,0:T(8,128)(2,1)}, bf16[8,64,128]{2,1,0:T(8,128)(2,1)}) custom-call(s32[2]{0:T(128)S(1)} %copy-done.8, bf16[1024,2048]{1,0:T(8,128)(2,1)S(1)} %get-tuple-element.108.blocks.refs_0_, bf16[1024,2048]{1,0:T(8,128)(2,1)S(1)} %get-tuple-element.109.blocks.refs_1_, ...), custom_call_target="tpu_custom_call" | custom-call | flops 1073741824 | bytes 9568256 | tf_op jit(solution)/shard_map/pallas_call | solution.py:31
  73.8 10.1 %collective-permute-done.19.refs_2_ = bf16[8,64,128]{2,1,0:T(8,128)(2,1)} collective-permute-done((bf16[8,64,128]{2,1,0:T(8,128)(2,1)}, bf16[8,64,128]{2,1,0:T(8,128)(2,1)}, u32[]{:S(2)}, u32[]{:S(2)}) %collective-permute-start.19) | collective-permute-done | bytes 131104 | tf_op jit(solution)/shard_map/ppermute | solution.py:49
  87.1 4.6 %collective-permute-start.27 = (bf16[4,64,128]{2,1,0:T(8,128)(2,1)S(1)}, bf16[4,64,128]{2,1,0:T(8,128)(2,1)S(1)}, u32[]{:S(2)}, u32[]{:S(2)}) collective-permute-start(bf16[4,64,128]{2,1,0:T(8,128)(2,1)S(1)} %get-tuple-element.141), channel_id=1, source_target_pairs={{0,28},{1,27},{2,30},{3,29},{4,24},{5,31},{6,26},{7,25},{8,17},{9,... | collective-permute-start | bytes 196616 | tf_op jit(solution)/shard_map/ppermute | solution.py:67
  91.7 2.8 %collective-permute-done.26.refs_6_ = bf16[4,64,128]{2,1,0:T(8,128)(2,1)S(1)} collective-permute-done((bf16[4,64,128]{2,1,0:T(8,128)(2,1)S(1)}, bf16[4,64,128]{2,1,0:T(8,128)(2,1)S(1)}, u32[]{:S(2)}, u32[]{:S(2)}) %collective-permute-start.26) | collective-permute-done | bytes 65568 | tf_op jit(solution)/shard_map/ppermute | solution.py:67
  96.5 2.5 %collective-permute-start.31 = (bf16[4,64,128]{2,1,0:T(8,128)(2,1)S(1)}, bf16[4,64,128]{2,1,0:T(8,128)(2,1)S(1)}, u32[]{:S(2)}, u32[]{:S(2)}) collective-permute-start(bf16[4,64,128]{2,1,0:T(8,128)(2,1)S(1)} %get-tuple-element.146), channel_id=1, source_target_pairs={{0,7},{1,6},{2,1},{3,0},{4,3},{5,2},{6,5},{7,4},{8,14},{9,13},{10,... | collective-permute-start | bytes 196616 | tf_op jit(solution)/shard_map/ppermute | solution.py:77
  100.3 2.3 %collective-permute-start.33 = (bf16[4,64,128]{2,1,0:T(8,128)(2,1)S(1)}, bf16[4,64,128]{2,1,0:T(8,128)(2,1)S(1)}, u32[]{:S(2)}, u32[]{:S(2)}) collective-permute-start(bf16[4,64,128]{2,1,0:T(8,128)(2,1)S(1)} %get-tuple-element.148), channel_id=1, source_target_pairs={{0,23},{1,22},{2,17},{3,16},{4,19},{5,18},{6,21},{7,20},{8,30},{9,... | collective-permute-start | bytes 196616 | tf_op jit(solution)/shard_map/ppermute | solution.py:77
  105.1 5.9 %collective-permute-done.34.refs_3_ = bf16[4,64,128]{2,1,0:T(8,128)(2,1)S(1)} collective-permute-done((bf16[4,64,128]{2,1,0:T(8,128)(2,1)S(1)}, bf16[4,64,128]{2,1,0:T(8,128)(2,1)S(1)}, u32[]{:S(2)}, u32[]{:S(2)}) %collective-permute-start.34) | collective-permute-done | bytes 65568 | tf_op jit(solution)/shard_map/ppermute | solution.py:77
  113.1 2.1 %collective-permute-start.35 = (bf16[8,64,128]{2,1,0:T(8,128)(2,1)S(1)}, bf16[8,64,128]{2,1,0:T(8,128)(2,1)S(1)}, u32[]{:S(2)}, u32[]{:S(2)}) collective-permute-start(bf16[8,64,128]{2,1,0:T(8,128)(2,1)S(1)} %shard_map.105.refs_0_), channel_id=1, source_target_pairs={{0,8},{8,0},{16,24},{24,16},{1,9},{9,1},{17,25},{25,17},{2,10},{10... | collective-permute-start | bytes 393224 | tf_op jit(solution)/shard_map/ppermute | solution.py:49
  115.1 2.7 %collective-permute-done.37.refs_3_ = bf16[8,64,128]{2,1,0:T(8,128)(2,1)S(1)} collective-permute-done((bf16[8,64,128]{2,1,0:T(8,128)(2,1)S(1)}, bf16[8,64,128]{2,1,0:T(8,128)(2,1)S(1)}, u32[]{:S(2)}, u32[]{:S(2)}) %collective-permute-start.37) | collective-permute-done | bytes 131104 | tf_op jit(solution)/shard_map/ppermute | solution.py:49
  127.9 2.3 %collective-permute-done.41 = bf16[256,128]{1,0:T(8,128)(2,1)S(1)} collective-permute-done((bf16[256,128]{1,0:T(8,128)(2,1)S(1)}, bf16[256,128]{1,0:T(8,128)(2,1)S(1)}, u32[]{:S(2)}, u32[]{:S(2)}) %collective-permute-start.41) | collective-permute-done | bytes 65568 | tf_op jit(solution)/shard_map/ppermute | solution.py:49
  130.1 3.1 %collective-permute-done.40 = bf16[256,128]{1,0:T(8,128)(2,1)S(1)} collective-permute-done((bf16[256,128]{1,0:T(8,128)(2,1)S(1)}, bf16[256,128]{1,0:T(8,128)(2,1)S(1)}, u32[]{:S(2)}, u32[]{:S(2)}) %collective-permute-start.40) | collective-permute-done | bytes 65568 | tf_op jit(solution)/shard_map/ppermute | solution.py:49
  133.9 2.1 %collective-permute-start.44 = (bf16[256,128]{1,0:T(8,128)(2,1)S(1)}, bf16[256,128]{1,0:T(8,128)(2,1)S(1)}, u32[]{:S(2)}, u32[]{:S(2)}) collective-permute-start(bf16[256,128]{1,0:T(8,128)(2,1)S(1)} %get-tuple-element.166.refs_2_), channel_id=1, source_target_pairs={{0,6},{1,7},{2,4},{3,5},{4,2},{5,3},{6,0},{7,1},{8,14},{9,15},{10,... | collective-permute-start | bytes 196616 | tf_op jit(solution)/shard_map/ppermute | solution.py:49
  136.0 2.3 %collective-permute-start.42 = (bf16[256,128]{1,0:T(8,128)(2,1)S(1)}, bf16[256,128]{1,0:T(8,128)(2,1)S(1)}, u32[]{:S(2)}, u32[]{:S(2)}) collective-permute-start(bf16[256,128]{1,0:T(8,128)(2,1)S(1)} %get-tuple-element.166.refs_2_), channel_id=1, source_target_pairs={{0,2},{1,3},{2,0},{3,1},{4,6},{5,7},{6,4},{7,5},{8,10},{9,11},{10,... | collective-permute-start | bytes 196616 | tf_op jit(solution)/shard_map/ppermute | solution.py:49
  143.5 2.0 %shard_map.108 = (f32[8,64,128]{2,1,0:T(8,128)S(1)}, bf16[8,64,128]{2,1,0:T(8,128)(2,1)S(1)}, bf16[8,64,128]{2,1,0:T(8,128)(2,1)S(1)}, bf16[8,64,128]{2,1,0:T(8,128)(2,1)S(1)}) custom-call(s32[2]{0:T(128)S(1)} %copy-done.9, bf16[1024,2048]{1,0:T(8,128)(2,1)S(1)} %copy-done.1, bf16[1024,2048]{1,0:T(8,128)(2,1)S(1)} %copy-done.3, ...), custom_call_target="tpu_custom_call" | custom-call | flops 1073741824 | bytes 9568256 | tf_op jit(solution)/shard_map/pallas_call | solution.py:31
  149.0 2.9 %collective-permute-done.49.refs_1_ = bf16[8,64,128]{2,1,0:T(8,128)(2,1)S(1)} collective-permute-done((bf16[8,64,128]{2,1,0:T(8,128)(2,1)S(1)}, bf16[8,64,128]{2,1,0:T(8,128)(2,1)S(1)}, u32[]{:S(2)}, u32[]{:S(2)}) %collective-permute-start.49) | collective-permute-done | bytes 131104 | tf_op jit(solution)/shard_map/ppermute | solution.py:49
  151.9 2.9 %collective-permute-done.50.refs_2_ = bf16[8,64,128]{2,1,0:T(8,128)(2,1)S(1)} collective-permute-done((bf16[8,64,128]{2,1,0:T(8,128)(2,1)S(1)}, bf16[8,64,128]{2,1,0:T(8,128)(2,1)S(1)}, u32[]{:S(2)}, u32[]{:S(2)}) %collective-permute-start.50) | collective-permute-done | bytes 131104 | tf_op jit(solution)/shard_map/ppermute | solution.py:49
  157.4 4.1 %collective-permute-start.55 = (bf16[4,64,128]{2,1,0:T(8,128)(2,1)S(1)}, bf16[4,64,128]{2,1,0:T(8,128)(2,1)S(1)}, u32[]{:S(2)}, u32[]{:S(2)}) collective-permute-start(bf16[4,64,128]{2,1,0:T(8,128)(2,1)S(1)} %get-tuple-element.157), channel_id=1, source_target_pairs={{0,28},{1,27},{2,30},{3,29},{4,24},{5,31},{6,26},{7,25},{8,17},{9,... | collective-permute-start | bytes 196616 | tf_op jit(solution)/shard_map/ppermute | solution.py:67
  162.6 2.1 %collective-permute-done.54.refs_6_ = bf16[4,64,128]{2,1,0:T(8,128)(2,1)S(1)} collective-permute-done((bf16[4,64,128]{2,1,0:T(8,128)(2,1)S(1)}, bf16[4,64,128]{2,1,0:T(8,128)(2,1)S(1)}, u32[]{:S(2)}, u32[]{:S(2)}) %collective-permute-start.54) | collective-permute-done | bytes 65568 | tf_op jit(solution)/shard_map/ppermute | solution.py:67
  166.8 2.9 %collective-permute-start.56 = (f32[4,64,128]{2,1,0:T(8,128)S(1)}, f32[4,64,128]{2,1,0:T(8,128)S(1)}, u32[]{:S(2)}, u32[]{:S(2)}) collective-permute-start(f32[4,64,128]{2,1,0:T(8,128)S(1)} %get-tuple-element.163), channel_id=1, source_target_pairs={{0,8},{8,0},{16,24},{24,16},{1,9},{9,1},{17,25},{25,17},{2,10},{10... | collective-permute-start | bytes 393224 | tf_op jit(solution)/shard_map/ppermute | solution.py:49
  171.3 2.5 %collective-permute-done.56.refs_1_ = f32[4,64,128]{2,1,0:T(8,128)S(1)} collective-permute-done((f32[4,64,128]{2,1,0:T(8,128)S(1)}, f32[4,64,128]{2,1,0:T(8,128)S(1)}, u32[]{:S(2)}, u32[]{:S(2)}) %collective-permute-start.56) | collective-permute-done | bytes 131104 | tf_op jit(solution)/shard_map/ppermute | solution.py:49
  173.7 4.0 %collective-permute-done.57.refs_2_ = f32[4,64,128]{2,1,0:T(8,128)S(1)} collective-permute-done((f32[4,64,128]{2,1,0:T(8,128)S(1)}, f32[4,64,128]{2,1,0:T(8,128)S(1)}, u32[]{:S(2)}, u32[]{:S(2)}) %collective-permute-start.57) | collective-permute-done | bytes 131104 | tf_op jit(solution)/shard_map/ppermute | solution.py:49
  (149 shorter events, 75.0 us)
Async XLA Ops:
  3.9 19.1 %collective-permute-start = (bf16[4,64,128]{2,1,0:T(8,128)(2,1)}, bf16[4,64,128]{2,1,0:T(8,128)(2,1)S(1)}, u32[]{:S(2)}, u32[]{:S(2)}) collective-permute-start(bf16[4,64,128]{2,1,0:T(8,128)(2,1)} %get-tuple-element.85), channel_id=1, source_target_pairs={{1,0},{2,1},{3,2},{4,3},{5,4},{6,5},{7,6},{0,7},{9,8},{10,9},{11,1... | collective-permute-start | bytes 196616 | tf_op jit(solution)/shard_map/ppermute | solution.py:44
  8.5 14.5 %collective-permute-start.1 = (bf16[4,64,128]{2,1,0:T(8,128)(2,1)}, bf16[4,64,128]{2,1,0:T(8,128)(2,1)S(1)}, u32[]{:S(2)}, u32[]{:S(2)}) collective-permute-start(bf16[4,64,128]{2,1,0:T(8,128)(2,1)} %get-tuple-element.86), channel_id=1, source_target_pairs={{2,0},{3,1},{4,2},{5,3},{6,4},{7,5},{0,6},{1,7},{10,8},{11,9},{12,... | collective-permute-start | bytes 196616 | tf_op jit(solution)/shard_map/ppermute | solution.py:44
  9.1 13.9 %collective-permute-start.2 = (bf16[4,64,128]{2,1,0:T(8,128)(2,1)}, bf16[4,64,128]{2,1,0:T(8,128)(2,1)S(1)}, u32[]{:S(2)}, u32[]{:S(2)}) collective-permute-start(bf16[4,64,128]{2,1,0:T(8,128)(2,1)} %get-tuple-element.87), channel_id=1, source_target_pairs={{3,0},{4,1},{5,2},{6,3},{7,4},{0,5},{1,6},{2,7},{11,8},{12,9},{13,... | collective-permute-start | bytes 196616 | tf_op jit(solution)/shard_map/ppermute | solution.py:44
  9.1 13.9 %collective-permute-start.3 = (bf16[4,64,128]{2,1,0:T(8,128)(2,1)}, bf16[4,64,128]{2,1,0:T(8,128)(2,1)S(1)}, u32[]{:S(2)}, u32[]{:S(2)}) collective-permute-start(bf16[4,64,128]{2,1,0:T(8,128)(2,1)} %get-tuple-element.88), channel_id=1, source_target_pairs={{4,0},{5,1},{6,2},{7,3},{0,4},{1,5},{2,6},{3,7},{12,8},{13,9},{14,... | collective-permute-start | bytes 196616 | tf_op jit(solution)/shard_map/ppermute | solution.py:44
  23.6 7.6 %collective-permute-start.6 = (bf16[8,64,128]{2,1,0:T(8,128)(2,1)S(1)}, bf16[8,64,128]{2,1,0:T(8,128)(2,1)S(1)}, u32[]{:S(2)}, u32[]{:S(2)}) collective-permute-start(bf16[8,64,128]{2,1,0:T(8,128)(2,1)S(1)} %shard_map.97.refs_0_), channel_id=1, source_target_pairs={{0,24},{8,16},{16,8},{24,0},{1,25},{9,17},{17,9},{25,1},{2,26},{10... | collective-permute-start | bytes 393224 | tf_op jit(solution)/shard_map/ppermute | solution.py:49
  26.1 6.7 %collective-permute-start.5 = (bf16[8,64,128]{2,1,0:T(8,128)(2,1)S(1)}, bf16[8,64,128]{2,1,0:T(8,128)(2,1)S(1)}, u32[]{:S(2)}, u32[]{:S(2)}) collective-permute-start(bf16[8,64,128]{2,1,0:T(8,128)(2,1)S(1)} %shard_map.97.refs_0_), channel_id=1, source_target_pairs={{0,16},{8,24},{16,0},{24,8},{1,17},{9,25},{17,1},{25,9},{2,18},{10... | collective-permute-start | bytes 393224 | tf_op jit(solution)/shard_map/ppermute | solution.py:49
  36.9 7.0 %collective-permute-start.10 = (bf16[256,128]{1,0:T(8,128)(2,1)S(1)}, bf16[256,128]{1,0:T(8,128)(2,1)S(1)}, u32[]{:S(2)}, u32[]{:S(2)}) collective-permute-start(bf16[256,128]{1,0:T(8,128)(2,1)S(1)} %get-tuple-element.176), channel_id=1, source_target_pairs={{0,6},{1,7},{2,4},{3,5},{4,2},{5,3},{6,0},{7,1},{8,14},{9,15},{10,... | collective-permute-start | bytes 196616 | tf_op jit(solution)/shard_map/ppermute | solution.py:49
  38.9 7.8 %collective-permute-start.9 = (bf16[256,128]{1,0:T(8,128)(2,1)S(1)}, bf16[256,128]{1,0:T(8,128)(2,1)S(1)}, u32[]{:S(2)}, u32[]{:S(2)}) collective-permute-start(bf16[256,128]{1,0:T(8,128)(2,1)S(1)} %get-tuple-element.177), channel_id=1, source_target_pairs={{0,4},{1,5},{2,6},{3,7},{4,0},{5,1},{6,2},{7,3},{8,12},{9,13},{10,... | collective-permute-start | bytes 196616 | tf_op jit(solution)/shard_map/ppermute | solution.py:49
  40.4 24.0 %collective-permute-start.21 = (bf16[4,64,4,256]{3,2,1,0:T(4,128)(2,1)S(1)}, bf16[4,64,4,256]{3,2,1,0:T(4,128)(2,1)S(1)}, u32[]{:S(2)}, u32[]{:S(2)}) collective-permute-start(bf16[4,64,4,256]{3,2,1,0:T(4,128)(2,1)S(1)} %get-tuple-element.119), channel_id=1, source_target_pairs={{0,8},{8,0},{16,24},{24,16},{1,9},{9,1},{17,25},{25,17},{2,10},{10... | collective-permute-start | bytes 1572872 | tf_op jit(solution)/shard_map/ppermute | solution.py:49
  41.9 24.4 %collective-permute-start.22 = (bf16[4,64,4,256]{3,2,1,0:T(4,128)(2,1)S(1)}, bf16[4,64,4,256]{3,2,1,0:T(4,128)(2,1)S(1)}, u32[]{:S(2)}, u32[]{:S(2)}) collective-permute-start(bf16[4,64,4,256]{3,2,1,0:T(4,128)(2,1)S(1)} %get-tuple-element.120), channel_id=1, source_target_pairs={{0,16},{8,24},{16,0},{24,8},{1,17},{9,25},{17,1},{25,9},{2,18},{10... | collective-permute-start | bytes 1572872 | tf_op jit(solution)/shard_map/ppermute | solution.py:49
  42.6 25.1 %collective-permute-start.23 = (bf16[4,64,4,256]{3,2,1,0:T(4,128)(2,1)S(1)}, bf16[4,64,4,256]{3,2,1,0:T(4,128)(2,1)S(1)}, u32[]{:S(2)}, u32[]{:S(2)}) collective-permute-start(bf16[4,64,4,256]{3,2,1,0:T(4,128)(2,1)S(1)} %get-tuple-element.121), channel_id=1, source_target_pairs={{0,24},{8,16},{16,8},{24,0},{1,25},{9,17},{17,9},{25,1},{2,26},{10... | collective-permute-start | bytes 1572872 | tf_op jit(solution)/shard_map/ppermute | solution.py:49
  46.8 6.9 %collective-permute-start.13 = (bf16[256,128]{1,0:T(8,128)(2,1)S(1)}, bf16[256,128]{1,0:T(8,128)(2,1)S(1)}, u32[]{:S(2)}, u32[]{:S(2)}) collective-permute-start(bf16[256,128]{1,0:T(8,128)(2,1)S(1)} %fusion.8.refs_2_), channel_id=1, source_target_pairs={{0,6},{1,7},{2,4},{3,5},{4,2},{5,3},{6,0},{7,1},{8,14},{9,15},{10,... | collective-permute-start | bytes 196616 | tf_op jit(solution)/shard_map/ppermute | solution.py:49
  48.6 7.5 %collective-permute-start.12 = (bf16[256,128]{1,0:T(8,128)(2,1)S(1)}, bf16[256,128]{1,0:T(8,128)(2,1)S(1)}, u32[]{:S(2)}, u32[]{:S(2)}) collective-permute-start(bf16[256,128]{1,0:T(8,128)(2,1)S(1)} %fusion.8.refs_2_), channel_id=1, source_target_pairs={{0,4},{1,5},{2,6},{3,7},{4,0},{5,1},{6,2},{7,3},{8,12},{9,13},{10,... | collective-permute-start | bytes 196616 | tf_op jit(solution)/shard_map/ppermute | solution.py:49
  63.9 23.2 %collective-permute-start.28 = (f32[2,4,64,128]{3,2,1,0:T(8,128)}, f32[2,4,64,128]{3,2,1,0:T(8,128)S(1)}, u32[]{:S(2)}, u32[]{:S(2)}) collective-permute-start(f32[2,4,64,128]{3,2,1,0:T(8,128)} %get-tuple-element.143), channel_id=1, source_target_pairs={{0,8},{8,0},{16,24},{24,16},{1,9},{9,1},{17,25},{25,17},{2,10},{10... | collective-permute-start | bytes 786440 | tf_op jit(solution)/shard_map/ppermute | solution.py:49
  64.4 22.7 %collective-permute-start.29 = (f32[2,4,64,128]{3,2,1,0:T(8,128)}, f32[2,4,64,128]{3,2,1,0:T(8,128)S(1)}, u32[]{:S(2)}, u32[]{:S(2)}) collective-permute-start(f32[2,4,64,128]{3,2,1,0:T(8,128)} %get-tuple-element.144), channel_id=1, source_target_pairs={{0,16},{8,24},{16,0},{24,8},{1,17},{9,25},{17,1},{25,9},{2,18},{10... | collective-permute-start | bytes 786440 | tf_op jit(solution)/shard_map/ppermute | solution.py:49
  66.3 25.4 %collective-permute-start.30 = (f32[2,4,64,128]{3,2,1,0:T(8,128)}, f32[2,4,64,128]{3,2,1,0:T(8,128)S(1)}, u32[]{:S(2)}, u32[]{:S(2)}) collective-permute-start(f32[2,4,64,128]{3,2,1,0:T(8,128)} %get-tuple-element.145), channel_id=1, source_target_pairs={{0,24},{8,16},{16,8},{24,0},{1,25},{9,17},{17,9},{25,1},{2,26},{10... | collective-permute-start | bytes 786440 | tf_op jit(solution)/shard_map/ppermute | solution.py:49
  67.7 16.2 %collective-permute-start.19 = (bf16[8,64,128]{2,1,0:T(8,128)(2,1)}, bf16[8,64,128]{2,1,0:T(8,128)(2,1)}, u32[]{:S(2)}, u32[]{:S(2)}) collective-permute-start(bf16[8,64,128]{2,1,0:T(8,128)(2,1)} %get-tuple-element.116), channel_id=1, source_target_pairs={{0,16},{8,24},{16,0},{24,8},{1,17},{9,25},{17,1},{25,9},{2,18},{10... | collective-permute-start | bytes 393224 | tf_op jit(solution)/shard_map/ppermute | solution.py:49
  68.7 15.2 %collective-permute-start.20 = (bf16[8,64,128]{2,1,0:T(8,128)(2,1)}, bf16[8,64,128]{2,1,0:T(8,128)(2,1)}, u32[]{:S(2)}, u32[]{:S(2)}) collective-permute-start(bf16[8,64,128]{2,1,0:T(8,128)(2,1)} %get-tuple-element.117), channel_id=1, source_target_pairs={{0,24},{8,16},{16,8},{24,0},{1,25},{9,17},{17,9},{25,1},{2,26},{10... | collective-permute-start | bytes 393224 | tf_op jit(solution)/shard_map/ppermute | solution.py:49
  85.1 6.6 %collective-permute-start.24 = (bf16[4,64,128]{2,1,0:T(8,128)(2,1)S(1)}, bf16[4,64,128]{2,1,0:T(8,128)(2,1)S(1)}, u32[]{:S(2)}, u32[]{:S(2)}) collective-permute-start(bf16[4,64,128]{2,1,0:T(8,128)(2,1)S(1)} %get-tuple-element.138), channel_id=1, source_target_pairs={{0,3},{1,2},{2,5},{3,4},{4,7},{5,6},{6,1},{7,0},{8,10},{9,13},{10,... | collective-permute-start | bytes 196616 | tf_op jit(solution)/shard_map/ppermute | solution.py:67
  87.1 7.4 %collective-permute-start.26 = (bf16[4,64,128]{2,1,0:T(8,128)(2,1)S(1)}, bf16[4,64,128]{2,1,0:T(8,128)(2,1)S(1)}, u32[]{:S(2)}, u32[]{:S(2)}) collective-permute-start(bf16[4,64,128]{2,1,0:T(8,128)(2,1)S(1)} %get-tuple-element.140), channel_id=1, source_target_pairs={{0,17},{1,20},{2,19},{3,22},{4,21},{5,16},{6,23},{7,18},{8,28},{9,... | collective-permute-start | bytes 196616 | tf_op jit(solution)/shard_map/ppermute | solution.py:67
  87.1 8.1 %collective-permute-start.27 = (bf16[4,64,128]{2,1,0:T(8,128)(2,1)S(1)}, bf16[4,64,128]{2,1,0:T(8,128)(2,1)S(1)}, u32[]{:S(2)}, u32[]{:S(2)}) collective-permute-start(bf16[4,64,128]{2,1,0:T(8,128)(2,1)S(1)} %get-tuple-element.141), channel_id=1, source_target_pairs={{0,28},{1,27},{2,30},{3,29},{4,24},{5,31},{6,26},{7,25},{8,17},{9,... | collective-permute-start | bytes 196616 | tf_op jit(solution)/shard_map/ppermute | solution.py:67
  96.5 8.0 %collective-permute-start.31 = (bf16[4,64,128]{2,1,0:T(8,128)(2,1)S(1)}, bf16[4,64,128]{2,1,0:T(8,128)(2,1)S(1)}, u32[]{:S(2)}, u32[]{:S(2)}) collective-permute-start(bf16[4,64,128]{2,1,0:T(8,128)(2,1)S(1)} %get-tuple-element.146), channel_id=1, source_target_pairs={{0,7},{1,6},{2,1},{3,0},{4,3},{5,2},{6,5},{7,4},{8,14},{9,13},{10,... | collective-permute-start | bytes 196616 | tf_op jit(solution)/shard_map/ppermute | solution.py:77
  102.7 8.3 %collective-permute-start.34 = (bf16[4,64,128]{2,1,0:T(8,128)(2,1)S(1)}, bf16[4,64,128]{2,1,0:T(8,128)(2,1)S(1)}, u32[]{:S(2)}, u32[]{:S(2)}) collective-permute-start(bf16[4,64,128]{2,1,0:T(8,128)(2,1)S(1)} %get-tuple-element.149), channel_id=1, source_target_pairs={{0,31},{1,30},{2,25},{3,24},{4,27},{5,26},{6,29},{7,28},{8,22},{9,... | collective-permute-start | bytes 196616 | tf_op jit(solution)/shard_map/ppermute | solution.py:77
  125.6 7.7 %collective-permute-start.40 = (bf16[256,128]{1,0:T(8,128)(2,1)S(1)}, bf16[256,128]{1,0:T(8,128)(2,1)S(1)}, u32[]{:S(2)}, u32[]{:S(2)}) collective-permute-start(bf16[256,128]{1,0:T(8,128)(2,1)S(1)} %get-tuple-element.174), channel_id=1, source_target_pairs={{0,4},{1,5},{2,6},{3,7},{4,0},{5,1},{6,2},{7,3},{8,12},{9,13},{10,... | collective-permute-start | bytes 196616 | tf_op jit(solution)/shard_map/ppermute | solution.py:49
  146.5 8.3 %collective-permute-start.50 = (bf16[8,64,128]{2,1,0:T(8,128)(2,1)S(1)}, bf16[8,64,128]{2,1,0:T(8,128)(2,1)S(1)}, u32[]{:S(2)}, u32[]{:S(2)}) collective-permute-start(bf16[8,64,128]{2,1,0:T(8,128)(2,1)S(1)} %get-tuple-element.152), channel_id=1, source_target_pairs={{0,16},{8,24},{16,0},{24,8},{1,17},{9,25},{17,1},{25,9},{2,18},{10... | collective-permute-start | bytes 393224 | tf_op jit(solution)/shard_map/ppermute | solution.py:49
  147.4 7.4 %collective-permute-start.51 = (bf16[8,64,128]{2,1,0:T(8,128)(2,1)S(1)}, bf16[8,64,128]{2,1,0:T(8,128)(2,1)S(1)}, u32[]{:S(2)}, u32[]{:S(2)}) collective-permute-start(bf16[8,64,128]{2,1,0:T(8,128)(2,1)S(1)} %get-tuple-element.153), channel_id=1, source_target_pairs={{0,24},{8,16},{16,8},{24,0},{1,25},{9,17},{17,9},{25,1},{2,26},{10... | collective-permute-start | bytes 393224 | tf_op jit(solution)/shard_map/ppermute | solution.py:49
  155.5 7.1 %collective-permute-start.53 = (bf16[4,64,128]{2,1,0:T(8,128)(2,1)S(1)}, bf16[4,64,128]{2,1,0:T(8,128)(2,1)S(1)}, u32[]{:S(2)}, u32[]{:S(2)}) collective-permute-start(bf16[4,64,128]{2,1,0:T(8,128)(2,1)S(1)} %get-tuple-element.155), channel_id=1, source_target_pairs={{0,10},{1,13},{2,12},{3,15},{4,14},{5,9},{6,8},{7,11},{8,3},{9,2},... | collective-permute-start | bytes 196616 | tf_op jit(solution)/shard_map/ppermute | solution.py:67
  157.4 7.3 %collective-permute-start.54 = (bf16[4,64,128]{2,1,0:T(8,128)(2,1)S(1)}, bf16[4,64,128]{2,1,0:T(8,128)(2,1)S(1)}, u32[]{:S(2)}, u32[]{:S(2)}) collective-permute-start(bf16[4,64,128]{2,1,0:T(8,128)(2,1)S(1)} %get-tuple-element.156), channel_id=1, source_target_pairs={{0,17},{1,20},{2,19},{3,22},{4,21},{5,16},{6,23},{7,18},{8,28},{9,... | collective-permute-start | bytes 196616 | tf_op jit(solution)/shard_map/ppermute | solution.py:67
  157.4 8.1 %collective-permute-start.55 = (bf16[4,64,128]{2,1,0:T(8,128)(2,1)S(1)}, bf16[4,64,128]{2,1,0:T(8,128)(2,1)S(1)}, u32[]{:S(2)}, u32[]{:S(2)}) collective-permute-start(bf16[4,64,128]{2,1,0:T(8,128)(2,1)S(1)} %get-tuple-element.157), channel_id=1, source_target_pairs={{0,28},{1,27},{2,30},{3,29},{4,24},{5,31},{6,26},{7,25},{8,17},{9,... | collective-permute-start | bytes 196616 | tf_op jit(solution)/shard_map/ppermute | solution.py:67
  166.8 6.9 %collective-permute-start.56 = (f32[4,64,128]{2,1,0:T(8,128)S(1)}, f32[4,64,128]{2,1,0:T(8,128)S(1)}, u32[]{:S(2)}, u32[]{:S(2)}) collective-permute-start(f32[4,64,128]{2,1,0:T(8,128)S(1)} %get-tuple-element.163), channel_id=1, source_target_pairs={{0,8},{8,0},{16,24},{24,16},{1,9},{9,1},{17,25},{25,17},{2,10},{10... | collective-permute-start | bytes 393224 | tf_op jit(solution)/shard_map/ppermute | solution.py:49
  169.7 8.0 %collective-permute-start.57 = (f32[4,64,128]{2,1,0:T(8,128)S(1)}, f32[4,64,128]{2,1,0:T(8,128)S(1)}, u32[]{:S(2)}, u32[]{:S(2)}) collective-permute-start(f32[4,64,128]{2,1,0:T(8,128)S(1)} %get-tuple-element.164), channel_id=1, source_target_pairs={{0,16},{8,24},{16,0},{24,8},{1,17},{9,25},{17,1},{25,9},{2,18},{10... | collective-permute-start | bytes 393224 | tf_op jit(solution)/shard_map/ppermute | solution.py:49
  170.9 6.9 %collective-permute-start.58 = (f32[4,64,128]{2,1,0:T(8,128)S(1)}, f32[4,64,128]{2,1,0:T(8,128)S(1)}, u32[]{:S(2)}, u32[]{:S(2)}) collective-permute-start(f32[4,64,128]{2,1,0:T(8,128)S(1)} %get-tuple-element.165), channel_id=1, source_target_pairs={{0,24},{8,16},{16,8},{24,0},{1,25},{9,17},{17,9},{25,1},{2,26},{10... | collective-permute-start | bytes 393224 | tf_op jit(solution)/shard_map/ppermute | solution.py:49
  (44 other events, 336.9 us)

commit v2 on v1

--- a/solution.py
+++ b/solution.py
@@ -13,6 +13,7 @@
 CORES = 2
 MIB = 1 << 20
 LARGE = 45
+LARGE_PREPARE = 57
 
 
 SMEM = pl.BlockSpec(memory_space=pltpu.SMEM)
@@ -39,6 +40,10 @@
     )(*scalars, *arrays)
 
 
+def indices():
+    return [lax.axis_index(axis).astype(jnp.int32) for axis in ("var", "samp")]
+
+
 def shifted(block, axis, distance):
     count = lax.axis_size(axis)
     return lax.ppermute(block, axis, [((i - distance) % count, i) for i in range(count)])
@@ -88,7 +93,7 @@
         self.size = self.unit + codes
 
 
-def begin_body(spot, owners, reach, pair, per_device, momentum, where, start, owner, now, before, out, *refs):
+def begin_body(spot, owners, reach, pair, per_device, momentum, start, owner, now, before, out, *refs):
     sent, (now_here, before_here, arrived) = refs[:reach], refs[reach:]
     copies = [
         pltpu.make_async_copy(now, now_here, arrived.at[0]),
@@ -96,7 +101,7 @@
     ]
     for copy in copies:
         copy.start()
-    tables_body(spot, owners, reach, pair, per_device, where, start, owner, out)
+    tables_body(spot, owners, reach, pair, per_device, start, owner, out)
     for copy in copies:
         copy.wait()
     for g in range(reach):
@@ -107,7 +112,8 @@
             sent[g][p] = jnp.where(live == 1, point, 0.0).astype(HALF)
 
 
-def tables_body(spot, owners, reach, pair, per_device, where, start, owner, out):
+def tables_body(spot, owners, reach, pair, per_device, start, owner, out):
+    where = indices()
     var = where[0]
     for i in range(spot.size):
         empty = spot.code_of_slot <= i < spot.local or i >= spot.unit
@@ -148,31 +154,36 @@
         out[spot.unit + code] = jnp.int32(j)
 
 
-def states_body(spot, quarters, pair, where, table, now, before, *outs):
+def prepare_body(spot, quarters, pair, table, now, before, inverses, *refs):
+    states, chosen = refs[:quarters], refs[quarters : 2 * quarters]
+    now_here, before_here, arrived = refs[2 * quarters :]
+    where = indices()
+    copies = [
+        pltpu.make_async_copy(now, now_here, arrived.at[0]),
+        pltpu.make_async_copy(before, before_here, arrived.at[1]),
+    ]
+    for k in range(quarters):
+        for p in range(pair):
+            slot = table[spot.slot + held_by(where[1] ^ k, where[0]) * pair + p]
+            ready = arrived.at[2 + k * pair + p]
+            copies.append(pltpu.make_async_copy(inverses.at[slot], chosen[k].at[p], ready))
+    for copy in copies:
+        copy.start()
+    for copy in copies[:2]:
+        copy.wait()
     for k in range(quarters):
         for p in range(pair):
             code = held_by(where[1] ^ k, where[0]) * pair + p
             slot = table[spot.slot + code]
             live = table[spot.live + code] == 1
-            outs[k][0, p] = jnp.where(live, now[slot], 0.0)
-            outs[k][1, p] = jnp.where(live, before[slot], 0.0)
-
-
-def choose_body(spot, quarters, pair, where, table, inverses, *refs):
-    outs, arrived = refs[:quarters], refs[quarters]
-    copies = []
-    for k in range(quarters):
-        for p in range(pair):
-            slot = table[spot.slot + held_by(where[1] ^ k, where[0]) * pair + p]
-            copies.append(
-                pltpu.make_async_copy(inverses.at[slot], outs[k].at[p], arrived.at[k * pair + p])
-            )
-            copies[-1].start()
-    for copy in copies:
+            states[k][0, p] = jnp.where(live, now_here[slot], 0.0)
+            states[k][1, p] = jnp.where(live, before_here[slot], 0.0)
+    for copy in copies[2:]:
         copy.wait()
 
 
-def panels_body(spot, quarters, pair, most, where, table, *refs):
+def panels_body(spot, quarters, pair, most, table, *refs):
+    where = indices()
     panels, outs = refs[:quarters], refs[quarters:]
     width = panels[0].shape[2] // most
     row = held_by(where[1], where[0]) * pair
@@ -188,7 +199,8 @@
                 outs[k][p, :, q * width : (q + 1) * width] = jnp.where(same & live, block, jnp.zeros_like(block))
 
 
-def local_values_body(spot, pair, turned, where, table, *refs):
+def local_values_body(spot, pair, turned, table, *refs):
+    where = indices()
     pieces, out, held = refs[:-2], refs[-2], refs[-1]
     for k, piece in enumerate(pieces):
         held[k] = piece[...]
@@ -207,7 +219,8 @@
             values[pl.ds(pl.multiple_of(at, quarter_rows), quarter_rows), :] = pieces[k][u]
 
 
-def load_body(where, dosage, *refs):
+def load_body(dosage, *refs):
+    where = indices()
     outs, arrived = refs[:CORES], refs[CORES]
     core, chip = lax.rem(where[0], CORES), lax.div(where[0], CORES)
     chips = arrived.shape[0] // CORES
@@ -224,7 +237,8 @@
         copy.wait()
 
 
-def predict_body(quarters, scale, where, blocks, *refs):
+def predict_body(quarters, scale, blocks, *refs):
+    where = indices()
     pieces, (out, values) = refs[:quarters], refs[quarters:]
     place_values(quarters, where, pieces, values)
     chips, rows = out.shape[:2]
@@ -233,7 +247,8 @@
         out[i] = jnp.dot(block, values[...], preferred_element_type=F32) * scale
 
 
-def gradient_body(quarters, units, scale, where, *refs):
+def gradient_body(quarters, units, scale, *refs):
+    where = indices()
     sides, pieces, outs = refs[:CORES], refs[CORES : -quarters - 2], refs[-quarters - 2 : -2]
     residual, total = refs[-2:]
     chips, rows = len(pieces) // CORES, pieces[0].shape[0]
@@ -251,7 +266,8 @@
             outs[k][u] = total[u, pl.ds(at, quarter_rows), :].astype(outs[k].dtype)
 
 
-def leave_body(spot, quarters, pair, where, table, *refs):
+def leave_body(spot, quarters, pair, table, *refs):
+    where = indices()
     sums, outs = refs[:quarters], refs[quarters:]
     for k in range(quarters):
         for p in range(pair):
@@ -263,7 +279,8 @@
             outs[k][p] = jnp.where(unit >= 0, total, 0.0).astype(HALF)
 
 
-def update_body(quarters, momenta, where, penalty, *refs):
+def update_body(quarters, momenta, penalty, *refs):
+    where = indices()
     last = len(momenta) == 1
     panels, pieces, states = refs[:quarters], refs[quarters : 2 * quarters], refs[2 * quarters : 3 * quarters]
     outs, gradient = refs[3 * quarters : -1], refs[-1]
@@ -292,7 +309,8 @@
             outs[quarters + k][...] = following.astype(HALF)
 
 
-def finish_body(spot, pair, where, table, *refs):
+def finish_body(spot, pair, table, *refs):
+    where = indices()
     pieces, out, held = refs[:-2], refs[-2], refs[-1]
     for k, piece in enumerate(pieces):
         held[k] = piece[...]
@@ -306,8 +324,6 @@
 def steps(dosage, traits, coef_now, coef_prev, block_inverse, penalty, block_start, unit_owner):
     owners = lax.axis_size("var")
     quarters = lax.axis_size("samp")
-    var_index = lax.axis_index("var").astype(jnp.int32)
-    samp_index = lax.axis_index("samp").astype(jnp.int32)
     capacity, quarter_rows, right_cols = coef_now.shape
     block_most, unit_rows = block_inverse.shape[2:]
     per_device = dosage.shape[1] // unit_rows
@@ -320,7 +336,6 @@
     inv_scale = 1.0 / math.sqrt(dosage.shape[1] * owners)
     grad_scale = 0.5 / math.sqrt(dosage.shape[0] * quarters)
     spot = Layout(codes, capacity, per_device)
-    where = jnp.stack([var_index, samp_index])
     ranks = range(quarters)
     piece = (pair, quarter_rows, right_cols)
     share = (per_device, quarter_rows, right_cols)
@@ -328,43 +343,40 @@
     table, *sent = pl.pallas_call(
         functools.partial(begin_body, spot, owners, reach, pair, per_device, MOMENTA[0]),
         name="begin",
-        in_specs=[SMEM] * 3 + [FAR] * 2,
+        in_specs=[SMEM] * 2 + [FAR] * 2,
         out_specs=[SMEM] + [VMEM] * reach,
         out_shape=[like((spot.size,), jnp.int32)] + [like(piece, HALF)] * reach,
         scratch_shapes=[pltpu.VMEM(coef_now.shape, F32)] * 2 + [pltpu.SemaphoreType.DMA((2,))],
         compiler_params=pltpu.CompilerParams(vmem_limit_bytes=60 * MIB),
-    )(where, block_start, unit_owner, coef_now, coef_prev)
+    )(block_start, unit_owner, coef_now, coef_prev)
     arrived = [shifted(sent[g], "var", -g - 1) for g in range(reach)]
-    states = local(
-        functools.partial(states_body, spot, quarters, pair),
-        [where, table], [coef_now, coef_prev], [like((2, *piece), F32)] * quarters,
-    )
-    chosen = local(
-        functools.partial(choose_body, spot, quarters, pair),
-        [where, table], [block_inverse], [like((pair, *block_inverse.shape[1:]), HALF)] * quarters,
-        [pltpu.SemaphoreType.DMA((codes,))], limit=LARGE, far=1,
-    )
-    arrived, states, chosen = lax.optimization_barrier((arrived, states, chosen))
+    prepared = local(
+        functools.partial(prepare_body, spot, quarters, pair),
+        [table], [coef_now, coef_prev, block_inverse],
+        [like((2, *piece), F32)] * quarters + [like((pair, *block_inverse.shape[1:]), HALF)] * quarters,
+        [pltpu.VMEM(coef_now.shape, F32)] * 2 + [pltpu.SemaphoreType.DMA((2 + codes,))], limit=LARGE_PREPARE, far=3,
+    )
+    block = like((chips * rows, dosage.shape[1]), HALF)
+    dosage = lax.optimization_barrier((prepared[0], dosage))[1]
+    kept_rows, given_rows = local(
+        load_body, [], [dosage], [block, block], [pltpu.SemaphoreType.DMA((owners,))], limit=LARGE, far=1
+    )
+    arrived, prepared, kept_rows, given_rows = lax.optimization_barrier(
+        (arrived, prepared, kept_rows, given_rows)
+    )
+    states, chosen = prepared[:quarters], prepared[quarters:]
     states = [states[0]] + [crossed(states[k], "samp", k) for k in ranks[1:]]
     penalty = penalty.reshape(1, 1, right_cols)
 
     for step in range(len(MOMENTA)):
         own = local(
             functools.partial(local_values_body, spot, pair, step > 0),
-            [where, table], arrived, like(share, HALF),
+            [table], arrived, like(share, HALF),
             [pltpu.VMEM((reach, *piece), HALF)],
         )
         pieces = [own] + [crossed(own, "samp", k) for k in ranks[1:]]
         if step == 0:
-            block = like((chips * rows, dosage.shape[1]), HALF)
-            dosage = lax.optimization_barrier((own, dosage))[1]
-            kept_rows, given_rows = local(
-                load_body, [where], [dosage], [block, block],
-                [pltpu.SemaphoreType.DMA((owners,))], limit=LARGE, far=1,
-            )
-            pieces, kept_rows, given_rows, chosen = lax.optimization_barrier(
-                (pieces, kept_rows, given_rows, chosen)
-            )
+            pieces, chosen = lax.optimization_barrier((pieces, chosen))
             chosen = [chosen[0]] + [crossed(chosen[k], "samp", k) for k in ranks[1:]]
         buffers = [pltpu.VMEM((dosage.shape[1], right_cols), HALF)]
         half = like((chips, rows, right_cols), F32)
@@ -372,7 +384,7 @@
         given, kept = (
             local(
                 functools.partial(predict_body, quarters, inv_scale),
-                [where], [side, *pieces], half, buffers, limit=8, flops=flops,
+                [], [side, *pieces], half, buffers, limit=8, flops=flops,
             )
             for side in (given_rows, kept_rows)
         )
@@ -381,40 +393,39 @@
         total = both[0]
         for i in range(1, chips):
             total = total + crossed(both[i].astype(HALF), "var", CORES * i).astype(F32)
-        residual = total - traits
-        residual_b = residual.astype(HALF)
+        residual_b = (total - traits).astype(HALF)
         mine = [residual_b] + [crossed(residual_b, "var", CORES * i) for i in range(1, chips)]
         others = [crossed(block, "var", 1) for block in mine]
         sums = local(
             functools.partial(gradient_body, quarters, per_device, grad_scale),
-            [where], [kept_rows, given_rows, *mine, *others],
+            [], [kept_rows, given_rows, *mine, *others],
             [like(share, F32 if k == 0 else HALF) for k in ranks],
             [
                 pltpu.VMEM((dosage.shape[0], right_cols), HALF),
                 pltpu.VMEM((per_device, unit_rows, right_cols), F32),
             ], limit=15, flops=2 * dosage.shape[0] * dosage.shape[1] * right_cols,
         )
-        owned = sums[0]
-        sums = [owned] + [crossed(sums[k], "samp", k) for k in ranks[1:]]
+        if step == len(MOMENTA) - 1:
+            residual = lax.optimization_barrier((sums[0], total))[1] - traits
+        sums = [sums[0]] + [crossed(sums[k], "samp", k) for k in ranks[1:]]
+        leaving = local(
+            functools.partial(leave_body, spot, quarters, pair),
+            [table], sums, [like(piece, HALF)] * quarters,
+        )
+        landed = [to_owners(leaving[k], k) for k in ranks]
         if step == 0:
-            chosen = lax.optimization_barrier((owned, chosen))[1]
+            chosen = lax.optimization_barrier((leaving, chosen))[1]
             panels = local(
                 functools.partial(panels_body, spot, quarters, pair, block_most),
-                [where, table],
+                [table],
                 [part.reshape(pair, quarter_rows, block_most * unit_rows) for part in chosen],
                 [like((pair, quarter_rows, block_most * unit_rows), HALF)] * quarters, limit=10,
             )
-            sums, panels = lax.optimization_barrier((sums, panels))
-        leaving = local(
-            functools.partial(leave_body, spot, quarters, pair),
-            [where, table], sums, [like(piece, HALF)] * quarters,
-        )
-        landed = [to_owners(leaving[k], k) for k in ranks]
         last = step == len(MOMENTA) - 1
         outs = [like(piece, F32)] * quarters + ([] if last else [like(piece, HALF)] * quarters)
         result = local(
             functools.partial(update_body, quarters, MOMENTA[step : step + 2]),
-            [where], [penalty, *panels, *landed, *states], outs,
+            [], [penalty, *panels, *landed, *states], outs,
             [pltpu.VMEM((pair * unit_rows, right_cols), HALF)], limit=12,
             flops=2 * (pair * unit_rows) ** 2 * right_cols,
         )
@@ -424,7 +435,7 @@
     states = [states[0]] + [crossed(states[k], "samp", k) for k in ranks[1:]]
     current = local(
         functools.partial(finish_body, spot, pair),
-        [where, table], states, like((capacity, quarter_rows, right_cols), F32),
+        [table], states, like((capacity, quarter_rows, right_cols), F32),
         [pltpu.VMEM((quarters, *piece), F32)],
     )
     return (current, residual)

time: 180 us -> 188 us (1.044)
  waiting for transfers between devices: 67.6 us -> 80.3 us
  starting transfers between devices: 68.6 us -> 74.6 us
  local copies, waits for them, and re-layouts: 8.73 us -> 3.39 us
  Pallas kernels: 31.7 us -> 27.1 us
    ppermute x43, waiting for transfers between devices: 53.7 us -> 71.2 us  [crossed(): return lax.ppermute(block, axis, [(i, i ^ mask) for i in range(count)])]
    ppermute x43, starting transfers between devices: 40.1 us -> 45.9 us  [crossed(): return lax.ppermute(block, axis, [(i, i ^ mask) for i in range(count)])]
    unnamed x34 -> x32, local copies, waits for them, and re-layouts: 6.2 us -> 0.86 us
    ppermute x8, waiting for transfers between devices: 7.49 us -> 2.68 us  [to_owners(): return lax.ppermute(block, ('samp', 'var'), route)]
    pallas_call x17 -> x16, Pallas kernels: 29.1 us -> 24.4 us  [local(): pl.pallas_call(body, in_specs=[SMEM] * len(scalars) + [FAR] * far + [VMEM...]
  transfers between devices with their start and end apart: 59 -> 59, of which waited for: 34 -> 32; matrix products, arithmetic and copies ran while one was open for 1% -> 2% of each run, Pallas kernels for 10% -> 8%
where the time goes in v2:
time: 188 us; the launch traced here: 187 us
  waiting for transfers between devices  80.3 us (43%)
  starting transfers between devices  74.6 us (40%)
  Pallas kernels  27.1 us (14%)
  local copies, waits for them, and re-layouts  3.39 us (2%)
    ppermute x43, waiting for transfers between devices, crossed(): return lax.ppermute(block, axis, [(i, i ^ mask) for i in range(count)])  71.2 us
    ppermute x43, starting transfers between devices, crossed(): return lax.ppermute(block, axis, [(i, i ^ mask) for i in range(count)])  45.9 us
    pallas_call x16, Pallas kernels, local(): pl.pallas_call(body, in_specs=[SMEM] * len(scalars) + [FAR] * far + [VMEM...  24.4 us
    ppermute x8, starting transfers between devices, to_owners(): return lax.ppermute(block, ('samp', 'var'), route)  13.2 us
    ppermute x4, starting transfers between devices, shifted(): lax.ppermute(block, axis, [((i - distance) % count, i) for i in range(cou...  7.89 us
    ppermute x4, starting transfers between devices, to_variants(): return lax.ppermute(block, ('samp', 'var'), route)  7.63 us
    ppermute x4, waiting for transfers between devices, to_variants(): return lax.ppermute(block, ('samp', 'var'), route)  6.43 us
  transfers between devices with their start and end apart: 59, of which 32 were waited for; matrix products, arithmetic and copies ran while one was open for 2% of the time, Pallas kernels for 8%

profile of v2, /device:TPU:0, one launch (start us, length us, event | category | flops | bytes accessed | tf_op | source)
XLA Modules:
  0.0 187.3 jit_solution(11545508363862101870)
XLA Ops:
  0.6 2.6 %begin.1 = (s32[88]{0:T(128)}, bf16[4,64,128]{2,1,0:T(8,128)(2,1)}, bf16[4,64,128]{2,1,0:T(8,128)(2,1)}, bf16[4,64,128]{2,1,0:T(8,128)(2,1)}, bf16[4,64,128]{2,1,0:T(8,128)(2,1)}) custom-call(s32[64]{0:T(128)} %start.1, s32[64]{0:T(128)} %owner.1, f32[16,64,128]{2,1,0:T(8,128)} %now.3, f32[16,64,128]{2,1,0:T(8,128)} %before.3), custom_call_target="tpu_custom_call" | custom-call | tf_op jit(solution)/shard_map/begin/pallas_call | solution.py:343
  3.3 4.6 %collective-permute-start = (bf16[4,64,128]{2,1,0:T(8,128)(2,1)}, bf16[4,64,128]{2,1,0:T(8,128)(2,1)S(1)}, u32[]{:S(2)}, u32[]{:S(2)}) collective-permute-start(bf16[4,64,128]{2,1,0:T(8,128)(2,1)} %get-tuple-element.78), channel_id=1, source_target_pairs={{1,0},{2,1},{3,2},{4,3},{5,4},{6,5},{7,6},{0,7},{9,8},{10,9},{11,1... | collective-permute-start | bytes 196616 | tf_op jit(solution)/shard_map/ppermute | solution.py:49
  8.5 2.7 %collective-permute-start.3 = (bf16[4,64,128]{2,1,0:T(8,128)(2,1)}, bf16[4,64,128]{2,1,0:T(8,128)(2,1)S(1)}, u32[]{:S(2)}, u32[]{:S(2)}) collective-permute-start(bf16[4,64,128]{2,1,0:T(8,128)(2,1)} %get-tuple-element.81), channel_id=1, source_target_pairs={{4,0},{5,1},{6,2},{7,3},{0,4},{1,5},{2,6},{3,7},{12,8},{13,9},{14,... | collective-permute-start | bytes 196616 | tf_op jit(solution)/shard_map/ppermute | solution.py:49
  11.2 5.6 %shard_map.95 = (f32[2,4,64,128]{3,2,1,0:T(8,128)}, f32[2,4,64,128]{3,2,1,0:T(8,128)}, f32[2,4,64,128]{3,2,1,0:T(8,128)}, f32[2,4,64,128]{3,2,1,0:T(8,128)}, bf1...) custom-call(s32[88]{0:T(128)} %get-tuple-element.77.table, ...), custom_call_target="tpu_custom_call" | custom-call | bytes 6291456 | tf_op jit(solution)/shard_map/pallas_call | solution.py:32
  16.8 3.5 %shard_map.96 = (bf16[1024,2048]{1,0:T(8,128)(2,1)S(1)}, bf16[1024,2048]{1,0:T(8,128)(2,1)S(1)}) custom-call(bf16[2048,2048]{1,0:T(8,128)(2,1)} %dosage), custom_call_target="tpu_custom_call" | custom-call | bytes 16777216 | tf_op jit(solution)/shard_map/pallas_call | solution.py:32
  20.9 2.5 %collective-permute-start.6 = (bf16[8,64,128]{2,1,0:T(8,128)(2,1)S(1)}, bf16[8,64,128]{2,1,0:T(8,128)(2,1)S(1)}, u32[]{:S(2)}, u32[]{:S(2)}) collective-permute-start(bf16[8,64,128]{2,1,0:T(8,128)(2,1)S(1)} %shard_map.97.refs_0_), channel_id=1, source_target_pairs={{0,24},{8,16},{16,8},{24,0},{1,25},{9,17},{17,9},{25,1},{2,26},{10... | collective-permute-start | bytes 393224 | tf_op jit(solution)/shard_map/ppermute | solution.py:54
  24.5 3.0 %collective-permute-done.6.refs_3_ = bf16[8,64,128]{2,1,0:T(8,128)(2,1)S(1)} collective-permute-done((bf16[8,64,128]{2,1,0:T(8,128)(2,1)S(1)}, bf16[8,64,128]{2,1,0:T(8,128)(2,1)S(1)}, u32[]{:S(2)}, u32[]{:S(2)}) %collective-permute-start.6) | collective-permute-done | bytes 131104 | tf_op jit(solution)/shard_map/ppermute | solution.py:54
  33.0 2.0 %collective-permute-start.10 = (bf16[256,128]{1,0:T(8,128)(2,1)S(1)}, bf16[256,128]{1,0:T(8,128)(2,1)S(1)}, u32[]{:S(2)}, u32[]{:S(2)}) collective-permute-start(bf16[256,128]{1,0:T(8,128)(2,1)S(1)} %get-tuple-element.162), channel_id=1, source_target_pairs={{0,6},{1,7},{2,4},{3,5},{4,2},{5,3},{6,0},{7,1},{8,14},{9,15},{10,... | collective-permute-start | bytes 196616 | tf_op jit(solution)/shard_map/ppermute | solution.py:54
  37.2 2.5 %collective-permute-done.10 = bf16[256,128]{1,0:T(8,128)(2,1)S(1)} collective-permute-done((bf16[256,128]{1,0:T(8,128)(2,1)S(1)}, bf16[256,128]{1,0:T(8,128)(2,1)S(1)}, u32[]{:S(2)}, u32[]{:S(2)}) %collective-permute-start.10) | collective-permute-done | bytes 65568 | tf_op jit(solution)/shard_map/ppermute | solution.py:54
  39.8 2.7 %collective-permute-done.9 = bf16[256,128]{1,0:T(8,128)(2,1)S(1)} collective-permute-done((bf16[256,128]{1,0:T(8,128)(2,1)S(1)}, bf16[256,128]{1,0:T(8,128)(2,1)S(1)}, u32[]{:S(2)}, u32[]{:S(2)}) %collective-permute-start.9) | collective-permute-done | bytes 65568 | tf_op jit(solution)/shard_map/ppermute | solution.py:54
  44.3 2.7 %collective-permute-start.11 = (bf16[256,128]{1,0:T(8,128)(2,1)S(1)}, bf16[256,128]{1,0:T(8,128)(2,1)S(1)}, u32[]{:S(2)}, u32[]{:S(2)}) collective-permute-start(bf16[256,128]{1,0:T(8,128)(2,1)S(1)} %fusion.7.refs_2_), channel_id=1, source_target_pairs={{0,2},{1,3},{2,0},{3,1},{4,6},{5,7},{6,4},{7,5},{8,10},{9,11},{10,... | collective-permute-start | bytes 196616 | tf_op jit(solution)/shard_map/ppermute | solution.py:54
  58.6 20.3 %collective-permute-done.18.refs_1_ = bf16[8,64,128]{2,1,0:T(8,128)(2,1)S(1)} collective-permute-done((bf16[8,64,128]{2,1,0:T(8,128)(2,1)S(1)}, bf16[8,64,128]{2,1,0:T(8,128)(2,1)S(1)}, u32[]{:S(2)}, u32[]{:S(2)}) %collective-permute-start.18) | collective-permute-done | bytes 131104 | tf_op jit(solution)/shard_map/ppermute | solution.py:54
  78.9 1.9 %collective-permute-start.20 = (bf16[8,64,128]{2,1,0:T(8,128)(2,1)S(1)}, bf16[8,64,128]{2,1,0:T(8,128)(2,1)S(1)}, u32[]{:S(2)}, u32[]{:S(2)}) collective-permute-start(bf16[8,64,128]{2,1,0:T(8,128)(2,1)S(1)} %get-tuple-element.110), channel_id=1, source_target_pairs={{0,24},{8,16},{16,8},{24,0},{1,25},{9,17},{17,9},{25,1},{2,26},{10... | collective-permute-start | bytes 393224 | tf_op jit(solution)/shard_map/ppermute | solution.py:54
  81.9 2.9 %collective-permute-done.20.refs_3_ = bf16[8,64,128]{2,1,0:T(8,128)(2,1)S(1)} collective-permute-done((bf16[8,64,128]{2,1,0:T(8,128)(2,1)S(1)}, bf16[8,64,128]{2,1,0:T(8,128)(2,1)S(1)}, u32[]{:S(2)}, u32[]{:S(2)}) %collective-permute-start.20) | collective-permute-done | bytes 131104 | tf_op jit(solution)/shard_map/ppermute | solution.py:54
  84.8 1.9 %collective-permute-start.30 = (f32[2,4,64,128]{3,2,1,0:T(8,128)}, f32[2,4,64,128]{3,2,1,0:T(8,128)S(1)}, u32[]{:S(2)}, u32[]{:S(2)}) collective-permute-start(f32[2,4,64,128]{3,2,1,0:T(8,128)} %get-tuple-element.130), channel_id=1, source_target_pairs={{0,24},{8,16},{16,8},{24,0},{1,25},{9,17},{17,9},{25,1},{2,26},{10... | collective-permute-start | bytes 786440 | tf_op jit(solution)/shard_map/ppermute | solution.py:54
  88.0 7.7 %collective-permute-done.29.refs_10_ = f32[2,4,64,128]{3,2,1,0:T(8,128)S(1)} collective-permute-done((f32[2,4,64,128]{3,2,1,0:T(8,128)S(1)}, f32[2,4,64,128]{3,2,1,0:T(8,128)S(1)}, u32[]{:S(2)}, u32[]{:S(2)}) %collective-permute-start.29) | collective-permute-done | bytes 262176 | tf_op jit(solution)/shard_map/ppermute | solution.py:54
  96.5 2.1 %collective-permute-start.25 = (bf16[4,64,128]{2,1,0:T(8,128)(2,1)}, bf16[4,64,128]{2,1,0:T(8,128)(2,1)S(1)}, u32[]{:S(2)}, u32[]{:S(2)}) collective-permute-start(bf16[4,64,128]{2,1,0:T(8,128)(2,1)} %get-tuple-element.112), channel_id=1, source_target_pairs={{0,10},{1,13},{2,12},{3,15},{4,14},{5,9},{6,8},{7,11},{8,3},{9,2},... | collective-permute-start | bytes 196616 | tf_op jit(solution)/shard_map/ppermute | solution.py:72
  99.4 4.2 %collective-permute-start.27 = (bf16[4,64,128]{2,1,0:T(8,128)(2,1)S(1)}, bf16[4,64,128]{2,1,0:T(8,128)(2,1)S(1)}, u32[]{:S(2)}, u32[]{:S(2)}) collective-permute-start(bf16[4,64,128]{2,1,0:T(8,128)(2,1)S(1)} %get-tuple-element.114), channel_id=1, source_target_pairs={{0,28},{1,27},{2,30},{3,29},{4,24},{5,31},{6,26},{7,25},{8,17},{9,... | collective-permute-start | bytes 196616 | tf_op jit(solution)/shard_map/ppermute | solution.py:72
  107.8 2.2 %collective-permute-start.31 = (bf16[4,64,128]{2,1,0:T(8,128)(2,1)S(1)}, bf16[4,64,128]{2,1,0:T(8,128)(2,1)S(1)}, u32[]{:S(2)}, u32[]{:S(2)}) collective-permute-start(bf16[4,64,128]{2,1,0:T(8,128)(2,1)S(1)} %get-tuple-element.131), channel_id=1, source_target_pairs={{0,7},{1,6},{2,1},{3,0},{4,3},{5,2},{6,5},{7,4},{8,14},{9,13},{10,... | collective-permute-start | bytes 196616 | tf_op jit(solution)/shard_map/ppermute | solution.py:82
  111.5 2.1 %collective-permute-start.33 = (bf16[4,64,128]{2,1,0:T(8,128)(2,1)S(1)}, bf16[4,64,128]{2,1,0:T(8,128)(2,1)S(1)}, u32[]{:S(2)}, u32[]{:S(2)}) collective-permute-start(bf16[4,64,128]{2,1,0:T(8,128)(2,1)S(1)} %get-tuple-element.133), channel_id=1, source_target_pairs={{0,23},{1,22},{2,17},{3,16},{4,19},{5,18},{6,21},{7,20},{8,30},{9,... | collective-permute-start | bytes 196616 | tf_op jit(solution)/shard_map/ppermute | solution.py:82
  116.0 5.9 %collective-permute-done.34.refs_3_ = bf16[4,64,128]{2,1,0:T(8,128)(2,1)S(1)} collective-permute-done((bf16[4,64,128]{2,1,0:T(8,128)(2,1)S(1)}, bf16[4,64,128]{2,1,0:T(8,128)(2,1)S(1)}, u32[]{:S(2)}, u32[]{:S(2)}) %collective-permute-start.34) | collective-permute-done | bytes 65568 | tf_op jit(solution)/shard_map/ppermute | solution.py:82
  126.1 2.6 %collective-permute-done.37.refs_3_ = bf16[8,64,128]{2,1,0:T(8,128)(2,1)S(1)} collective-permute-done((bf16[8,64,128]{2,1,0:T(8,128)(2,1)S(1)}, bf16[8,64,128]{2,1,0:T(8,128)(2,1)S(1)}, u32[]{:S(2)}, u32[]{:S(2)}) %collective-permute-start.37) | collective-permute-done | bytes 131104 | tf_op jit(solution)/shard_map/ppermute | solution.py:54
  137.4 2.8 %collective-permute-done.41 = bf16[256,128]{1,0:T(8,128)(2,1)S(1)} collective-permute-done((bf16[256,128]{1,0:T(8,128)(2,1)S(1)}, bf16[256,128]{1,0:T(8,128)(2,1)S(1)}, u32[]{:S(2)}, u32[]{:S(2)}) %collective-permute-start.41) | collective-permute-done | bytes 65568 | tf_op jit(solution)/shard_map/ppermute | solution.py:54
  140.2 2.5 %collective-permute-done.40 = bf16[256,128]{1,0:T(8,128)(2,1)S(1)} collective-permute-done((bf16[256,128]{1,0:T(8,128)(2,1)S(1)}, bf16[256,128]{1,0:T(8,128)(2,1)S(1)}, u32[]{:S(2)}, u32[]{:S(2)}) %collective-permute-start.40) | collective-permute-done | bytes 65568 | tf_op jit(solution)/shard_map/ppermute | solution.py:54
  142.7 2.1 %collective-permute-start.44 = (bf16[256,128]{1,0:T(8,128)(2,1)S(1)}, bf16[256,128]{1,0:T(8,128)(2,1)S(1)}, u32[]{:S(2)}, u32[]{:S(2)}) collective-permute-start(bf16[256,128]{1,0:T(8,128)(2,1)S(1)} %get-tuple-element.152.refs_2_), channel_id=1, source_target_pairs={{0,6},{1,7},{2,4},{3,5},{4,2},{5,3},{6,0},{7,1},{8,14},{9,15},{10,... | collective-permute-start | bytes 196616 | tf_op jit(solution)/shard_map/ppermute | solution.py:54
  144.8 2.3 %collective-permute-start.42 = (bf16[256,128]{1,0:T(8,128)(2,1)S(1)}, bf16[256,128]{1,0:T(8,128)(2,1)S(1)}, u32[]{:S(2)}, u32[]{:S(2)}) collective-permute-start(bf16[256,128]{1,0:T(8,128)(2,1)S(1)} %get-tuple-element.152.refs_2_), channel_id=1, source_target_pairs={{0,2},{1,3},{2,0},{3,1},{4,6},{5,7},{6,4},{7,5},{8,10},{9,11},{10,... | collective-permute-start | bytes 196616 | tf_op jit(solution)/shard_map/ppermute | solution.py:54
  149.0 1.9 %collective-permute-done.43.refs_4_ = bf16[256,128]{1,0:T(8,128)(2,1)S(1)} collective-permute-done((bf16[256,128]{1,0:T(8,128)(2,1)S(1)}, bf16[256,128]{1,0:T(8,128)(2,1)S(1)}, u32[]{:S(2)}, u32[]{:S(2)}) %collective-permute-start.43) | collective-permute-done | bytes 65568 | tf_op jit(solution)/shard_map/ppermute | solution.py:54
  157.5 2.4 %collective-permute-done.49.refs_1_ = bf16[8,64,128]{2,1,0:T(8,128)(2,1)S(1)} collective-permute-done((bf16[8,64,128]{2,1,0:T(8,128)(2,1)S(1)}, bf16[8,64,128]{2,1,0:T(8,128)(2,1)S(1)}, u32[]{:S(2)}, u32[]{:S(2)}) %collective-permute-start.49) | collective-permute-done | bytes 131104 | tf_op jit(solution)/shard_map/ppermute | solution.py:54
  159.9 4.1 %collective-permute-done.50.refs_2_ = bf16[8,64,128]{2,1,0:T(8,128)(2,1)S(1)} collective-permute-done((bf16[8,64,128]{2,1,0:T(8,128)(2,1)S(1)}, bf16[8,64,128]{2,1,0:T(8,128)(2,1)S(1)}, u32[]{:S(2)}, u32[]{:S(2)}) %collective-permute-start.50) | collective-permute-done | bytes 131104 | tf_op jit(solution)/shard_map/ppermute | solution.py:54
  165.9 5.0 %collective-permute-start.55 = (bf16[4,64,128]{2,1,0:T(8,128)(2,1)S(1)}, bf16[4,64,128]{2,1,0:T(8,128)(2,1)S(1)}, u32[]{:S(2)}, u32[]{:S(2)}) collective-permute-start(bf16[4,64,128]{2,1,0:T(8,128)(2,1)S(1)} %get-tuple-element.142), channel_id=1, source_target_pairs={{0,28},{1,27},{2,30},{3,29},{4,24},{5,31},{6,26},{7,25},{8,17},{9,... | collective-permute-start | bytes 196616 | tf_op jit(solution)/shard_map/ppermute | solution.py:72
  174.3 4.1 %collective-permute-start.56 = (f32[4,64,128]{2,1,0:T(8,128)S(1)}, f32[4,64,128]{2,1,0:T(8,128)S(1)}, u32[]{:S(2)}, u32[]{:S(2)}) collective-permute-start(f32[4,64,128]{2,1,0:T(8,128)S(1)} %get-tuple-element.148), channel_id=1, source_target_pairs={{0,8},{8,0},{16,24},{24,16},{1,9},{9,1},{17,25},{25,17},{2,10},{10... | collective-permute-start | bytes 393224 | tf_op jit(solution)/shard_map/ppermute | solution.py:54
  182.4 3.5 %collective-permute-done.57.refs_2_ = f32[4,64,128]{2,1,0:T(8,128)S(1)} collective-permute-done((f32[4,64,128]{2,1,0:T(8,128)S(1)}, f32[4,64,128]{2,1,0:T(8,128)S(1)}, u32[]{:S(2)}, u32[]{:S(2)}) %collective-permute-start.57) | collective-permute-done | bytes 131104 | tf_op jit(solution)/shard_map/ppermute | solution.py:54
  (146 shorter events, 67.1 us)
Async XLA Ops:
  3.3 17.0 %collective-permute-start = (bf16[4,64,128]{2,1,0:T(8,128)(2,1)}, bf16[4,64,128]{2,1,0:T(8,128)(2,1)S(1)}, u32[]{:S(2)}, u32[]{:S(2)}) collective-permute-start(bf16[4,64,128]{2,1,0:T(8,128)(2,1)} %get-tuple-element.78), channel_id=1, source_target_pairs={{1,0},{2,1},{3,2},{4,3},{5,4},{6,5},{7,6},{0,7},{9,8},{10,9},{11,1... | collective-permute-start | bytes 196616 | tf_op jit(solution)/shard_map/ppermute | solution.py:49
  7.9 12.5 %collective-permute-start.1 = (bf16[4,64,128]{2,1,0:T(8,128)(2,1)}, bf16[4,64,128]{2,1,0:T(8,128)(2,1)S(1)}, u32[]{:S(2)}, u32[]{:S(2)}) collective-permute-start(bf16[4,64,128]{2,1,0:T(8,128)(2,1)} %get-tuple-element.79), channel_id=1, source_target_pairs={{2,0},{3,1},{4,2},{5,3},{6,4},{7,5},{0,6},{1,7},{10,8},{11,9},{12,... | collective-permute-start | bytes 196616 | tf_op jit(solution)/shard_map/ppermute | solution.py:49
  8.5 11.8 %collective-permute-start.2 = (bf16[4,64,128]{2,1,0:T(8,128)(2,1)}, bf16[4,64,128]{2,1,0:T(8,128)(2,1)S(1)}, u32[]{:S(2)}, u32[]{:S(2)}) collective-permute-start(bf16[4,64,128]{2,1,0:T(8,128)(2,1)} %get-tuple-element.80), channel_id=1, source_target_pairs={{3,0},{4,1},{5,2},{6,3},{7,4},{0,5},{1,6},{2,7},{11,8},{12,9},{13,... | collective-permute-start | bytes 196616 | tf_op jit(solution)/shard_map/ppermute | solution.py:49
  8.5 11.8 %collective-permute-start.3 = (bf16[4,64,128]{2,1,0:T(8,128)(2,1)}, bf16[4,64,128]{2,1,0:T(8,128)(2,1)S(1)}, u32[]{:S(2)}, u32[]{:S(2)}) collective-permute-start(bf16[4,64,128]{2,1,0:T(8,128)(2,1)} %get-tuple-element.81), channel_id=1, source_target_pairs={{4,0},{5,1},{6,2},{7,3},{0,4},{1,5},{2,6},{3,7},{12,8},{13,9},{14,... | collective-permute-start | bytes 196616 | tf_op jit(solution)/shard_map/ppermute | solution.py:49
  20.9 6.6 %collective-permute-start.6 = (bf16[8,64,128]{2,1,0:T(8,128)(2,1)S(1)}, bf16[8,64,128]{2,1,0:T(8,128)(2,1)S(1)}, u32[]{:S(2)}, u32[]{:S(2)}) collective-permute-start(bf16[8,64,128]{2,1,0:T(8,128)(2,1)S(1)} %shard_map.97.refs_0_), channel_id=1, source_target_pairs={{0,24},{8,16},{16,8},{24,0},{1,25},{9,17},{17,9},{25,1},{2,26},{10... | collective-permute-start | bytes 393224 | tf_op jit(solution)/shard_map/ppermute | solution.py:54
  33.0 6.8 %collective-permute-start.10 = (bf16[256,128]{1,0:T(8,128)(2,1)S(1)}, bf16[256,128]{1,0:T(8,128)(2,1)S(1)}, u32[]{:S(2)}, u32[]{:S(2)}) collective-permute-start(bf16[256,128]{1,0:T(8,128)(2,1)S(1)} %get-tuple-element.162), channel_id=1, source_target_pairs={{0,6},{1,7},{2,4},{3,5},{4,2},{5,3},{6,0},{7,1},{8,14},{9,15},{10,... | collective-permute-start | bytes 196616 | tf_op jit(solution)/shard_map/ppermute | solution.py:54
  35.0 7.5 %collective-permute-start.9 = (bf16[256,128]{1,0:T(8,128)(2,1)S(1)}, bf16[256,128]{1,0:T(8,128)(2,1)S(1)}, u32[]{:S(2)}, u32[]{:S(2)}) collective-permute-start(bf16[256,128]{1,0:T(8,128)(2,1)S(1)} %get-tuple-element.163), channel_id=1, source_target_pairs={{0,4},{1,5},{2,6},{3,7},{4,0},{5,1},{6,2},{7,3},{8,12},{9,13},{10,... | collective-permute-start | bytes 196616 | tf_op jit(solution)/shard_map/ppermute | solution.py:54
  42.6 6.4 %collective-permute-start.13 = (bf16[256,128]{1,0:T(8,128)(2,1)S(1)}, bf16[256,128]{1,0:T(8,128)(2,1)S(1)}, u32[]{:S(2)}, u32[]{:S(2)}) collective-permute-start(bf16[256,128]{1,0:T(8,128)(2,1)S(1)} %fusion.7.refs_2_), channel_id=1, source_target_pairs={{0,6},{1,7},{2,4},{3,5},{4,2},{5,3},{6,0},{7,1},{8,14},{9,15},{10,... | collective-permute-start | bytes 196616 | tf_op jit(solution)/shard_map/ppermute | solution.py:54
  47.0 10.6 %collective-permute-start.28 = (f32[2,4,64,128]{3,2,1,0:T(8,128)S(1)}, f32[2,4,64,128]{3,2,1,0:T(8,128)S(1)}, u32[]{:S(2)}, u32[]{:S(2)}) collective-permute-start(f32[2,4,64,128]{3,2,1,0:T(8,128)S(1)} %copy-done.15), channel_id=1, source_target_pairs={{0,8},{8,0},{16,24},{24,16},{1,9},{9,1},{17,25},{25,17},{2,10},{10... | collective-permute-start | bytes 786440 | tf_op jit(solution)/shard_map/ppermute | solution.py:54
  50.9 45.5 %collective-permute-start.21 = (bf16[4,64,4,256]{3,2,1,0:T(4,128)(2,1)S(1)}, bf16[4,64,4,256]{3,2,1,0:T(4,128)(2,1)S(1)}, u32[]{:S(2)}, u32[]{:S(2)}) collective-permute-start(bf16[4,64,4,256]{3,2,1,0:T(4,128)(2,1)S(1)} %copy-done.13), channel_id=1, source_target_pairs={{0,8},{8,0},{16,24},{24,16},{1,9},{9,1},{17,25},{25,17},{2,10},{10... | collective-permute-start | bytes 1572872 | tf_op jit(solution)/shard_map/ppermute | solution.py:54
  52.4 46.1 %collective-permute-start.22 = (bf16[4,64,4,256]{3,2,1,0:T(4,128)(2,1)S(1)}, bf16[4,64,4,256]{3,2,1,0:T(4,128)(2,1)S(1)}, u32[]{:S(2)}, u32[]{:S(2)}) collective-permute-start(bf16[4,64,4,256]{3,2,1,0:T(4,128)(2,1)S(1)} %copy-done.12), channel_id=1, source_target_pairs={{0,16},{8,24},{16,0},{24,8},{1,17},{9,25},{17,1},{25,9},{2,18},{10... | collective-permute-start | bytes 1572872 | tf_op jit(solution)/shard_map/ppermute | solution.py:54
  53.4 45.2 %collective-permute-start.23 = (bf16[4,64,4,256]{3,2,1,0:T(4,128)(2,1)S(1)}, bf16[4,64,4,256]{3,2,1,0:T(4,128)(2,1)S(1)}, u32[]{:S(2)}, u32[]{:S(2)}) collective-permute-start(bf16[4,64,4,256]{3,2,1,0:T(4,128)(2,1)S(1)} %copy-done.11), channel_id=1, source_target_pairs={{0,24},{8,16},{16,8},{24,0},{1,25},{9,17},{17,9},{25,1},{2,26},{10... | collective-permute-start | bytes 1572872 | tf_op jit(solution)/shard_map/ppermute | solution.py:54
  56.1 22.9 %collective-permute-start.18 = (bf16[8,64,128]{2,1,0:T(8,128)(2,1)S(1)}, bf16[8,64,128]{2,1,0:T(8,128)(2,1)S(1)}, u32[]{:S(2)}, u32[]{:S(2)}) collective-permute-start(bf16[8,64,128]{2,1,0:T(8,128)(2,1)S(1)} %get-tuple-element.108), channel_id=1, source_target_pairs={{0,8},{8,0},{16,24},{24,16},{1,9},{9,1},{17,25},{25,17},{2,10},{10... | collective-permute-start | bytes 393224 | tf_op jit(solution)/shard_map/ppermute | solution.py:54
  57.6 23.2 %collective-permute-start.19 = (bf16[8,64,128]{2,1,0:T(8,128)(2,1)S(1)}, bf16[8,64,128]{2,1,0:T(8,128)(2,1)S(1)}, u32[]{:S(2)}, u32[]{:S(2)}) collective-permute-start(bf16[8,64,128]{2,1,0:T(8,128)(2,1)S(1)} %get-tuple-element.109), channel_id=1, source_target_pairs={{0,16},{8,24},{16,0},{24,8},{1,17},{9,25},{17,1},{25,9},{2,18},{10... | collective-permute-start | bytes 393224 | tf_op jit(solution)/shard_map/ppermute | solution.py:54
  80.8 14.8 %collective-permute-start.29 = (f32[2,4,64,128]{3,2,1,0:T(8,128)S(1)}, f32[2,4,64,128]{3,2,1,0:T(8,128)S(1)}, u32[]{:S(2)}, u32[]{:S(2)}) collective-permute-start(f32[2,4,64,128]{3,2,1,0:T(8,128)S(1)} %copy-done.14), channel_id=1, source_target_pairs={{0,16},{8,24},{16,0},{24,8},{1,17},{9,25},{17,1},{25,9},{2,18},{10... | collective-permute-start | bytes 786440 | tf_op jit(solution)/shard_map/ppermute | solution.py:54
  84.8 22.2 %collective-permute-start.30 = (f32[2,4,64,128]{3,2,1,0:T(8,128)}, f32[2,4,64,128]{3,2,1,0:T(8,128)S(1)}, u32[]{:S(2)}, u32[]{:S(2)}) collective-permute-start(f32[2,4,64,128]{3,2,1,0:T(8,128)} %get-tuple-element.130), channel_id=1, source_target_pairs={{0,24},{8,16},{16,8},{24,0},{1,25},{9,17},{17,9},{25,1},{2,26},{10... | collective-permute-start | bytes 786440 | tf_op jit(solution)/shard_map/ppermute | solution.py:54
  95.7 11.3 %collective-permute-start.24 = (bf16[4,64,128]{2,1,0:T(8,128)(2,1)}, bf16[4,64,128]{2,1,0:T(8,128)(2,1)S(1)}, u32[]{:S(2)}, u32[]{:S(2)}) collective-permute-start(bf16[4,64,128]{2,1,0:T(8,128)(2,1)} %get-tuple-element.111), channel_id=1, source_target_pairs={{0,3},{1,2},{2,5},{3,4},{4,7},{5,6},{6,1},{7,0},{8,10},{9,13},{10,... | collective-permute-start | bytes 196616 | tf_op jit(solution)/shard_map/ppermute | solution.py:72
  96.5 10.5 %collective-permute-start.25 = (bf16[4,64,128]{2,1,0:T(8,128)(2,1)}, bf16[4,64,128]{2,1,0:T(8,128)(2,1)S(1)}, u32[]{:S(2)}, u32[]{:S(2)}) collective-permute-start(bf16[4,64,128]{2,1,0:T(8,128)(2,1)} %get-tuple-element.112), channel_id=1, source_target_pairs={{0,10},{1,13},{2,12},{3,15},{4,14},{5,9},{6,8},{7,11},{8,3},{9,2},... | collective-permute-start | bytes 196616 | tf_op jit(solution)/shard_map/ppermute | solution.py:72
  98.6 8.4 %collective-permute-start.26 = (bf16[4,64,128]{2,1,0:T(8,128)(2,1)S(1)}, bf16[4,64,128]{2,1,0:T(8,128)(2,1)S(1)}, u32[]{:S(2)}, u32[]{:S(2)}) collective-permute-start(bf16[4,64,128]{2,1,0:T(8,128)(2,1)S(1)} %get-tuple-element.113), channel_id=1, source_target_pairs={{0,17},{1,20},{2,19},{3,22},{4,21},{5,16},{6,23},{7,18},{8,28},{9,... | collective-permute-start | bytes 196616 | tf_op jit(solution)/shard_map/ppermute | solution.py:72
  99.4 7.7 %collective-permute-start.27 = (bf16[4,64,128]{2,1,0:T(8,128)(2,1)S(1)}, bf16[4,64,128]{2,1,0:T(8,128)(2,1)S(1)}, u32[]{:S(2)}, u32[]{:S(2)}) collective-permute-start(bf16[4,64,128]{2,1,0:T(8,128)(2,1)S(1)} %get-tuple-element.114), channel_id=1, source_target_pairs={{0,28},{1,27},{2,30},{3,29},{4,24},{5,31},{6,26},{7,25},{8,17},{9,... | collective-permute-start | bytes 196616 | tf_op jit(solution)/shard_map/ppermute | solution.py:72
  107.8 7.6 %collective-permute-start.31 = (bf16[4,64,128]{2,1,0:T(8,128)(2,1)S(1)}, bf16[4,64,128]{2,1,0:T(8,128)(2,1)S(1)}, u32[]{:S(2)}, u32[]{:S(2)}) collective-permute-start(bf16[4,64,128]{2,1,0:T(8,128)(2,1)S(1)} %get-tuple-element.131), channel_id=1, source_target_pairs={{0,7},{1,6},{2,1},{3,0},{4,3},{5,2},{6,5},{7,4},{8,14},{9,13},{10,... | collective-permute-start | bytes 196616 | tf_op jit(solution)/shard_map/ppermute | solution.py:82
  113.6 8.3 %collective-permute-start.34 = (bf16[4,64,128]{2,1,0:T(8,128)(2,1)S(1)}, bf16[4,64,128]{2,1,0:T(8,128)(2,1)S(1)}, u32[]{:S(2)}, u32[]{:S(2)}) collective-permute-start(bf16[4,64,128]{2,1,0:T(8,128)(2,1)S(1)} %get-tuple-element.134), channel_id=1, source_target_pairs={{0,31},{1,30},{2,25},{3,24},{4,27},{5,26},{6,29},{7,28},{8,22},{9,... | collective-permute-start | bytes 196616 | tf_op jit(solution)/shard_map/ppermute | solution.py:82
  133.4 6.7 %collective-permute-start.41 = (bf16[256,128]{1,0:T(8,128)(2,1)S(1)}, bf16[256,128]{1,0:T(8,128)(2,1)S(1)}, u32[]{:S(2)}, u32[]{:S(2)}) collective-permute-start(bf16[256,128]{1,0:T(8,128)(2,1)S(1)} %get-tuple-element.159), channel_id=1, source_target_pairs={{0,6},{1,7},{2,4},{3,5},{4,2},{5,3},{6,0},{7,1},{8,14},{9,15},{10,... | collective-permute-start | bytes 196616 | tf_op jit(solution)/shard_map/ppermute | solution.py:54
  135.3 7.4 %collective-permute-start.40 = (bf16[256,128]{1,0:T(8,128)(2,1)S(1)}, bf16[256,128]{1,0:T(8,128)(2,1)S(1)}, u32[]{:S(2)}, u32[]{:S(2)}) collective-permute-start(bf16[256,128]{1,0:T(8,128)(2,1)S(1)} %get-tuple-element.160), channel_id=1, source_target_pairs={{0,4},{1,5},{2,6},{3,7},{4,0},{5,1},{6,2},{7,3},{8,12},{9,13},{10,... | collective-permute-start | bytes 196616 | tf_op jit(solution)/shard_map/ppermute | solution.py:54
  155.8 8.3 %collective-permute-start.50 = (bf16[8,64,128]{2,1,0:T(8,128)(2,1)S(1)}, bf16[8,64,128]{2,1,0:T(8,128)(2,1)S(1)}, u32[]{:S(2)}, u32[]{:S(2)}) collective-permute-start(bf16[8,64,128]{2,1,0:T(8,128)(2,1)S(1)} %get-tuple-element.137), channel_id=1, source_target_pairs={{0,16},{8,24},{16,0},{24,8},{1,17},{9,25},{17,1},{25,9},{2,18},{10... | collective-permute-start | bytes 393224 | tf_op jit(solution)/shard_map/ppermute | solution.py:54
  156.5 7.5 %collective-permute-start.51 = (bf16[8,64,128]{2,1,0:T(8,128)(2,1)S(1)}, bf16[8,64,128]{2,1,0:T(8,128)(2,1)S(1)}, u32[]{:S(2)}, u32[]{:S(2)}) collective-permute-start(bf16[8,64,128]{2,1,0:T(8,128)(2,1)S(1)} %get-tuple-element.138), channel_id=1, source_target_pairs={{0,24},{8,16},{16,8},{24,0},{1,25},{9,17},{17,9},{25,1},{2,26},{10... | collective-permute-start | bytes 393224 | tf_op jit(solution)/shard_map/ppermute | solution.py:54
  164.8 7.2 %collective-permute-start.53 = (bf16[4,64,128]{2,1,0:T(8,128)(2,1)S(1)}, bf16[4,64,128]{2,1,0:T(8,128)(2,1)S(1)}, u32[]{:S(2)}, u32[]{:S(2)}) collective-permute-start(bf16[4,64,128]{2,1,0:T(8,128)(2,1)S(1)} %get-tuple-element.140), channel_id=1, source_target_pairs={{0,10},{1,13},{2,12},{3,15},{4,14},{5,9},{6,8},{7,11},{8,3},{9,2},... | collective-permute-start | bytes 196616 | tf_op jit(solution)/shard_map/ppermute | solution.py:72
  165.9 7.0 %collective-permute-start.54 = (bf16[4,64,128]{2,1,0:T(8,128)(2,1)S(1)}, bf16[4,64,128]{2,1,0:T(8,128)(2,1)S(1)}, u32[]{:S(2)}, u32[]{:S(2)}) collective-permute-start(bf16[4,64,128]{2,1,0:T(8,128)(2,1)S(1)} %get-tuple-element.141), channel_id=1, source_target_pairs={{0,17},{1,20},{2,19},{3,22},{4,21},{5,16},{6,23},{7,18},{8,28},{9,... | collective-permute-start | bytes 196616 | tf_op jit(solution)/shard_map/ppermute | solution.py:72
  165.9 7.7 %collective-permute-start.55 = (bf16[4,64,128]{2,1,0:T(8,128)(2,1)S(1)}, bf16[4,64,128]{2,1,0:T(8,128)(2,1)S(1)}, u32[]{:S(2)}, u32[]{:S(2)}) collective-permute-start(bf16[4,64,128]{2,1,0:T(8,128)(2,1)S(1)} %get-tuple-element.142), channel_id=1, source_target_pairs={{0,28},{1,27},{2,30},{3,29},{4,24},{5,31},{6,26},{7,25},{8,17},{9,... | collective-permute-start | bytes 196616 | tf_op jit(solution)/shard_map/ppermute | solution.py:72
  174.3 8.1 %collective-permute-start.56 = (f32[4,64,128]{2,1,0:T(8,128)S(1)}, f32[4,64,128]{2,1,0:T(8,128)S(1)}, u32[]{:S(2)}, u32[]{:S(2)}) collective-permute-start(f32[4,64,128]{2,1,0:T(8,128)S(1)} %get-tuple-element.148), channel_id=1, source_target_pairs={{0,8},{8,0},{16,24},{24,16},{1,9},{9,1},{17,25},{25,17},{2,10},{10... | collective-permute-start | bytes 393224 | tf_op jit(solution)/shard_map/ppermute | solution.py:54
  178.3 7.6 %collective-permute-start.57 = (f32[4,64,128]{2,1,0:T(8,128)S(1)}, f32[4,64,128]{2,1,0:T(8,128)S(1)}, u32[]{:S(2)}, u32[]{:S(2)}) collective-permute-start(f32[4,64,128]{2,1,0:T(8,128)S(1)} %get-tuple-element.149), channel_id=1, source_target_pairs={{0,16},{8,24},{16,0},{24,8},{1,17},{9,25},{17,1},{25,9},{2,18},{10... | collective-permute-start | bytes 393224 | tf_op jit(solution)/shard_map/ppermute | solution.py:54
  179.4 6.6 %collective-permute-start.58 = (f32[4,64,128]{2,1,0:T(8,128)S(1)}, f32[4,64,128]{2,1,0:T(8,128)S(1)}, u32[]{:S(2)}, u32[]{:S(2)}) collective-permute-start(f32[4,64,128]{2,1,0:T(8,128)S(1)} %get-tuple-element.150), channel_id=1, source_target_pairs={{0,24},{8,16},{16,8},{24,0},{1,25},{9,17},{17,9},{25,1},{2,26},{10... | collective-permute-start | bytes 393224 | tf_op jit(solution)/shard_map/ppermute | solution.py:54
  (43 other events, 548.9 us)

commit v3 on v2

--- a/solution.py
+++ b/solution.py
@@ -13,7 +13,7 @@
 CORES = 2
 MIB = 1 << 20
 LARGE = 45
-LARGE_PREPARE = 57
+LARGE_PREPARE = 50
 
 
 SMEM = pl.BlockSpec(memory_space=pltpu.SMEM)
@@ -356,16 +356,8 @@
         [like((2, *piece), F32)] * quarters + [like((pair, *block_inverse.shape[1:]), HALF)] * quarters,
         [pltpu.VMEM(coef_now.shape, F32)] * 2 + [pltpu.SemaphoreType.DMA((2 + codes,))], limit=LARGE_PREPARE, far=3,
     )
-    block = like((chips * rows, dosage.shape[1]), HALF)
-    dosage = lax.optimization_barrier((prepared[0], dosage))[1]
-    kept_rows, given_rows = local(
-        load_body, [], [dosage], [block, block], [pltpu.SemaphoreType.DMA((owners,))], limit=LARGE, far=1
-    )
-    arrived, prepared, kept_rows, given_rows = lax.optimization_barrier(
-        (arrived, prepared, kept_rows, given_rows)
-    )
     states, chosen = prepared[:quarters], prepared[quarters:]
-    states = [states[0]] + [crossed(states[k], "samp", k) for k in ranks[1:]]
+    chosen = [chosen[0]] + [crossed(chosen[k], "samp", k) for k in ranks[1:-1]] + [chosen[-1]]
     penalty = penalty.reshape(1, 1, right_cols)
 
     for step in range(len(MOMENTA)):
@@ -376,8 +368,15 @@
         )
         pieces = [own] + [crossed(own, "samp", k) for k in ranks[1:]]
         if step == 0:
-            pieces, chosen = lax.optimization_barrier((pieces, chosen))
-            chosen = [chosen[0]] + [crossed(chosen[k], "samp", k) for k in ranks[1:]]
+            block = like((chips * rows, dosage.shape[1]), HALF)
+            dosage, chosen[-1] = lax.optimization_barrier((own, dosage, chosen[-1]))[1:]
+            kept_rows, given_rows = local(
+                load_body, [], [dosage], [block, block],
+                [pltpu.SemaphoreType.DMA((owners,))], limit=LARGE, far=1,
+            )
+            chosen[-1] = crossed(chosen[-1], "samp", quarters - 1)
+            pieces, kept_rows, given_rows, states = lax.optimization_barrier((pieces, kept_rows, given_rows, states))
+            states = [states[0]] + [crossed(states[k], "samp", k) for k in ranks[1:]]
         buffers = [pltpu.VMEM((dosage.shape[1], right_cols), HALF)]
         half = like((chips, rows, right_cols), F32)
         flops = dosage.shape[0] * dosage.shape[1] * right_cols

time: 188 us -> 190 us (1.011)
  waiting for transfers between devices: 80.3 us -> 82.2 us
    ppermute x4, waiting for transfers between devices: 0.01 us -> 6.25 us  [shifted(): lax.ppermute(block, axis, [((i - distance) % count, i) for i in range(cou...]
    ppermute x43, waiting for transfers between devices: 71.2 us -> 65.5 us  [crossed(): return lax.ppermute(block, axis, [(i, i ^ mask) for i in range(count)])]
  transfers between devices with their start and end apart: 59 -> 59, of which waited for: 32 -> 33; matrix products, arithmetic and copies ran while one was open for 2% -> 2% of each run, Pallas kernels for 8% -> 7%
where the time goes in v3:
time: 190 us
  waiting for transfers between devices  82.2 us (43%)
  starting transfers between devices  74.8 us (39%)
  Pallas kernels  25.8 us (14%)
  local copies, waits for them, and re-layouts  4.83 us (3%)
    ppermute x43, waiting for transfers between devices, crossed(): return lax.ppermute(block, axis, [(i, i ^ mask) for i in range(count)])  65.5 us
    ppermute x43, starting transfers between devices, crossed(): return lax.ppermute(block, axis, [(i, i ^ mask) for i in range(count)])  46 us
    pallas_call x16, Pallas kernels, local(): pl.pallas_call(body, in_specs=[SMEM] * len(scalars) + [FAR] * far + [VMEM...  23.2 us
    ppermute x8, starting transfers between devices, to_owners(): return lax.ppermute(block, ('samp', 'var'), route)  13.3 us
    ppermute x4, starting transfers between devices, shifted(): lax.ppermute(block, axis, [((i - distance) % count, i) for i in range(cou...  7.89 us
    ppermute x4, starting transfers between devices, to_variants(): return lax.ppermute(block, ('samp', 'var'), route)  7.64 us
    ppermute x4, waiting for transfers between devices, to_variants(): return lax.ppermute(block, ('samp', 'var'), route)  6.31 us
    ppermute x4, waiting for transfers between devices, shifted(): lax.ppermute(block, axis, [((i - distance) % count, i) for i in range(cou...  6.25 us
  transfers between devices with their start and end apart: 59, of which 33 were waited for; matrix products, arithmetic and copies ran while one was open for 2% of the time, Pallas kernels for 7%

profile of v3, /device:TPU:0, one launch (start us, length us, event | category | flops | bytes accessed | tf_op | source)
XLA Modules:
  0.0 189.5 jit_solution(11633595039818102049)
XLA Ops:
  0.6 2.6 %begin.1 = (s32[88]{0:T(128)}, bf16[4,64,128]{2,1,0:T(8,128)(2,1)}, bf16[4,64,128]{2,1,0:T(8,128)(2,1)}, bf16[4,64,128]{2,1,0:T(8,128)(2,1)}, bf16[4,64,128]{2,1,0:T(8,128)(2,1)}) custom-call(s32[64]{0:T(128)} %start.1, s32[64]{0:T(128)} %owner.1, f32[16,64,128]{2,1,0:T(8,128)} %now.3, f32[16,64,128]{2,1,0:T(8,128)} %before.3), custom_call_target="tpu_custom_call" | custom-call | tf_op jit(solution)/shard_map/begin/pallas_call | solution.py:343
  3.3 4.6 %collective-permute-start = (bf16[4,64,128]{2,1,0:T(8,128)(2,1)}, bf16[4,64,128]{2,1,0:T(8,128)(2,1)S(1)}, u32[]{:S(2)}, u32[]{:S(2)}) collective-permute-start(bf16[4,64,128]{2,1,0:T(8,128)(2,1)} %get-tuple-element.67), channel_id=1, source_target_pairs={{1,0},{2,1},{3,2},{4,3},{5,4},{6,5},{7,6},{0,7},{9,8},{10,9},{11,1... | collective-permute-start | bytes 196616 | tf_op jit(solution)/shard_map/ppermute | solution.py:49
  8.5 2.7 %collective-permute-start.3 = (bf16[4,64,128]{2,1,0:T(8,128)(2,1)}, bf16[4,64,128]{2,1,0:T(8,128)(2,1)S(1)}, u32[]{:S(2)}, u32[]{:S(2)}) collective-permute-start(bf16[4,64,128]{2,1,0:T(8,128)(2,1)} %get-tuple-element.70), channel_id=1, source_target_pairs={{4,0},{5,1},{6,2},{7,3},{0,4},{1,5},{2,6},{3,7},{12,8},{13,9},{14,... | collective-permute-start | bytes 196616 | tf_op jit(solution)/shard_map/ppermute | solution.py:49
  13.4 4.0 %collective-permute-done.3.refs_3_ = bf16[4,64,128]{2,1,0:T(8,128)(2,1)S(1)} collective-permute-done((bf16[4,64,128]{2,1,0:T(8,128)(2,1)}, bf16[4,64,128]{2,1,0:T(8,128)(2,1)S(1)}, u32[]{:S(2)}, u32[]{:S(2)}) %collective-permute-start.3) | collective-permute-done | bytes 65568 | tf_op jit(solution)/shard_map/ppermute | solution.py:49
  18.6 2.5 %collective-permute-start.6 = (bf16[8,64,128]{2,1,0:T(8,128)(2,1)S(1)}, bf16[8,64,128]{2,1,0:T(8,128)(2,1)S(1)}, u32[]{:S(2)}, u32[]{:S(2)}) collective-permute-start(bf16[8,64,128]{2,1,0:T(8,128)(2,1)S(1)} %shard_map.95.refs_0_), channel_id=1, source_target_pairs={{0,24},{8,16},{16,8},{24,0},{1,25},{9,17},{17,9},{25,1},{2,26},{10... | collective-permute-start | bytes 393224 | tf_op jit(solution)/shard_map/ppermute | solution.py:54
  23.8 4.4 %shard_map.96 = (f32[2,4,64,128]{3,2,1,0:T(8,128)S(1)}, f32[2,4,64,128]{3,2,1,0:T(8,128)S(1)}, f32[2,4,64,128]{3,2,1,0:T(8,128)S(1)}, f32[2,4,64,128]{3,2,1,0:T(...) custom-call(s32[88]{0:T(128)S(1)} %copy-done.6, ...), custom_call_target="tpu_custom_call" | custom-call | bytes 6291456 | tf_op jit(solution)/shard_map/pallas_call | solution.py:32
  28.2 3.5 %shard_map.97 = (bf16[1024,2048]{1,0:T(8,128)(2,1)S(1)}, bf16[1024,2048]{1,0:T(8,128)(2,1)S(1)}) custom-call(bf16[2048,2048]{1,0:T(8,128)(2,1)} %dosage), custom_call_target="tpu_custom_call" | custom-call | bytes 16777216 | tf_op jit(solution)/shard_map/pallas_call | solution.py:32
  39.5 2.5 %collective-permute-done.10 = bf16[256,128]{1,0:T(8,128)(2,1)S(1)} collective-permute-done((bf16[256,128]{1,0:T(8,128)(2,1)S(1)}, bf16[256,128]{1,0:T(8,128)(2,1)S(1)}, u32[]{:S(2)}, u32[]{:S(2)}) %collective-permute-start.10) | collective-permute-done | bytes 65568 | tf_op jit(solution)/shard_map/ppermute | solution.py:54
  42.0 2.7 %collective-permute-done.9 = bf16[256,128]{1,0:T(8,128)(2,1)S(1)} collective-permute-done((bf16[256,128]{1,0:T(8,128)(2,1)S(1)}, bf16[256,128]{1,0:T(8,128)(2,1)S(1)}, u32[]{:S(2)}, u32[]{:S(2)}) %collective-permute-start.9) | collective-permute-done | bytes 65568 | tf_op jit(solution)/shard_map/ppermute | solution.py:54
  46.6 2.6 %collective-permute-start.11 = (bf16[256,128]{1,0:T(8,128)(2,1)S(1)}, bf16[256,128]{1,0:T(8,128)(2,1)S(1)}, u32[]{:S(2)}, u32[]{:S(2)}) collective-permute-start(bf16[256,128]{1,0:T(8,128)(2,1)S(1)} %fusion.7.refs_2_), channel_id=1, source_target_pairs={{0,2},{1,3},{2,0},{3,1},{4,6},{5,7},{6,4},{7,5},{8,10},{9,11},{10,... | collective-permute-start | bytes 196616 | tf_op jit(solution)/shard_map/ppermute | solution.py:54
  61.6 19.8 %collective-permute-done.18.refs_1_ = bf16[8,64,128]{2,1,0:T(8,128)(2,1)S(1)} collective-permute-done((bf16[8,64,128]{2,1,0:T(8,128)(2,1)S(1)}, bf16[8,64,128]{2,1,0:T(8,128)(2,1)S(1)}, u32[]{:S(2)}, u32[]{:S(2)}) %collective-permute-start.18) | collective-permute-done | bytes 131104 | tf_op jit(solution)/shard_map/ppermute | solution.py:54
  81.4 2.5 %collective-permute-start.20 = (bf16[8,64,128]{2,1,0:T(8,128)(2,1)S(1)}, bf16[8,64,128]{2,1,0:T(8,128)(2,1)S(1)}, u32[]{:S(2)}, u32[]{:S(2)}) collective-permute-start(bf16[8,64,128]{2,1,0:T(8,128)(2,1)S(1)} %get-tuple-element.88), channel_id=1, source_target_pairs={{0,24},{8,16},{16,8},{24,0},{1,25},{9,17},{17,9},{25,1},{2,26},{10... | collective-permute-start | bytes 393224 | tf_op jit(solution)/shard_map/ppermute | solution.py:54
  84.3 2.9 %collective-permute-done.20.refs_3_ = bf16[8,64,128]{2,1,0:T(8,128)(2,1)S(1)} collective-permute-done((bf16[8,64,128]{2,1,0:T(8,128)(2,1)S(1)}, bf16[8,64,128]{2,1,0:T(8,128)(2,1)S(1)}, u32[]{:S(2)}, u32[]{:S(2)}) %collective-permute-start.20) | collective-permute-done | bytes 131104 | tf_op jit(solution)/shard_map/ppermute | solution.py:54
  87.3 2.5 %collective-permute-start.30 = (f32[2,4,64,128]{3,2,1,0:T(8,128)}, f32[2,4,64,128]{3,2,1,0:T(8,128)S(1)}, u32[]{:S(2)}, u32[]{:S(2)}) collective-permute-start(f32[2,4,64,128]{3,2,1,0:T(8,128)} %get-tuple-element.108), channel_id=1, source_target_pairs={{0,24},{8,16},{16,8},{24,0},{1,25},{9,17},{17,9},{25,1},{2,26},{10... | collective-permute-start | bytes 786440 | tf_op jit(solution)/shard_map/ppermute | solution.py:54
  91.0 7.2 %collective-permute-done.29.refs_10_ = f32[2,4,64,128]{3,2,1,0:T(8,128)S(1)} collective-permute-done((f32[2,4,64,128]{3,2,1,0:T(8,128)S(1)}, f32[2,4,64,128]{3,2,1,0:T(8,128)S(1)}, u32[]{:S(2)}, u32[]{:S(2)}) %collective-permute-start.29) | collective-permute-done | bytes 262176 | tf_op jit(solution)/shard_map/ppermute | solution.py:54
  98.8 2.1 %collective-permute-start.25 = (bf16[4,64,128]{2,1,0:T(8,128)(2,1)}, bf16[4,64,128]{2,1,0:T(8,128)(2,1)S(1)}, u32[]{:S(2)}, u32[]{:S(2)}) collective-permute-start(bf16[4,64,128]{2,1,0:T(8,128)(2,1)} %get-tuple-element.90), channel_id=1, source_target_pairs={{0,10},{1,13},{2,12},{3,15},{4,14},{5,9},{6,8},{7,11},{8,3},{9,2},... | collective-permute-start | bytes 196616 | tf_op jit(solution)/shard_map/ppermute | solution.py:72
  100.9 4.1 %collective-permute-start.27 = (bf16[4,64,128]{2,1,0:T(8,128)(2,1)S(1)}, bf16[4,64,128]{2,1,0:T(8,128)(2,1)S(1)}, u32[]{:S(2)}, u32[]{:S(2)}) collective-permute-start(bf16[4,64,128]{2,1,0:T(8,128)(2,1)S(1)} %get-tuple-element.92), channel_id=1, source_target_pairs={{0,28},{1,27},{2,30},{3,29},{4,24},{5,31},{6,26},{7,25},{8,17},{9,... | collective-permute-start | bytes 196616 | tf_op jit(solution)/shard_map/ppermute | solution.py:72
  109.4 2.3 %collective-permute-start.31 = (bf16[4,64,128]{2,1,0:T(8,128)(2,1)S(1)}, bf16[4,64,128]{2,1,0:T(8,128)(2,1)S(1)}, u32[]{:S(2)}, u32[]{:S(2)}) collective-permute-start(bf16[4,64,128]{2,1,0:T(8,128)(2,1)S(1)} %get-tuple-element.109), channel_id=1, source_target_pairs={{0,7},{1,6},{2,1},{3,0},{4,3},{5,2},{6,5},{7,4},{8,14},{9,13},{10,... | collective-permute-start | bytes 196616 | tf_op jit(solution)/shard_map/ppermute | solution.py:82
  117.7 5.7 %collective-permute-done.34.refs_3_ = bf16[4,64,128]{2,1,0:T(8,128)(2,1)S(1)} collective-permute-done((bf16[4,64,128]{2,1,0:T(8,128)(2,1)S(1)}, bf16[4,64,128]{2,1,0:T(8,128)(2,1)S(1)}, u32[]{:S(2)}, u32[]{:S(2)}) %collective-permute-start.34) | collective-permute-done | bytes 65568 | tf_op jit(solution)/shard_map/ppermute | solution.py:82
  127.6 3.5 %collective-permute-done.37.refs_3_ = bf16[8,64,128]{2,1,0:T(8,128)(2,1)S(1)} collective-permute-done((bf16[8,64,128]{2,1,0:T(8,128)(2,1)S(1)}, bf16[8,64,128]{2,1,0:T(8,128)(2,1)S(1)}, u32[]{:S(2)}, u32[]{:S(2)}) %collective-permute-start.37) | collective-permute-done | bytes 131104 | tf_op jit(solution)/shard_map/ppermute | solution.py:54
  140.4 2.4 %collective-permute-done.41 = bf16[256,128]{1,0:T(8,128)(2,1)S(1)} collective-permute-done((bf16[256,128]{1,0:T(8,128)(2,1)S(1)}, bf16[256,128]{1,0:T(8,128)(2,1)S(1)}, u32[]{:S(2)}, u32[]{:S(2)}) %collective-permute-start.41) | collective-permute-done | bytes 65568 | tf_op jit(solution)/shard_map/ppermute | solution.py:54
  142.9 2.8 %collective-permute-done.40 = bf16[256,128]{1,0:T(8,128)(2,1)S(1)} collective-permute-done((bf16[256,128]{1,0:T(8,128)(2,1)S(1)}, bf16[256,128]{1,0:T(8,128)(2,1)S(1)}, u32[]{:S(2)}, u32[]{:S(2)}) %collective-permute-start.40) | collective-permute-done | bytes 65568 | tf_op jit(solution)/shard_map/ppermute | solution.py:54
  145.7 2.0 %collective-permute-start.44 = (bf16[256,128]{1,0:T(8,128)(2,1)S(1)}, bf16[256,128]{1,0:T(8,128)(2,1)S(1)}, u32[]{:S(2)}, u32[]{:S(2)}) collective-permute-start(bf16[256,128]{1,0:T(8,128)(2,1)S(1)} %get-tuple-element.130.refs_2_), channel_id=1, source_target_pairs={{0,6},{1,7},{2,4},{3,5},{4,2},{5,3},{6,0},{7,1},{8,14},{9,15},{10,... | collective-permute-start | bytes 196616 | tf_op jit(solution)/shard_map/ppermute | solution.py:54
  147.8 2.4 %collective-permute-start.42 = (bf16[256,128]{1,0:T(8,128)(2,1)S(1)}, bf16[256,128]{1,0:T(8,128)(2,1)S(1)}, u32[]{:S(2)}, u32[]{:S(2)}) collective-permute-start(bf16[256,128]{1,0:T(8,128)(2,1)S(1)} %get-tuple-element.130.refs_2_), channel_id=1, source_target_pairs={{0,2},{1,3},{2,0},{3,1},{4,6},{5,7},{6,4},{7,5},{8,10},{9,11},{10,... | collective-permute-start | bytes 196616 | tf_op jit(solution)/shard_map/ppermute | solution.py:54
  160.4 2.9 %collective-permute-done.49.refs_1_ = bf16[8,64,128]{2,1,0:T(8,128)(2,1)S(1)} collective-permute-done((bf16[8,64,128]{2,1,0:T(8,128)(2,1)S(1)}, bf16[8,64,128]{2,1,0:T(8,128)(2,1)S(1)}, u32[]{:S(2)}, u32[]{:S(2)}) %collective-permute-start.49) | collective-permute-done | bytes 131104 | tf_op jit(solution)/shard_map/ppermute | solution.py:54
  163.5 2.2 %collective-permute-done.51.refs_3_ = bf16[8,64,128]{2,1,0:T(8,128)(2,1)S(1)} collective-permute-done((bf16[8,64,128]{2,1,0:T(8,128)(2,1)S(1)}, bf16[8,64,128]{2,1,0:T(8,128)(2,1)S(1)}, u32[]{:S(2)}, u32[]{:S(2)}) %collective-permute-start.51) | collective-permute-done | bytes 131104 | tf_op jit(solution)/shard_map/ppermute | solution.py:54
  166.4 2.3 %collective-permute-start.53 = (bf16[4,64,128]{2,1,0:T(8,128)(2,1)S(1)}, bf16[4,64,128]{2,1,0:T(8,128)(2,1)S(1)}, u32[]{:S(2)}, u32[]{:S(2)}) collective-permute-start(bf16[4,64,128]{2,1,0:T(8,128)(2,1)S(1)} %get-tuple-element.118), channel_id=1, source_target_pairs={{0,10},{1,13},{2,12},{3,15},{4,14},{5,9},{6,8},{7,11},{8,3},{9,2},... | collective-permute-start | bytes 196616 | tf_op jit(solution)/shard_map/ppermute | solution.py:72
  168.7 4.0 %collective-permute-start.55 = (bf16[4,64,128]{2,1,0:T(8,128)(2,1)S(1)}, bf16[4,64,128]{2,1,0:T(8,128)(2,1)S(1)}, u32[]{:S(2)}, u32[]{:S(2)}) collective-permute-start(bf16[4,64,128]{2,1,0:T(8,128)(2,1)S(1)} %get-tuple-element.120), channel_id=1, source_target_pairs={{0,28},{1,27},{2,30},{3,29},{4,24},{5,31},{6,26},{7,25},{8,17},{9,... | collective-permute-start | bytes 196616 | tf_op jit(solution)/shard_map/ppermute | solution.py:72
  172.9 3.4 %collective-permute-done.54.refs_6_ = bf16[4,64,128]{2,1,0:T(8,128)(2,1)S(1)} collective-permute-done((bf16[4,64,128]{2,1,0:T(8,128)(2,1)S(1)}, bf16[4,64,128]{2,1,0:T(8,128)(2,1)S(1)}, u32[]{:S(2)}, u32[]{:S(2)}) %collective-permute-start.54) | collective-permute-done | bytes 65568 | tf_op jit(solution)/shard_map/ppermute | solution.py:72
  177.5 3.1 %collective-permute-start.56 = (f32[4,64,128]{2,1,0:T(8,128)S(1)}, f32[4,64,128]{2,1,0:T(8,128)S(1)}, u32[]{:S(2)}, u32[]{:S(2)}) collective-permute-start(f32[4,64,128]{2,1,0:T(8,128)S(1)} %get-tuple-element.126), channel_id=1, source_target_pairs={{0,8},{8,0},{16,24},{24,16},{1,9},{9,1},{17,25},{25,17},{2,10},{10... | collective-permute-start | bytes 393224 | tf_op jit(solution)/shard_map/ppermute | solution.py:54
  182.7 2.1 %collective-permute-done.56.refs_1_ = f32[4,64,128]{2,1,0:T(8,128)S(1)} collective-permute-done((f32[4,64,128]{2,1,0:T(8,128)S(1)}, f32[4,64,128]{2,1,0:T(8,128)S(1)}, u32[]{:S(2)}, u32[]{:S(2)}) %collective-permute-start.56) | collective-permute-done | bytes 131104 | tf_op jit(solution)/shard_map/ppermute | solution.py:54
  184.9 3.2 %collective-permute-done.57.refs_2_ = f32[4,64,128]{2,1,0:T(8,128)S(1)} collective-permute-done((f32[4,64,128]{2,1,0:T(8,128)S(1)}, f32[4,64,128]{2,1,0:T(8,128)S(1)}, u32[]{:S(2)}, u32[]{:S(2)}) %collective-permute-start.57) | collective-permute-done | bytes 131104 | tf_op jit(solution)/shard_map/ppermute | solution.py:54
  (138 shorter events, 70.9 us)
Async XLA Ops:
  3.3 7.9 %collective-permute-start = (bf16[4,64,128]{2,1,0:T(8,128)(2,1)}, bf16[4,64,128]{2,1,0:T(8,128)(2,1)S(1)}, u32[]{:S(2)}, u32[]{:S(2)}) collective-permute-start(bf16[4,64,128]{2,1,0:T(8,128)(2,1)} %get-tuple-element.67), channel_id=1, source_target_pairs={{1,0},{2,1},{3,2},{4,3},{5,4},{6,5},{7,6},{0,7},{9,8},{10,9},{11,1... | collective-permute-start | bytes 196616 | tf_op jit(solution)/shard_map/ppermute | solution.py:49
  8.5 8.9 %collective-permute-start.3 = (bf16[4,64,128]{2,1,0:T(8,128)(2,1)}, bf16[4,64,128]{2,1,0:T(8,128)(2,1)S(1)}, u32[]{:S(2)}, u32[]{:S(2)}) collective-permute-start(bf16[4,64,128]{2,1,0:T(8,128)(2,1)} %get-tuple-element.70), channel_id=1, source_target_pairs={{4,0},{5,1},{6,2},{7,3},{0,4},{1,5},{2,6},{3,7},{12,8},{13,9},{14,... | collective-permute-start | bytes 196616 | tf_op jit(solution)/shard_map/ppermute | solution.py:49
  18.6 13.1 %collective-permute-start.6 = (bf16[8,64,128]{2,1,0:T(8,128)(2,1)S(1)}, bf16[8,64,128]{2,1,0:T(8,128)(2,1)S(1)}, u32[]{:S(2)}, u32[]{:S(2)}) collective-permute-start(bf16[8,64,128]{2,1,0:T(8,128)(2,1)S(1)} %shard_map.95.refs_0_), channel_id=1, source_target_pairs={{0,24},{8,16},{16,8},{24,0},{1,25},{9,17},{17,9},{25,1},{2,26},{10... | collective-permute-start | bytes 393224 | tf_op jit(solution)/shard_map/ppermute | solution.py:54
  21.1 10.6 %collective-permute-start.5 = (bf16[8,64,128]{2,1,0:T(8,128)(2,1)S(1)}, bf16[8,64,128]{2,1,0:T(8,128)(2,1)S(1)}, u32[]{:S(2)}, u32[]{:S(2)}) collective-permute-start(bf16[8,64,128]{2,1,0:T(8,128)(2,1)S(1)} %shard_map.95.refs_0_), channel_id=1, source_target_pairs={{0,16},{8,24},{16,0},{24,8},{1,17},{9,25},{17,1},{25,9},{2,18},{10... | collective-permute-start | bytes 393224 | tf_op jit(solution)/shard_map/ppermute | solution.py:54
  21.6 10.1 %collective-permute-start.4 = (bf16[8,64,128]{2,1,0:T(8,128)(2,1)S(1)}, bf16[8,64,128]{2,1,0:T(8,128)(2,1)S(1)}, u32[]{:S(2)}, u32[]{:S(2)}) collective-permute-start(bf16[8,64,128]{2,1,0:T(8,128)(2,1)S(1)} %shard_map.95.refs_0_), channel_id=1, source_target_pairs={{0,8},{8,0},{16,24},{24,16},{1,9},{9,1},{17,25},{25,17},{2,10},{10... | collective-permute-start | bytes 393224 | tf_op jit(solution)/shard_map/ppermute | solution.py:54
  35.2 6.8 %collective-permute-start.10 = (bf16[256,128]{1,0:T(8,128)(2,1)S(1)}, bf16[256,128]{1,0:T(8,128)(2,1)S(1)}, u32[]{:S(2)}, u32[]{:S(2)}) collective-permute-start(bf16[256,128]{1,0:T(8,128)(2,1)S(1)} %get-tuple-element.140), channel_id=1, source_target_pairs={{0,6},{1,7},{2,4},{3,5},{4,2},{5,3},{6,0},{7,1},{8,14},{9,15},{10,... | collective-permute-start | bytes 196616 | tf_op jit(solution)/shard_map/ppermute | solution.py:54
  37.0 7.7 %collective-permute-start.9 = (bf16[256,128]{1,0:T(8,128)(2,1)S(1)}, bf16[256,128]{1,0:T(8,128)(2,1)S(1)}, u32[]{:S(2)}, u32[]{:S(2)}) collective-permute-start(bf16[256,128]{1,0:T(8,128)(2,1)S(1)} %get-tuple-element.141), channel_id=1, source_target_pairs={{0,4},{1,5},{2,6},{3,7},{4,0},{5,1},{6,2},{7,3},{8,12},{9,13},{10,... | collective-permute-start | bytes 196616 | tf_op jit(solution)/shard_map/ppermute | solution.py:54
  49.2 10.8 %collective-permute-start.28 = (f32[2,4,64,128]{3,2,1,0:T(8,128)S(1)}, f32[2,4,64,128]{3,2,1,0:T(8,128)S(1)}, u32[]{:S(2)}, u32[]{:S(2)}) collective-permute-start(f32[2,4,64,128]{3,2,1,0:T(8,128)S(1)} %get-tuple-element.106), channel_id=1, source_target_pairs={{0,8},{8,0},{16,24},{24,16},{1,9},{9,1},{17,25},{25,17},{2,10},{10... | collective-permute-start | bytes 786440 | tf_op jit(solution)/shard_map/ppermute | solution.py:54
  53.4 45.4 %collective-permute-start.21 = (bf16[4,64,4,256]{3,2,1,0:T(4,128)(2,1)S(1)}, bf16[4,64,4,256]{3,2,1,0:T(4,128)(2,1)S(1)}, u32[]{:S(2)}, u32[]{:S(2)}) collective-permute-start(bf16[4,64,4,256]{3,2,1,0:T(4,128)(2,1)S(1)} %get-tuple-element.94), channel_id=1, source_target_pairs={{0,8},{8,0},{16,24},{24,16},{1,9},{9,1},{17,25},{25,17},{2,10},{10... | collective-permute-start | bytes 1572872 | tf_op jit(solution)/shard_map/ppermute | solution.py:54
  54.9 46.0 %collective-permute-start.22 = (bf16[4,64,4,256]{3,2,1,0:T(4,128)(2,1)S(1)}, bf16[4,64,4,256]{3,2,1,0:T(4,128)(2,1)S(1)}, u32[]{:S(2)}, u32[]{:S(2)}) collective-permute-start(bf16[4,64,4,256]{3,2,1,0:T(4,128)(2,1)S(1)} %get-tuple-element.95), channel_id=1, source_target_pairs={{0,16},{8,24},{16,0},{24,8},{1,17},{9,25},{17,1},{25,9},{2,18},{10... | collective-permute-start | bytes 1572872 | tf_op jit(solution)/shard_map/ppermute | solution.py:54
  56.4 44.5 %collective-permute-start.23 = (bf16[4,64,4,256]{3,2,1,0:T(4,128)(2,1)S(1)}, bf16[4,64,4,256]{3,2,1,0:T(4,128)(2,1)S(1)}, u32[]{:S(2)}, u32[]{:S(2)}) collective-permute-start(bf16[4,64,4,256]{3,2,1,0:T(4,128)(2,1)S(1)} %get-tuple-element.96), channel_id=1, source_target_pairs={{0,24},{8,16},{16,8},{24,0},{1,25},{9,17},{17,9},{25,1},{2,26},{10... | collective-permute-start | bytes 1572872 | tf_op jit(solution)/shard_map/ppermute | solution.py:54
  58.5 22.9 %collective-permute-start.18 = (bf16[8,64,128]{2,1,0:T(8,128)(2,1)S(1)}, bf16[8,64,128]{2,1,0:T(8,128)(2,1)S(1)}, u32[]{:S(2)}, u32[]{:S(2)}) collective-permute-start(bf16[8,64,128]{2,1,0:T(8,128)(2,1)S(1)} %get-tuple-element.86), channel_id=1, source_target_pairs={{0,8},{8,0},{16,24},{24,16},{1,9},{9,1},{17,25},{25,17},{2,10},{10... | collective-permute-start | bytes 393224 | tf_op jit(solution)/shard_map/ppermute | solution.py:54
  60.1 23.8 %collective-permute-start.19 = (bf16[8,64,128]{2,1,0:T(8,128)(2,1)S(1)}, bf16[8,64,128]{2,1,0:T(8,128)(2,1)S(1)}, u32[]{:S(2)}, u32[]{:S(2)}) collective-permute-start(bf16[8,64,128]{2,1,0:T(8,128)(2,1)S(1)} %get-tuple-element.87), channel_id=1, source_target_pairs={{0,16},{8,24},{16,0},{24,8},{1,17},{9,25},{17,1},{25,9},{2,18},{10... | collective-permute-start | bytes 393224 | tf_op jit(solution)/shard_map/ppermute | solution.py:54
  83.8 14.3 %collective-permute-start.29 = (f32[2,4,64,128]{3,2,1,0:T(8,128)S(1)}, f32[2,4,64,128]{3,2,1,0:T(8,128)S(1)}, u32[]{:S(2)}, u32[]{:S(2)}) collective-permute-start(f32[2,4,64,128]{3,2,1,0:T(8,128)S(1)} %get-tuple-element.107), channel_id=1, source_target_pairs={{0,16},{8,24},{16,0},{24,8},{1,17},{9,25},{17,1},{25,9},{2,18},{10... | collective-permute-start | bytes 786440 | tf_op jit(solution)/shard_map/ppermute | solution.py:54
  87.3 21.2 %collective-permute-start.30 = (f32[2,4,64,128]{3,2,1,0:T(8,128)}, f32[2,4,64,128]{3,2,1,0:T(8,128)S(1)}, u32[]{:S(2)}, u32[]{:S(2)}) collective-permute-start(f32[2,4,64,128]{3,2,1,0:T(8,128)} %get-tuple-element.108), channel_id=1, source_target_pairs={{0,24},{8,16},{16,8},{24,0},{1,25},{9,17},{17,9},{25,1},{2,26},{10... | collective-permute-start | bytes 786440 | tf_op jit(solution)/shard_map/ppermute | solution.py:54
  98.1 10.3 %collective-permute-start.24 = (bf16[4,64,128]{2,1,0:T(8,128)(2,1)}, bf16[4,64,128]{2,1,0:T(8,128)(2,1)S(1)}, u32[]{:S(2)}, u32[]{:S(2)}) collective-permute-start(bf16[4,64,128]{2,1,0:T(8,128)(2,1)} %get-tuple-element.89), channel_id=1, source_target_pairs={{0,3},{1,2},{2,5},{3,4},{4,7},{5,6},{6,1},{7,0},{8,10},{9,13},{10,... | collective-permute-start | bytes 196616 | tf_op jit(solution)/shard_map/ppermute | solution.py:72
  98.8 9.7 %collective-permute-start.25 = (bf16[4,64,128]{2,1,0:T(8,128)(2,1)}, bf16[4,64,128]{2,1,0:T(8,128)(2,1)S(1)}, u32[]{:S(2)}, u32[]{:S(2)}) collective-permute-start(bf16[4,64,128]{2,1,0:T(8,128)(2,1)} %get-tuple-element.90), channel_id=1, source_target_pairs={{0,10},{1,13},{2,12},{3,15},{4,14},{5,9},{6,8},{7,11},{8,3},{9,2},... | collective-permute-start | bytes 196616 | tf_op jit(solution)/shard_map/ppermute | solution.py:72
  100.9 7.6 %collective-permute-start.26 = (bf16[4,64,128]{2,1,0:T(8,128)(2,1)S(1)}, bf16[4,64,128]{2,1,0:T(8,128)(2,1)S(1)}, u32[]{:S(2)}, u32[]{:S(2)}) collective-permute-start(bf16[4,64,128]{2,1,0:T(8,128)(2,1)S(1)} %get-tuple-element.91), channel_id=1, source_target_pairs={{0,17},{1,20},{2,19},{3,22},{4,21},{5,16},{6,23},{7,18},{8,28},{9,... | collective-permute-start | bytes 196616 | tf_op jit(solution)/shard_map/ppermute | solution.py:72
  100.9 7.7 %collective-permute-start.27 = (bf16[4,64,128]{2,1,0:T(8,128)(2,1)S(1)}, bf16[4,64,128]{2,1,0:T(8,128)(2,1)S(1)}, u32[]{:S(2)}, u32[]{:S(2)}) collective-permute-start(bf16[4,64,128]{2,1,0:T(8,128)(2,1)S(1)} %get-tuple-element.92), channel_id=1, source_target_pairs={{0,28},{1,27},{2,30},{3,29},{4,24},{5,31},{6,26},{7,25},{8,17},{9,... | collective-permute-start | bytes 196616 | tf_op jit(solution)/shard_map/ppermute | solution.py:72
  109.4 7.6 %collective-permute-start.31 = (bf16[4,64,128]{2,1,0:T(8,128)(2,1)S(1)}, bf16[4,64,128]{2,1,0:T(8,128)(2,1)S(1)}, u32[]{:S(2)}, u32[]{:S(2)}) collective-permute-start(bf16[4,64,128]{2,1,0:T(8,128)(2,1)S(1)} %get-tuple-element.109), channel_id=1, source_target_pairs={{0,7},{1,6},{2,1},{3,0},{4,3},{5,2},{6,5},{7,4},{8,14},{9,13},{10,... | collective-permute-start | bytes 196616 | tf_op jit(solution)/shard_map/ppermute | solution.py:82
  115.1 8.3 %collective-permute-start.34 = (bf16[4,64,128]{2,1,0:T(8,128)(2,1)S(1)}, bf16[4,64,128]{2,1,0:T(8,128)(2,1)S(1)}, u32[]{:S(2)}, u32[]{:S(2)}) collective-permute-start(bf16[4,64,128]{2,1,0:T(8,128)(2,1)S(1)} %get-tuple-element.112), channel_id=1, source_target_pairs={{0,31},{1,30},{2,25},{3,24},{4,27},{5,26},{6,29},{7,28},{8,22},{9,... | collective-permute-start | bytes 196616 | tf_op jit(solution)/shard_map/ppermute | solution.py:82
  124.0 7.1 %collective-permute-start.37 = (bf16[8,64,128]{2,1,0:T(8,128)(2,1)S(1)}, bf16[8,64,128]{2,1,0:T(8,128)(2,1)S(1)}, u32[]{:S(2)}, u32[]{:S(2)}) collective-permute-start(bf16[8,64,128]{2,1,0:T(8,128)(2,1)S(1)} %shard_map.104.refs_0_), channel_id=1, source_target_pairs={{0,24},{8,16},{16,8},{24,0},{1,25},{9,17},{17,9},{25,1},{2,26},{10... | collective-permute-start | bytes 393224 | tf_op jit(solution)/shard_map/ppermute | solution.py:54
  124.1 7.0 %collective-permute-start.36 = (bf16[8,64,128]{2,1,0:T(8,128)(2,1)S(1)}, bf16[8,64,128]{2,1,0:T(8,128)(2,1)S(1)}, u32[]{:S(2)}, u32[]{:S(2)}) collective-permute-start(bf16[8,64,128]{2,1,0:T(8,128)(2,1)S(1)} %shard_map.104.refs_0_), channel_id=1, source_target_pairs={{0,16},{8,24},{16,0},{24,8},{1,17},{9,25},{17,1},{25,9},{2,18},{10... | collective-permute-start | bytes 393224 | tf_op jit(solution)/shard_map/ppermute | solution.py:54
  125.8 6.9 %collective-permute-start.35 = (bf16[8,64,128]{2,1,0:T(8,128)(2,1)S(1)}, bf16[8,64,128]{2,1,0:T(8,128)(2,1)S(1)}, u32[]{:S(2)}, u32[]{:S(2)}) collective-permute-start(bf16[8,64,128]{2,1,0:T(8,128)(2,1)S(1)} %shard_map.104.refs_0_), channel_id=1, source_target_pairs={{0,8},{8,0},{16,24},{24,16},{1,9},{9,1},{17,25},{25,17},{2,10},{10... | collective-permute-start | bytes 393224 | tf_op jit(solution)/shard_map/ppermute | solution.py:54
  136.2 6.7 %collective-permute-start.41 = (bf16[256,128]{1,0:T(8,128)(2,1)S(1)}, bf16[256,128]{1,0:T(8,128)(2,1)S(1)}, u32[]{:S(2)}, u32[]{:S(2)}) collective-permute-start(bf16[256,128]{1,0:T(8,128)(2,1)S(1)} %get-tuple-element.137), channel_id=1, source_target_pairs={{0,6},{1,7},{2,4},{3,5},{4,2},{5,3},{6,0},{7,1},{8,14},{9,15},{10,... | collective-permute-start | bytes 196616 | tf_op jit(solution)/shard_map/ppermute | solution.py:54
  138.2 7.5 %collective-permute-start.40 = (bf16[256,128]{1,0:T(8,128)(2,1)S(1)}, bf16[256,128]{1,0:T(8,128)(2,1)S(1)}, u32[]{:S(2)}, u32[]{:S(2)}) collective-permute-start(bf16[256,128]{1,0:T(8,128)(2,1)S(1)} %get-tuple-element.138), channel_id=1, source_target_pairs={{0,4},{1,5},{2,6},{3,7},{4,0},{5,1},{6,2},{7,3},{8,12},{9,13},{10,... | collective-permute-start | bytes 196616 | tf_op jit(solution)/shard_map/ppermute | solution.py:54
  158.5 7.1 %collective-permute-start.51 = (bf16[8,64,128]{2,1,0:T(8,128)(2,1)S(1)}, bf16[8,64,128]{2,1,0:T(8,128)(2,1)S(1)}, u32[]{:S(2)}, u32[]{:S(2)}) collective-permute-start(bf16[8,64,128]{2,1,0:T(8,128)(2,1)S(1)} %get-tuple-element.116), channel_id=1, source_target_pairs={{0,24},{8,16},{16,8},{24,0},{1,25},{9,17},{17,9},{25,1},{2,26},{10... | collective-permute-start | bytes 393224 | tf_op jit(solution)/shard_map/ppermute | solution.py:54
  168.7 7.6 %collective-permute-start.54 = (bf16[4,64,128]{2,1,0:T(8,128)(2,1)S(1)}, bf16[4,64,128]{2,1,0:T(8,128)(2,1)S(1)}, u32[]{:S(2)}, u32[]{:S(2)}) collective-permute-start(bf16[4,64,128]{2,1,0:T(8,128)(2,1)S(1)} %get-tuple-element.119), channel_id=1, source_target_pairs={{0,17},{1,20},{2,19},{3,22},{4,21},{5,16},{6,23},{7,18},{8,28},{9,... | collective-permute-start | bytes 196616 | tf_op jit(solution)/shard_map/ppermute | solution.py:72
  168.7 8.0 %collective-permute-start.55 = (bf16[4,64,128]{2,1,0:T(8,128)(2,1)S(1)}, bf16[4,64,128]{2,1,0:T(8,128)(2,1)S(1)}, u32[]{:S(2)}, u32[]{:S(2)}) collective-permute-start(bf16[4,64,128]{2,1,0:T(8,128)(2,1)S(1)} %get-tuple-element.120), channel_id=1, source_target_pairs={{0,28},{1,27},{2,30},{3,29},{4,24},{5,31},{6,26},{7,25},{8,17},{9,... | collective-permute-start | bytes 196616 | tf_op jit(solution)/shard_map/ppermute | solution.py:72
  177.5 7.4 %collective-permute-start.56 = (f32[4,64,128]{2,1,0:T(8,128)S(1)}, f32[4,64,128]{2,1,0:T(8,128)S(1)}, u32[]{:S(2)}, u32[]{:S(2)}) collective-permute-start(f32[4,64,128]{2,1,0:T(8,128)S(1)} %get-tuple-element.126), channel_id=1, source_target_pairs={{0,8},{8,0},{16,24},{24,16},{1,9},{9,1},{17,25},{25,17},{2,10},{10... | collective-permute-start | bytes 393224 | tf_op jit(solution)/shard_map/ppermute | solution.py:54
  180.5 7.6 %collective-permute-start.57 = (f32[4,64,128]{2,1,0:T(8,128)S(1)}, f32[4,64,128]{2,1,0:T(8,128)S(1)}, u32[]{:S(2)}, u32[]{:S(2)}) collective-permute-start(f32[4,64,128]{2,1,0:T(8,128)S(1)} %get-tuple-element.127), channel_id=1, source_target_pairs={{0,16},{8,24},{16,0},{24,8},{1,17},{9,25},{17,1},{25,9},{2,18},{10... | collective-permute-start | bytes 393224 | tf_op jit(solution)/shard_map/ppermute | solution.py:54
  181.4 6.7 %collective-permute-start.58 = (f32[4,64,128]{2,1,0:T(8,128)S(1)}, f32[4,64,128]{2,1,0:T(8,128)S(1)}, u32[]{:S(2)}, u32[]{:S(2)}) collective-permute-start(f32[4,64,128]{2,1,0:T(8,128)S(1)} %get-tuple-element.128), channel_id=1, source_target_pairs={{0,24},{8,16},{16,8},{24,0},{1,25},{9,17},{17,9},{25,1},{2,26},{10... | collective-permute-start | bytes 393224 | tf_op jit(solution)/shard_map/ppermute | solution.py:54
  (39 other events, 340.6 us)

commit v4 on v2

--- a/solution.py
+++ b/solution.py
@@ -13,7 +13,7 @@
 CORES = 2
 MIB = 1 << 20
 LARGE = 45
-LARGE_PREPARE = 57
+LARGE_CHOOSE = 57
 
 
 SMEM = pl.BlockSpec(memory_space=pltpu.SMEM)
@@ -154,32 +154,29 @@
         out[spot.unit + code] = jnp.int32(j)
 
 
-def prepare_body(spot, quarters, pair, table, now, before, inverses, *refs):
-    states, chosen = refs[:quarters], refs[quarters : 2 * quarters]
-    now_here, before_here, arrived = refs[2 * quarters :]
-    where = indices()
-    copies = [
-        pltpu.make_async_copy(now, now_here, arrived.at[0]),
-        pltpu.make_async_copy(before, before_here, arrived.at[1]),
-    ]
+def choose_body(spot, quarters, pair, table, inverses, *refs):
+    where = indices()
+    outs, arrived = refs[:quarters], refs[quarters]
+    copies = []
     for k in range(quarters):
         for p in range(pair):
             slot = table[spot.slot + held_by(where[1] ^ k, where[0]) * pair + p]
-            ready = arrived.at[2 + k * pair + p]
-            copies.append(pltpu.make_async_copy(inverses.at[slot], chosen[k].at[p], ready))
+            ready = arrived.at[k * pair + p]
+            copies.append(pltpu.make_async_copy(inverses.at[slot], outs[k].at[p], ready))
+            copies[-1].start()
     for copy in copies:
-        copy.start()
-    for copy in copies[:2]:
         copy.wait()
+
+
+def states_body(spot, quarters, pair, table, now, before, *outs):
+    where = indices()
     for k in range(quarters):
         for p in range(pair):
             code = held_by(where[1] ^ k, where[0]) * pair + p
             slot = table[spot.slot + code]
             live = table[spot.live + code] == 1
-            states[k][0, p] = jnp.where(live, now_here[slot], 0.0)
-            states[k][1, p] = jnp.where(live, before_here[slot], 0.0)
-    for copy in copies[2:]:
-        copy.wait()
+            outs[k][0, p] = jnp.where(live, now[slot], 0.0)
+            outs[k][1, p] = jnp.where(live, before[slot], 0.0)
 
 
 def panels_body(spot, quarters, pair, most, table, *refs):
@@ -350,22 +347,20 @@
         compiler_params=pltpu.CompilerParams(vmem_limit_bytes=60 * MIB),
     )(block_start, unit_owner, coef_now, coef_prev)
     arrived = [shifted(sent[g], "var", -g - 1) for g in range(reach)]
-    prepared = local(
-        functools.partial(prepare_body, spot, quarters, pair),
-        [table], [coef_now, coef_prev, block_inverse],
-        [like((2, *piece), F32)] * quarters + [like((pair, *block_inverse.shape[1:]), HALF)] * quarters,
-        [pltpu.VMEM(coef_now.shape, F32)] * 2 + [pltpu.SemaphoreType.DMA((2 + codes,))], limit=LARGE_PREPARE, far=3,
+    chosen = local(
+        functools.partial(choose_body, spot, quarters, pair),
+        [table], [block_inverse], [like((pair, *block_inverse.shape[1:]), HALF)] * quarters,
+        [pltpu.SemaphoreType.DMA((codes,))], limit=LARGE_CHOOSE, far=1,
     )
     block = like((chips * rows, dosage.shape[1]), HALF)
-    dosage = lax.optimization_barrier((prepared[0], dosage))[1]
+    dosage = lax.optimization_barrier((chosen[0], dosage))[1]
     kept_rows, given_rows = local(
         load_body, [], [dosage], [block, block], [pltpu.SemaphoreType.DMA((owners,))], limit=LARGE, far=1
     )
-    arrived, prepared, kept_rows, given_rows = lax.optimization_barrier(
-        (arrived, prepared, kept_rows, given_rows)
-    )
-    states, chosen = prepared[:quarters], prepared[quarters:]
-    states = [states[0]] + [crossed(states[k], "samp", k) for k in ranks[1:]]
+    arrived, chosen, kept_rows, given_rows = lax.optimization_barrier(
+        (arrived, chosen, kept_rows, given_rows)
+    )
+    chosen = [chosen[0]] + [crossed(chosen[k], "samp", k) for k in ranks[1:]]
     penalty = penalty.reshape(1, 1, right_cols)
 
     for step in range(len(MOMENTA)):
@@ -375,9 +370,6 @@
             [pltpu.VMEM((reach, *piece), HALF)],
         )
         pieces = [own] + [crossed(own, "samp", k) for k in ranks[1:]]
-        if step == 0:
-            pieces, chosen = lax.optimization_barrier((pieces, chosen))
-            chosen = [chosen[0]] + [crossed(chosen[k], "samp", k) for k in ranks[1:]]
         buffers = [pltpu.VMEM((dosage.shape[1], right_cols), HALF)]
         half = like((chips, rows, right_cols), F32)
         flops = dosage.shape[0] * dosage.shape[1] * right_cols
@@ -407,7 +399,15 @@
         )
         if step == len(MOMENTA) - 1:
             residual = lax.optimization_barrier((sums[0], total))[1] - traits
-        sums = [sums[0]] + [crossed(sums[k], "samp", k) for k in ranks[1:]]
+        summed = sums[0]
+        sums = [summed] + [crossed(sums[k], "samp", k) for k in ranks[1:]]
+        if step == 0:
+            held = lax.optimization_barrier((summed, coef_now, coef_prev))[1:]
+            states = local(
+                functools.partial(states_body, spot, quarters, pair),
+                [table], list(held), [like((2, *piece), F32)] * quarters,
+            )
+            states = [states[0]] + [crossed(states[k], "samp", k) for k in ranks[1:]]
         leaving = local(
             functools.partial(leave_body, spot, quarters, pair),
             [table], sums, [like(piece, HALF)] * quarters,

time: 188 us -> 173 us (0.920)
  waiting for transfers between devices: 80.3 us -> 69.4 us
  starting transfers between devices: 74.6 us -> 71.5 us
    ppermute x43, waiting for transfers between devices: 71.2 us -> 56.1 us  [crossed(): return lax.ppermute(block, axis, [(i, i ^ mask) for i in range(count)])]
    ppermute x8, waiting for transfers between devices: 2.68 us -> 7.46 us  [to_owners(): return lax.ppermute(block, ('samp', 'var'), route)]
    ppermute x43, starting transfers between devices: 45.9 us -> 43.6 us  [crossed(): return lax.ppermute(block, axis, [(i, i ^ mask) for i in range(count)])]
    pallas_call x16 -> x17, Pallas kernels: 24.4 us -> 24.8 us  [local(): pl.pallas_call(body, in_specs=[SMEM] * len(scalars) + [FAR] * far + [VMEM...]
  transfers between devices with their start and end apart: 59 -> 59, of which waited for: 32 -> 36; matrix products, arithmetic and copies ran while one was open for 2% -> 2% of each run, Pallas kernels for 8% -> 9%
where the time goes in v4:
time: 173 us
  starting transfers between devices  71.5 us (41%)
  waiting for transfers between devices  69.4 us (40%)
  Pallas kernels  27.4 us (16%)
  local copies, waits for them, and re-layouts  2.61 us (2%)
    ppermute x43, waiting for transfers between devices, crossed(): return lax.ppermute(block, axis, [(i, i ^ mask) for i in range(count)])  56.1 us
    ppermute x43, starting transfers between devices, crossed(): return lax.ppermute(block, axis, [(i, i ^ mask) for i in range(count)])  43.6 us
    pallas_call x17, Pallas kernels, local(): pl.pallas_call(body, in_specs=[SMEM] * len(scalars) + [FAR] * far + [VMEM...  24.8 us
    ppermute x8, starting transfers between devices, to_owners(): return lax.ppermute(block, ('samp', 'var'), route)  12.3 us
    ppermute x4, starting transfers between devices, shifted(): lax.ppermute(block, axis, [((i - distance) % count, i) for i in range(cou...  7.89 us
    ppermute x4, starting transfers between devices, to_variants(): return lax.ppermute(block, ('samp', 'var'), route)  7.68 us
    ppermute x8, waiting for transfers between devices, to_owners(): return lax.ppermute(block, ('samp', 'var'), route)  7.46 us
    ppermute x4, waiting for transfers between devices, to_variants(): return lax.ppermute(block, ('samp', 'var'), route)  5.79 us
  transfers between devices with their start and end apart: 59, of which 36 were waited for; matrix products, arithmetic and copies ran while one was open for 2% of the time, Pallas kernels for 9%

profile of v4, /device:TPU:0, one launch (start us, length us, event | category | flops | bytes accessed | tf_op | source)
XLA Modules:
  0.0 172.9 jit_solution(4111952607761368945)
XLA Ops:
  0.6 2.6 %begin.1 = (s32[88]{0:T(128)}, bf16[4,64,128]{2,1,0:T(8,128)(2,1)}, bf16[4,64,128]{2,1,0:T(8,128)(2,1)}, bf16[4,64,128]{2,1,0:T(8,128)(2,1)}, bf16[4,64,128]{2,1,0:T(8,128)(2,1)}) custom-call(s32[64]{0:T(128)} %start.1, s32[64]{0:T(128)} %owner.1, f32[16,64,128]{2,1,0:T(8,128)} %now.2, f32[16,64,128]{2,1,0:T(8,128)} %before.2), custom_call_target="tpu_custom_call" | custom-call | tf_op jit(solution)/shard_map/begin/pallas_call | solution.py:340
  3.3 4.6 %collective-permute-start = (bf16[4,64,128]{2,1,0:T(8,128)(2,1)}, bf16[4,64,128]{2,1,0:T(8,128)(2,1)S(1)}, u32[]{:S(2)}, u32[]{:S(2)}) collective-permute-start(bf16[4,64,128]{2,1,0:T(8,128)(2,1)} %get-tuple-element.68), channel_id=1, source_target_pairs={{1,0},{2,1},{3,2},{4,3},{5,4},{6,5},{7,6},{0,7},{9,8},{10,9},{11,1... | collective-permute-start | bytes 196616 | tf_op jit(solution)/shard_map/ppermute | solution.py:49
  8.5 2.7 %collective-permute-start.3 = (bf16[4,64,128]{2,1,0:T(8,128)(2,1)}, bf16[4,64,128]{2,1,0:T(8,128)(2,1)S(1)}, u32[]{:S(2)}, u32[]{:S(2)}) collective-permute-start(bf16[4,64,128]{2,1,0:T(8,128)(2,1)} %get-tuple-element.71), channel_id=1, source_target_pairs={{4,0},{5,1},{6,2},{7,3},{0,4},{1,5},{2,6},{3,7},{12,8},{13,9},{14,... | collective-permute-start | bytes 196616 | tf_op jit(solution)/shard_map/ppermute | solution.py:49
  11.2 5.0 %shard_map.95 = (bf16[4,64,4,256]{3,2,1,0:T(4,128)(2,1)}, bf16[4,64,4,256]{3,2,1,0:T(4,128)(2,1)}, bf16[4,64,4,256]{3,2,1,0:T(4,128)(2,1)}, bf16[4,64,4,256]{3,2,1,0:T(4,128)(2,1)}) custom-call(s32[88]{0:T(128)} %get-tuple-element.67.table, bf16[16,64,4,256]{3,2,1,0:T(4,128)(2,1)} %inverses.1), custom_call_target="tpu_custom_call" | custom-call | bytes 4194304 | tf_op jit(solution)/shard_map/pallas_call | solution.py:32
  16.2 3.5 %shard_map.96 = (bf16[1024,2048]{1,0:T(8,128)(2,1)S(1)}, bf16[1024,2048]{1,0:T(8,128)(2,1)S(1)}) custom-call(bf16[2048,2048]{1,0:T(8,128)(2,1)} %dosage), custom_call_target="tpu_custom_call" | custom-call | bytes 16777216 | tf_op jit(solution)/shard_map/pallas_call | solution.py:32
  20.4 2.5 %collective-permute-start.6 = (bf16[8,64,128]{2,1,0:T(8,128)(2,1)S(1)}, bf16[8,64,128]{2,1,0:T(8,128)(2,1)S(1)}, u32[]{:S(2)}, u32[]{:S(2)}) collective-permute-start(bf16[8,64,128]{2,1,0:T(8,128)(2,1)S(1)} %shard_map.97.refs_0_), channel_id=1, source_target_pairs={{0,24},{8,16},{16,8},{24,0},{1,25},{9,17},{17,9},{25,1},{2,26},{10... | collective-permute-start | bytes 393224 | tf_op jit(solution)/shard_map/ppermute | solution.py:54
  23.9 3.1 %collective-permute-done.6.refs_3_ = bf16[8,64,128]{2,1,0:T(8,128)(2,1)S(1)} collective-permute-done((bf16[8,64,128]{2,1,0:T(8,128)(2,1)S(1)}, bf16[8,64,128]{2,1,0:T(8,128)(2,1)S(1)}, u32[]{:S(2)}, u32[]{:S(2)}) %collective-permute-start.6) | collective-permute-done | bytes 131104 | tf_op jit(solution)/shard_map/ppermute | solution.py:54
  32.4 2.0 %collective-permute-start.10 = (bf16[256,128]{1,0:T(8,128)(2,1)S(1)}, bf16[256,128]{1,0:T(8,128)(2,1)S(1)}, u32[]{:S(2)}, u32[]{:S(2)}) collective-permute-start(bf16[256,128]{1,0:T(8,128)(2,1)S(1)} %get-tuple-element.142), channel_id=1, source_target_pairs={{0,6},{1,7},{2,4},{3,5},{4,2},{5,3},{6,0},{7,1},{8,14},{9,15},{10,... | collective-permute-start | bytes 196616 | tf_op jit(solution)/shard_map/ppermute | solution.py:54
  39.2 2.7 %collective-permute-done.9 = bf16[256,128]{1,0:T(8,128)(2,1)S(1)} collective-permute-done((bf16[256,128]{1,0:T(8,128)(2,1)S(1)}, bf16[256,128]{1,0:T(8,128)(2,1)S(1)}, u32[]{:S(2)}, u32[]{:S(2)}) %collective-permute-start.9) | collective-permute-done | bytes 65568 | tf_op jit(solution)/shard_map/ppermute | solution.py:54
  46.8 2.2 %collective-permute-done.13.refs_5_ = bf16[256,128]{1,0:T(8,128)(2,1)S(1)} collective-permute-done((bf16[256,128]{1,0:T(8,128)(2,1)S(1)}, bf16[256,128]{1,0:T(8,128)(2,1)S(1)}, u32[]{:S(2)}, u32[]{:S(2)}) %collective-permute-start.13) | collective-permute-done | bytes 65568 | tf_op jit(solution)/shard_map/ppermute | solution.py:54
  51.2 2.0 %collective-permute-done.11.refs_3_ = bf16[256,128]{1,0:T(8,128)(2,1)S(1)} collective-permute-done((bf16[256,128]{1,0:T(8,128)(2,1)S(1)}, bf16[256,128]{1,0:T(8,128)(2,1)S(1)}, u32[]{:S(2)}, u32[]{:S(2)}) %collective-permute-start.11) | collective-permute-done | bytes 65568 | tf_op jit(solution)/shard_map/ppermute | solution.py:54
  61.3 2.7 %collective-permute-done.18.refs_1_ = bf16[8,64,128]{2,1,0:T(8,128)(2,1)S(1)} collective-permute-done((bf16[8,64,128]{2,1,0:T(8,128)(2,1)S(1)}, bf16[8,64,128]{2,1,0:T(8,128)(2,1)S(1)}, u32[]{:S(2)}, u32[]{:S(2)}) %collective-permute-start.18) | collective-permute-done | bytes 131104 | tf_op jit(solution)/shard_map/ppermute | solution.py:54
  65.5 9.1 %collective-permute-done.19.refs_2_ = bf16[8,64,128]{2,1,0:T(8,128)(2,1)S(1)} collective-permute-done((bf16[8,64,128]{2,1,0:T(8,128)(2,1)S(1)}, bf16[8,64,128]{2,1,0:T(8,128)(2,1)S(1)}, u32[]{:S(2)}, u32[]{:S(2)}) %collective-permute-start.19) | collective-permute-done | bytes 131104 | tf_op jit(solution)/shard_map/ppermute | solution.py:54
  78.9 2.7 %collective-permute-start.25 = (bf16[4,64,128]{2,1,0:T(8,128)(2,1)S(1)}, bf16[4,64,128]{2,1,0:T(8,128)(2,1)S(1)}, u32[]{:S(2)}, u32[]{:S(2)}) collective-permute-start(bf16[4,64,128]{2,1,0:T(8,128)(2,1)S(1)} %get-tuple-element.90), channel_id=1, source_target_pairs={{0,10},{1,13},{2,12},{3,15},{4,14},{5,9},{6,8},{7,11},{8,3},{9,2},... | collective-permute-start | bytes 196616 | tf_op jit(solution)/shard_map/ppermute | solution.py:72
  81.5 2.3 %collective-permute-done.24.refs_4_ = bf16[4,64,128]{2,1,0:T(8,128)(2,1)S(1)} collective-permute-done((bf16[4,64,128]{2,1,0:T(8,128)(2,1)S(1)}, bf16[4,64,128]{2,1,0:T(8,128)(2,1)S(1)}, u32[]{:S(2)}, u32[]{:S(2)}) %collective-permute-start.24) | collective-permute-done | bytes 65568 | tf_op jit(solution)/shard_map/ppermute | solution.py:72
  85.2 3.0 %collective-permute-start.27 = (bf16[4,64,128]{2,1,0:T(8,128)(2,1)S(1)}, bf16[4,64,128]{2,1,0:T(8,128)(2,1)S(1)}, u32[]{:S(2)}, u32[]{:S(2)}) collective-permute-start(bf16[4,64,128]{2,1,0:T(8,128)(2,1)S(1)} %get-tuple-element.92), channel_id=1, source_target_pairs={{0,28},{1,27},{2,30},{3,29},{4,24},{5,31},{6,26},{7,25},{8,17},{9,... | collective-permute-start | bytes 196616 | tf_op jit(solution)/shard_map/ppermute | solution.py:72
  94.0 2.0 %collective-permute-start.32 = (bf16[4,64,128]{2,1,0:T(8,128)(2,1)S(1)}, bf16[4,64,128]{2,1,0:T(8,128)(2,1)S(1)}, u32[]{:S(2)}, u32[]{:S(2)}) collective-permute-start(bf16[4,64,128]{2,1,0:T(8,128)(2,1)S(1)} %get-tuple-element.112), channel_id=1, source_target_pairs={{0,15},{1,14},{2,9},{3,8},{4,11},{5,10},{6,13},{7,12},{8,6},{9,5},... | collective-permute-start | bytes 196616 | tf_op jit(solution)/shard_map/ppermute | solution.py:82
  95.9 2.6 %collective-permute-start.33 = (bf16[4,64,128]{2,1,0:T(8,128)(2,1)S(1)}, bf16[4,64,128]{2,1,0:T(8,128)(2,1)S(1)}, u32[]{:S(2)}, u32[]{:S(2)}) collective-permute-start(bf16[4,64,128]{2,1,0:T(8,128)(2,1)S(1)} %get-tuple-element.113), channel_id=1, source_target_pairs={{0,23},{1,22},{2,17},{3,16},{4,19},{5,18},{6,21},{7,20},{8,30},{9,... | collective-permute-start | bytes 196616 | tf_op jit(solution)/shard_map/ppermute | solution.py:82
  98.5 2.5 %collective-permute-start.34 = (bf16[4,64,128]{2,1,0:T(8,128)(2,1)S(1)}, bf16[4,64,128]{2,1,0:T(8,128)(2,1)S(1)}, u32[]{:S(2)}, u32[]{:S(2)}) collective-permute-start(bf16[4,64,128]{2,1,0:T(8,128)(2,1)S(1)} %get-tuple-element.114), channel_id=1, source_target_pairs={{0,31},{1,30},{2,25},{3,24},{4,27},{5,26},{6,29},{7,28},{8,22},{9,... | collective-permute-start | bytes 196616 | tf_op jit(solution)/shard_map/ppermute | solution.py:82
  102.0 4.8 %collective-permute-done.34.refs_3_ = bf16[4,64,128]{2,1,0:T(8,128)(2,1)S(1)} collective-permute-done((bf16[4,64,128]{2,1,0:T(8,128)(2,1)S(1)}, bf16[4,64,128]{2,1,0:T(8,128)(2,1)S(1)}, u32[]{:S(2)}, u32[]{:S(2)}) %collective-permute-start.34) | collective-permute-done | bytes 65568 | tf_op jit(solution)/shard_map/ppermute | solution.py:82
  108.9 2.1 %collective-permute-start.35 = (bf16[8,64,128]{2,1,0:T(8,128)(2,1)S(1)}, bf16[8,64,128]{2,1,0:T(8,128)(2,1)S(1)}, u32[]{:S(2)}, u32[]{:S(2)}) collective-permute-start(bf16[8,64,128]{2,1,0:T(8,128)(2,1)S(1)} %shard_map.105.refs_0_), channel_id=1, source_target_pairs={{0,8},{8,0},{16,24},{24,16},{1,9},{9,1},{17,25},{25,17},{2,10},{10... | collective-permute-start | bytes 393224 | tf_op jit(solution)/shard_map/ppermute | solution.py:54
  111.0 2.8 %collective-permute-done.37.refs_3_ = bf16[8,64,128]{2,1,0:T(8,128)(2,1)S(1)} collective-permute-done((bf16[8,64,128]{2,1,0:T(8,128)(2,1)S(1)}, bf16[8,64,128]{2,1,0:T(8,128)(2,1)S(1)}, u32[]{:S(2)}, u32[]{:S(2)}) %collective-permute-start.37) | collective-permute-done | bytes 131104 | tf_op jit(solution)/shard_map/ppermute | solution.py:54
  123.1 2.7 %collective-permute-done.41 = bf16[256,128]{1,0:T(8,128)(2,1)S(1)} collective-permute-done((bf16[256,128]{1,0:T(8,128)(2,1)S(1)}, bf16[256,128]{1,0:T(8,128)(2,1)S(1)}, u32[]{:S(2)}, u32[]{:S(2)}) %collective-permute-start.41) | collective-permute-done | bytes 65568 | tf_op jit(solution)/shard_map/ppermute | solution.py:54
  125.8 2.6 %collective-permute-done.40 = bf16[256,128]{1,0:T(8,128)(2,1)S(1)} collective-permute-done((bf16[256,128]{1,0:T(8,128)(2,1)S(1)}, bf16[256,128]{1,0:T(8,128)(2,1)S(1)}, u32[]{:S(2)}, u32[]{:S(2)}) %collective-permute-start.40) | collective-permute-done | bytes 65568 | tf_op jit(solution)/shard_map/ppermute | solution.py:54
  128.5 1.9 %collective-permute-start.44 = (bf16[256,128]{1,0:T(8,128)(2,1)S(1)}, bf16[256,128]{1,0:T(8,128)(2,1)S(1)}, u32[]{:S(2)}, u32[]{:S(2)}) collective-permute-start(bf16[256,128]{1,0:T(8,128)(2,1)S(1)} %get-tuple-element.132.refs_2_), channel_id=1, source_target_pairs={{0,6},{1,7},{2,4},{3,5},{4,2},{5,3},{6,0},{7,1},{8,14},{9,15},{10,... | collective-permute-start | bytes 196616 | tf_op jit(solution)/shard_map/ppermute | solution.py:54
  130.4 2.5 %collective-permute-start.42 = (bf16[256,128]{1,0:T(8,128)(2,1)S(1)}, bf16[256,128]{1,0:T(8,128)(2,1)S(1)}, u32[]{:S(2)}, u32[]{:S(2)}) collective-permute-start(bf16[256,128]{1,0:T(8,128)(2,1)S(1)} %get-tuple-element.132.refs_2_), channel_id=1, source_target_pairs={{0,2},{1,3},{2,0},{3,1},{4,6},{5,7},{6,4},{7,5},{8,10},{9,11},{10,... | collective-permute-start | bytes 196616 | tf_op jit(solution)/shard_map/ppermute | solution.py:54
  133.0 2.0 %collective-permute-done.44.refs_5_ = bf16[256,128]{1,0:T(8,128)(2,1)S(1)} collective-permute-done((bf16[256,128]{1,0:T(8,128)(2,1)S(1)}, bf16[256,128]{1,0:T(8,128)(2,1)S(1)}, u32[]{:S(2)}, u32[]{:S(2)}) %collective-permute-start.44) | collective-permute-done | bytes 65568 | tf_op jit(solution)/shard_map/ppermute | solution.py:54
  143.2 2.7 %collective-permute-done.49.refs_1_ = bf16[8,64,128]{2,1,0:T(8,128)(2,1)S(1)} collective-permute-done((bf16[8,64,128]{2,1,0:T(8,128)(2,1)S(1)}, bf16[8,64,128]{2,1,0:T(8,128)(2,1)S(1)}, u32[]{:S(2)}, u32[]{:S(2)}) %collective-permute-start.49) | collective-permute-done | bytes 131104 | tf_op jit(solution)/shard_map/ppermute | solution.py:54
  145.9 3.5 %collective-permute-done.50.refs_2_ = bf16[8,64,128]{2,1,0:T(8,128)(2,1)S(1)} collective-permute-done((bf16[8,64,128]{2,1,0:T(8,128)(2,1)S(1)}, bf16[8,64,128]{2,1,0:T(8,128)(2,1)S(1)}, u32[]{:S(2)}, u32[]{:S(2)}) %collective-permute-start.50) | collective-permute-done | bytes 131104 | tf_op jit(solution)/shard_map/ppermute | solution.py:54
  151.5 4.7 %collective-permute-start.55 = (bf16[4,64,128]{2,1,0:T(8,128)(2,1)S(1)}, bf16[4,64,128]{2,1,0:T(8,128)(2,1)S(1)}, u32[]{:S(2)}, u32[]{:S(2)}) collective-permute-start(bf16[4,64,128]{2,1,0:T(8,128)(2,1)S(1)} %get-tuple-element.122), channel_id=1, source_target_pairs={{0,28},{1,27},{2,30},{3,29},{4,24},{5,31},{6,26},{7,25},{8,17},{9,... | collective-permute-start | bytes 196616 | tf_op jit(solution)/shard_map/ppermute | solution.py:72
  159.9 3.9 %collective-permute-start.56 = (f32[4,64,128]{2,1,0:T(8,128)S(1)}, f32[4,64,128]{2,1,0:T(8,128)S(1)}, u32[]{:S(2)}, u32[]{:S(2)}) collective-permute-start(f32[4,64,128]{2,1,0:T(8,128)S(1)} %get-tuple-element.128), channel_id=1, source_target_pairs={{0,8},{8,0},{16,24},{24,16},{1,9},{9,1},{17,25},{25,17},{2,10},{10... | collective-permute-start | bytes 393224 | tf_op jit(solution)/shard_map/ppermute | solution.py:54
  167.7 3.8 %collective-permute-done.57.refs_2_ = f32[4,64,128]{2,1,0:T(8,128)S(1)} collective-permute-done((f32[4,64,128]{2,1,0:T(8,128)S(1)}, f32[4,64,128]{2,1,0:T(8,128)S(1)}, u32[]{:S(2)}, u32[]{:S(2)}) %collective-permute-start.57) | collective-permute-done | bytes 131104 | tf_op jit(solution)/shard_map/ppermute | solution.py:54
  (145 shorter events, 71.8 us)
Async XLA Ops:
  3.3 16.4 %collective-permute-start = (bf16[4,64,128]{2,1,0:T(8,128)(2,1)}, bf16[4,64,128]{2,1,0:T(8,128)(2,1)S(1)}, u32[]{:S(2)}, u32[]{:S(2)}) collective-permute-start(bf16[4,64,128]{2,1,0:T(8,128)(2,1)} %get-tuple-element.68), channel_id=1, source_target_pairs={{1,0},{2,1},{3,2},{4,3},{5,4},{6,5},{7,6},{0,7},{9,8},{10,9},{11,1... | collective-permute-start | bytes 196616 | tf_op jit(solution)/shard_map/ppermute | solution.py:49
  7.9 11.9 %collective-permute-start.1 = (bf16[4,64,128]{2,1,0:T(8,128)(2,1)}, bf16[4,64,128]{2,1,0:T(8,128)(2,1)S(1)}, u32[]{:S(2)}, u32[]{:S(2)}) collective-permute-start(bf16[4,64,128]{2,1,0:T(8,128)(2,1)} %get-tuple-element.69), channel_id=1, source_target_pairs={{2,0},{3,1},{4,2},{5,3},{6,4},{7,5},{0,6},{1,7},{10,8},{11,9},{12,... | collective-permute-start | bytes 196616 | tf_op jit(solution)/shard_map/ppermute | solution.py:49
  8.5 11.3 %collective-permute-start.2 = (bf16[4,64,128]{2,1,0:T(8,128)(2,1)}, bf16[4,64,128]{2,1,0:T(8,128)(2,1)S(1)}, u32[]{:S(2)}, u32[]{:S(2)}) collective-permute-start(bf16[4,64,128]{2,1,0:T(8,128)(2,1)} %get-tuple-element.70), channel_id=1, source_target_pairs={{3,0},{4,1},{5,2},{6,3},{7,4},{0,5},{1,6},{2,7},{11,8},{12,9},{13,... | collective-permute-start | bytes 196616 | tf_op jit(solution)/shard_map/ppermute | solution.py:49
  8.5 11.3 %collective-permute-start.3 = (bf16[4,64,128]{2,1,0:T(8,128)(2,1)}, bf16[4,64,128]{2,1,0:T(8,128)(2,1)S(1)}, u32[]{:S(2)}, u32[]{:S(2)}) collective-permute-start(bf16[4,64,128]{2,1,0:T(8,128)(2,1)} %get-tuple-element.71), channel_id=1, source_target_pairs={{4,0},{5,1},{6,2},{7,3},{0,4},{1,5},{2,6},{3,7},{12,8},{13,9},{14,... | collective-permute-start | bytes 196616 | tf_op jit(solution)/shard_map/ppermute | solution.py:49
  20.4 6.6 %collective-permute-start.6 = (bf16[8,64,128]{2,1,0:T(8,128)(2,1)S(1)}, bf16[8,64,128]{2,1,0:T(8,128)(2,1)S(1)}, u32[]{:S(2)}, u32[]{:S(2)}) collective-permute-start(bf16[8,64,128]{2,1,0:T(8,128)(2,1)S(1)} %shard_map.97.refs_0_), channel_id=1, source_target_pairs={{0,24},{8,16},{16,8},{24,0},{1,25},{9,17},{17,9},{25,1},{2,26},{10... | collective-permute-start | bytes 393224 | tf_op jit(solution)/shard_map/ppermute | solution.py:54
  32.4 6.8 %collective-permute-start.10 = (bf16[256,128]{1,0:T(8,128)(2,1)S(1)}, bf16[256,128]{1,0:T(8,128)(2,1)S(1)}, u32[]{:S(2)}, u32[]{:S(2)}) collective-permute-start(bf16[256,128]{1,0:T(8,128)(2,1)S(1)} %get-tuple-element.142), channel_id=1, source_target_pairs={{0,6},{1,7},{2,4},{3,5},{4,2},{5,3},{6,0},{7,1},{8,14},{9,15},{10,... | collective-permute-start | bytes 196616 | tf_op jit(solution)/shard_map/ppermute | solution.py:54
  34.4 7.5 %collective-permute-start.9 = (bf16[256,128]{1,0:T(8,128)(2,1)S(1)}, bf16[256,128]{1,0:T(8,128)(2,1)S(1)}, u32[]{:S(2)}, u32[]{:S(2)}) collective-permute-start(bf16[256,128]{1,0:T(8,128)(2,1)S(1)} %get-tuple-element.143), channel_id=1, source_target_pairs={{0,4},{1,5},{2,6},{3,7},{4,0},{5,1},{6,2},{7,3},{8,12},{9,13},{10,... | collective-permute-start | bytes 196616 | tf_op jit(solution)/shard_map/ppermute | solution.py:54
  35.8 22.7 %collective-permute-start.21 = (bf16[4,64,4,256]{3,2,1,0:T(4,128)(2,1)S(1)}, bf16[4,64,4,256]{3,2,1,0:T(4,128)(2,1)S(1)}, u32[]{:S(2)}, u32[]{:S(2)}) collective-permute-start(bf16[4,64,4,256]{3,2,1,0:T(4,128)(2,1)S(1)} %copy-done.14), channel_id=1, source_target_pairs={{0,8},{8,0},{16,24},{24,16},{1,9},{9,1},{17,25},{25,17},{2,10},{10... | collective-permute-start | bytes 1572872 | tf_op jit(solution)/shard_map/ppermute | solution.py:54
  42.0 6.9 %collective-permute-start.13 = (bf16[256,128]{1,0:T(8,128)(2,1)S(1)}, bf16[256,128]{1,0:T(8,128)(2,1)S(1)}, u32[]{:S(2)}, u32[]{:S(2)}) collective-permute-start(bf16[256,128]{1,0:T(8,128)(2,1)S(1)} %fusion.7.refs_2_), channel_id=1, source_target_pairs={{0,6},{1,7},{2,4},{3,5},{4,2},{5,3},{6,0},{7,1},{8,14},{9,15},{10,... | collective-permute-start | bytes 196616 | tf_op jit(solution)/shard_map/ppermute | solution.py:54
  43.8 7.4 %collective-permute-start.12 = (bf16[256,128]{1,0:T(8,128)(2,1)S(1)}, bf16[256,128]{1,0:T(8,128)(2,1)S(1)}, u32[]{:S(2)}, u32[]{:S(2)}) collective-permute-start(bf16[256,128]{1,0:T(8,128)(2,1)S(1)} %fusion.7.refs_2_), channel_id=1, source_target_pairs={{0,4},{1,5},{2,6},{3,7},{4,0},{5,1},{6,2},{7,3},{8,12},{9,13},{10,... | collective-permute-start | bytes 196616 | tf_op jit(solution)/shard_map/ppermute | solution.py:54
  43.8 34.5 %collective-permute-start.22 = (bf16[4,64,4,256]{3,2,1,0:T(4,128)(2,1)S(1)}, bf16[4,64,4,256]{3,2,1,0:T(4,128)(2,1)S(1)}, u32[]{:S(2)}, u32[]{:S(2)}) collective-permute-start(bf16[4,64,4,256]{3,2,1,0:T(4,128)(2,1)S(1)} %copy-done.13), channel_id=1, source_target_pairs={{0,16},{8,24},{16,0},{24,8},{1,17},{9,25},{17,1},{25,9},{2,18},{10... | collective-permute-start | bytes 1572872 | tf_op jit(solution)/shard_map/ppermute | solution.py:54
  45.2 33.6 %collective-permute-start.23 = (bf16[4,64,4,256]{3,2,1,0:T(4,128)(2,1)S(1)}, bf16[4,64,4,256]{3,2,1,0:T(4,128)(2,1)S(1)}, u32[]{:S(2)}, u32[]{:S(2)}) collective-permute-start(bf16[4,64,4,256]{3,2,1,0:T(4,128)(2,1)S(1)} %copy-done.12), channel_id=1, source_target_pairs={{0,24},{8,16},{16,8},{24,0},{1,25},{9,17},{17,9},{25,1},{2,26},{10... | collective-permute-start | bytes 1572872 | tf_op jit(solution)/shard_map/ppermute | solution.py:54
  56.2 7.8 %collective-permute-start.18 = (bf16[8,64,128]{2,1,0:T(8,128)(2,1)S(1)}, bf16[8,64,128]{2,1,0:T(8,128)(2,1)S(1)}, u32[]{:S(2)}, u32[]{:S(2)}) collective-permute-start(bf16[8,64,128]{2,1,0:T(8,128)(2,1)S(1)} %get-tuple-element.86), channel_id=1, source_target_pairs={{0,8},{8,0},{16,24},{24,16},{1,9},{9,1},{17,25},{25,17},{2,10},{10... | collective-permute-start | bytes 393224 | tf_op jit(solution)/shard_map/ppermute | solution.py:54
  57.8 16.8 %collective-permute-start.19 = (bf16[8,64,128]{2,1,0:T(8,128)(2,1)S(1)}, bf16[8,64,128]{2,1,0:T(8,128)(2,1)S(1)}, u32[]{:S(2)}, u32[]{:S(2)}) collective-permute-start(bf16[8,64,128]{2,1,0:T(8,128)(2,1)S(1)} %get-tuple-element.87), channel_id=1, source_target_pairs={{0,16},{8,24},{16,0},{24,8},{1,17},{9,25},{17,1},{25,9},{2,18},{10... | collective-permute-start | bytes 393224 | tf_op jit(solution)/shard_map/ppermute | solution.py:54
  58.6 17.5 %collective-permute-start.20 = (bf16[8,64,128]{2,1,0:T(8,128)(2,1)S(1)}, bf16[8,64,128]{2,1,0:T(8,128)(2,1)S(1)}, u32[]{:S(2)}, u32[]{:S(2)}) collective-permute-start(bf16[8,64,128]{2,1,0:T(8,128)(2,1)S(1)} %get-tuple-element.88), channel_id=1, source_target_pairs={{0,24},{8,16},{16,8},{24,0},{1,25},{9,17},{17,9},{25,1},{2,26},{10... | collective-permute-start | bytes 393224 | tf_op jit(solution)/shard_map/ppermute | solution.py:54
  64.0 28.5 %collective-permute-start.28 = (f32[2,4,64,128]{3,2,1,0:T(8,128)}, f32[2,4,64,128]{3,2,1,0:T(8,128)S(1)}, u32[]{:S(2)}, u32[]{:S(2)}) collective-permute-start(f32[2,4,64,128]{3,2,1,0:T(8,128)} %get-tuple-element.108), channel_id=1, source_target_pairs={{0,8},{8,0},{16,24},{24,16},{1,9},{9,1},{17,25},{25,17},{2,10},{10... | collective-permute-start | bytes 786440 | tf_op jit(solution)/shard_map/ppermute | solution.py:54
  74.6 17.9 %collective-permute-start.29 = (f32[2,4,64,128]{3,2,1,0:T(8,128)}, f32[2,4,64,128]{3,2,1,0:T(8,128)S(1)}, u32[]{:S(2)}, u32[]{:S(2)}) collective-permute-start(f32[2,4,64,128]{3,2,1,0:T(8,128)} %get-tuple-element.109), channel_id=1, source_target_pairs={{0,16},{8,24},{16,0},{24,8},{1,17},{9,25},{17,1},{25,9},{2,18},{10... | collective-permute-start | bytes 786440 | tf_op jit(solution)/shard_map/ppermute | solution.py:54
  76.1 16.5 %collective-permute-start.30 = (f32[2,4,64,128]{3,2,1,0:T(8,128)}, f32[2,4,64,128]{3,2,1,0:T(8,128)S(1)}, u32[]{:S(2)}, u32[]{:S(2)}) collective-permute-start(f32[2,4,64,128]{3,2,1,0:T(8,128)} %get-tuple-element.110), channel_id=1, source_target_pairs={{0,24},{8,16},{16,8},{24,0},{1,25},{9,17},{17,9},{25,1},{2,26},{10... | collective-permute-start | bytes 786440 | tf_op jit(solution)/shard_map/ppermute | solution.py:54
  83.8 7.9 %collective-permute-start.26 = (bf16[4,64,128]{2,1,0:T(8,128)(2,1)S(1)}, bf16[4,64,128]{2,1,0:T(8,128)(2,1)S(1)}, u32[]{:S(2)}, u32[]{:S(2)}) collective-permute-start(bf16[4,64,128]{2,1,0:T(8,128)(2,1)S(1)} %get-tuple-element.91), channel_id=1, source_target_pairs={{0,17},{1,20},{2,19},{3,22},{4,21},{5,16},{6,23},{7,18},{8,28},{9,... | collective-permute-start | bytes 196616 | tf_op jit(solution)/shard_map/ppermute | solution.py:72
  85.2 7.3 %collective-permute-start.27 = (bf16[4,64,128]{2,1,0:T(8,128)(2,1)S(1)}, bf16[4,64,128]{2,1,0:T(8,128)(2,1)S(1)}, u32[]{:S(2)}, u32[]{:S(2)}) collective-permute-start(bf16[4,64,128]{2,1,0:T(8,128)(2,1)S(1)} %get-tuple-element.92), channel_id=1, source_target_pairs={{0,28},{1,27},{2,30},{3,29},{4,24},{5,31},{6,26},{7,25},{8,17},{9,... | collective-permute-start | bytes 196616 | tf_op jit(solution)/shard_map/ppermute | solution.py:72
  93.3 7.7 %collective-permute-start.31 = (bf16[4,64,128]{2,1,0:T(8,128)(2,1)S(1)}, bf16[4,64,128]{2,1,0:T(8,128)(2,1)S(1)}, u32[]{:S(2)}, u32[]{:S(2)}) collective-permute-start(bf16[4,64,128]{2,1,0:T(8,128)(2,1)S(1)} %get-tuple-element.111), channel_id=1, source_target_pairs={{0,7},{1,6},{2,1},{3,0},{4,3},{5,2},{6,5},{7,4},{8,14},{9,13},{10,... | collective-permute-start | bytes 196616 | tf_op jit(solution)/shard_map/ppermute | solution.py:82
  94.0 8.0 %collective-permute-start.32 = (bf16[4,64,128]{2,1,0:T(8,128)(2,1)S(1)}, bf16[4,64,128]{2,1,0:T(8,128)(2,1)S(1)}, u32[]{:S(2)}, u32[]{:S(2)}) collective-permute-start(bf16[4,64,128]{2,1,0:T(8,128)(2,1)S(1)} %get-tuple-element.112), channel_id=1, source_target_pairs={{0,15},{1,14},{2,9},{3,8},{4,11},{5,10},{6,13},{7,12},{8,6},{9,5},... | collective-permute-start | bytes 196616 | tf_op jit(solution)/shard_map/ppermute | solution.py:82
  98.5 8.3 %collective-permute-start.34 = (bf16[4,64,128]{2,1,0:T(8,128)(2,1)S(1)}, bf16[4,64,128]{2,1,0:T(8,128)(2,1)S(1)}, u32[]{:S(2)}, u32[]{:S(2)}) collective-permute-start(bf16[4,64,128]{2,1,0:T(8,128)(2,1)S(1)} %get-tuple-element.114), channel_id=1, source_target_pairs={{0,31},{1,30},{2,25},{3,24},{4,27},{5,26},{6,29},{7,28},{8,22},{9,... | collective-permute-start | bytes 196616 | tf_op jit(solution)/shard_map/ppermute | solution.py:82
  119.3 6.5 %collective-permute-start.41 = (bf16[256,128]{1,0:T(8,128)(2,1)S(1)}, bf16[256,128]{1,0:T(8,128)(2,1)S(1)}, u32[]{:S(2)}, u32[]{:S(2)}) collective-permute-start(bf16[256,128]{1,0:T(8,128)(2,1)S(1)} %get-tuple-element.139), channel_id=1, source_target_pairs={{0,6},{1,7},{2,4},{3,5},{4,2},{5,3},{6,0},{7,1},{8,14},{9,15},{10,... | collective-permute-start | bytes 196616 | tf_op jit(solution)/shard_map/ppermute | solution.py:54
  120.9 7.6 %collective-permute-start.40 = (bf16[256,128]{1,0:T(8,128)(2,1)S(1)}, bf16[256,128]{1,0:T(8,128)(2,1)S(1)}, u32[]{:S(2)}, u32[]{:S(2)}) collective-permute-start(bf16[256,128]{1,0:T(8,128)(2,1)S(1)} %get-tuple-element.140), channel_id=1, source_target_pairs={{0,4},{1,5},{2,6},{3,7},{4,0},{5,1},{6,2},{7,3},{8,12},{9,13},{10,... | collective-permute-start | bytes 196616 | tf_op jit(solution)/shard_map/ppermute | solution.py:54
  141.1 8.3 %collective-permute-start.50 = (bf16[8,64,128]{2,1,0:T(8,128)(2,1)S(1)}, bf16[8,64,128]{2,1,0:T(8,128)(2,1)S(1)}, u32[]{:S(2)}, u32[]{:S(2)}) collective-permute-start(bf16[8,64,128]{2,1,0:T(8,128)(2,1)S(1)} %get-tuple-element.117), channel_id=1, source_target_pairs={{0,16},{8,24},{16,0},{24,8},{1,17},{9,25},{17,1},{25,9},{2,18},{10... | collective-permute-start | bytes 393224 | tf_op jit(solution)/shard_map/ppermute | solution.py:54
  141.9 7.5 %collective-permute-start.51 = (bf16[8,64,128]{2,1,0:T(8,128)(2,1)S(1)}, bf16[8,64,128]{2,1,0:T(8,128)(2,1)S(1)}, u32[]{:S(2)}, u32[]{:S(2)}) collective-permute-start(bf16[8,64,128]{2,1,0:T(8,128)(2,1)S(1)} %get-tuple-element.118), channel_id=1, source_target_pairs={{0,24},{8,16},{16,8},{24,0},{1,25},{9,17},{17,9},{25,1},{2,26},{10... | collective-permute-start | bytes 393224 | tf_op jit(solution)/shard_map/ppermute | solution.py:54
  150.2 7.2 %collective-permute-start.53 = (bf16[4,64,128]{2,1,0:T(8,128)(2,1)S(1)}, bf16[4,64,128]{2,1,0:T(8,128)(2,1)S(1)}, u32[]{:S(2)}, u32[]{:S(2)}) collective-permute-start(bf16[4,64,128]{2,1,0:T(8,128)(2,1)S(1)} %get-tuple-element.120), channel_id=1, source_target_pairs={{0,10},{1,13},{2,12},{3,15},{4,14},{5,9},{6,8},{7,11},{8,3},{9,2},... | collective-permute-start | bytes 196616 | tf_op jit(solution)/shard_map/ppermute | solution.py:72
  151.5 7.0 %collective-permute-start.54 = (bf16[4,64,128]{2,1,0:T(8,128)(2,1)S(1)}, bf16[4,64,128]{2,1,0:T(8,128)(2,1)S(1)}, u32[]{:S(2)}, u32[]{:S(2)}) collective-permute-start(bf16[4,64,128]{2,1,0:T(8,128)(2,1)S(1)} %get-tuple-element.121), channel_id=1, source_target_pairs={{0,17},{1,20},{2,19},{3,22},{4,21},{5,16},{6,23},{7,18},{8,28},{9,... | collective-permute-start | bytes 196616 | tf_op jit(solution)/shard_map/ppermute | solution.py:72
  151.5 7.7 %collective-permute-start.55 = (bf16[4,64,128]{2,1,0:T(8,128)(2,1)S(1)}, bf16[4,64,128]{2,1,0:T(8,128)(2,1)S(1)}, u32[]{:S(2)}, u32[]{:S(2)}) collective-permute-start(bf16[4,64,128]{2,1,0:T(8,128)(2,1)S(1)} %get-tuple-element.122), channel_id=1, source_target_pairs={{0,28},{1,27},{2,30},{3,29},{4,24},{5,31},{6,26},{7,25},{8,17},{9,... | collective-permute-start | bytes 196616 | tf_op jit(solution)/shard_map/ppermute | solution.py:72
  159.9 7.8 %collective-permute-start.56 = (f32[4,64,128]{2,1,0:T(8,128)S(1)}, f32[4,64,128]{2,1,0:T(8,128)S(1)}, u32[]{:S(2)}, u32[]{:S(2)}) collective-permute-start(f32[4,64,128]{2,1,0:T(8,128)S(1)} %get-tuple-element.128), channel_id=1, source_target_pairs={{0,8},{8,0},{16,24},{24,16},{1,9},{9,1},{17,25},{25,17},{2,10},{10... | collective-permute-start | bytes 393224 | tf_op jit(solution)/shard_map/ppermute | solution.py:54
  163.8 7.7 %collective-permute-start.57 = (f32[4,64,128]{2,1,0:T(8,128)S(1)}, f32[4,64,128]{2,1,0:T(8,128)S(1)}, u32[]{:S(2)}, u32[]{:S(2)}) collective-permute-start(f32[4,64,128]{2,1,0:T(8,128)S(1)} %get-tuple-element.129), channel_id=1, source_target_pairs={{0,16},{8,24},{16,0},{24,8},{1,17},{9,25},{17,1},{25,9},{2,18},{10... | collective-permute-start | bytes 393224 | tf_op jit(solution)/shard_map/ppermute | solution.py:54
  (42 other events, 425.9 us)

commit v5 on v4

--- a/solution.py
+++ b/solution.py
@@ -13,6 +13,7 @@
 CORES = 2
 MIB = 1 << 20
 LARGE = 45
+LARGE_FIRST = 46
 LARGE_CHOOSE = 57
 
 
@@ -60,6 +61,21 @@
 
 def held_by_seen(rank, variant):
     return rank ^ (2 * ((variant + rank + 1) & 1))
+
+
+def fan(send, blocks, ranks):
+    sent = []
+    for k in ranks:
+        sent.append(send(blocks[k], k))
+    return sent
+
+
+def over_samp(block, mask):
+    return crossed(block, "samp", mask)
+
+
+def over_chips(block, mask):
+    return crossed(block, "var", CORES * mask)
 
 
 def to_owners(block, mask):
@@ -168,15 +184,19 @@
         copy.wait()
 
 
-def states_body(spot, quarters, pair, table, now, before, *outs):
+def states_body(spot, quarters, pair, momentum, table, now, before, *outs):
     where = indices()
     for k in range(quarters):
         for p in range(pair):
             code = held_by(where[1] ^ k, where[0]) * pair + p
             slot = table[spot.slot + code]
             live = table[spot.live + code] == 1
-            outs[k][0, p] = jnp.where(live, now[slot], 0.0)
-            outs[k][1, p] = jnp.where(live, before[slot], 0.0)
+            held = jnp.where(live, now[slot], 0.0)
+            point = held + momentum * (held - jnp.where(live, before[slot], 0.0))
+            high = point.astype(HALF)
+            outs[k][0, p] = high
+            outs[k][1, p] = (point - high.astype(F32)).astype(HALF)
+            outs[k][2, p] = held.astype(HALF)
 
 
 def panels_body(spot, quarters, pair, most, table, *refs):
@@ -216,20 +236,18 @@
             values[pl.ds(pl.multiple_of(at, quarter_rows), quarter_rows), :] = pieces[k][u]
 
 
-def load_body(dosage, *refs):
-    where = indices()
-    outs, arrived = refs[:CORES], refs[CORES]
+def load_body(partner, dosage, out, arrived):
+    where = indices()
     core, chip = lax.rem(where[0], CORES), lax.div(where[0], CORES)
-    chips = arrived.shape[0] // CORES
-    rows = outs[0].shape[0] // chips
+    chips = arrived.shape[0]
+    rows = out.shape[0] // chips
     copies = []
-    for c in reversed(range(CORES)):
-        for i in range(chips):
-            at = pl.multiple_of(((chip ^ i) * CORES + (core ^ c)) * rows, rows)
-            here = outs[c].at[pl.ds(i * rows, rows), :]
-            ready = arrived.at[c * chips + i]
-            copies.append(pltpu.make_async_copy(dosage.at[pl.ds(at, rows), :], here, ready))
-            copies[-1].start()
+    for i in range(chips):
+        at = pl.multiple_of(((chip ^ i) * CORES + (core ^ partner)) * rows, rows)
+        copies.append(
+            pltpu.make_async_copy(dosage.at[pl.ds(at, rows), :], out.at[pl.ds(i * rows, rows), :], arrived.at[i])
+        )
+        copies[-1].start()
     for copy in copies:
         copy.wait()
 
@@ -276,9 +294,9 @@
             outs[k][p] = jnp.where(unit >= 0, total, 0.0).astype(HALF)
 
 
-def update_body(quarters, momenta, penalty, *refs):
-    where = indices()
-    last = len(momenta) == 1
+def update_body(quarters, momentum, penalty, *refs):
+    where = indices()
+    last = momentum is None
     panels, pieces, states = refs[:quarters], refs[quarters : 2 * quarters], refs[2 * quarters : 3 * quarters]
     outs, gradient = refs[3 * quarters : -1], refs[-1]
     pair, quarter_rows = pieces[0].shape[:2]
@@ -293,15 +311,15 @@
         if last:
             point = states[k][...]
         else:
-            now = states[k][0]
-            point = now + momenta[0] * (now - states[k][1])
+            point = states[k][0].astype(F32) + states[k][1].astype(F32)
+            now = states[k][2].astype(F32)
         stepped = point - direction
         size = jnp.maximum(jnp.abs(stepped) - penalty[...], 0.0)
         updated = jnp.where(stepped > 0, size, jnp.where(stepped < 0, -size, 0.0))
         if last:
             outs[k][...] = updated
         else:
-            following = updated + momenta[1] * (updated - now)
+            following = updated + momentum * (updated - now)
             outs[k][...] = following
             outs[quarters + k][...] = following.astype(HALF)
 
@@ -353,13 +371,12 @@
         [pltpu.SemaphoreType.DMA((codes,))], limit=LARGE_CHOOSE, far=1,
     )
     block = like((chips * rows, dosage.shape[1]), HALF)
-    dosage = lax.optimization_barrier((chosen[0], dosage))[1]
-    kept_rows, given_rows = local(
-        load_body, [], [dosage], [block, block], [pltpu.SemaphoreType.DMA((owners,))], limit=LARGE, far=1
+    later = lax.optimization_barrier((chosen[0], dosage))[1]
+    given_rows = local(
+        functools.partial(load_body, 1), [], [later], block,
+        [pltpu.SemaphoreType.DMA((chips,))], limit=LARGE_FIRST, far=1,
     )
-    arrived, chosen, kept_rows, given_rows = lax.optimization_barrier(
-        (arrived, chosen, kept_rows, given_rows)
-    )
+    arrived, chosen, given_rows = lax.optimization_barrier((arrived, chosen, given_rows))
     chosen = [chosen[0]] + [crossed(chosen[k], "samp", k) for k in ranks[1:]]
     penalty = penalty.reshape(1, 1, right_cols)
 
@@ -370,6 +387,13 @@
             [pltpu.VMEM((reach, *piece), HALF)],
         )
         pieces = [own] + [crossed(own, "samp", k) for k in ranks[1:]]
+        if step == 0:
+            later = lax.optimization_barrier((own, dosage))[1]
+            kept_rows = local(
+                functools.partial(load_body, 0), [], [later], block,
+                [pltpu.SemaphoreType.DMA((chips,))], limit=LARGE, far=1,
+            )
+            pieces, kept_rows = lax.optimization_barrier((pieces, kept_rows))
         buffers = [pltpu.VMEM((dosage.shape[1], right_cols), HALF)]
         half = like((chips, rows, right_cols), F32)
         flops = dosage.shape[0] * dosage.shape[1] * right_cols
@@ -383,10 +407,10 @@
         given = crossed(given, "var", 1)
         both = kept + given
         total = both[0]
-        for i in range(1, chips):
-            total = total + crossed(both[i].astype(HALF), "var", CORES * i).astype(F32)
+        for part in fan(over_chips, both.astype(HALF), range(1, chips)):
+            total = total + part.astype(F32)
         residual_b = (total - traits).astype(HALF)
-        mine = [residual_b] + [crossed(residual_b, "var", CORES * i) for i in range(1, chips)]
+        mine = [residual_b] + fan(over_chips, [residual_b] * chips, range(1, chips))
         others = [crossed(block, "var", 1) for block in mine]
         sums = local(
             functools.partial(gradient_body, quarters, per_device, grad_scale),
@@ -400,12 +424,12 @@
         if step == len(MOMENTA) - 1:
             residual = lax.optimization_barrier((sums[0], total))[1] - traits
         summed = sums[0]
-        sums = [summed] + [crossed(sums[k], "samp", k) for k in ranks[1:]]
+        sums = [summed] + fan(over_samp, sums, ranks[1:])
         if step == 0:
             held = lax.optimization_barrier((summed, coef_now, coef_prev))[1:]
             states = local(
-                functools.partial(states_body, spot, quarters, pair),
-                [table], list(held), [like((2, *piece), F32)] * quarters,
+                functools.partial(states_body, spot, quarters, pair, MOMENTA[0]),
+                [table], list(held), [like((3, *piece), HALF)] * quarters,
             )
             states = [states[0]] + [crossed(states[k], "samp", k) for k in ranks[1:]]
         leaving = local(
@@ -424,15 +448,15 @@
         last = step == len(MOMENTA) - 1
         outs = [like(piece, F32)] * quarters + ([] if last else [like(piece, HALF)] * quarters)
         result = local(
-            functools.partial(update_body, quarters, MOMENTA[step : step + 2]),
+            functools.partial(update_body, quarters, None if last else MOMENTA[step + 1]),
             [], [penalty, *panels, *landed, *states], outs,
             [pltpu.VMEM((pair * unit_rows, right_cols), HALF)], limit=12,
             flops=2 * (pair * unit_rows) ** 2 * right_cols,
         )
         states = list(result[:quarters])
         if not last:
-            arrived = [to_variants(result[quarters + k], k) for k in ranks]
-    states = [states[0]] + [crossed(states[k], "samp", k) for k in ranks[1:]]
+            arrived = fan(to_variants, result[quarters:], ranks)
+    states = [states[0]] + fan(over_samp, states, ranks[1:])
     current = local(
         functools.partial(finish_body, spot, pair),
         [table], states, like((capacity, quarter_rows, right_cols), F32),

time: 173 us -> 170 us (0.983)
  starting transfers between devices: 71.5 us -> 65.2 us
  waiting for transfers between devices: 69.4 us -> 71.3 us
    ppermute x8, waiting for transfers between devices: 7.46 us -> 10.9 us  [to_owners(): return lax.ppermute(block, ('samp', 'var'), route)]
    ppermute x43, waiting for transfers between devices: 56.1 us -> 53.5 us  [crossed(): return lax.ppermute(block, axis, [(i, i ^ mask) for i in range(count)])]
    ppermute x8, starting transfers between devices: 12.3 us -> 9.87 us  [to_owners(): return lax.ppermute(block, ('samp', 'var'), route)]
    ppermute x4, starting transfers between devices: 7.68 us -> 5.46 us  [to_variants(): return lax.ppermute(block, ('samp', 'var'), route)]
    pallas_call x17 -> x18, Pallas kernels: 24.8 us -> 26.1 us  [local(): pl.pallas_call(body, in_specs=[SMEM] * len(scalars) + [FAR] * far + [VMEM...]
  transfers between devices with their start and end apart: 59 -> 59, of which waited for: 36 -> 36; matrix products, arithmetic and copies ran while one was open for 2% -> 2% of each run, Pallas kernels for 9% -> 10%
where the time goes in v5:
time: 170 us
  waiting for transfers between devices  71.3 us (42%)
  starting transfers between devices  65.2 us (38%)
  Pallas kernels  28.7 us (17%)
  local copies, waits for them, and re-layouts  2.61 us (2%)
    ppermute x43, waiting for transfers between devices, crossed(): return lax.ppermute(block, axis, [(i, i ^ mask) for i in range(count)])  53.5 us
    ppermute x43, starting transfers between devices, crossed(): return lax.ppermute(block, axis, [(i, i ^ mask) for i in range(count)])  42 us
    pallas_call x18, Pallas kernels, local(): pl.pallas_call(body, in_specs=[SMEM] * len(scalars) + [FAR] * far + [VMEM...  26.1 us
    ppermute x8, waiting for transfers between devices, to_owners(): return lax.ppermute(block, ('samp', 'var'), route)  10.9 us
    ppermute x8, starting transfers between devices, to_owners(): return lax.ppermute(block, ('samp', 'var'), route)  9.87 us
    ppermute x4, starting transfers between devices, shifted(): lax.ppermute(block, axis, [((i - distance) % count, i) for i in range(cou...  7.89 us
    ppermute x4, waiting for transfers between devices, to_variants(): return lax.ppermute(block, ('samp', 'var'), route)  7.01 us
    ppermute x4, starting transfers between devices, to_variants(): return lax.ppermute(block, ('samp', 'var'), route)  5.46 us
  transfers between devices with their start and end apart: 59, of which 36 were waited for; matrix products, arithmetic and copies ran while one was open for 2% of the time, Pallas kernels for 10%

profile of v5, /device:TPU:0, one launch (start us, length us, event | category | flops | bytes accessed | tf_op | source)
XLA Modules:
  0.0 169.9 jit_solution(8812857864061305361)
XLA Ops:
  0.6 2.7 %begin.1 = (s32[88]{0:T(128)}, bf16[4,64,128]{2,1,0:T(8,128)(2,1)}, bf16[4,64,128]{2,1,0:T(8,128)(2,1)}, bf16[4,64,128]{2,1,0:T(8,128)(2,1)}, bf16[4,64,128]{2,1,0:T(8,128)(2,1)}) custom-call(s32[64]{0:T(128)} %start.1, s32[64]{0:T(128)} %owner.1, f32[16,64,128]{2,1,0:T(8,128)} %now.2, f32[16,64,128]{2,1,0:T(8,128)} %before.2), custom_call_target="tpu_custom_call" | custom-call | tf_op jit(solution)/shard_map/begin/pallas_call | solution.py:358
  3.3 4.6 %collective-permute-start = (bf16[4,64,128]{2,1,0:T(8,128)(2,1)}, bf16[4,64,128]{2,1,0:T(8,128)(2,1)S(1)}, u32[]{:S(2)}, u32[]{:S(2)}) collective-permute-start(bf16[4,64,128]{2,1,0:T(8,128)(2,1)} %get-tuple-element.71), channel_id=1, source_target_pairs={{1,0},{2,1},{3,2},{4,3},{5,4},{6,5},{7,6},{0,7},{9,8},{10,9},{11,1... | collective-permute-start | bytes 196616 | tf_op jit(solution)/shard_map/ppermute | solution.py:50
  8.5 2.7 %collective-permute-start.3 = (bf16[4,64,128]{2,1,0:T(8,128)(2,1)}, bf16[4,64,128]{2,1,0:T(8,128)(2,1)S(1)}, u32[]{:S(2)}, u32[]{:S(2)}) collective-permute-start(bf16[4,64,128]{2,1,0:T(8,128)(2,1)} %get-tuple-element.74), channel_id=1, source_target_pairs={{4,0},{5,1},{6,2},{7,3},{0,4},{1,5},{2,6},{3,7},{12,8},{13,9},{14,... | collective-permute-start | bytes 196616 | tf_op jit(solution)/shard_map/ppermute | solution.py:50
  11.2 5.0 %shard_map.95 = (bf16[4,64,4,256]{3,2,1,0:T(4,128)(2,1)}, bf16[4,64,4,256]{3,2,1,0:T(4,128)(2,1)}, bf16[4,64,4,256]{3,2,1,0:T(4,128)(2,1)}, bf16[4,64,4,256]{3,2,1,0:T(4,128)(2,1)}) custom-call(s32[88]{0:T(128)} %get-tuple-element.70.table, bf16[16,64,4,256]{3,2,1,0:T(4,128)(2,1)} %inverses.1), custom_call_target="tpu_custom_call" | custom-call | bytes 4194304 | tf_op jit(solution)/shard_map/pallas_call | solution.py:33
  16.2 2.2 %shard_map.96.blocks.refs_1_ = bf16[1024,2048]{1,0:T(8,128)(2,1)S(1)} custom-call(bf16[2048,2048]{1,0:T(8,128)(2,1)} %dosage.1), custom_call_target="tpu_custom_call" | custom-call | bytes 12582912 | tf_op jit(solution)/shard_map/pallas_call | solution.py:33
  19.1 2.5 %collective-permute-start.6 = (bf16[8,64,128]{2,1,0:T(8,128)(2,1)S(1)}, bf16[8,64,128]{2,1,0:T(8,128)(2,1)S(1)}, u32[]{:S(2)}, u32[]{:S(2)}) collective-permute-start(bf16[8,64,128]{2,1,0:T(8,128)(2,1)S(1)} %shard_map.97.refs_0_), channel_id=1, source_target_pairs={{0,24},{8,16},{16,8},{24,0},{1,25},{9,17},{17,9},{25,1},{2,26},{10... | collective-permute-start | bytes 393224 | tf_op jit(solution)/shard_map/ppermute | solution.py:55
  22.6 2.2 %shard_map.98.blocks.refs_0_ = bf16[1024,2048]{1,0:T(8,128)(2,1)S(1)} custom-call(bf16[2048,2048]{1,0:T(8,128)(2,1)} %dosage.1), custom_call_target="tpu_custom_call" | custom-call | bytes 12582912 | tf_op jit(solution)/shard_map/pallas_call | solution.py:33
  31.1 2.0 %collective-permute-start.10 = (bf16[256,128]{1,0:T(8,128)(2,1)S(1)}, bf16[256,128]{1,0:T(8,128)(2,1)S(1)}, u32[]{:S(2)}, u32[]{:S(2)}) collective-permute-start(bf16[256,128]{1,0:T(8,128)(2,1)S(1)} %get-tuple-element.148), channel_id=1, source_target_pairs={{0,6},{1,7},{2,4},{3,5},{4,2},{5,3},{6,0},{7,1},{8,14},{9,15},{10,... | collective-permute-start | bytes 196616 | tf_op jit(solution)/shard_map/ppermute | solution.py:55
  37.9 2.7 %collective-permute-done.9 = bf16[256,128]{1,0:T(8,128)(2,1)S(1)} collective-permute-done((bf16[256,128]{1,0:T(8,128)(2,1)S(1)}, bf16[256,128]{1,0:T(8,128)(2,1)S(1)}, u32[]{:S(2)}, u32[]{:S(2)}) %collective-permute-start.9) | collective-permute-done | bytes 65568 | tf_op jit(solution)/shard_map/ppermute | solution.py:55
  43.8 1.8 %collective-permute-start.13 = (bf16[256,128]{1,0:T(8,128)(2,1)S(1)}, bf16[256,128]{1,0:T(8,128)(2,1)S(1)}, u32[]{:S(2)}, u32[]{:S(2)}) collective-permute-start(bf16[256,128]{1,0:T(8,128)(2,1)S(1)} %fusion.7.refs_2_), channel_id=1, source_target_pairs={{0,6},{1,7},{2,4},{3,5},{4,2},{5,3},{6,0},{7,1},{8,14},{9,15},{10,... | collective-permute-start | bytes 196616 | tf_op jit(solution)/shard_map/ppermute | solution.py:55
  45.7 4.6 %collective-permute-done.13.refs_5_ = bf16[256,128]{1,0:T(8,128)(2,1)S(1)} collective-permute-done((bf16[256,128]{1,0:T(8,128)(2,1)S(1)}, bf16[256,128]{1,0:T(8,128)(2,1)S(1)}, u32[]{:S(2)}, u32[]{:S(2)}) %collective-permute-start.13) | collective-permute-done | bytes 65568 | tf_op jit(solution)/shard_map/ppermute | solution.py:55
  50.3 2.1 %collective-permute-done.12.refs_4_ = bf16[256,128]{1,0:T(8,128)(2,1)S(1)} collective-permute-done((bf16[256,128]{1,0:T(8,128)(2,1)S(1)}, bf16[256,128]{1,0:T(8,128)(2,1)S(1)}, u32[]{:S(2)}, u32[]{:S(2)}) %collective-permute-start.12) | collective-permute-done | bytes 65568 | tf_op jit(solution)/shard_map/ppermute | solution.py:55
  52.4 2.2 %collective-permute-done.11.refs_3_ = bf16[256,128]{1,0:T(8,128)(2,1)S(1)} collective-permute-done((bf16[256,128]{1,0:T(8,128)(2,1)S(1)}, bf16[256,128]{1,0:T(8,128)(2,1)S(1)}, u32[]{:S(2)}, u32[]{:S(2)}) %collective-permute-start.11) | collective-permute-done | bytes 65568 | tf_op jit(solution)/shard_map/ppermute | solution.py:55
  64.3 7.6 %collective-permute-done.19.refs_2_ = bf16[8,64,128]{2,1,0:T(8,128)(2,1)S(1)} collective-permute-done((bf16[8,64,128]{2,1,0:T(8,128)(2,1)S(1)}, bf16[8,64,128]{2,1,0:T(8,128)(2,1)S(1)}, u32[]{:S(2)}, u32[]{:S(2)}) %collective-permute-start.19) | collective-permute-done | bytes 131104 | tf_op jit(solution)/shard_map/ppermute | solution.py:55
  76.9 4.9 %collective-permute-done.24.refs_4_ = bf16[4,64,128]{2,1,0:T(8,128)(2,1)S(1)} collective-permute-done((bf16[4,64,128]{2,1,0:T(8,128)(2,1)S(1)}, bf16[4,64,128]{2,1,0:T(8,128)(2,1)S(1)}, u32[]{:S(2)}, u32[]{:S(2)}) %collective-permute-start.24) | collective-permute-done | bytes 65568 | tf_op jit(solution)/shard_map/ppermute | solution.py:88
  83.4 3.0 %collective-permute-start.27 = (bf16[4,64,128]{2,1,0:T(8,128)(2,1)}, bf16[4,64,128]{2,1,0:T(8,128)(2,1)S(1)}, u32[]{:S(2)}, u32[]{:S(2)}) collective-permute-start(bf16[4,64,128]{2,1,0:T(8,128)(2,1)} %get-tuple-element.98), channel_id=1, source_target_pairs={{0,28},{1,27},{2,30},{3,29},{4,24},{5,31},{6,26},{7,25},{8,17},{9,... | collective-permute-start | bytes 196616 | tf_op jit(solution)/shard_map/ppermute | solution.py:88
  92.9 3.3 %collective-permute-start.33 = (bf16[4,64,128]{2,1,0:T(8,128)(2,1)S(1)}, bf16[4,64,128]{2,1,0:T(8,128)(2,1)S(1)}, u32[]{:S(2)}, u32[]{:S(2)}) collective-permute-start(bf16[4,64,128]{2,1,0:T(8,128)(2,1)S(1)} %get-tuple-element.119), channel_id=1, source_target_pairs={{0,23},{1,22},{2,17},{3,16},{4,19},{5,18},{6,21},{7,20},{8,30},{9,... | collective-permute-start | bytes 196616 | tf_op jit(solution)/shard_map/ppermute | solution.py:98
  99.0 5.6 %collective-permute-done.34.refs_3_ = bf16[4,64,128]{2,1,0:T(8,128)(2,1)S(1)} collective-permute-done((bf16[4,64,128]{2,1,0:T(8,128)(2,1)S(1)}, bf16[4,64,128]{2,1,0:T(8,128)(2,1)S(1)}, u32[]{:S(2)}, u32[]{:S(2)}) %collective-permute-start.34) | collective-permute-done | bytes 65568 | tf_op jit(solution)/shard_map/ppermute | solution.py:98
  106.8 1.9 %collective-permute-start.35 = (bf16[8,64,128]{2,1,0:T(8,128)(2,1)S(1)}, bf16[8,64,128]{2,1,0:T(8,128)(2,1)S(1)}, u32[]{:S(2)}, u32[]{:S(2)}) collective-permute-start(bf16[8,64,128]{2,1,0:T(8,128)(2,1)S(1)} %shard_map.106.refs_0_), channel_id=1, source_target_pairs={{0,8},{8,0},{16,24},{24,16},{1,9},{9,1},{17,25},{25,17},{2,10},{10... | collective-permute-start | bytes 393224 | tf_op jit(solution)/shard_map/ppermute | solution.py:55
  108.7 2.5 %collective-permute-done.37.refs_3_ = bf16[8,64,128]{2,1,0:T(8,128)(2,1)S(1)} collective-permute-done((bf16[8,64,128]{2,1,0:T(8,128)(2,1)S(1)}, bf16[8,64,128]{2,1,0:T(8,128)(2,1)S(1)}, u32[]{:S(2)}, u32[]{:S(2)}) %collective-permute-start.37) | collective-permute-done | bytes 131104 | tf_op jit(solution)/shard_map/ppermute | solution.py:55
  116.2 1.9 %collective-permute-start.41 = (bf16[256,128]{1,0:T(8,128)(2,1)S(1)}, bf16[256,128]{1,0:T(8,128)(2,1)S(1)}, u32[]{:S(2)}, u32[]{:S(2)}) collective-permute-start(bf16[256,128]{1,0:T(8,128)(2,1)S(1)} %get-tuple-element.145), channel_id=1, source_target_pairs={{0,6},{1,7},{2,4},{3,5},{4,2},{5,3},{6,0},{7,1},{8,14},{9,15},{10,... | collective-permute-start | bytes 196616 | tf_op jit(solution)/shard_map/ppermute | solution.py:55
  120.4 2.6 %collective-permute-done.41 = bf16[256,128]{1,0:T(8,128)(2,1)S(1)} collective-permute-done((bf16[256,128]{1,0:T(8,128)(2,1)S(1)}, bf16[256,128]{1,0:T(8,128)(2,1)S(1)}, u32[]{:S(2)}, u32[]{:S(2)}) %collective-permute-start.41) | collective-permute-done | bytes 65568 | tf_op jit(solution)/shard_map/ppermute | solution.py:55
  123.0 2.7 %collective-permute-done.40 = bf16[256,128]{1,0:T(8,128)(2,1)S(1)} collective-permute-done((bf16[256,128]{1,0:T(8,128)(2,1)S(1)}, bf16[256,128]{1,0:T(8,128)(2,1)S(1)}, u32[]{:S(2)}, u32[]{:S(2)}) %collective-permute-start.40) | collective-permute-done | bytes 65568 | tf_op jit(solution)/shard_map/ppermute | solution.py:55
  125.8 1.9 %collective-permute-start.44 = (bf16[256,128]{1,0:T(8,128)(2,1)S(1)}, bf16[256,128]{1,0:T(8,128)(2,1)S(1)}, u32[]{:S(2)}, u32[]{:S(2)}) collective-permute-start(bf16[256,128]{1,0:T(8,128)(2,1)S(1)} %get-tuple-element.138.refs_2_), channel_id=1, source_target_pairs={{0,6},{1,7},{2,4},{3,5},{4,2},{5,3},{6,0},{7,1},{8,14},{9,15},{10,... | collective-permute-start | bytes 196616 | tf_op jit(solution)/shard_map/ppermute | solution.py:55
  127.6 2.6 %collective-permute-start.42 = (bf16[256,128]{1,0:T(8,128)(2,1)S(1)}, bf16[256,128]{1,0:T(8,128)(2,1)S(1)}, u32[]{:S(2)}, u32[]{:S(2)}) collective-permute-start(bf16[256,128]{1,0:T(8,128)(2,1)S(1)} %get-tuple-element.138.refs_2_), channel_id=1, source_target_pairs={{0,2},{1,3},{2,0},{3,1},{4,6},{5,7},{6,4},{7,5},{8,10},{9,11},{10,... | collective-permute-start | bytes 196616 | tf_op jit(solution)/shard_map/ppermute | solution.py:55
  130.2 2.0 %collective-permute-done.44.refs_5_ = bf16[256,128]{1,0:T(8,128)(2,1)S(1)} collective-permute-done((bf16[256,128]{1,0:T(8,128)(2,1)S(1)}, bf16[256,128]{1,0:T(8,128)(2,1)S(1)}, u32[]{:S(2)}, u32[]{:S(2)}) %collective-permute-start.44) | collective-permute-done | bytes 65568 | tf_op jit(solution)/shard_map/ppermute | solution.py:55
  140.4 2.7 %collective-permute-done.49.refs_1_ = bf16[8,64,128]{2,1,0:T(8,128)(2,1)S(1)} collective-permute-done((bf16[8,64,128]{2,1,0:T(8,128)(2,1)S(1)}, bf16[8,64,128]{2,1,0:T(8,128)(2,1)S(1)}, u32[]{:S(2)}, u32[]{:S(2)}) %collective-permute-start.49) | collective-permute-done | bytes 131104 | tf_op jit(solution)/shard_map/ppermute | solution.py:55
  143.2 3.5 %collective-permute-done.50.refs_2_ = bf16[8,64,128]{2,1,0:T(8,128)(2,1)S(1)} collective-permute-done((bf16[8,64,128]{2,1,0:T(8,128)(2,1)S(1)}, bf16[8,64,128]{2,1,0:T(8,128)(2,1)S(1)}, u32[]{:S(2)}, u32[]{:S(2)}) %collective-permute-start.50) | collective-permute-done | bytes 131104 | tf_op jit(solution)/shard_map/ppermute | solution.py:55
  148.7 4.8 %collective-permute-start.55 = (bf16[4,64,128]{2,1,0:T(8,128)(2,1)S(1)}, bf16[4,64,128]{2,1,0:T(8,128)(2,1)S(1)}, u32[]{:S(2)}, u32[]{:S(2)}) collective-permute-start(bf16[4,64,128]{2,1,0:T(8,128)(2,1)S(1)} %get-tuple-element.128), channel_id=1, source_target_pairs={{0,28},{1,27},{2,30},{3,29},{4,24},{5,31},{6,26},{7,25},{8,17},{9,... | collective-permute-start | bytes 196616 | tf_op jit(solution)/shard_map/ppermute | solution.py:88
  157.2 3.8 %collective-permute-start.56 = (f32[4,64,128]{2,1,0:T(8,128)S(1)}, f32[4,64,128]{2,1,0:T(8,128)S(1)}, u32[]{:S(2)}, u32[]{:S(2)}) collective-permute-start(f32[4,64,128]{2,1,0:T(8,128)S(1)} %get-tuple-element.134), channel_id=1, source_target_pairs={{0,8},{8,0},{16,24},{24,16},{1,9},{9,1},{17,25},{25,17},{2,10},{10... | collective-permute-start | bytes 393224 | tf_op jit(solution)/shard_map/ppermute | solution.py:55
  163.2 2.0 %collective-permute-done.56.refs_1_ = f32[4,64,128]{2,1,0:T(8,128)S(1)} collective-permute-done((f32[4,64,128]{2,1,0:T(8,128)S(1)}, f32[4,64,128]{2,1,0:T(8,128)S(1)}, u32[]{:S(2)}, u32[]{:S(2)}) %collective-permute-start.56) | collective-permute-done | bytes 131104 | tf_op jit(solution)/shard_map/ppermute | solution.py:55
  165.1 3.4 %collective-permute-done.57.refs_2_ = f32[4,64,128]{2,1,0:T(8,128)S(1)} collective-permute-done((f32[4,64,128]{2,1,0:T(8,128)S(1)}, f32[4,64,128]{2,1,0:T(8,128)S(1)}, u32[]{:S(2)}, u32[]{:S(2)}) %collective-permute-start.57) | collective-permute-done | bytes 131104 | tf_op jit(solution)/shard_map/ppermute | solution.py:55
  (146 shorter events, 68.9 us)
Async XLA Ops:
  3.3 15.2 %collective-permute-start = (bf16[4,64,128]{2,1,0:T(8,128)(2,1)}, bf16[4,64,128]{2,1,0:T(8,128)(2,1)S(1)}, u32[]{:S(2)}, u32[]{:S(2)}) collective-permute-start(bf16[4,64,128]{2,1,0:T(8,128)(2,1)} %get-tuple-element.71), channel_id=1, source_target_pairs={{1,0},{2,1},{3,2},{4,3},{5,4},{6,5},{7,6},{0,7},{9,8},{10,9},{11,1... | collective-permute-start | bytes 196616 | tf_op jit(solution)/shard_map/ppermute | solution.py:50
  7.9 10.6 %collective-permute-start.1 = (bf16[4,64,128]{2,1,0:T(8,128)(2,1)}, bf16[4,64,128]{2,1,0:T(8,128)(2,1)S(1)}, u32[]{:S(2)}, u32[]{:S(2)}) collective-permute-start(bf16[4,64,128]{2,1,0:T(8,128)(2,1)} %get-tuple-element.72), channel_id=1, source_target_pairs={{2,0},{3,1},{4,2},{5,3},{6,4},{7,5},{0,6},{1,7},{10,8},{11,9},{12,... | collective-permute-start | bytes 196616 | tf_op jit(solution)/shard_map/ppermute | solution.py:50
  8.5 10.0 %collective-permute-start.2 = (bf16[4,64,128]{2,1,0:T(8,128)(2,1)}, bf16[4,64,128]{2,1,0:T(8,128)(2,1)S(1)}, u32[]{:S(2)}, u32[]{:S(2)}) collective-permute-start(bf16[4,64,128]{2,1,0:T(8,128)(2,1)} %get-tuple-element.73), channel_id=1, source_target_pairs={{3,0},{4,1},{5,2},{6,3},{7,4},{0,5},{1,6},{2,7},{11,8},{12,9},{13,... | collective-permute-start | bytes 196616 | tf_op jit(solution)/shard_map/ppermute | solution.py:50
  8.5 10.0 %collective-permute-start.3 = (bf16[4,64,128]{2,1,0:T(8,128)(2,1)}, bf16[4,64,128]{2,1,0:T(8,128)(2,1)S(1)}, u32[]{:S(2)}, u32[]{:S(2)}) collective-permute-start(bf16[4,64,128]{2,1,0:T(8,128)(2,1)} %get-tuple-element.74), channel_id=1, source_target_pairs={{4,0},{5,1},{6,2},{7,3},{0,4},{1,5},{2,6},{3,7},{12,8},{13,9},{14,... | collective-permute-start | bytes 196616 | tf_op jit(solution)/shard_map/ppermute | solution.py:50
  19.1 6.6 %collective-permute-start.6 = (bf16[8,64,128]{2,1,0:T(8,128)(2,1)S(1)}, bf16[8,64,128]{2,1,0:T(8,128)(2,1)S(1)}, u32[]{:S(2)}, u32[]{:S(2)}) collective-permute-start(bf16[8,64,128]{2,1,0:T(8,128)(2,1)S(1)} %shard_map.97.refs_0_), channel_id=1, source_target_pairs={{0,24},{8,16},{16,8},{24,0},{1,25},{9,17},{17,9},{25,1},{2,26},{10... | collective-permute-start | bytes 393224 | tf_op jit(solution)/shard_map/ppermute | solution.py:55
  31.1 6.8 %collective-permute-start.10 = (bf16[256,128]{1,0:T(8,128)(2,1)S(1)}, bf16[256,128]{1,0:T(8,128)(2,1)S(1)}, u32[]{:S(2)}, u32[]{:S(2)}) collective-permute-start(bf16[256,128]{1,0:T(8,128)(2,1)S(1)} %get-tuple-element.148), channel_id=1, source_target_pairs={{0,6},{1,7},{2,4},{3,5},{4,2},{5,3},{6,0},{7,1},{8,14},{9,15},{10,... | collective-permute-start | bytes 196616 | tf_op jit(solution)/shard_map/ppermute | solution.py:55
  33.1 7.5 %collective-permute-start.9 = (bf16[256,128]{1,0:T(8,128)(2,1)S(1)}, bf16[256,128]{1,0:T(8,128)(2,1)S(1)}, u32[]{:S(2)}, u32[]{:S(2)}) collective-permute-start(bf16[256,128]{1,0:T(8,128)(2,1)S(1)} %get-tuple-element.149), channel_id=1, source_target_pairs={{0,4},{1,5},{2,6},{3,7},{4,0},{5,1},{6,2},{7,3},{8,12},{9,13},{10,... | collective-permute-start | bytes 196616 | tf_op jit(solution)/shard_map/ppermute | solution.py:55
  34.6 25.1 %collective-permute-start.21 = (bf16[4,64,4,256]{3,2,1,0:T(4,128)(2,1)S(1)}, bf16[4,64,4,256]{3,2,1,0:T(4,128)(2,1)S(1)}, u32[]{:S(2)}, u32[]{:S(2)}) collective-permute-start(bf16[4,64,4,256]{3,2,1,0:T(4,128)(2,1)S(1)} %copy-done.14), channel_id=1, source_target_pairs={{0,8},{8,0},{16,24},{24,16},{1,9},{9,1},{17,25},{25,17},{2,10},{10... | collective-permute-start | bytes 1572872 | tf_op jit(solution)/shard_map/ppermute | solution.py:55
  40.8 35.4 %collective-permute-start.22 = (bf16[4,64,4,256]{3,2,1,0:T(4,128)(2,1)S(1)}, bf16[4,64,4,256]{3,2,1,0:T(4,128)(2,1)S(1)}, u32[]{:S(2)}, u32[]{:S(2)}) collective-permute-start(bf16[4,64,4,256]{3,2,1,0:T(4,128)(2,1)S(1)} %copy-done.13), channel_id=1, source_target_pairs={{0,16},{8,24},{16,0},{24,8},{1,17},{9,25},{17,1},{25,9},{2,18},{10... | collective-permute-start | bytes 1572872 | tf_op jit(solution)/shard_map/ppermute | solution.py:55
  42.3 33.9 %collective-permute-start.23 = (bf16[4,64,4,256]{3,2,1,0:T(4,128)(2,1)S(1)}, bf16[4,64,4,256]{3,2,1,0:T(4,128)(2,1)S(1)}, u32[]{:S(2)}, u32[]{:S(2)}) collective-permute-start(bf16[4,64,4,256]{3,2,1,0:T(4,128)(2,1)S(1)} %copy-done.12), channel_id=1, source_target_pairs={{0,24},{8,16},{16,8},{24,0},{1,25},{9,17},{17,9},{25,1},{2,26},{10... | collective-permute-start | bytes 1572872 | tf_op jit(solution)/shard_map/ppermute | solution.py:55
  43.8 6.5 %collective-permute-start.13 = (bf16[256,128]{1,0:T(8,128)(2,1)S(1)}, bf16[256,128]{1,0:T(8,128)(2,1)S(1)}, u32[]{:S(2)}, u32[]{:S(2)}) collective-permute-start(bf16[256,128]{1,0:T(8,128)(2,1)S(1)} %fusion.7.refs_2_), channel_id=1, source_target_pairs={{0,6},{1,7},{2,4},{3,5},{4,2},{5,3},{6,0},{7,1},{8,14},{9,15},{10,... | collective-permute-start | bytes 196616 | tf_op jit(solution)/shard_map/ppermute | solution.py:55
  45.7 6.7 %collective-permute-start.12 = (bf16[256,128]{1,0:T(8,128)(2,1)S(1)}, bf16[256,128]{1,0:T(8,128)(2,1)S(1)}, u32[]{:S(2)}, u32[]{:S(2)}) collective-permute-start(bf16[256,128]{1,0:T(8,128)(2,1)S(1)} %fusion.7.refs_2_), channel_id=1, source_target_pairs={{0,4},{1,5},{2,6},{3,7},{4,0},{5,1},{6,2},{7,3},{8,12},{9,13},{10,... | collective-permute-start | bytes 196616 | tf_op jit(solution)/shard_map/ppermute | solution.py:55
  58.2 13.8 %collective-permute-start.19 = (bf16[8,64,128]{2,1,0:T(8,128)(2,1)S(1)}, bf16[8,64,128]{2,1,0:T(8,128)(2,1)S(1)}, u32[]{:S(2)}, u32[]{:S(2)}) collective-permute-start(bf16[8,64,128]{2,1,0:T(8,128)(2,1)S(1)} %get-tuple-element.93), channel_id=1, source_target_pairs={{0,16},{8,24},{16,0},{24,8},{1,17},{9,25},{17,1},{25,9},{2,18},{10... | collective-permute-start | bytes 393224 | tf_op jit(solution)/shard_map/ppermute | solution.py:55
  59.6 13.8 %collective-permute-start.20 = (bf16[8,64,128]{2,1,0:T(8,128)(2,1)S(1)}, bf16[8,64,128]{2,1,0:T(8,128)(2,1)S(1)}, u32[]{:S(2)}, u32[]{:S(2)}) collective-permute-start(bf16[8,64,128]{2,1,0:T(8,128)(2,1)S(1)} %get-tuple-element.94), channel_id=1, source_target_pairs={{0,24},{8,16},{16,8},{24,0},{1,25},{9,17},{17,9},{25,1},{2,26},{10... | collective-permute-start | bytes 393224 | tf_op jit(solution)/shard_map/ppermute | solution.py:55
  64.0 27.3 %collective-permute-start.28 = (bf16[3,4,64,128]{3,2,1,0:T(8,128)(2,1)}, bf16[3,4,64,128]{3,2,1,0:T(8,128)(2,1)S(1)}, u32[]{:S(2)}, u32[]{:S(2)}) collective-permute-start(bf16[3,4,64,128]{3,2,1,0:T(8,128)(2,1)} %get-tuple-element.114), channel_id=1, source_target_pairs={{0,8},{8,0},{16,24},{24,16},{1,9},{9,1},{17,25},{25,17},{2,10},{10... | collective-permute-start | bytes 589832 | tf_op jit(solution)/shard_map/ppermute | solution.py:55
  71.9 19.3 %collective-permute-start.29 = (bf16[3,4,64,128]{3,2,1,0:T(8,128)(2,1)S(1)}, bf16[3,4,64,128]{3,2,1,0:T(8,128)(2,1)S(1)}, u32[]{:S(2)}, u32[]{:S(2)}) collective-permute-start(bf16[3,4,64,128]{3,2,1,0:T(8,128)(2,1)S(1)} %get-tuple-element.115), channel_id=1, source_target_pairs={{0,16},{8,24},{16,0},{24,8},{1,17},{9,25},{17,1},{25,9},{2,18},{10... | collective-permute-start | bytes 589832 | tf_op jit(solution)/shard_map/ppermute | solution.py:55
  73.4 17.9 %collective-permute-start.30 = (bf16[3,4,64,128]{3,2,1,0:T(8,128)(2,1)S(1)}, bf16[3,4,64,128]{3,2,1,0:T(8,128)(2,1)S(1)}, u32[]{:S(2)}, u32[]{:S(2)}) collective-permute-start(bf16[3,4,64,128]{3,2,1,0:T(8,128)(2,1)S(1)} %get-tuple-element.116), channel_id=1, source_target_pairs={{0,24},{8,16},{16,8},{24,0},{1,25},{9,17},{17,9},{25,1},{2,26},{10... | collective-permute-start | bytes 589832 | tf_op jit(solution)/shard_map/ppermute | solution.py:55
  76.2 7.1 %collective-permute-start.25 = (bf16[4,64,128]{2,1,0:T(8,128)(2,1)S(1)}, bf16[4,64,128]{2,1,0:T(8,128)(2,1)S(1)}, u32[]{:S(2)}, u32[]{:S(2)}) collective-permute-start(bf16[4,64,128]{2,1,0:T(8,128)(2,1)S(1)} %get-tuple-element.96), channel_id=1, source_target_pairs={{0,10},{1,13},{2,12},{3,15},{4,14},{5,9},{6,8},{7,11},{8,3},{9,2},... | collective-permute-start | bytes 196616 | tf_op jit(solution)/shard_map/ppermute | solution.py:88
  81.8 8.0 %collective-permute-start.26 = (bf16[4,64,128]{2,1,0:T(8,128)(2,1)}, bf16[4,64,128]{2,1,0:T(8,128)(2,1)S(1)}, u32[]{:S(2)}, u32[]{:S(2)}) collective-permute-start(bf16[4,64,128]{2,1,0:T(8,128)(2,1)} %get-tuple-element.97), channel_id=1, source_target_pairs={{0,17},{1,20},{2,19},{3,22},{4,21},{5,16},{6,23},{7,18},{8,28},{9,... | collective-permute-start | bytes 196616 | tf_op jit(solution)/shard_map/ppermute | solution.py:88
  83.4 7.9 %collective-permute-start.27 = (bf16[4,64,128]{2,1,0:T(8,128)(2,1)}, bf16[4,64,128]{2,1,0:T(8,128)(2,1)S(1)}, u32[]{:S(2)}, u32[]{:S(2)}) collective-permute-start(bf16[4,64,128]{2,1,0:T(8,128)(2,1)} %get-tuple-element.98), channel_id=1, source_target_pairs={{0,28},{1,27},{2,30},{3,29},{4,24},{5,31},{6,26},{7,25},{8,17},{9,... | collective-permute-start | bytes 196616 | tf_op jit(solution)/shard_map/ppermute | solution.py:88
  92.1 6.9 %collective-permute-start.32 = (bf16[4,64,128]{2,1,0:T(8,128)(2,1)S(1)}, bf16[4,64,128]{2,1,0:T(8,128)(2,1)S(1)}, u32[]{:S(2)}, u32[]{:S(2)}) collective-permute-start(bf16[4,64,128]{2,1,0:T(8,128)(2,1)S(1)} %get-tuple-element.118), channel_id=1, source_target_pairs={{0,15},{1,14},{2,9},{3,8},{4,11},{5,10},{6,13},{7,12},{8,6},{9,5},... | collective-permute-start | bytes 196616 | tf_op jit(solution)/shard_map/ppermute | solution.py:98
  96.3 8.3 %collective-permute-start.34 = (bf16[4,64,128]{2,1,0:T(8,128)(2,1)S(1)}, bf16[4,64,128]{2,1,0:T(8,128)(2,1)S(1)}, u32[]{:S(2)}, u32[]{:S(2)}) collective-permute-start(bf16[4,64,128]{2,1,0:T(8,128)(2,1)S(1)} %get-tuple-element.120), channel_id=1, source_target_pairs={{0,31},{1,30},{2,25},{3,24},{4,27},{5,26},{6,29},{7,28},{8,22},{9,... | collective-permute-start | bytes 196616 | tf_op jit(solution)/shard_map/ppermute | solution.py:98
  105.2 6.7 %collective-permute-start.36 = (bf16[8,64,128]{2,1,0:T(8,128)(2,1)S(1)}, bf16[8,64,128]{2,1,0:T(8,128)(2,1)S(1)}, u32[]{:S(2)}, u32[]{:S(2)}) collective-permute-start(bf16[8,64,128]{2,1,0:T(8,128)(2,1)S(1)} %shard_map.106.refs_0_), channel_id=1, source_target_pairs={{0,16},{8,24},{16,0},{24,8},{1,17},{9,25},{17,1},{25,9},{2,18},{10... | collective-permute-start | bytes 393224 | tf_op jit(solution)/shard_map/ppermute | solution.py:55
  116.2 6.8 %collective-permute-start.41 = (bf16[256,128]{1,0:T(8,128)(2,1)S(1)}, bf16[256,128]{1,0:T(8,128)(2,1)S(1)}, u32[]{:S(2)}, u32[]{:S(2)}) collective-permute-start(bf16[256,128]{1,0:T(8,128)(2,1)S(1)} %get-tuple-element.145), channel_id=1, source_target_pairs={{0,6},{1,7},{2,4},{3,5},{4,2},{5,3},{6,0},{7,1},{8,14},{9,15},{10,... | collective-permute-start | bytes 196616 | tf_op jit(solution)/shard_map/ppermute | solution.py:55
  118.1 7.6 %collective-permute-start.40 = (bf16[256,128]{1,0:T(8,128)(2,1)S(1)}, bf16[256,128]{1,0:T(8,128)(2,1)S(1)}, u32[]{:S(2)}, u32[]{:S(2)}) collective-permute-start(bf16[256,128]{1,0:T(8,128)(2,1)S(1)} %get-tuple-element.146), channel_id=1, source_target_pairs={{0,4},{1,5},{2,6},{3,7},{4,0},{5,1},{6,2},{7,3},{8,12},{9,13},{10,... | collective-permute-start | bytes 196616 | tf_op jit(solution)/shard_map/ppermute | solution.py:55
  138.3 8.3 %collective-permute-start.50 = (bf16[8,64,128]{2,1,0:T(8,128)(2,1)S(1)}, bf16[8,64,128]{2,1,0:T(8,128)(2,1)S(1)}, u32[]{:S(2)}, u32[]{:S(2)}) collective-permute-start(bf16[8,64,128]{2,1,0:T(8,128)(2,1)S(1)} %get-tuple-element.123), channel_id=1, source_target_pairs={{0,16},{8,24},{16,0},{24,8},{1,17},{9,25},{17,1},{25,9},{2,18},{10... | collective-permute-start | bytes 393224 | tf_op jit(solution)/shard_map/ppermute | solution.py:55
  139.2 7.5 %collective-permute-start.51 = (bf16[8,64,128]{2,1,0:T(8,128)(2,1)S(1)}, bf16[8,64,128]{2,1,0:T(8,128)(2,1)S(1)}, u32[]{:S(2)}, u32[]{:S(2)}) collective-permute-start(bf16[8,64,128]{2,1,0:T(8,128)(2,1)S(1)} %get-tuple-element.124), channel_id=1, source_target_pairs={{0,24},{8,16},{16,8},{24,0},{1,25},{9,17},{17,9},{25,1},{2,26},{10... | collective-permute-start | bytes 393224 | tf_op jit(solution)/shard_map/ppermute | solution.py:55
  147.4 7.2 %collective-permute-start.53 = (bf16[4,64,128]{2,1,0:T(8,128)(2,1)S(1)}, bf16[4,64,128]{2,1,0:T(8,128)(2,1)S(1)}, u32[]{:S(2)}, u32[]{:S(2)}) collective-permute-start(bf16[4,64,128]{2,1,0:T(8,128)(2,1)S(1)} %get-tuple-element.126), channel_id=1, source_target_pairs={{0,10},{1,13},{2,12},{3,15},{4,14},{5,9},{6,8},{7,11},{8,3},{9,2},... | collective-permute-start | bytes 196616 | tf_op jit(solution)/shard_map/ppermute | solution.py:88
  148.7 7.2 %collective-permute-start.54 = (bf16[4,64,128]{2,1,0:T(8,128)(2,1)S(1)}, bf16[4,64,128]{2,1,0:T(8,128)(2,1)S(1)}, u32[]{:S(2)}, u32[]{:S(2)}) collective-permute-start(bf16[4,64,128]{2,1,0:T(8,128)(2,1)S(1)} %get-tuple-element.127), channel_id=1, source_target_pairs={{0,17},{1,20},{2,19},{3,22},{4,21},{5,16},{6,23},{7,18},{8,28},{9,... | collective-permute-start | bytes 196616 | tf_op jit(solution)/shard_map/ppermute | solution.py:88
  148.7 7.7 %collective-permute-start.55 = (bf16[4,64,128]{2,1,0:T(8,128)(2,1)S(1)}, bf16[4,64,128]{2,1,0:T(8,128)(2,1)S(1)}, u32[]{:S(2)}, u32[]{:S(2)}) collective-permute-start(bf16[4,64,128]{2,1,0:T(8,128)(2,1)S(1)} %get-tuple-element.128), channel_id=1, source_target_pairs={{0,28},{1,27},{2,30},{3,29},{4,24},{5,31},{6,26},{7,25},{8,17},{9,... | collective-permute-start | bytes 196616 | tf_op jit(solution)/shard_map/ppermute | solution.py:88
  157.2 8.0 %collective-permute-start.56 = (f32[4,64,128]{2,1,0:T(8,128)S(1)}, f32[4,64,128]{2,1,0:T(8,128)S(1)}, u32[]{:S(2)}, u32[]{:S(2)}) collective-permute-start(f32[4,64,128]{2,1,0:T(8,128)S(1)} %get-tuple-element.134), channel_id=1, source_target_pairs={{0,8},{8,0},{16,24},{24,16},{1,9},{9,1},{17,25},{25,17},{2,10},{10... | collective-permute-start | bytes 393224 | tf_op jit(solution)/shard_map/ppermute | solution.py:55
  161.0 7.5 %collective-permute-start.57 = (f32[4,64,128]{2,1,0:T(8,128)S(1)}, f32[4,64,128]{2,1,0:T(8,128)S(1)}, u32[]{:S(2)}, u32[]{:S(2)}) collective-permute-start(f32[4,64,128]{2,1,0:T(8,128)S(1)} %get-tuple-element.135), channel_id=1, source_target_pairs={{0,16},{8,24},{16,0},{24,8},{1,17},{9,25},{17,1},{25,9},{2,18},{10... | collective-permute-start | bytes 393224 | tf_op jit(solution)/shard_map/ppermute | solution.py:55
  (42 other events, 420.5 us)

commit v6 on v5

--- a/solution.py
+++ b/solution.py
@@ -259,23 +259,34 @@
     chips, rows = out.shape[:2]
     for i in range(chips):
         block = blocks[i * rows : (i + 1) * rows, :]
-        out[i] = jnp.dot(block, values[...], preferred_element_type=F32) * scale
-
-
-def gradient_body(quarters, units, scale, *refs):
-    where = indices()
-    sides, pieces, outs = refs[:CORES], refs[CORES : -quarters - 2], refs[-quarters - 2 : -2]
-    residual, total = refs[-2:]
-    chips, rows = len(pieces) // CORES, pieces[0].shape[0]
+        out[i] = (jnp.dot(block, values[...], preferred_element_type=F32) * scale).astype(out.dtype)
+
+
+def turned_rows(pieces, residual):
+    rows = pieces[0].shape[0]
     for i, piece in enumerate(pieces):
         residual[i * rows : (i + 1) * rows, :] = piece[...]
-    turned = [residual[c * chips * rows : (c + 1) * chips * rows, :].T for c in range(CORES)]
-    width = sides[0].shape[1] // units
+    return residual[...].T
+
+
+def first_gradient_body(side, *refs):
+    pieces, (out, residual) = refs[:-2], refs[-2:]
+    turned = turned_rows(pieces, residual)
+    width = out.shape[2]
+    for u in range(out.shape[0]):
+        out[u] = jnp.dot(turned, side[:, u * width : (u + 1) * width], preferred_element_type=F32)
+
+
+def gradient_body(quarters, scale, side, started, *refs):
+    where = indices()
+    pieces, outs = refs[: -quarters - 2], refs[-quarters - 2 : -2]
+    residual, total = refs[-2:]
+    turned = turned_rows(pieces, residual)
+    width = started.shape[2]
     quarter_rows = width // quarters
-    for u in range(units):
-        product = jnp.dot(turned[0], sides[0][:, u * width : (u + 1) * width], preferred_element_type=F32)
-        product += jnp.dot(turned[1], sides[1][:, u * width : (u + 1) * width], preferred_element_type=F32)
-        total[u] = product.T * scale
+    for u in range(started.shape[0]):
+        product = jnp.dot(turned, side[:, u * width : (u + 1) * width], preferred_element_type=F32)
+        total[u] = (started[u] + product).T * scale
         for k in range(quarters):
             at = pl.multiple_of((where[1] ^ k) * quarter_rows, quarter_rows)
             outs[k][u] = total[u, pl.ds(at, quarter_rows), :].astype(outs[k].dtype)
@@ -317,7 +328,7 @@
         size = jnp.maximum(jnp.abs(stepped) - penalty[...], 0.0)
         updated = jnp.where(stepped > 0, size, jnp.where(stepped < 0, -size, 0.0))
         if last:
-            outs[k][...] = updated
+            outs[k][...] = updated.astype(outs[k].dtype)
         else:
             following = updated + momentum * (updated - now)
             outs[k][...] = following
@@ -328,7 +339,7 @@
     where = indices()
     pieces, out, held = refs[:-2], refs[-2], refs[-1]
     for k, piece in enumerate(pieces):
-        held[k] = piece[...]
+        held[k] = piece[...].astype(F32)
     for slot in range(out.shape[0]):
         code = table[spot.code_of_slot + slot]
         known = jnp.maximum(code, 0)
@@ -395,31 +406,33 @@
             )
             pieces, kept_rows = lax.optimization_barrier((pieces, kept_rows))
         buffers = [pltpu.VMEM((dosage.shape[1], right_cols), HALF)]
-        half = like((chips, rows, right_cols), F32)
         flops = dosage.shape[0] * dosage.shape[1] * right_cols
         given, kept = (
             local(
                 functools.partial(predict_body, quarters, inv_scale),
-                [], [side, *pieces], half, buffers, limit=8, flops=flops,
+                [], [side, *pieces], like((chips, rows, right_cols), kind), buffers, limit=8, flops=flops,
             )
-            for side in (given_rows, kept_rows)
+            for side, kind in ((given_rows, HALF), (kept_rows, F32))
         )
         given = crossed(given, "var", 1)
-        both = kept + given
+        both = kept + given.astype(F32)
         total = both[0]
         for part in fan(over_chips, both.astype(HALF), range(1, chips)):
             total = total + part.astype(F32)
         residual_b = (total - traits).astype(HALF)
         mine = [residual_b] + fan(over_chips, [residual_b] * chips, range(1, chips))
         others = [crossed(block, "var", 1) for block in mine]
+        flops = dosage.shape[0] * dosage.shape[1] * right_cols
+        stacked = pltpu.VMEM((chips * rows, right_cols), HALF)
+        started = local(
+            first_gradient_body, [], [kept_rows, *mine],
+            like((per_device, right_cols, unit_rows), F32), [stacked], limit=8, flops=flops,
+        )
         sums = local(
-            functools.partial(gradient_body, quarters, per_device, grad_scale),
-            [], [kept_rows, given_rows, *mine, *others],
+            functools.partial(gradient_body, quarters, grad_scale),
+            [], [given_rows, started, *others],
             [like(share, F32 if k == 0 else HALF) for k in ranks],
-            [
-                pltpu.VMEM((dosage.shape[0], right_cols), HALF),
-                pltpu.VMEM((per_device, unit_rows, right_cols), F32),
-            ], limit=15, flops=2 * dosage.shape[0] * dosage.shape[1] * right_cols,
+            [stacked, pltpu.VMEM((per_device, unit_rows, right_cols), F32)], limit=10, flops=flops,
         )
         if step == len(MOMENTA) - 1:
             residual = lax.optimization_barrier((sums[0], total))[1] - traits
@@ -446,7 +459,10 @@
                 [like((pair, quarter_rows, block_most * unit_rows), HALF)] * quarters, limit=10,
             )
         last = step == len(MOMENTA) - 1
-        outs = [like(piece, F32)] * quarters + ([] if last else [like(piece, HALF)] * quarters)
+        if last:
+            outs = [like(piece, F32 if k == 0 else HALF) for k in ranks]
+        else:
+            outs = [like(piece, F32)] * quarters + [like(piece, HALF)] * quarters
         result = local(
             functools.partial(update_body, quarters, None if last else MOMENTA[step + 1]),
             [], [penalty, *panels, *landed, *states], outs,

time: 170 us -> 162 us (0.953)
  waiting for transfers between devices: 71.3 us -> 61.3 us
    ppermute x43, waiting for transfers between devices: 53.5 us -> 44.9 us  [crossed(): return lax.ppermute(block, axis, [(i, i ^ mask) for i in range(count)])]
    pallas_call x18 -> x20, Pallas kernels: 26.1 us -> 26.5 us  [local(): pl.pallas_call(body, in_specs=[SMEM] * len(scalars) + [FAR] * far + [VMEM...]
  transfers between devices with their start and end apart: 59 -> 59, of which waited for: 36 -> 34; matrix products, arithmetic and copies ran while one was open for 2% -> 2% of each run, Pallas kernels for 10% -> 11%
where the time goes in v6:
time: 162 us
  starting transfers between devices  66.4 us (41%)
  waiting for transfers between devices  61.3 us (38%)
  Pallas kernels  29.2 us (18%)
  local copies, waits for them, and re-layouts  2.61 us (2%)
    ppermute x43, waiting for transfers between devices, crossed(): return lax.ppermute(block, axis, [(i, i ^ mask) for i in range(count)])  44.9 us
    ppermute x43, starting transfers between devices, crossed(): return lax.ppermute(block, axis, [(i, i ^ mask) for i in range(count)])  40.9 us
    pallas_call x20, Pallas kernels, local(): pl.pallas_call(body, in_specs=[SMEM] * len(scalars) + [FAR] * far + [VMEM...  26.5 us
    ppermute x8, starting transfers between devices, to_owners(): return lax.ppermute(block, ('samp', 'var'), route)  11.3 us
    ppermute x8, waiting for transfers between devices, to_owners(): return lax.ppermute(block, ('samp', 'var'), route)  9.34 us
    ppermute x4, starting transfers between devices, shifted(): lax.ppermute(block, axis, [((i - distance) % count, i) for i in range(cou...  7.89 us
    ppermute x4, waiting for transfers between devices, to_variants(): return lax.ppermute(block, ('samp', 'var'), route)  6.98 us
    ppermute x4, starting transfers between devices, to_variants(): return lax.ppermute(block, ('samp', 'var'), route)  6.41 us
  transfers between devices with their start and end apart: 59, of which 34 were waited for; matrix products, arithmetic and copies ran while one was open for 2% of the time, Pallas kernels for 11%

profile of v6, /device:TPU:0, one launch (start us, length us, event | category | flops | bytes accessed | tf_op | source)
XLA Modules:
  0.0 161.5 jit_solution(13114253157620252713)
XLA Ops:
  0.6 2.7 %begin.1 = (s32[88]{0:T(128)}, bf16[4,64,128]{2,1,0:T(8,128)(2,1)}, bf16[4,64,128]{2,1,0:T(8,128)(2,1)}, bf16[4,64,128]{2,1,0:T(8,128)(2,1)}, bf16[4,64,128]{2,1,0:T(8,128)(2,1)}) custom-call(s32[64]{0:T(128)} %start.1, s32[64]{0:T(128)} %owner.1, f32[16,64,128]{2,1,0:T(8,128)} %now.2, f32[16,64,128]{2,1,0:T(8,128)} %before.2), custom_call_target="tpu_custom_call" | custom-call | tf_op jit(solution)/shard_map/begin/pallas_call | solution.py:369
  3.3 4.6 %collective-permute-start = (bf16[4,64,128]{2,1,0:T(8,128)(2,1)}, bf16[4,64,128]{2,1,0:T(8,128)(2,1)S(1)}, u32[]{:S(2)}, u32[]{:S(2)}) collective-permute-start(bf16[4,64,128]{2,1,0:T(8,128)(2,1)} %get-tuple-element.71), channel_id=1, source_target_pairs={{1,0},{2,1},{3,2},{4,3},{5,4},{6,5},{7,6},{0,7},{9,8},{10,9},{11,1... | collective-permute-start | bytes 196616 | tf_op jit(solution)/shard_map/ppermute | solution.py:50
  8.5 2.7 %collective-permute-start.3 = (bf16[4,64,128]{2,1,0:T(8,128)(2,1)}, bf16[4,64,128]{2,1,0:T(8,128)(2,1)S(1)}, u32[]{:S(2)}, u32[]{:S(2)}) collective-permute-start(bf16[4,64,128]{2,1,0:T(8,128)(2,1)} %get-tuple-element.74), channel_id=1, source_target_pairs={{4,0},{5,1},{6,2},{7,3},{0,4},{1,5},{2,6},{3,7},{12,8},{13,9},{14,... | collective-permute-start | bytes 196616 | tf_op jit(solution)/shard_map/ppermute | solution.py:50
  11.2 5.0 %shard_map.95 = (bf16[4,64,4,256]{3,2,1,0:T(4,128)(2,1)}, bf16[4,64,4,256]{3,2,1,0:T(4,128)(2,1)}, bf16[4,64,4,256]{3,2,1,0:T(4,128)(2,1)}, bf16[4,64,4,256]{3,2,1,0:T(4,128)(2,1)}) custom-call(s32[88]{0:T(128)} %get-tuple-element.70.table, bf16[16,64,4,256]{3,2,1,0:T(4,128)(2,1)} %inverses.1), custom_call_target="tpu_custom_call" | custom-call | bytes 4194304 | tf_op jit(solution)/shard_map/pallas_call | solution.py:33
  16.2 2.2 %shard_map.96.blocks.side = bf16[1024,2048]{1,0:T(8,128)(2,1)S(1)} custom-call(bf16[2048,2048]{1,0:T(8,128)(2,1)} %dosage.1), custom_call_target="tpu_custom_call" | custom-call | bytes 12582912 | tf_op jit(solution)/shard_map/pallas_call | solution.py:33
  19.1 2.5 %collective-permute-start.6 = (bf16[8,64,128]{2,1,0:T(8,128)(2,1)S(1)}, bf16[8,64,128]{2,1,0:T(8,128)(2,1)S(1)}, u32[]{:S(2)}, u32[]{:S(2)}) collective-permute-start(bf16[8,64,128]{2,1,0:T(8,128)(2,1)S(1)} %shard_map.97.refs_0_), channel_id=1, source_target_pairs={{0,24},{8,16},{16,8},{24,0},{1,25},{9,17},{17,9},{25,1},{2,26},{10... | collective-permute-start | bytes 393224 | tf_op jit(solution)/shard_map/ppermute | solution.py:55
  22.6 2.2 %shard_map.98.blocks.side = bf16[1024,2048]{1,0:T(8,128)(2,1)S(1)} custom-call(bf16[2048,2048]{1,0:T(8,128)(2,1)} %dosage.1), custom_call_target="tpu_custom_call" | custom-call | bytes 12582912 | tf_op jit(solution)/shard_map/pallas_call | solution.py:33
  30.7 2.0 %collective-permute-start.10 = (bf16[256,128]{1,0:T(8,128)(2,1)S(1)}, bf16[256,128]{1,0:T(8,128)(2,1)S(1)}, u32[]{:S(2)}, u32[]{:S(2)}) collective-permute-start(bf16[256,128]{1,0:T(8,128)(2,1)S(1)} %get-tuple-element.148), channel_id=1, source_target_pairs={{0,6},{1,7},{2,4},{3,5},{4,2},{5,3},{6,0},{7,1},{8,14},{9,15},{10,... | collective-permute-start | bytes 196616 | tf_op jit(solution)/shard_map/ppermute | solution.py:55
  37.7 2.7 %collective-permute-done.9 = bf16[256,128]{1,0:T(8,128)(2,1)S(1)} collective-permute-done((bf16[256,128]{1,0:T(8,128)(2,1)S(1)}, bf16[256,128]{1,0:T(8,128)(2,1)S(1)}, u32[]{:S(2)}, u32[]{:S(2)}) %collective-permute-start.9) | collective-permute-done | bytes 65568 | tf_op jit(solution)/shard_map/ppermute | solution.py:55
  40.6 1.9 %collective-permute-start.13 = (bf16[256,128]{1,0:T(8,128)(2,1)S(1)}, bf16[256,128]{1,0:T(8,128)(2,1)S(1)}, u32[]{:S(2)}, u32[]{:S(2)}) collective-permute-start(bf16[256,128]{1,0:T(8,128)(2,1)S(1)} %fusion.7.refs_0_), channel_id=1, source_target_pairs={{0,6},{1,7},{2,4},{3,5},{4,2},{5,3},{6,0},{7,1},{8,14},{9,15},{10,... | collective-permute-start | bytes 196616 | tf_op jit(solution)/shard_map/ppermute | solution.py:55
  42.5 5.0 %collective-permute-done.13.refs_3_ = bf16[256,128]{1,0:T(8,128)(2,1)S(1)} collective-permute-done((bf16[256,128]{1,0:T(8,128)(2,1)S(1)}, bf16[256,128]{1,0:T(8,128)(2,1)S(1)}, u32[]{:S(2)}, u32[]{:S(2)}) %collective-permute-start.13) | collective-permute-done | bytes 65568 | tf_op jit(solution)/shard_map/ppermute | solution.py:55
  47.5 2.2 %collective-permute-done.12.refs_2_ = bf16[256,128]{1,0:T(8,128)(2,1)S(1)} collective-permute-done((bf16[256,128]{1,0:T(8,128)(2,1)S(1)}, bf16[256,128]{1,0:T(8,128)(2,1)S(1)}, u32[]{:S(2)}, u32[]{:S(2)}) %collective-permute-start.12) | collective-permute-done | bytes 65568 | tf_op jit(solution)/shard_map/ppermute | solution.py:55
  49.7 2.0 %collective-permute-done.11.refs_1_ = bf16[256,128]{1,0:T(8,128)(2,1)S(1)} collective-permute-done((bf16[256,128]{1,0:T(8,128)(2,1)S(1)}, bf16[256,128]{1,0:T(8,128)(2,1)S(1)}, u32[]{:S(2)}, u32[]{:S(2)}) %collective-permute-start.11) | collective-permute-done | bytes 65568 | tf_op jit(solution)/shard_map/ppermute | solution.py:55
  59.1 3.9 %collective-permute-done.18.refs_1_ = bf16[8,64,128]{2,1,0:T(8,128)(2,1)S(1)} collective-permute-done((bf16[8,64,128]{2,1,0:T(8,128)(2,1)S(1)}, bf16[8,64,128]{2,1,0:T(8,128)(2,1)S(1)}, u32[]{:S(2)}, u32[]{:S(2)}) %collective-permute-start.18) | collective-permute-done | bytes 131104 | tf_op jit(solution)/shard_map/ppermute | solution.py:55
  69.5 2.0 %collective-permute-start.25 = (bf16[4,64,128]{2,1,0:T(8,128)(2,1)S(1)}, bf16[4,64,128]{2,1,0:T(8,128)(2,1)S(1)}, u32[]{:S(2)}, u32[]{:S(2)}) collective-permute-start(bf16[4,64,128]{2,1,0:T(8,128)(2,1)S(1)} %get-tuple-element.96), channel_id=1, source_target_pairs={{0,10},{1,13},{2,12},{3,15},{4,14},{5,9},{6,8},{7,11},{8,3},{9,2},... | collective-permute-start | bytes 196616 | tf_op jit(solution)/shard_map/ppermute | solution.py:88
  71.5 3.5 %collective-permute-done.24.refs_4_ = bf16[4,64,128]{2,1,0:T(8,128)(2,1)S(1)} collective-permute-done((bf16[4,64,128]{2,1,0:T(8,128)(2,1)S(1)}, bf16[4,64,128]{2,1,0:T(8,128)(2,1)S(1)}, u32[]{:S(2)}, u32[]{:S(2)}) %collective-permute-start.24) | collective-permute-done | bytes 65568 | tf_op jit(solution)/shard_map/ppermute | solution.py:88
  76.2 3.2 %collective-permute-start.27 = (bf16[4,64,128]{2,1,0:T(8,128)(2,1)}, bf16[4,64,128]{2,1,0:T(8,128)(2,1)S(1)}, u32[]{:S(2)}, u32[]{:S(2)}) collective-permute-start(bf16[4,64,128]{2,1,0:T(8,128)(2,1)} %get-tuple-element.98), channel_id=1, source_target_pairs={{0,28},{1,27},{2,30},{3,29},{4,24},{5,31},{6,26},{7,25},{8,17},{9,... | collective-permute-start | bytes 196616 | tf_op jit(solution)/shard_map/ppermute | solution.py:88
  86.5 3.2 %collective-permute-start.33 = (bf16[4,64,128]{2,1,0:T(8,128)(2,1)S(1)}, bf16[4,64,128]{2,1,0:T(8,128)(2,1)S(1)}, u32[]{:S(2)}, u32[]{:S(2)}) collective-permute-start(bf16[4,64,128]{2,1,0:T(8,128)(2,1)S(1)} %get-tuple-element.119), channel_id=1, source_target_pairs={{0,23},{1,22},{2,17},{3,16},{4,19},{5,18},{6,21},{7,20},{8,30},{9,... | collective-permute-start | bytes 196616 | tf_op jit(solution)/shard_map/ppermute | solution.py:98
  92.0 6.0 %collective-permute-done.34.refs_3_ = bf16[4,64,128]{2,1,0:T(8,128)(2,1)S(1)} collective-permute-done((bf16[4,64,128]{2,1,0:T(8,128)(2,1)S(1)}, bf16[4,64,128]{2,1,0:T(8,128)(2,1)S(1)}, u32[]{:S(2)}, u32[]{:S(2)}) %collective-permute-start.34) | collective-permute-done | bytes 65568 | tf_op jit(solution)/shard_map/ppermute | solution.py:98
  102.1 2.5 %collective-permute-done.37.refs_3_ = bf16[8,64,128]{2,1,0:T(8,128)(2,1)S(1)} collective-permute-done((bf16[8,64,128]{2,1,0:T(8,128)(2,1)S(1)}, bf16[8,64,128]{2,1,0:T(8,128)(2,1)S(1)}, u32[]{:S(2)}, u32[]{:S(2)}) %collective-permute-start.37) | collective-permute-done | bytes 131104 | tf_op jit(solution)/shard_map/ppermute | solution.py:55
  113.4 2.9 %collective-permute-done.41 = bf16[256,128]{1,0:T(8,128)(2,1)S(1)} collective-permute-done((bf16[256,128]{1,0:T(8,128)(2,1)S(1)}, bf16[256,128]{1,0:T(8,128)(2,1)S(1)}, u32[]{:S(2)}, u32[]{:S(2)}) %collective-permute-start.41) | collective-permute-done | bytes 65568 | tf_op jit(solution)/shard_map/ppermute | solution.py:55
  116.3 2.8 %collective-permute-done.40 = bf16[256,128]{1,0:T(8,128)(2,1)S(1)} collective-permute-done((bf16[256,128]{1,0:T(8,128)(2,1)S(1)}, bf16[256,128]{1,0:T(8,128)(2,1)S(1)}, u32[]{:S(2)}, u32[]{:S(2)}) %collective-permute-start.40) | collective-permute-done | bytes 65568 | tf_op jit(solution)/shard_map/ppermute | solution.py:55
  119.1 2.2 %collective-permute-start.44 = (bf16[256,128]{1,0:T(8,128)(2,1)S(1)}, bf16[256,128]{1,0:T(8,128)(2,1)S(1)}, u32[]{:S(2)}, u32[]{:S(2)}) collective-permute-start(bf16[256,128]{1,0:T(8,128)(2,1)S(1)} %get-tuple-element.138.refs_0_), channel_id=1, source_target_pairs={{0,6},{1,7},{2,4},{3,5},{4,2},{5,3},{6,0},{7,1},{8,14},{9,15},{10,... | collective-permute-start | bytes 196616 | tf_op jit(solution)/shard_map/ppermute | solution.py:55
  121.4 2.2 %collective-permute-start.42 = (bf16[256,128]{1,0:T(8,128)(2,1)S(1)}, bf16[256,128]{1,0:T(8,128)(2,1)S(1)}, u32[]{:S(2)}, u32[]{:S(2)}) collective-permute-start(bf16[256,128]{1,0:T(8,128)(2,1)S(1)} %get-tuple-element.138.refs_0_), channel_id=1, source_target_pairs={{0,2},{1,3},{2,0},{3,1},{4,6},{5,7},{6,4},{7,5},{8,10},{9,11},{10,... | collective-permute-start | bytes 196616 | tf_op jit(solution)/shard_map/ppermute | solution.py:55
  123.6 2.0 %collective-permute-done.44.refs_3_ = bf16[256,128]{1,0:T(8,128)(2,1)S(1)} collective-permute-done((bf16[256,128]{1,0:T(8,128)(2,1)S(1)}, bf16[256,128]{1,0:T(8,128)(2,1)S(1)}, u32[]{:S(2)}, u32[]{:S(2)}) %collective-permute-start.44) | collective-permute-done | bytes 65568 | tf_op jit(solution)/shard_map/ppermute | solution.py:55
  125.5 1.9 %collective-permute-done.43.refs_2_ = bf16[256,128]{1,0:T(8,128)(2,1)S(1)} collective-permute-done((bf16[256,128]{1,0:T(8,128)(2,1)S(1)}, bf16[256,128]{1,0:T(8,128)(2,1)S(1)}, u32[]{:S(2)}, u32[]{:S(2)}) %collective-permute-start.43) | collective-permute-done | bytes 65568 | tf_op jit(solution)/shard_map/ppermute | solution.py:55
  133.5 2.9 %collective-permute-done.49.refs_1_ = bf16[8,64,128]{2,1,0:T(8,128)(2,1)S(1)} collective-permute-done((bf16[8,64,128]{2,1,0:T(8,128)(2,1)S(1)}, bf16[8,64,128]{2,1,0:T(8,128)(2,1)S(1)}, u32[]{:S(2)}, u32[]{:S(2)}) %collective-permute-start.49) | collective-permute-done | bytes 131104 | tf_op jit(solution)/shard_map/ppermute | solution.py:55
  136.4 3.0 %collective-permute-done.50.refs_2_ = bf16[8,64,128]{2,1,0:T(8,128)(2,1)S(1)} collective-permute-done((bf16[8,64,128]{2,1,0:T(8,128)(2,1)S(1)}, bf16[8,64,128]{2,1,0:T(8,128)(2,1)S(1)}, u32[]{:S(2)}, u32[]{:S(2)}) %collective-permute-start.50) | collective-permute-done | bytes 131104 | tf_op jit(solution)/shard_map/ppermute | solution.py:55
  141.8 4.3 %collective-permute-start.55 = (bf16[4,64,128]{2,1,0:T(8,128)(2,1)S(1)}, bf16[4,64,128]{2,1,0:T(8,128)(2,1)S(1)}, u32[]{:S(2)}, u32[]{:S(2)}) collective-permute-start(bf16[4,64,128]{2,1,0:T(8,128)(2,1)S(1)} %get-tuple-element.128), channel_id=1, source_target_pairs={{0,28},{1,27},{2,30},{3,29},{4,24},{5,31},{6,26},{7,25},{8,17},{9,... | collective-permute-start | bytes 196616 | tf_op jit(solution)/shard_map/ppermute | solution.py:88
  147.2 1.9 %collective-permute-done.54.refs_6_ = bf16[4,64,128]{2,1,0:T(8,128)(2,1)S(1)} collective-permute-done((bf16[4,64,128]{2,1,0:T(8,128)(2,1)S(1)}, bf16[4,64,128]{2,1,0:T(8,128)(2,1)S(1)}, u32[]{:S(2)}, u32[]{:S(2)}) %collective-permute-start.54) | collective-permute-done | bytes 65568 | tf_op jit(solution)/shard_map/ppermute | solution.py:88
  150.6 3.0 %collective-permute-start.56 = (bf16[4,64,128]{2,1,0:T(8,128)(2,1)S(1)}, bf16[4,64,128]{2,1,0:T(8,128)(2,1)S(1)}, u32[]{:S(2)}, u32[]{:S(2)}) collective-permute-start(bf16[4,64,128]{2,1,0:T(8,128)(2,1)S(1)} %get-tuple-element.134), channel_id=1, source_target_pairs={{0,8},{8,0},{16,24},{24,16},{1,9},{9,1},{17,25},{25,17},{2,10},{10... | collective-permute-start | bytes 196616 | tf_op jit(solution)/shard_map/ppermute | solution.py:55
  156.5 2.0 %collective-permute-done.57.refs_2_ = bf16[4,64,128]{2,1,0:T(8,128)(2,1)S(1)} collective-permute-done((bf16[4,64,128]{2,1,0:T(8,128)(2,1)S(1)}, bf16[4,64,128]{2,1,0:T(8,128)(2,1)S(1)}, u32[]{:S(2)}, u32[]{:S(2)}) %collective-permute-start.57) | collective-permute-done | bytes 65568 | tf_op jit(solution)/shard_map/ppermute | solution.py:55
  (148 shorter events, 67.3 us)
Async XLA Ops:
  3.3 15.2 %collective-permute-start = (bf16[4,64,128]{2,1,0:T(8,128)(2,1)}, bf16[4,64,128]{2,1,0:T(8,128)(2,1)S(1)}, u32[]{:S(2)}, u32[]{:S(2)}) collective-permute-start(bf16[4,64,128]{2,1,0:T(8,128)(2,1)} %get-tuple-element.71), channel_id=1, source_target_pairs={{1,0},{2,1},{3,2},{4,3},{5,4},{6,5},{7,6},{0,7},{9,8},{10,9},{11,1... | collective-permute-start | bytes 196616 | tf_op jit(solution)/shard_map/ppermute | solution.py:50
  7.9 10.6 %collective-permute-start.1 = (bf16[4,64,128]{2,1,0:T(8,128)(2,1)}, bf16[4,64,128]{2,1,0:T(8,128)(2,1)S(1)}, u32[]{:S(2)}, u32[]{:S(2)}) collective-permute-start(bf16[4,64,128]{2,1,0:T(8,128)(2,1)} %get-tuple-element.72), channel_id=1, source_target_pairs={{2,0},{3,1},{4,2},{5,3},{6,4},{7,5},{0,6},{1,7},{10,8},{11,9},{12,... | collective-permute-start | bytes 196616 | tf_op jit(solution)/shard_map/ppermute | solution.py:50
  8.5 10.0 %collective-permute-start.2 = (bf16[4,64,128]{2,1,0:T(8,128)(2,1)}, bf16[4,64,128]{2,1,0:T(8,128)(2,1)S(1)}, u32[]{:S(2)}, u32[]{:S(2)}) collective-permute-start(bf16[4,64,128]{2,1,0:T(8,128)(2,1)} %get-tuple-element.73), channel_id=1, source_target_pairs={{3,0},{4,1},{5,2},{6,3},{7,4},{0,5},{1,6},{2,7},{11,8},{12,9},{13,... | collective-permute-start | bytes 196616 | tf_op jit(solution)/shard_map/ppermute | solution.py:50
  8.5 10.0 %collective-permute-start.3 = (bf16[4,64,128]{2,1,0:T(8,128)(2,1)}, bf16[4,64,128]{2,1,0:T(8,128)(2,1)S(1)}, u32[]{:S(2)}, u32[]{:S(2)}) collective-permute-start(bf16[4,64,128]{2,1,0:T(8,128)(2,1)} %get-tuple-element.74), channel_id=1, source_target_pairs={{4,0},{5,1},{6,2},{7,3},{0,4},{1,5},{2,6},{3,7},{12,8},{13,9},{14,... | collective-permute-start | bytes 196616 | tf_op jit(solution)/shard_map/ppermute | solution.py:50
  19.1 6.6 %collective-permute-start.6 = (bf16[8,64,128]{2,1,0:T(8,128)(2,1)S(1)}, bf16[8,64,128]{2,1,0:T(8,128)(2,1)S(1)}, u32[]{:S(2)}, u32[]{:S(2)}) collective-permute-start(bf16[8,64,128]{2,1,0:T(8,128)(2,1)S(1)} %shard_map.97.refs_0_), channel_id=1, source_target_pairs={{0,24},{8,16},{16,8},{24,0},{1,25},{9,17},{17,9},{25,1},{2,26},{10... | collective-permute-start | bytes 393224 | tf_op jit(solution)/shard_map/ppermute | solution.py:55
  30.7 7.0 %collective-permute-start.10 = (bf16[256,128]{1,0:T(8,128)(2,1)S(1)}, bf16[256,128]{1,0:T(8,128)(2,1)S(1)}, u32[]{:S(2)}, u32[]{:S(2)}) collective-permute-start(bf16[256,128]{1,0:T(8,128)(2,1)S(1)} %get-tuple-element.148), channel_id=1, source_target_pairs={{0,6},{1,7},{2,4},{3,5},{4,2},{5,3},{6,0},{7,1},{8,14},{9,15},{10,... | collective-permute-start | bytes 196616 | tf_op jit(solution)/shard_map/ppermute | solution.py:55
  32.8 7.6 %collective-permute-start.9 = (bf16[256,128]{1,0:T(8,128)(2,1)S(1)}, bf16[256,128]{1,0:T(8,128)(2,1)S(1)}, u32[]{:S(2)}, u32[]{:S(2)}) collective-permute-start(bf16[256,128]{1,0:T(8,128)(2,1)S(1)} %get-tuple-element.149), channel_id=1, source_target_pairs={{0,4},{1,5},{2,6},{3,7},{4,0},{5,1},{6,2},{7,3},{8,12},{9,13},{10,... | collective-permute-start | bytes 196616 | tf_op jit(solution)/shard_map/ppermute | solution.py:55
  34.2 22.3 %collective-permute-start.21 = (bf16[4,64,4,256]{3,2,1,0:T(4,128)(2,1)S(1)}, bf16[4,64,4,256]{3,2,1,0:T(4,128)(2,1)S(1)}, u32[]{:S(2)}, u32[]{:S(2)}) collective-permute-start(bf16[4,64,4,256]{3,2,1,0:T(4,128)(2,1)S(1)} %copy-done.14), channel_id=1, source_target_pairs={{0,8},{8,0},{16,24},{24,16},{1,9},{9,1},{17,25},{25,17},{2,10},{10... | collective-permute-start | bytes 1572872 | tf_op jit(solution)/shard_map/ppermute | solution.py:55
  35.7 33.7 %collective-permute-start.22 = (bf16[4,64,4,256]{3,2,1,0:T(4,128)(2,1)S(1)}, bf16[4,64,4,256]{3,2,1,0:T(4,128)(2,1)S(1)}, u32[]{:S(2)}, u32[]{:S(2)}) collective-permute-start(bf16[4,64,4,256]{3,2,1,0:T(4,128)(2,1)S(1)} %copy-done.13), channel_id=1, source_target_pairs={{0,16},{8,24},{16,0},{24,8},{1,17},{9,25},{17,1},{25,9},{2,18},{10... | collective-permute-start | bytes 1572872 | tf_op jit(solution)/shard_map/ppermute | solution.py:55
  36.4 33.0 %collective-permute-start.23 = (bf16[4,64,4,256]{3,2,1,0:T(4,128)(2,1)S(1)}, bf16[4,64,4,256]{3,2,1,0:T(4,128)(2,1)S(1)}, u32[]{:S(2)}, u32[]{:S(2)}) collective-permute-start(bf16[4,64,4,256]{3,2,1,0:T(4,128)(2,1)S(1)} %copy-done.12), channel_id=1, source_target_pairs={{0,24},{8,16},{16,8},{24,0},{1,25},{9,17},{17,9},{25,1},{2,26},{10... | collective-permute-start | bytes 1572872 | tf_op jit(solution)/shard_map/ppermute | solution.py:55
  40.6 6.9 %collective-permute-start.13 = (bf16[256,128]{1,0:T(8,128)(2,1)S(1)}, bf16[256,128]{1,0:T(8,128)(2,1)S(1)}, u32[]{:S(2)}, u32[]{:S(2)}) collective-permute-start(bf16[256,128]{1,0:T(8,128)(2,1)S(1)} %fusion.7.refs_0_), channel_id=1, source_target_pairs={{0,6},{1,7},{2,4},{3,5},{4,2},{5,3},{6,0},{7,1},{8,14},{9,15},{10,... | collective-permute-start | bytes 196616 | tf_op jit(solution)/shard_map/ppermute | solution.py:55
  42.5 7.2 %collective-permute-start.12 = (bf16[256,128]{1,0:T(8,128)(2,1)S(1)}, bf16[256,128]{1,0:T(8,128)(2,1)S(1)}, u32[]{:S(2)}, u32[]{:S(2)}) collective-permute-start(bf16[256,128]{1,0:T(8,128)(2,1)S(1)} %fusion.7.refs_0_), channel_id=1, source_target_pairs={{0,4},{1,5},{2,6},{3,7},{4,0},{5,1},{6,2},{7,3},{8,12},{9,13},{10,... | collective-permute-start | bytes 196616 | tf_op jit(solution)/shard_map/ppermute | solution.py:55
  54.2 8.8 %collective-permute-start.18 = (bf16[8,64,128]{2,1,0:T(8,128)(2,1)S(1)}, bf16[8,64,128]{2,1,0:T(8,128)(2,1)S(1)}, u32[]{:S(2)}, u32[]{:S(2)}) collective-permute-start(bf16[8,64,128]{2,1,0:T(8,128)(2,1)S(1)} %get-tuple-element.92), channel_id=1, source_target_pairs={{0,8},{8,0},{16,24},{24,16},{1,9},{9,1},{17,25},{25,17},{2,10},{10... | collective-permute-start | bytes 393224 | tf_op jit(solution)/shard_map/ppermute | solution.py:55
  55.8 8.7 %collective-permute-start.19 = (bf16[8,64,128]{2,1,0:T(8,128)(2,1)S(1)}, bf16[8,64,128]{2,1,0:T(8,128)(2,1)S(1)}, u32[]{:S(2)}, u32[]{:S(2)}) collective-permute-start(bf16[8,64,128]{2,1,0:T(8,128)(2,1)S(1)} %get-tuple-element.93), channel_id=1, source_target_pairs={{0,16},{8,24},{16,0},{24,8},{1,17},{9,25},{17,1},{25,9},{2,18},{10... | collective-permute-start | bytes 393224 | tf_op jit(solution)/shard_map/ppermute | solution.py:55
  56.5 10.2 %collective-permute-start.20 = (bf16[8,64,128]{2,1,0:T(8,128)(2,1)S(1)}, bf16[8,64,128]{2,1,0:T(8,128)(2,1)S(1)}, u32[]{:S(2)}, u32[]{:S(2)}) collective-permute-start(bf16[8,64,128]{2,1,0:T(8,128)(2,1)S(1)} %get-tuple-element.94), channel_id=1, source_target_pairs={{0,24},{8,16},{16,8},{24,0},{1,25},{9,17},{17,9},{25,1},{2,26},{10... | collective-permute-start | bytes 393224 | tf_op jit(solution)/shard_map/ppermute | solution.py:55
  63.0 20.7 %collective-permute-start.28 = (bf16[3,4,64,128]{3,2,1,0:T(8,128)(2,1)}, bf16[3,4,64,128]{3,2,1,0:T(8,128)(2,1)S(1)}, u32[]{:S(2)}, u32[]{:S(2)}) collective-permute-start(bf16[3,4,64,128]{3,2,1,0:T(8,128)(2,1)} %get-tuple-element.114), channel_id=1, source_target_pairs={{0,8},{8,0},{16,24},{24,16},{1,9},{9,1},{17,25},{25,17},{2,10},{10... | collective-permute-start | bytes 589832 | tf_op jit(solution)/shard_map/ppermute | solution.py:55
  64.5 19.2 %collective-permute-start.29 = (bf16[3,4,64,128]{3,2,1,0:T(8,128)(2,1)S(1)}, bf16[3,4,64,128]{3,2,1,0:T(8,128)(2,1)S(1)}, u32[]{:S(2)}, u32[]{:S(2)}) collective-permute-start(bf16[3,4,64,128]{3,2,1,0:T(8,128)(2,1)S(1)} %get-tuple-element.115), channel_id=1, source_target_pairs={{0,16},{8,24},{16,0},{24,8},{1,17},{9,25},{17,1},{25,9},{2,18},{10... | collective-permute-start | bytes 589832 | tf_op jit(solution)/shard_map/ppermute | solution.py:55
  66.7 17.0 %collective-permute-start.30 = (bf16[3,4,64,128]{3,2,1,0:T(8,128)(2,1)S(1)}, bf16[3,4,64,128]{3,2,1,0:T(8,128)(2,1)S(1)}, u32[]{:S(2)}, u32[]{:S(2)}) collective-permute-start(bf16[3,4,64,128]{3,2,1,0:T(8,128)(2,1)S(1)} %get-tuple-element.116), channel_id=1, source_target_pairs={{0,24},{8,16},{16,8},{24,0},{1,25},{9,17},{17,9},{25,1},{2,26},{10... | collective-permute-start | bytes 589832 | tf_op jit(solution)/shard_map/ppermute | solution.py:55
  69.5 6.7 %collective-permute-start.25 = (bf16[4,64,128]{2,1,0:T(8,128)(2,1)S(1)}, bf16[4,64,128]{2,1,0:T(8,128)(2,1)S(1)}, u32[]{:S(2)}, u32[]{:S(2)}) collective-permute-start(bf16[4,64,128]{2,1,0:T(8,128)(2,1)S(1)} %get-tuple-element.96), channel_id=1, source_target_pairs={{0,10},{1,13},{2,12},{3,15},{4,14},{5,9},{6,8},{7,11},{8,3},{9,2},... | collective-permute-start | bytes 196616 | tf_op jit(solution)/shard_map/ppermute | solution.py:88
  75.0 7.9 %collective-permute-start.26 = (bf16[4,64,128]{2,1,0:T(8,128)(2,1)}, bf16[4,64,128]{2,1,0:T(8,128)(2,1)S(1)}, u32[]{:S(2)}, u32[]{:S(2)}) collective-permute-start(bf16[4,64,128]{2,1,0:T(8,128)(2,1)} %get-tuple-element.97), channel_id=1, source_target_pairs={{0,17},{1,20},{2,19},{3,22},{4,21},{5,16},{6,23},{7,18},{8,28},{9,... | collective-permute-start | bytes 196616 | tf_op jit(solution)/shard_map/ppermute | solution.py:88
  76.2 7.5 %collective-permute-start.27 = (bf16[4,64,128]{2,1,0:T(8,128)(2,1)}, bf16[4,64,128]{2,1,0:T(8,128)(2,1)S(1)}, u32[]{:S(2)}, u32[]{:S(2)}) collective-permute-start(bf16[4,64,128]{2,1,0:T(8,128)(2,1)} %get-tuple-element.98), channel_id=1, source_target_pairs={{0,28},{1,27},{2,30},{3,29},{4,24},{5,31},{6,26},{7,25},{8,17},{9,... | collective-permute-start | bytes 196616 | tf_op jit(solution)/shard_map/ppermute | solution.py:88
  84.6 7.4 %collective-permute-start.32 = (bf16[4,64,128]{2,1,0:T(8,128)(2,1)S(1)}, bf16[4,64,128]{2,1,0:T(8,128)(2,1)S(1)}, u32[]{:S(2)}, u32[]{:S(2)}) collective-permute-start(bf16[4,64,128]{2,1,0:T(8,128)(2,1)S(1)} %get-tuple-element.118), channel_id=1, source_target_pairs={{0,15},{1,14},{2,9},{3,8},{4,11},{5,10},{6,13},{7,12},{8,6},{9,5},... | collective-permute-start | bytes 196616 | tf_op jit(solution)/shard_map/ppermute | solution.py:98
  89.6 8.3 %collective-permute-start.34 = (bf16[4,64,128]{2,1,0:T(8,128)(2,1)S(1)}, bf16[4,64,128]{2,1,0:T(8,128)(2,1)S(1)}, u32[]{:S(2)}, u32[]{:S(2)}) collective-permute-start(bf16[4,64,128]{2,1,0:T(8,128)(2,1)S(1)} %get-tuple-element.120), channel_id=1, source_target_pairs={{0,31},{1,30},{2,25},{3,24},{4,27},{5,26},{6,29},{7,28},{8,22},{9,... | collective-permute-start | bytes 196616 | tf_op jit(solution)/shard_map/ppermute | solution.py:98
  98.6 6.4 %collective-permute-start.36 = (bf16[8,64,128]{2,1,0:T(8,128)(2,1)S(1)}, bf16[8,64,128]{2,1,0:T(8,128)(2,1)S(1)}, u32[]{:S(2)}, u32[]{:S(2)}) collective-permute-start(bf16[8,64,128]{2,1,0:T(8,128)(2,1)S(1)} %shard_map.107.refs_0_), channel_id=1, source_target_pairs={{0,16},{8,24},{16,0},{24,8},{1,17},{9,25},{17,1},{25,9},{2,18},{10... | collective-permute-start | bytes 393224 | tf_op jit(solution)/shard_map/ppermute | solution.py:55
  109.8 6.6 %collective-permute-start.41 = (bf16[256,128]{1,0:T(8,128)(2,1)S(1)}, bf16[256,128]{1,0:T(8,128)(2,1)S(1)}, u32[]{:S(2)}, u32[]{:S(2)}) collective-permute-start(bf16[256,128]{1,0:T(8,128)(2,1)S(1)} %get-tuple-element.145), channel_id=1, source_target_pairs={{0,6},{1,7},{2,4},{3,5},{4,2},{5,3},{6,0},{7,1},{8,14},{9,15},{10,... | collective-permute-start | bytes 196616 | tf_op jit(solution)/shard_map/ppermute | solution.py:55
  111.6 7.5 %collective-permute-start.40 = (bf16[256,128]{1,0:T(8,128)(2,1)S(1)}, bf16[256,128]{1,0:T(8,128)(2,1)S(1)}, u32[]{:S(2)}, u32[]{:S(2)}) collective-permute-start(bf16[256,128]{1,0:T(8,128)(2,1)S(1)} %get-tuple-element.146), channel_id=1, source_target_pairs={{0,4},{1,5},{2,6},{3,7},{4,0},{5,1},{6,2},{7,3},{8,12},{9,13},{10,... | collective-permute-start | bytes 196616 | tf_op jit(solution)/shard_map/ppermute | solution.py:55
  129.9 6.4 %collective-permute-start.49 = (bf16[8,64,128]{2,1,0:T(8,128)(2,1)S(1)}, bf16[8,64,128]{2,1,0:T(8,128)(2,1)S(1)}, u32[]{:S(2)}, u32[]{:S(2)}) collective-permute-start(bf16[8,64,128]{2,1,0:T(8,128)(2,1)S(1)} %get-tuple-element.122), channel_id=1, source_target_pairs={{0,8},{8,0},{16,24},{24,16},{1,9},{9,1},{17,25},{25,17},{2,10},{10... | collective-permute-start | bytes 393224 | tf_op jit(solution)/shard_map/ppermute | solution.py:55
  131.0 8.3 %collective-permute-start.50 = (bf16[8,64,128]{2,1,0:T(8,128)(2,1)S(1)}, bf16[8,64,128]{2,1,0:T(8,128)(2,1)S(1)}, u32[]{:S(2)}, u32[]{:S(2)}) collective-permute-start(bf16[8,64,128]{2,1,0:T(8,128)(2,1)S(1)} %get-tuple-element.123), channel_id=1, source_target_pairs={{0,16},{8,24},{16,0},{24,8},{1,17},{9,25},{17,1},{25,9},{2,18},{10... | collective-permute-start | bytes 393224 | tf_op jit(solution)/shard_map/ppermute | solution.py:55
  131.8 7.5 %collective-permute-start.51 = (bf16[8,64,128]{2,1,0:T(8,128)(2,1)S(1)}, bf16[8,64,128]{2,1,0:T(8,128)(2,1)S(1)}, u32[]{:S(2)}, u32[]{:S(2)}) collective-permute-start(bf16[8,64,128]{2,1,0:T(8,128)(2,1)S(1)} %get-tuple-element.124), channel_id=1, source_target_pairs={{0,24},{8,16},{16,8},{24,0},{1,25},{9,17},{17,9},{25,1},{2,26},{10... | collective-permute-start | bytes 393224 | tf_op jit(solution)/shard_map/ppermute | solution.py:55
  140.1 7.2 %collective-permute-start.53 = (bf16[4,64,128]{2,1,0:T(8,128)(2,1)S(1)}, bf16[4,64,128]{2,1,0:T(8,128)(2,1)S(1)}, u32[]{:S(2)}, u32[]{:S(2)}) collective-permute-start(bf16[4,64,128]{2,1,0:T(8,128)(2,1)S(1)} %get-tuple-element.126), channel_id=1, source_target_pairs={{0,10},{1,13},{2,12},{3,15},{4,14},{5,9},{6,8},{7,11},{8,3},{9,2},... | collective-permute-start | bytes 196616 | tf_op jit(solution)/shard_map/ppermute | solution.py:88
  141.8 7.4 %collective-permute-start.54 = (bf16[4,64,128]{2,1,0:T(8,128)(2,1)S(1)}, bf16[4,64,128]{2,1,0:T(8,128)(2,1)S(1)}, u32[]{:S(2)}, u32[]{:S(2)}) collective-permute-start(bf16[4,64,128]{2,1,0:T(8,128)(2,1)S(1)} %get-tuple-element.127), channel_id=1, source_target_pairs={{0,17},{1,20},{2,19},{3,22},{4,21},{5,16},{6,23},{7,18},{8,28},{9,... | collective-permute-start | bytes 196616 | tf_op jit(solution)/shard_map/ppermute | solution.py:88
  141.8 8.1 %collective-permute-start.55 = (bf16[4,64,128]{2,1,0:T(8,128)(2,1)S(1)}, bf16[4,64,128]{2,1,0:T(8,128)(2,1)S(1)}, u32[]{:S(2)}, u32[]{:S(2)}) collective-permute-start(bf16[4,64,128]{2,1,0:T(8,128)(2,1)S(1)} %get-tuple-element.128), channel_id=1, source_target_pairs={{0,28},{1,27},{2,30},{3,29},{4,24},{5,31},{6,26},{7,25},{8,17},{9,... | collective-permute-start | bytes 196616 | tf_op jit(solution)/shard_map/ppermute | solution.py:88
  (42 other events, 369.1 us)

commit v7 on v6

--- a/solution.py
+++ b/solution.py
@@ -237,6 +237,11 @@
 
 
 def load_body(partner, dosage, out, arrived):
+    for copy in started_load(partner, dosage, out, arrived):
+        copy.wait()
+
+
+def started_load(partner, dosage, out, arrived):
     where = indices()
     core, chip = lax.rem(where[0], CORES), lax.div(where[0], CORES)
     chips = arrived.shape[0]
@@ -248,6 +253,13 @@
             pltpu.make_async_copy(dosage.at[pl.ds(at, rows), :], out.at[pl.ds(i * rows, rows), :], arrived.at[i])
         )
         copies[-1].start()
+    return copies
+
+
+def loading_predict_body(quarters, scale, dosage, blocks, *refs):
+    pieces, (out, kept, values, arrived) = refs[:quarters], refs[quarters:]
+    copies = started_load(0, dosage, kept, arrived)
+    predict_body(quarters, scale, blocks, *pieces, out, values)
     for copy in copies:
         copy.wait()
 
@@ -398,21 +410,23 @@
             [pltpu.VMEM((reach, *piece), HALF)],
         )
         pieces = [own] + [crossed(own, "samp", k) for k in ranks[1:]]
-        if step == 0:
-            later = lax.optimization_barrier((own, dosage))[1]
-            kept_rows = local(
-                functools.partial(load_body, 0), [], [later], block,
-                [pltpu.SemaphoreType.DMA((chips,))], limit=LARGE, far=1,
-            )
-            pieces, kept_rows = lax.optimization_barrier((pieces, kept_rows))
         buffers = [pltpu.VMEM((dosage.shape[1], right_cols), HALF)]
         flops = dosage.shape[0] * dosage.shape[1] * right_cols
-        given, kept = (
-            local(
+        given, kept = (like((chips, rows, right_cols), kind) for kind in (HALF, F32))
+        if step == 0:
+            given, kept_rows = local(
+                functools.partial(loading_predict_body, quarters, inv_scale),
+                [], [dosage, given_rows, *pieces], [given, block],
+                [*buffers, pltpu.SemaphoreType.DMA((chips,))], limit=LARGE, flops=flops, far=1,
+            )
+        else:
+            given = local(
                 functools.partial(predict_body, quarters, inv_scale),
-                [], [side, *pieces], like((chips, rows, right_cols), kind), buffers, limit=8, flops=flops,
+                [], [given_rows, *pieces], given, buffers, limit=8, flops=flops,
             )
-            for side, kind in ((given_rows, HALF), (kept_rows, F32))
+        kept = local(
+            functools.partial(predict_body, quarters, inv_scale),
+            [], [kept_rows, *pieces], kept, buffers, limit=8, flops=flops,
         )
         given = crossed(given, "var", 1)
         both = kept + given.astype(F32)

time: 162 us -> 164 us (1.012)
  waiting for transfers between devices: 61.3 us -> 63.5 us
    ppermute x43, waiting for transfers between devices: 44.9 us -> 47.2 us  [crossed(): return lax.ppermute(block, axis, [(i, i ^ mask) for i in range(count)])]
    pallas_call x20 -> x19, Pallas kernels: 26.5 us -> 26.4 us  [local(): pl.pallas_call(body, in_specs=[SMEM] * len(scalars) + [FAR] * far + [VMEM...]
  transfers between devices with their start and end apart: 59 -> 59, of which waited for: 34 -> 34; matrix products, arithmetic and copies ran while one was open for 2% -> 2% of each run, Pallas kernels for 11% -> 10%
where the time goes in v7:
time: 164 us
  starting transfers between devices  66.4 us (40%)
  waiting for transfers between devices  63.5 us (39%)
  Pallas kernels  29 us (18%)
  local copies, waits for them, and re-layouts  2.61 us (2%)
    ppermute x43, waiting for transfers between devices, crossed(): return lax.ppermute(block, axis, [(i, i ^ mask) for i in range(count)])  47.2 us
    ppermute x43, starting transfers between devices, crossed(): return lax.ppermute(block, axis, [(i, i ^ mask) for i in range(count)])  40.8 us
    pallas_call x19, Pallas kernels, local(): pl.pallas_call(body, in_specs=[SMEM] * len(scalars) + [FAR] * far + [VMEM...  26.4 us
    ppermute x8, starting transfers between devices, to_owners(): return lax.ppermute(block, ('samp', 'var'), route)  11.3 us
    ppermute x8, waiting for transfers between devices, to_owners(): return lax.ppermute(block, ('samp', 'var'), route)  9.34 us
    ppermute x4, starting transfers between devices, shifted(): lax.ppermute(block, axis, [((i - distance) % count, i) for i in range(cou...  7.89 us
    ppermute x4, waiting for transfers between devices, to_variants(): return lax.ppermute(block, ('samp', 'var'), route)  6.98 us
    ppermute x4, starting transfers between devices, to_variants(): return lax.ppermute(block, ('samp', 'var'), route)  6.4 us
  transfers between devices with their start and end apart: 59, of which 34 were waited for; matrix products, arithmetic and copies ran while one was open for 2% of the time, Pallas kernels for 10%

profile of v7, /device:TPU:0, one launch (start us, length us, event | category | flops | bytes accessed | tf_op | source)
XLA Modules:
  0.0 163.6 jit_solution(2978768943065938468)
XLA Ops:
  0.6 2.6 %begin.1 = (s32[88]{0:T(128)}, bf16[4,64,128]{2,1,0:T(8,128)(2,1)}, bf16[4,64,128]{2,1,0:T(8,128)(2,1)}, bf16[4,64,128]{2,1,0:T(8,128)(2,1)}, bf16[4,64,128]{2,1,0:T(8,128)(2,1)}) custom-call(s32[64]{0:T(128)} %start.1, s32[64]{0:T(128)} %owner.1, f32[16,64,128]{2,1,0:T(8,128)} %now.2, f32[16,64,128]{2,1,0:T(8,128)} %before.2), custom_call_target="tpu_custom_call" | custom-call | tf_op jit(solution)/shard_map/begin/pallas_call | solution.py:381
  3.3 4.6 %collective-permute-start = (bf16[4,64,128]{2,1,0:T(8,128)(2,1)}, bf16[4,64,128]{2,1,0:T(8,128)(2,1)S(1)}, u32[]{:S(2)}, u32[]{:S(2)}) collective-permute-start(bf16[4,64,128]{2,1,0:T(8,128)(2,1)} %get-tuple-element.67), channel_id=1, source_target_pairs={{1,0},{2,1},{3,2},{4,3},{5,4},{6,5},{7,6},{0,7},{9,8},{10,9},{11,1... | collective-permute-start | bytes 196616 | tf_op jit(solution)/shard_map/ppermute | solution.py:50
  8.5 2.7 %collective-permute-start.3 = (bf16[4,64,128]{2,1,0:T(8,128)(2,1)}, bf16[4,64,128]{2,1,0:T(8,128)(2,1)S(1)}, u32[]{:S(2)}, u32[]{:S(2)}) collective-permute-start(bf16[4,64,128]{2,1,0:T(8,128)(2,1)} %get-tuple-element.70), channel_id=1, source_target_pairs={{4,0},{5,1},{6,2},{7,3},{0,4},{1,5},{2,6},{3,7},{12,8},{13,9},{14,... | collective-permute-start | bytes 196616 | tf_op jit(solution)/shard_map/ppermute | solution.py:50
  11.2 5.0 %shard_map.95 = (bf16[4,64,4,256]{3,2,1,0:T(4,128)(2,1)}, bf16[4,64,4,256]{3,2,1,0:T(4,128)(2,1)}, bf16[4,64,4,256]{3,2,1,0:T(4,128)(2,1)}, bf16[4,64,4,256]{3,2,1,0:T(4,128)(2,1)}) custom-call(s32[88]{0:T(128)} %get-tuple-element.66.table, bf16[16,64,4,256]{3,2,1,0:T(4,128)(2,1)} %inverses.1), custom_call_target="tpu_custom_call" | custom-call | bytes 4194304 | tf_op jit(solution)/shard_map/pallas_call | solution.py:33
  16.2 2.2 %shard_map.96.blocks.side = bf16[1024,2048]{1,0:T(8,128)(2,1)S(1)} custom-call(bf16[2048,2048]{1,0:T(8,128)(2,1)} %dosage.2), custom_call_target="tpu_custom_call" | custom-call | bytes 12582912 | tf_op jit(solution)/shard_map/pallas_call | solution.py:33
  19.1 2.5 %collective-permute-start.6 = (bf16[8,64,128]{2,1,0:T(8,128)(2,1)S(1)}, bf16[8,64,128]{2,1,0:T(8,128)(2,1)S(1)}, u32[]{:S(2)}, u32[]{:S(2)}) collective-permute-start(bf16[8,64,128]{2,1,0:T(8,128)(2,1)S(1)} %shard_map.97.refs_0_), channel_id=1, source_target_pairs={{0,24},{8,16},{16,8},{24,0},{1,25},{9,17},{17,9},{25,1},{2,26},{10... | collective-permute-start | bytes 393224 | tf_op jit(solution)/shard_map/ppermute | solution.py:55
  22.6 3.1 %collective-permute-done.6.refs_3_ = bf16[8,64,128]{2,1,0:T(8,128)(2,1)S(1)} collective-permute-done((bf16[8,64,128]{2,1,0:T(8,128)(2,1)S(1)}, bf16[8,64,128]{2,1,0:T(8,128)(2,1)S(1)}, u32[]{:S(2)}, u32[]{:S(2)}) %collective-permute-start.6) | collective-permute-done | bytes 131104 | tf_op jit(solution)/shard_map/ppermute | solution.py:55
  27.6 3.4 %shard_map.98 = (bf16[4,256,128]{2,1,0:T(8,128)(2,1)S(1)}, bf16[1024,2048]{1,0:T(8,128)(2,1)S(1)}) custom-call(bf16[2048,2048]{1,0:T(8,128)(2,1)} %dosage.2, bf16[1024,2048]{1,0:T(8,128)(2,1)S(1)} %shard_map.96.blocks.side, bf16[8,64,128]{2,1,0:T(8,128)(2,1)S(1)} %shard_map.97.refs_0_, bf16[8,64,128]{2,1,0:T(8,128)(2,1)S(1)} %collective-permute-done.4.refs_1_, ...), custom_call_target="tpu_custom_call" | custom-call | flops 536870912 | bytes 17563648 | tf_op jit(solution)/shard_map/pallas_call | solution.py:33
  32.8 2.0 %collective-permute-start.10 = (bf16[256,128]{1,0:T(8,128)(2,1)S(1)}, bf16[256,128]{1,0:T(8,128)(2,1)S(1)}, u32[]{:S(2)}, u32[]{:S(2)}) collective-permute-start(bf16[256,128]{1,0:T(8,128)(2,1)S(1)} %get-tuple-element.140), channel_id=1, source_target_pairs={{0,6},{1,7},{2,4},{3,5},{4,2},{5,3},{6,0},{7,1},{8,14},{9,15},{10,... | collective-permute-start | bytes 196616 | tf_op jit(solution)/shard_map/ppermute | solution.py:55
  39.8 2.7 %collective-permute-done.9 = bf16[256,128]{1,0:T(8,128)(2,1)S(1)} collective-permute-done((bf16[256,128]{1,0:T(8,128)(2,1)S(1)}, bf16[256,128]{1,0:T(8,128)(2,1)S(1)}, u32[]{:S(2)}, u32[]{:S(2)}) %collective-permute-start.9) | collective-permute-done | bytes 65568 | tf_op jit(solution)/shard_map/ppermute | solution.py:55
  42.6 1.9 %collective-permute-start.13 = (bf16[256,128]{1,0:T(8,128)(2,1)S(1)}, bf16[256,128]{1,0:T(8,128)(2,1)S(1)}, u32[]{:S(2)}, u32[]{:S(2)}) collective-permute-start(bf16[256,128]{1,0:T(8,128)(2,1)S(1)} %fusion.7.refs_0_), channel_id=1, source_target_pairs={{0,6},{1,7},{2,4},{3,5},{4,2},{5,3},{6,0},{7,1},{8,14},{9,15},{10,... | collective-permute-start | bytes 196616 | tf_op jit(solution)/shard_map/ppermute | solution.py:55
  44.6 5.0 %collective-permute-done.13.refs_3_ = bf16[256,128]{1,0:T(8,128)(2,1)S(1)} collective-permute-done((bf16[256,128]{1,0:T(8,128)(2,1)S(1)}, bf16[256,128]{1,0:T(8,128)(2,1)S(1)}, u32[]{:S(2)}, u32[]{:S(2)}) %collective-permute-start.13) | collective-permute-done | bytes 65568 | tf_op jit(solution)/shard_map/ppermute | solution.py:55
  49.6 2.2 %collective-permute-done.12.refs_2_ = bf16[256,128]{1,0:T(8,128)(2,1)S(1)} collective-permute-done((bf16[256,128]{1,0:T(8,128)(2,1)S(1)}, bf16[256,128]{1,0:T(8,128)(2,1)S(1)}, u32[]{:S(2)}, u32[]{:S(2)}) %collective-permute-start.12) | collective-permute-done | bytes 65568 | tf_op jit(solution)/shard_map/ppermute | solution.py:55
  51.8 2.0 %collective-permute-done.11.refs_1_ = bf16[256,128]{1,0:T(8,128)(2,1)S(1)} collective-permute-done((bf16[256,128]{1,0:T(8,128)(2,1)S(1)}, bf16[256,128]{1,0:T(8,128)(2,1)S(1)}, u32[]{:S(2)}, u32[]{:S(2)}) %collective-permute-start.11) | collective-permute-done | bytes 65568 | tf_op jit(solution)/shard_map/ppermute | solution.py:55
  61.2 3.9 %collective-permute-done.18.refs_1_ = bf16[8,64,128]{2,1,0:T(8,128)(2,1)S(1)} collective-permute-done((bf16[8,64,128]{2,1,0:T(8,128)(2,1)S(1)}, bf16[8,64,128]{2,1,0:T(8,128)(2,1)S(1)}, u32[]{:S(2)}, u32[]{:S(2)}) %collective-permute-start.18) | collective-permute-done | bytes 131104 | tf_op jit(solution)/shard_map/ppermute | solution.py:55
  71.6 2.0 %collective-permute-start.25 = (bf16[4,64,128]{2,1,0:T(8,128)(2,1)S(1)}, bf16[4,64,128]{2,1,0:T(8,128)(2,1)S(1)}, u32[]{:S(2)}, u32[]{:S(2)}) collective-permute-start(bf16[4,64,128]{2,1,0:T(8,128)(2,1)S(1)} %get-tuple-element.88), channel_id=1, source_target_pairs={{0,10},{1,13},{2,12},{3,15},{4,14},{5,9},{6,8},{7,11},{8,3},{9,2},... | collective-permute-start | bytes 196616 | tf_op jit(solution)/shard_map/ppermute | solution.py:88
  73.6 3.5 %collective-permute-done.24.refs_4_ = bf16[4,64,128]{2,1,0:T(8,128)(2,1)S(1)} collective-permute-done((bf16[4,64,128]{2,1,0:T(8,128)(2,1)S(1)}, bf16[4,64,128]{2,1,0:T(8,128)(2,1)S(1)}, u32[]{:S(2)}, u32[]{:S(2)}) %collective-permute-start.24) | collective-permute-done | bytes 65568 | tf_op jit(solution)/shard_map/ppermute | solution.py:88
  78.3 3.2 %collective-permute-start.27 = (bf16[4,64,128]{2,1,0:T(8,128)(2,1)}, bf16[4,64,128]{2,1,0:T(8,128)(2,1)S(1)}, u32[]{:S(2)}, u32[]{:S(2)}) collective-permute-start(bf16[4,64,128]{2,1,0:T(8,128)(2,1)} %get-tuple-element.90), channel_id=1, source_target_pairs={{0,28},{1,27},{2,30},{3,29},{4,24},{5,31},{6,26},{7,25},{8,17},{9,... | collective-permute-start | bytes 196616 | tf_op jit(solution)/shard_map/ppermute | solution.py:88
  88.5 3.2 %collective-permute-start.33 = (bf16[4,64,128]{2,1,0:T(8,128)(2,1)S(1)}, bf16[4,64,128]{2,1,0:T(8,128)(2,1)S(1)}, u32[]{:S(2)}, u32[]{:S(2)}) collective-permute-start(bf16[4,64,128]{2,1,0:T(8,128)(2,1)S(1)} %get-tuple-element.111), channel_id=1, source_target_pairs={{0,23},{1,22},{2,17},{3,16},{4,19},{5,18},{6,21},{7,20},{8,30},{9,... | collective-permute-start | bytes 196616 | tf_op jit(solution)/shard_map/ppermute | solution.py:98
  94.1 5.9 %collective-permute-done.34.refs_3_ = bf16[4,64,128]{2,1,0:T(8,128)(2,1)S(1)} collective-permute-done((bf16[4,64,128]{2,1,0:T(8,128)(2,1)S(1)}, bf16[4,64,128]{2,1,0:T(8,128)(2,1)S(1)}, u32[]{:S(2)}, u32[]{:S(2)}) %collective-permute-start.34) | collective-permute-done | bytes 65568 | tf_op jit(solution)/shard_map/ppermute | solution.py:98
  104.2 2.5 %collective-permute-done.37.refs_3_ = bf16[8,64,128]{2,1,0:T(8,128)(2,1)S(1)} collective-permute-done((bf16[8,64,128]{2,1,0:T(8,128)(2,1)S(1)}, bf16[8,64,128]{2,1,0:T(8,128)(2,1)S(1)}, u32[]{:S(2)}, u32[]{:S(2)}) %collective-permute-start.37) | collective-permute-done | bytes 131104 | tf_op jit(solution)/shard_map/ppermute | solution.py:55
  115.5 2.9 %collective-permute-done.41 = bf16[256,128]{1,0:T(8,128)(2,1)S(1)} collective-permute-done((bf16[256,128]{1,0:T(8,128)(2,1)S(1)}, bf16[256,128]{1,0:T(8,128)(2,1)S(1)}, u32[]{:S(2)}, u32[]{:S(2)}) %collective-permute-start.41) | collective-permute-done | bytes 65568 | tf_op jit(solution)/shard_map/ppermute | solution.py:55
  118.4 2.7 %collective-permute-done.40 = bf16[256,128]{1,0:T(8,128)(2,1)S(1)} collective-permute-done((bf16[256,128]{1,0:T(8,128)(2,1)S(1)}, bf16[256,128]{1,0:T(8,128)(2,1)S(1)}, u32[]{:S(2)}, u32[]{:S(2)}) %collective-permute-start.40) | collective-permute-done | bytes 65568 | tf_op jit(solution)/shard_map/ppermute | solution.py:55
  121.2 2.3 %collective-permute-start.44 = (bf16[256,128]{1,0:T(8,128)(2,1)S(1)}, bf16[256,128]{1,0:T(8,128)(2,1)S(1)}, u32[]{:S(2)}, u32[]{:S(2)}) collective-permute-start(bf16[256,128]{1,0:T(8,128)(2,1)S(1)} %get-tuple-element.130.refs_0_), channel_id=1, source_target_pairs={{0,6},{1,7},{2,4},{3,5},{4,2},{5,3},{6,0},{7,1},{8,14},{9,15},{10,... | collective-permute-start | bytes 196616 | tf_op jit(solution)/shard_map/ppermute | solution.py:55
  123.5 2.2 %collective-permute-start.42 = (bf16[256,128]{1,0:T(8,128)(2,1)S(1)}, bf16[256,128]{1,0:T(8,128)(2,1)S(1)}, u32[]{:S(2)}, u32[]{:S(2)}) collective-permute-start(bf16[256,128]{1,0:T(8,128)(2,1)S(1)} %get-tuple-element.130.refs_0_), channel_id=1, source_target_pairs={{0,2},{1,3},{2,0},{3,1},{4,6},{5,7},{6,4},{7,5},{8,10},{9,11},{10,... | collective-permute-start | bytes 196616 | tf_op jit(solution)/shard_map/ppermute | solution.py:55
  125.7 2.0 %collective-permute-done.44.refs_3_ = bf16[256,128]{1,0:T(8,128)(2,1)S(1)} collective-permute-done((bf16[256,128]{1,0:T(8,128)(2,1)S(1)}, bf16[256,128]{1,0:T(8,128)(2,1)S(1)}, u32[]{:S(2)}, u32[]{:S(2)}) %collective-permute-start.44) | collective-permute-done | bytes 65568 | tf_op jit(solution)/shard_map/ppermute | solution.py:55
  127.7 1.9 %collective-permute-done.43.refs_2_ = bf16[256,128]{1,0:T(8,128)(2,1)S(1)} collective-permute-done((bf16[256,128]{1,0:T(8,128)(2,1)S(1)}, bf16[256,128]{1,0:T(8,128)(2,1)S(1)}, u32[]{:S(2)}, u32[]{:S(2)}) %collective-permute-start.43) | collective-permute-done | bytes 65568 | tf_op jit(solution)/shard_map/ppermute | solution.py:55
  135.6 2.9 %collective-permute-done.49.refs_1_ = bf16[8,64,128]{2,1,0:T(8,128)(2,1)S(1)} collective-permute-done((bf16[8,64,128]{2,1,0:T(8,128)(2,1)S(1)}, bf16[8,64,128]{2,1,0:T(8,128)(2,1)S(1)}, u32[]{:S(2)}, u32[]{:S(2)}) %collective-permute-start.49) | collective-permute-done | bytes 131104 | tf_op jit(solution)/shard_map/ppermute | solution.py:55
  138.5 3.0 %collective-permute-done.50.refs_2_ = bf16[8,64,128]{2,1,0:T(8,128)(2,1)S(1)} collective-permute-done((bf16[8,64,128]{2,1,0:T(8,128)(2,1)S(1)}, bf16[8,64,128]{2,1,0:T(8,128)(2,1)S(1)}, u32[]{:S(2)}, u32[]{:S(2)}) %collective-permute-start.50) | collective-permute-done | bytes 131104 | tf_op jit(solution)/shard_map/ppermute | solution.py:55
  143.9 4.4 %collective-permute-start.55 = (bf16[4,64,128]{2,1,0:T(8,128)(2,1)S(1)}, bf16[4,64,128]{2,1,0:T(8,128)(2,1)S(1)}, u32[]{:S(2)}, u32[]{:S(2)}) collective-permute-start(bf16[4,64,128]{2,1,0:T(8,128)(2,1)S(1)} %get-tuple-element.120), channel_id=1, source_target_pairs={{0,28},{1,27},{2,30},{3,29},{4,24},{5,31},{6,26},{7,25},{8,17},{9,... | collective-permute-start | bytes 196616 | tf_op jit(solution)/shard_map/ppermute | solution.py:88
  152.7 3.0 %collective-permute-start.56 = (bf16[4,64,128]{2,1,0:T(8,128)(2,1)S(1)}, bf16[4,64,128]{2,1,0:T(8,128)(2,1)S(1)}, u32[]{:S(2)}, u32[]{:S(2)}) collective-permute-start(bf16[4,64,128]{2,1,0:T(8,128)(2,1)S(1)} %get-tuple-element.126), channel_id=1, source_target_pairs={{0,8},{8,0},{16,24},{24,16},{1,9},{9,1},{17,25},{25,17},{2,10},{10... | collective-permute-start | bytes 196616 | tf_op jit(solution)/shard_map/ppermute | solution.py:55
  158.6 2.0 %collective-permute-done.57.refs_2_ = bf16[4,64,128]{2,1,0:T(8,128)(2,1)S(1)} collective-permute-done((bf16[4,64,128]{2,1,0:T(8,128)(2,1)S(1)}, bf16[4,64,128]{2,1,0:T(8,128)(2,1)S(1)}, u32[]{:S(2)}, u32[]{:S(2)}) %collective-permute-start.57) | collective-permute-done | bytes 65568 | tf_op jit(solution)/shard_map/ppermute | solution.py:55
  (147 shorter events, 67.0 us)
Async XLA Ops:
  3.3 15.2 %collective-permute-start = (bf16[4,64,128]{2,1,0:T(8,128)(2,1)}, bf16[4,64,128]{2,1,0:T(8,128)(2,1)S(1)}, u32[]{:S(2)}, u32[]{:S(2)}) collective-permute-start(bf16[4,64,128]{2,1,0:T(8,128)(2,1)} %get-tuple-element.67), channel_id=1, source_target_pairs={{1,0},{2,1},{3,2},{4,3},{5,4},{6,5},{7,6},{0,7},{9,8},{10,9},{11,1... | collective-permute-start | bytes 196616 | tf_op jit(solution)/shard_map/ppermute | solution.py:50
  7.9 10.6 %collective-permute-start.1 = (bf16[4,64,128]{2,1,0:T(8,128)(2,1)}, bf16[4,64,128]{2,1,0:T(8,128)(2,1)S(1)}, u32[]{:S(2)}, u32[]{:S(2)}) collective-permute-start(bf16[4,64,128]{2,1,0:T(8,128)(2,1)} %get-tuple-element.68), channel_id=1, source_target_pairs={{2,0},{3,1},{4,2},{5,3},{6,4},{7,5},{0,6},{1,7},{10,8},{11,9},{12,... | collective-permute-start | bytes 196616 | tf_op jit(solution)/shard_map/ppermute | solution.py:50
  8.5 10.0 %collective-permute-start.2 = (bf16[4,64,128]{2,1,0:T(8,128)(2,1)}, bf16[4,64,128]{2,1,0:T(8,128)(2,1)S(1)}, u32[]{:S(2)}, u32[]{:S(2)}) collective-permute-start(bf16[4,64,128]{2,1,0:T(8,128)(2,1)} %get-tuple-element.69), channel_id=1, source_target_pairs={{3,0},{4,1},{5,2},{6,3},{7,4},{0,5},{1,6},{2,7},{11,8},{12,9},{13,... | collective-permute-start | bytes 196616 | tf_op jit(solution)/shard_map/ppermute | solution.py:50
  8.5 10.0 %collective-permute-start.3 = (bf16[4,64,128]{2,1,0:T(8,128)(2,1)}, bf16[4,64,128]{2,1,0:T(8,128)(2,1)S(1)}, u32[]{:S(2)}, u32[]{:S(2)}) collective-permute-start(bf16[4,64,128]{2,1,0:T(8,128)(2,1)} %get-tuple-element.70), channel_id=1, source_target_pairs={{4,0},{5,1},{6,2},{7,3},{0,4},{1,5},{2,6},{3,7},{12,8},{13,9},{14,... | collective-permute-start | bytes 196616 | tf_op jit(solution)/shard_map/ppermute | solution.py:50
  19.1 6.6 %collective-permute-start.6 = (bf16[8,64,128]{2,1,0:T(8,128)(2,1)S(1)}, bf16[8,64,128]{2,1,0:T(8,128)(2,1)S(1)}, u32[]{:S(2)}, u32[]{:S(2)}) collective-permute-start(bf16[8,64,128]{2,1,0:T(8,128)(2,1)S(1)} %shard_map.97.refs_0_), channel_id=1, source_target_pairs={{0,24},{8,16},{16,8},{24,0},{1,25},{9,17},{17,9},{25,1},{2,26},{10... | collective-permute-start | bytes 393224 | tf_op jit(solution)/shard_map/ppermute | solution.py:55
  32.8 7.0 %collective-permute-start.10 = (bf16[256,128]{1,0:T(8,128)(2,1)S(1)}, bf16[256,128]{1,0:T(8,128)(2,1)S(1)}, u32[]{:S(2)}, u32[]{:S(2)}) collective-permute-start(bf16[256,128]{1,0:T(8,128)(2,1)S(1)} %get-tuple-element.140), channel_id=1, source_target_pairs={{0,6},{1,7},{2,4},{3,5},{4,2},{5,3},{6,0},{7,1},{8,14},{9,15},{10,... | collective-permute-start | bytes 196616 | tf_op jit(solution)/shard_map/ppermute | solution.py:55
  34.9 7.6 %collective-permute-start.9 = (bf16[256,128]{1,0:T(8,128)(2,1)S(1)}, bf16[256,128]{1,0:T(8,128)(2,1)S(1)}, u32[]{:S(2)}, u32[]{:S(2)}) collective-permute-start(bf16[256,128]{1,0:T(8,128)(2,1)S(1)} %get-tuple-element.141), channel_id=1, source_target_pairs={{0,4},{1,5},{2,6},{3,7},{4,0},{5,1},{6,2},{7,3},{8,12},{9,13},{10,... | collective-permute-start | bytes 196616 | tf_op jit(solution)/shard_map/ppermute | solution.py:55
  36.3 22.3 %collective-permute-start.21 = (bf16[4,64,4,256]{3,2,1,0:T(4,128)(2,1)S(1)}, bf16[4,64,4,256]{3,2,1,0:T(4,128)(2,1)S(1)}, u32[]{:S(2)}, u32[]{:S(2)}) collective-permute-start(bf16[4,64,4,256]{3,2,1,0:T(4,128)(2,1)S(1)} %copy-done.14), channel_id=1, source_target_pairs={{0,8},{8,0},{16,24},{24,16},{1,9},{9,1},{17,25},{25,17},{2,10},{10... | collective-permute-start | bytes 1572872 | tf_op jit(solution)/shard_map/ppermute | solution.py:55
  37.8 33.7 %collective-permute-start.22 = (bf16[4,64,4,256]{3,2,1,0:T(4,128)(2,1)S(1)}, bf16[4,64,4,256]{3,2,1,0:T(4,128)(2,1)S(1)}, u32[]{:S(2)}, u32[]{:S(2)}) collective-permute-start(bf16[4,64,4,256]{3,2,1,0:T(4,128)(2,1)S(1)} %copy-done.13), channel_id=1, source_target_pairs={{0,16},{8,24},{16,0},{24,8},{1,17},{9,25},{17,1},{25,9},{2,18},{10... | collective-permute-start | bytes 1572872 | tf_op jit(solution)/shard_map/ppermute | solution.py:55
  38.5 33.0 %collective-permute-start.23 = (bf16[4,64,4,256]{3,2,1,0:T(4,128)(2,1)S(1)}, bf16[4,64,4,256]{3,2,1,0:T(4,128)(2,1)S(1)}, u32[]{:S(2)}, u32[]{:S(2)}) collective-permute-start(bf16[4,64,4,256]{3,2,1,0:T(4,128)(2,1)S(1)} %copy-done.12), channel_id=1, source_target_pairs={{0,24},{8,16},{16,8},{24,0},{1,25},{9,17},{17,9},{25,1},{2,26},{10... | collective-permute-start | bytes 1572872 | tf_op jit(solution)/shard_map/ppermute | solution.py:55
  42.6 6.9 %collective-permute-start.13 = (bf16[256,128]{1,0:T(8,128)(2,1)S(1)}, bf16[256,128]{1,0:T(8,128)(2,1)S(1)}, u32[]{:S(2)}, u32[]{:S(2)}) collective-permute-start(bf16[256,128]{1,0:T(8,128)(2,1)S(1)} %fusion.7.refs_0_), channel_id=1, source_target_pairs={{0,6},{1,7},{2,4},{3,5},{4,2},{5,3},{6,0},{7,1},{8,14},{9,15},{10,... | collective-permute-start | bytes 196616 | tf_op jit(solution)/shard_map/ppermute | solution.py:55
  44.6 7.2 %collective-permute-start.12 = (bf16[256,128]{1,0:T(8,128)(2,1)S(1)}, bf16[256,128]{1,0:T(8,128)(2,1)S(1)}, u32[]{:S(2)}, u32[]{:S(2)}) collective-permute-start(bf16[256,128]{1,0:T(8,128)(2,1)S(1)} %fusion.7.refs_0_), channel_id=1, source_target_pairs={{0,4},{1,5},{2,6},{3,7},{4,0},{5,1},{6,2},{7,3},{8,12},{9,13},{10,... | collective-permute-start | bytes 196616 | tf_op jit(solution)/shard_map/ppermute | solution.py:55
  56.3 8.8 %collective-permute-start.18 = (bf16[8,64,128]{2,1,0:T(8,128)(2,1)S(1)}, bf16[8,64,128]{2,1,0:T(8,128)(2,1)S(1)}, u32[]{:S(2)}, u32[]{:S(2)}) collective-permute-start(bf16[8,64,128]{2,1,0:T(8,128)(2,1)S(1)} %get-tuple-element.84), channel_id=1, source_target_pairs={{0,8},{8,0},{16,24},{24,16},{1,9},{9,1},{17,25},{25,17},{2,10},{10... | collective-permute-start | bytes 393224 | tf_op jit(solution)/shard_map/ppermute | solution.py:55
  57.9 8.7 %collective-permute-start.19 = (bf16[8,64,128]{2,1,0:T(8,128)(2,1)S(1)}, bf16[8,64,128]{2,1,0:T(8,128)(2,1)S(1)}, u32[]{:S(2)}, u32[]{:S(2)}) collective-permute-start(bf16[8,64,128]{2,1,0:T(8,128)(2,1)S(1)} %get-tuple-element.85), channel_id=1, source_target_pairs={{0,16},{8,24},{16,0},{24,8},{1,17},{9,25},{17,1},{25,9},{2,18},{10... | collective-permute-start | bytes 393224 | tf_op jit(solution)/shard_map/ppermute | solution.py:55
  58.6 10.2 %collective-permute-start.20 = (bf16[8,64,128]{2,1,0:T(8,128)(2,1)S(1)}, bf16[8,64,128]{2,1,0:T(8,128)(2,1)S(1)}, u32[]{:S(2)}, u32[]{:S(2)}) collective-permute-start(bf16[8,64,128]{2,1,0:T(8,128)(2,1)S(1)} %get-tuple-element.86), channel_id=1, source_target_pairs={{0,24},{8,16},{16,8},{24,0},{1,25},{9,17},{17,9},{25,1},{2,26},{10... | collective-permute-start | bytes 393224 | tf_op jit(solution)/shard_map/ppermute | solution.py:55
  65.1 20.7 %collective-permute-start.28 = (bf16[3,4,64,128]{3,2,1,0:T(8,128)(2,1)}, bf16[3,4,64,128]{3,2,1,0:T(8,128)(2,1)S(1)}, u32[]{:S(2)}, u32[]{:S(2)}) collective-permute-start(bf16[3,4,64,128]{3,2,1,0:T(8,128)(2,1)} %get-tuple-element.106), channel_id=1, source_target_pairs={{0,8},{8,0},{16,24},{24,16},{1,9},{9,1},{17,25},{25,17},{2,10},{10... | collective-permute-start | bytes 589832 | tf_op jit(solution)/shard_map/ppermute | solution.py:55
  66.6 19.2 %collective-permute-start.29 = (bf16[3,4,64,128]{3,2,1,0:T(8,128)(2,1)S(1)}, bf16[3,4,64,128]{3,2,1,0:T(8,128)(2,1)S(1)}, u32[]{:S(2)}, u32[]{:S(2)}) collective-permute-start(bf16[3,4,64,128]{3,2,1,0:T(8,128)(2,1)S(1)} %get-tuple-element.107), channel_id=1, source_target_pairs={{0,16},{8,24},{16,0},{24,8},{1,17},{9,25},{17,1},{25,9},{2,18},{10... | collective-permute-start | bytes 589832 | tf_op jit(solution)/shard_map/ppermute | solution.py:55
  68.8 17.0 %collective-permute-start.30 = (bf16[3,4,64,128]{3,2,1,0:T(8,128)(2,1)S(1)}, bf16[3,4,64,128]{3,2,1,0:T(8,128)(2,1)S(1)}, u32[]{:S(2)}, u32[]{:S(2)}) collective-permute-start(bf16[3,4,64,128]{3,2,1,0:T(8,128)(2,1)S(1)} %get-tuple-element.108), channel_id=1, source_target_pairs={{0,24},{8,16},{16,8},{24,0},{1,25},{9,17},{17,9},{25,1},{2,26},{10... | collective-permute-start | bytes 589832 | tf_op jit(solution)/shard_map/ppermute | solution.py:55
  71.6 6.7 %collective-permute-start.25 = (bf16[4,64,128]{2,1,0:T(8,128)(2,1)S(1)}, bf16[4,64,128]{2,1,0:T(8,128)(2,1)S(1)}, u32[]{:S(2)}, u32[]{:S(2)}) collective-permute-start(bf16[4,64,128]{2,1,0:T(8,128)(2,1)S(1)} %get-tuple-element.88), channel_id=1, source_target_pairs={{0,10},{1,13},{2,12},{3,15},{4,14},{5,9},{6,8},{7,11},{8,3},{9,2},... | collective-permute-start | bytes 196616 | tf_op jit(solution)/shard_map/ppermute | solution.py:88
  77.0 7.9 %collective-permute-start.26 = (bf16[4,64,128]{2,1,0:T(8,128)(2,1)}, bf16[4,64,128]{2,1,0:T(8,128)(2,1)S(1)}, u32[]{:S(2)}, u32[]{:S(2)}) collective-permute-start(bf16[4,64,128]{2,1,0:T(8,128)(2,1)} %get-tuple-element.89), channel_id=1, source_target_pairs={{0,17},{1,20},{2,19},{3,22},{4,21},{5,16},{6,23},{7,18},{8,28},{9,... | collective-permute-start | bytes 196616 | tf_op jit(solution)/shard_map/ppermute | solution.py:88
  78.3 7.5 %collective-permute-start.27 = (bf16[4,64,128]{2,1,0:T(8,128)(2,1)}, bf16[4,64,128]{2,1,0:T(8,128)(2,1)S(1)}, u32[]{:S(2)}, u32[]{:S(2)}) collective-permute-start(bf16[4,64,128]{2,1,0:T(8,128)(2,1)} %get-tuple-element.90), channel_id=1, source_target_pairs={{0,28},{1,27},{2,30},{3,29},{4,24},{5,31},{6,26},{7,25},{8,17},{9,... | collective-permute-start | bytes 196616 | tf_op jit(solution)/shard_map/ppermute | solution.py:88
  86.7 7.4 %collective-permute-start.32 = (bf16[4,64,128]{2,1,0:T(8,128)(2,1)S(1)}, bf16[4,64,128]{2,1,0:T(8,128)(2,1)S(1)}, u32[]{:S(2)}, u32[]{:S(2)}) collective-permute-start(bf16[4,64,128]{2,1,0:T(8,128)(2,1)S(1)} %get-tuple-element.110), channel_id=1, source_target_pairs={{0,15},{1,14},{2,9},{3,8},{4,11},{5,10},{6,13},{7,12},{8,6},{9,5},... | collective-permute-start | bytes 196616 | tf_op jit(solution)/shard_map/ppermute | solution.py:98
  91.7 8.3 %collective-permute-start.34 = (bf16[4,64,128]{2,1,0:T(8,128)(2,1)S(1)}, bf16[4,64,128]{2,1,0:T(8,128)(2,1)S(1)}, u32[]{:S(2)}, u32[]{:S(2)}) collective-permute-start(bf16[4,64,128]{2,1,0:T(8,128)(2,1)S(1)} %get-tuple-element.112), channel_id=1, source_target_pairs={{0,31},{1,30},{2,25},{3,24},{4,27},{5,26},{6,29},{7,28},{8,22},{9,... | collective-permute-start | bytes 196616 | tf_op jit(solution)/shard_map/ppermute | solution.py:98
  100.7 6.4 %collective-permute-start.36 = (bf16[8,64,128]{2,1,0:T(8,128)(2,1)S(1)}, bf16[8,64,128]{2,1,0:T(8,128)(2,1)S(1)}, u32[]{:S(2)}, u32[]{:S(2)}) collective-permute-start(bf16[8,64,128]{2,1,0:T(8,128)(2,1)S(1)} %shard_map.106.refs_0_), channel_id=1, source_target_pairs={{0,16},{8,24},{16,0},{24,8},{1,17},{9,25},{17,1},{25,9},{2,18},{10... | collective-permute-start | bytes 393224 | tf_op jit(solution)/shard_map/ppermute | solution.py:55
  111.9 6.6 %collective-permute-start.41 = (bf16[256,128]{1,0:T(8,128)(2,1)S(1)}, bf16[256,128]{1,0:T(8,128)(2,1)S(1)}, u32[]{:S(2)}, u32[]{:S(2)}) collective-permute-start(bf16[256,128]{1,0:T(8,128)(2,1)S(1)} %get-tuple-element.137), channel_id=1, source_target_pairs={{0,6},{1,7},{2,4},{3,5},{4,2},{5,3},{6,0},{7,1},{8,14},{9,15},{10,... | collective-permute-start | bytes 196616 | tf_op jit(solution)/shard_map/ppermute | solution.py:55
  113.7 7.4 %collective-permute-start.40 = (bf16[256,128]{1,0:T(8,128)(2,1)S(1)}, bf16[256,128]{1,0:T(8,128)(2,1)S(1)}, u32[]{:S(2)}, u32[]{:S(2)}) collective-permute-start(bf16[256,128]{1,0:T(8,128)(2,1)S(1)} %get-tuple-element.138), channel_id=1, source_target_pairs={{0,4},{1,5},{2,6},{3,7},{4,0},{5,1},{6,2},{7,3},{8,12},{9,13},{10,... | collective-permute-start | bytes 196616 | tf_op jit(solution)/shard_map/ppermute | solution.py:55
  121.2 6.5 %collective-permute-start.44 = (bf16[256,128]{1,0:T(8,128)(2,1)S(1)}, bf16[256,128]{1,0:T(8,128)(2,1)S(1)}, u32[]{:S(2)}, u32[]{:S(2)}) collective-permute-start(bf16[256,128]{1,0:T(8,128)(2,1)S(1)} %get-tuple-element.130.refs_0_), channel_id=1, source_target_pairs={{0,6},{1,7},{2,4},{3,5},{4,2},{5,3},{6,0},{7,1},{8,14},{9,15},{10,... | collective-permute-start | bytes 196616 | tf_op jit(solution)/shard_map/ppermute | solution.py:55
  133.2 8.3 %collective-permute-start.50 = (bf16[8,64,128]{2,1,0:T(8,128)(2,1)S(1)}, bf16[8,64,128]{2,1,0:T(8,128)(2,1)S(1)}, u32[]{:S(2)}, u32[]{:S(2)}) collective-permute-start(bf16[8,64,128]{2,1,0:T(8,128)(2,1)S(1)} %get-tuple-element.115), channel_id=1, source_target_pairs={{0,16},{8,24},{16,0},{24,8},{1,17},{9,25},{17,1},{25,9},{2,18},{10... | collective-permute-start | bytes 393224 | tf_op jit(solution)/shard_map/ppermute | solution.py:55
  134.0 7.5 %collective-permute-start.51 = (bf16[8,64,128]{2,1,0:T(8,128)(2,1)S(1)}, bf16[8,64,128]{2,1,0:T(8,128)(2,1)S(1)}, u32[]{:S(2)}, u32[]{:S(2)}) collective-permute-start(bf16[8,64,128]{2,1,0:T(8,128)(2,1)S(1)} %get-tuple-element.116), channel_id=1, source_target_pairs={{0,24},{8,16},{16,8},{24,0},{1,25},{9,17},{17,9},{25,1},{2,26},{10... | collective-permute-start | bytes 393224 | tf_op jit(solution)/shard_map/ppermute | solution.py:55
  142.2 7.2 %collective-permute-start.53 = (bf16[4,64,128]{2,1,0:T(8,128)(2,1)S(1)}, bf16[4,64,128]{2,1,0:T(8,128)(2,1)S(1)}, u32[]{:S(2)}, u32[]{:S(2)}) collective-permute-start(bf16[4,64,128]{2,1,0:T(8,128)(2,1)S(1)} %get-tuple-element.118), channel_id=1, source_target_pairs={{0,10},{1,13},{2,12},{3,15},{4,14},{5,9},{6,8},{7,11},{8,3},{9,2},... | collective-permute-start | bytes 196616 | tf_op jit(solution)/shard_map/ppermute | solution.py:88
  143.9 7.4 %collective-permute-start.54 = (bf16[4,64,128]{2,1,0:T(8,128)(2,1)S(1)}, bf16[4,64,128]{2,1,0:T(8,128)(2,1)S(1)}, u32[]{:S(2)}, u32[]{:S(2)}) collective-permute-start(bf16[4,64,128]{2,1,0:T(8,128)(2,1)S(1)} %get-tuple-element.119), channel_id=1, source_target_pairs={{0,17},{1,20},{2,19},{3,22},{4,21},{5,16},{6,23},{7,18},{8,28},{9,... | collective-permute-start | bytes 196616 | tf_op jit(solution)/shard_map/ppermute | solution.py:88
  143.9 8.1 %collective-permute-start.55 = (bf16[4,64,128]{2,1,0:T(8,128)(2,1)S(1)}, bf16[4,64,128]{2,1,0:T(8,128)(2,1)S(1)}, u32[]{:S(2)}, u32[]{:S(2)}) collective-permute-start(bf16[4,64,128]{2,1,0:T(8,128)(2,1)S(1)} %get-tuple-element.120), channel_id=1, source_target_pairs={{0,28},{1,27},{2,30},{3,29},{4,24},{5,31},{6,26},{7,25},{8,17},{9,... | collective-permute-start | bytes 196616 | tf_op jit(solution)/shard_map/ppermute | solution.py:88
  (42 other events, 367.9 us)
